TPU v7x, 32 devices: a whole 2x2x4 slice. The times are simulated.
32 devices in a mesh: fsdp: 8 (over z, y), replica: 4 (over x, core).
Axes of the slice: x: 2, y: 2, z: 4, core: 2. Of those that a mesh axis runs over, the one named last changes fastest.
Arguments:
- layer_stack: bfloat16 [2, 32, 64, 9, 1024], P(None, ('fsdp', 'replica')), may hold values from -6 to 6
- out_cotangent: bfloat16 [2, 32, 64, 1024], P(None, ('fsdp', 'replica')), may hold values from -6 to 6
- pic_start: int32 [2, 32], P(None, ('fsdp', 'replica')), may hold values from 0 to 32, as said below
- doc_split: int32 [2, 32], P(None, ('fsdp', 'replica')), may hold values from 16 to 64, as said below
- mix_gain: float32 [1024], replicated, may hold values from 0.25 to 1.75
- mix_up: bfloat16 [1024, 36], P('fsdp'), may hold values from -0.1875 to 0.1875
- mix_down: float32 [36, 36], replicated, may hold values from -1 to 1
- mix_static: float32 [4, 9], replicated, may hold values from -1 to 1
- norm_gain: float32 [4, 1024], replicated, may hold values from 0.25 to 1.75
- norm_bias: float32 [4, 1024], replicated, may hold values from -2 to 2
- query_key_value: bfloat16 [3, 1024, 1024], P(None, 'fsdp'), may hold values from -0.1875 to 0.1875
- out_weight: bfloat16 [1024, 1024], P('fsdp'), may hold values from -0.75 to 0.75
- up_weight: bfloat16 [1024, 4096], P('fsdp'), may hold values from -0.1875 to 0.1875
- down_weight: bfloat16 [4096, 1024], P('fsdp'), may hold values from -0.125 to 0.125
Outputs:
- layer_output: bfloat16 [2, 32, 64, 1024], P(None, ('fsdp', 'replica'))
- coefficients: float32 [2, 32, 64, 4, 9], P(None, ('fsdp', 'replica'))
- stack_grad: bfloat16 [2, 32, 64, 9, 1024], P(None, ('fsdp', 'replica'))
- mix_gain_grad: float32 [1024], replicated
- mix_up_grad: float32 [1024, 36], P('fsdp')
- mix_down_grad: float32 [36, 36], replicated
- mix_static_grad: float32 [4, 9], replicated
- norm_gain_grad: float32 [4, 1024], replicated
- norm_bias_grad: float32 [4, 1024], replicated
- projection_grad: float32 [3, 1024, 1024], P(None, 'fsdp')
- out_weight_grad: float32 [1024, 1024], P('fsdp')
- up_weight_grad: float32 [1024, 4096], P('fsdp')
- down_weight_grad: float32 [4096, 1024], P('fsdp')
Inputs may be any that keep to these rules, and one draw needn't show every extreme that they name: `pic_start`: a multiple of 16; the picture span lies inside its sequence. `doc_split`: a multiple of 16; 64 means a single document.
All inputs are finite; a program needn't handle non-finite values.
Results may differ from a plain program's by a relative error of at most 0.015.
Values may be sent and summed in bfloat16 or wider, within the bound.
No kernel may reach another device: no remote copies, remote signals or barrier semaphores. Data moves between devices by JAX's collectives and lax.ppermute only.
A program may use at most 256 MiB of HBM per device.

v0:
```python
import math

import jax
import jax.numpy as jnp
from jax import lax
from jax.sharding import PartitionSpec as P

HEADS = 16
HEAD_DIM = 64
ROTARY = 16
STREAMS_IN = 9
SEQ = 64
PIC = 32


EPSILON = 1e-05
ROOT_HALF = 0.7071067811865476
NORMAL_PEAK = 0.3989422804014327
HIGHEST = lax.Precision.HIGHEST


def as_sent(value):

    def short(part):
        return part.astype(jnp.bfloat16) if part.dtype == jnp.float32 else part

    return jax.tree.map(short, value)


def gelu_value(values):
    return 0.5 * values * (1.0 + lax.erf(values * ROOT_HALF))


def gelu_slope(values):
    return 0.5 * (1.0 + lax.erf(values * ROOT_HALF)) + values * NORMAL_PEAK * jnp.exp(
        -0.5 * values * values
    )


def matmul(left_side, right_side):
    return jnp.dot(left_side, right_side, preferred_element_type=jnp.float32)


def outer_sum(left_side, right_side):
    return lax.dot_general(
        left_side, right_side, (((0,), (0,)), ((), ())), preferred_element_type=jnp.float32
    )


def back_product(left_side, right_side):
    return lax.dot_general(
        left_side, right_side, (((1,), (1,)), ((), ())), preferred_element_type=jnp.float32
    )


def rotary_tables():
    half_rot = ROTARY // 2
    inverse = jnp.exp(-math.log(10000.0) * (2.0 * jnp.arange(half_rot, dtype=jnp.float32) / ROTARY))
    angles = jnp.arange(SEQ, dtype=jnp.float32)[:, None] * inverse[None, :]
    return (jnp.cos(angles)[:, None, :], jnp.sin(angles)[:, None, :])


def rotate(values, cos_table, sin_table):
    half_rot = ROTARY // 2
    first_half = values[..., :half_rot]
    second = values[..., half_rot:ROTARY]
    return jnp.concatenate(
        [
            first_half * cos_table - second * sin_table,
            second * cos_table + first_half * sin_table,
            values[..., ROTARY:],
        ],
        axis=-1,
    )


def allowed_mask(starts, splits):
    positions = jnp.arange(SEQ, dtype=jnp.int32)
    second_doc = positions[None, :] >= splits[:, None]
    picture = (positions[None, :] >= starts[:, None]) & (positions[None, :] < starts[:, None] + PIC)
    same_doc = second_doc[:, :, None] == second_doc[:, None, :]
    causal = positions[:, None] >= positions[None, :]
    both_pic = picture[:, :, None] & picture[:, None, :]
    return same_doc & (causal[None] | both_pic)


def masked_scores(queries, key_rot, allowed):
    scores = jnp.einsum(
        "nqhe,nkhe->nhqk", queries, key_rot, preferred_element_type=jnp.float32
    ) * HEAD_DIM ** (-0.5)
    return jnp.where(allowed[:, None], scores, -1e30)


def on_device(
    layer_stack,
    out_cotangent,
    pic_start,
    doc_split,
    mix_gain,
    mix_up,
    mix_down,
    mix_static,
    norm_gain,
    norm_bias,
    query_key_value,
    out_weight,
    up_weight,
    down_weight,
):
    micro_total = layer_stack.shape[0]
    local_seqs = layer_stack.shape[1]
    model_width = layer_stack.shape[-1]
    groups = [(index_micro, 1) for index_micro in range(micro_total)]
    cos_table, sin_table = rotary_tables()
    output_list = []
    coef_list = []
    grad_list = []
    shard_total = None
    small_total = None
    for first_micro, micro_count in groups:
        seq_count = micro_count * local_seqs
        row_count = seq_count * SEQ
        head_shape = (seq_count, SEQ, HEADS, HEAD_DIM)
        flat_stack = layer_stack[first_micro : first_micro + micro_count].reshape(
            row_count, STREAMS_IN, model_width
        )
        grad_rows = out_cotangent[first_micro : first_micro + micro_count].reshape(
            row_count, model_width
        )
        starts = pic_start[first_micro : first_micro + micro_count].reshape(seq_count)
        splits = doc_split[first_micro : first_micro + micro_count].reshape(seq_count)
        allowed = allowed_mask(starts, splits)
        mix_up_full, projection_full, out_full = (
            lax.all_gather(mix_up, "fsdp", axis=0, tiled=True),
            lax.all_gather(query_key_value, "fsdp", axis=1, tiled=True),
            lax.all_gather(out_weight, "fsdp", axis=0, tiled=True),
        )
        up_full, down_full = (
            lax.all_gather(up_weight, "fsdp", axis=0, tiled=True),
            lax.all_gather(down_weight, "fsdp", axis=0, tiled=True),
        )
        last_layer = flat_stack[:, STREAMS_IN - 1, :].astype(jnp.float32)
        rms_scale = lax.rsqrt(jnp.mean(last_layer * last_layer, axis=-1, keepdims=True) + EPSILON)
        mixed_in = (last_layer * rms_scale * mix_gain).astype(jnp.bfloat16)
        hidden_pre = matmul(mixed_in, mix_up_full)
        hidden_mix = gelu_value(hidden_pre).astype(jnp.bfloat16)
        hidden_wide = hidden_mix.astype(jnp.float32)
        coef_flat = jnp.dot(hidden_wide, mix_down, precision=HIGHEST) + mix_static.reshape(-1)
        coef_rows = coef_flat.reshape(row_count, 4, STREAMS_IN)
        streams = coef_rows[:, :, 0, None] * flat_stack[:, None, 0, :].astype(jnp.float32)
        for layer_index in range(1, STREAMS_IN):
            streams = streams + coef_rows[:, :, layer_index, None] * flat_stack[
                :, None, layer_index, :
            ].astype(jnp.float32)
        center = streams - jnp.mean(streams, axis=-1, keepdims=True)
        inv_std = lax.rsqrt(jnp.mean(center * center, axis=-1, keepdims=True) + EPSILON)
        scaled = center * inv_std
        normed = (scaled * norm_gain + norm_bias).astype(jnp.bfloat16)
        query_lin = matmul(normed[:, 0], projection_full[0])
        key_lin = matmul(normed[:, 1], projection_full[1])
        value_lin = matmul(normed[:, 2], projection_full[2])
        queries = rotate(query_lin.reshape(head_shape), cos_table, sin_table).astype(jnp.bfloat16)
        key_rot = rotate(key_lin.reshape(head_shape), cos_table, sin_table).astype(jnp.bfloat16)
        values = value_lin.astype(jnp.bfloat16).reshape(head_shape)
        scores = masked_scores(queries, key_rot, allowed)
        row_top = jnp.max(scores, axis=-1, keepdims=True)
        exponent = jnp.exp(scores - row_top)
        row_total = jnp.sum(exponent, axis=-1, keepdims=True)
        soft_probs = exponent / row_total
        log_total = row_top + jnp.log(row_total)
        attended = (
            jnp.einsum(
                "nhqk,nkhe->nqhe",
                soft_probs.astype(jnp.bfloat16),
                values,
                preferred_element_type=jnp.float32,
            )
            .astype(jnp.bfloat16)
            .reshape(row_count, model_width)
        )
        attn_out = matmul(attended, out_full)
        up_pre = matmul(normed[:, 3], up_full)
        gated_act = gelu_value(up_pre).astype(jnp.bfloat16)
        feed_out = matmul(gated_act, down_full)
        output_list.append((streams[:, 3] + attn_out + feed_out).astype(jnp.bfloat16))
        coef_list.append(coef_rows)
        mix_up_back, projection_back, out_back = (
            lax.all_gather(mix_up, "fsdp", axis=0, tiled=True),
            lax.all_gather(query_key_value, "fsdp", axis=1, tiled=True),
            lax.all_gather(out_weight, "fsdp", axis=0, tiled=True),
        )
        up_back, down_back = (
            lax.all_gather(up_weight, "fsdp", axis=0, tiled=True),
            lax.all_gather(down_weight, "fsdp", axis=0, tiled=True),
        )
        grad_down = outer_sum(gated_act, grad_rows)
        grad_gated = back_product(grad_rows, down_back)
        grad_up_pre = (grad_gated * gelu_slope(up_pre)).astype(jnp.bfloat16)
        grad_up = outer_sum(normed[:, 3], grad_up_pre)
        grad_norm_feed = back_product(grad_up_pre, up_back)
        feed_shards = (
            lax.psum_scatter(
                grad_up.astype(jnp.bfloat16), "fsdp", scatter_dimension=0, tiled=True
            ).astype(jnp.float32),
            lax.psum_scatter(
                grad_down.astype(jnp.bfloat16), "fsdp", scatter_dimension=0, tiled=True
            ).astype(jnp.float32),
        )
        grad_out_weight = outer_sum(attended, grad_rows)
        grad_attended = back_product(grad_rows, out_back).astype(jnp.bfloat16).reshape(head_shape)
        scores_again = masked_scores(queries, key_rot, allowed)
        probs_again = jnp.exp(scores_again - log_total)
        grad_probs = jnp.einsum(
            "nqhe,nkhe->nhqk", grad_attended, values, preferred_element_type=jnp.float32
        )
        grad_value = (
            jnp.einsum(
                "nhqk,nqhe->nkhe",
                probs_again.astype(jnp.bfloat16),
                grad_attended,
                preferred_element_type=jnp.float32,
            )
            .astype(jnp.bfloat16)
            .reshape(row_count, model_width)
        )
        delta_rows = jnp.sum(probs_again * grad_probs, axis=-1, keepdims=True)
        grad_scores = (probs_again * (grad_probs - delta_rows)).astype(jnp.bfloat16)
        score_scale = HEAD_DIM ** (-0.5)
        grad_query_rot = (
            jnp.einsum("nhqk,nkhe->nqhe", grad_scores, key_rot, preferred_element_type=jnp.float32)
            * score_scale
        )
        grad_key_rot = (
            jnp.einsum("nhqk,nqhe->nkhe", grad_scores, queries, preferred_element_type=jnp.float32)
            * score_scale
        )
        grad_query = (
            rotate(grad_query_rot, cos_table, -sin_table)
            .astype(jnp.bfloat16)
            .reshape(row_count, model_width)
        )
        grad_key = (
            rotate(grad_key_rot, cos_table, -sin_table)
            .astype(jnp.bfloat16)
            .reshape(row_count, model_width)
        )
        grad_linear = (grad_query, grad_key, grad_value)
        grad_projection = jnp.stack(
            [outer_sum(normed[:, stream], grad_linear[stream]) for stream in range(3)]
        )
        grad_normed = jnp.stack(
            [back_product(grad_linear[stream], projection_back[stream]) for stream in range(3)]
            + [grad_norm_feed],
            axis=1,
        )
        gain_grad = jnp.sum(grad_normed * scaled, axis=0)
        bias_grad = jnp.sum(grad_normed, axis=0)
        grad_scaled = grad_normed * norm_gain
        grad_streams = inv_std * (
            grad_scaled
            - jnp.mean(grad_scaled, axis=-1, keepdims=True)
            - scaled * jnp.mean(grad_scaled * scaled, axis=-1, keepdims=True)
        )
        grad_streams = grad_streams + jnp.concatenate(
            [
                jnp.zeros((row_count, 3, model_width), jnp.float32),
                grad_rows[:, None, :].astype(jnp.float32),
            ],
            axis=1,
        )
        grad_coef = jnp.stack(
            [
                jnp.sum(
                    grad_streams * flat_stack[:, None, layer_index, :].astype(jnp.float32), axis=-1
                )
                for layer_index in range(STREAMS_IN)
            ],
            axis=-1,
        )
        grad_coef_flat = grad_coef.reshape(row_count, 4 * STREAMS_IN)
        static_grad = jnp.sum(grad_coef_flat, axis=0).reshape(4, STREAMS_IN)
        down_mix_grad = jnp.dot(hidden_wide.T, grad_coef_flat, precision=HIGHEST)
        grad_hidden = (
            jnp.dot(grad_coef_flat, mix_down.T, precision=HIGHEST) * gelu_slope(hidden_pre)
        ).astype(jnp.bfloat16)
        grad_mix_up = outer_sum(mixed_in, grad_hidden)
        grad_mixed = back_product(grad_hidden, mix_up_back)
        gain_mix_grad = jnp.sum(grad_mixed * last_layer * rms_scale, axis=0)
        weighted = grad_mixed * mix_gain
        grad_last = rms_scale * (
            weighted
            - last_layer
            * rms_scale
            * rms_scale
            * jnp.mean(weighted * last_layer, axis=-1, keepdims=True)
        )
        per_layer = [
            jnp.sum(coef_rows[:, :, layer_index, None] * grad_streams, axis=1)
            for layer_index in range(STREAMS_IN)
        ]
        per_layer[STREAMS_IN - 1] = per_layer[STREAMS_IN - 1] + grad_last
        grad_list.append(jnp.stack(per_layer, axis=1).astype(jnp.bfloat16))
        attention_shards = (
            lax.psum_scatter(
                grad_mix_up.astype(jnp.bfloat16), "fsdp", scatter_dimension=0, tiled=True
            ).astype(jnp.float32),
            lax.psum_scatter(
                grad_projection.astype(jnp.bfloat16), "fsdp", scatter_dimension=1, tiled=True
            ).astype(jnp.float32),
            lax.psum_scatter(
                grad_out_weight.astype(jnp.bfloat16), "fsdp", scatter_dimension=0, tiled=True
            ).astype(jnp.float32),
        )
        shards = attention_shards + feed_shards
        shards = jax.tree.map(
            lambda part: part.astype(jnp.float32), lax.psum(as_sent(shards), "replica")
        )
        smalls = (gain_mix_grad, down_mix_grad, static_grad, gain_grad, bias_grad)
        if shard_total is None:
            shard_total = shards
            small_total = smalls
        else:
            shard_total = tuple(
                (total_item + new_item for total_item, new_item in zip(shard_total, shards))
            )
            small_total = tuple(
                (total_item + new_item for total_item, new_item in zip(small_total, smalls))
            )
    small_total = lax.psum(small_total, ("fsdp", "replica"))
    layer_output = jnp.concatenate(output_list, axis=0).reshape(
        micro_total, local_seqs, SEQ, model_width
    )
    coefficients = jnp.concatenate(coef_list, axis=0).reshape(
        micro_total, local_seqs, SEQ, 4, STREAMS_IN
    )
    stack_grad = jnp.concatenate(grad_list, axis=0).reshape(
        micro_total, local_seqs, SEQ, STREAMS_IN, model_width
    )
    return (
        layer_output,
        coefficients,
        stack_grad,
        small_total[0],
        shard_total[0],
        small_total[1],
        small_total[2],
        small_total[3],
        small_total[4],
        shard_total[1],
        shard_total[2],
        shard_total[3],
        shard_total[4],
    )


def solution(mesh):
    return jax.shard_map(
        on_device,
        mesh=mesh,
        in_specs=(
            P(None, ("fsdp", "replica"), None, None, None),
            P(None, ("fsdp", "replica"), None, None),
            P(None, ("fsdp", "replica")),
            P(None, ("fsdp", "replica")),
            P(),
            P("fsdp", None),
            P(),
            P(),
            P(),
            P(),
            P(None, "fsdp", None),
            P("fsdp", None),
            P("fsdp", None),
            P("fsdp", None),
        ),
        out_specs=(
            P(None, ("fsdp", "replica"), None, None),
            P(None, ("fsdp", "replica"), None, None, None),
            P(None, ("fsdp", "replica"), None, None, None),
            P(),
            P("fsdp", None),
            P(),
            P(),
            P(),
            P(),
            P(None, "fsdp", None),
            P("fsdp", None),
            P("fsdp", None),
            P("fsdp", None),
        ),
        check_vma=False,
    )
```

profile of v0, /device:TPU:0, one launch (start us, length us, event | category | flops | bytes accessed | tf_op | source)
XLA Modules:
  0.0 1667.9 jit_solution(6764582834897619502)
XLA Ops:
  10.2 28.5 %all_gather.10 = bf16[1024,36]{0,1:T(8,128)(2,1)S(1)} all-gather(bf16[128,36]{0,1:T(8,128)(2,1)S(1)} %copy-done.176), channel_id=1, replica_groups=mesh['fsdp'=8,'replica'=4] {'fsdp'}, dimensions={0}, use_global_device_ids=true | all-gather | bytes 82944 | tf_op jit(solution)/shard_map/all_gather | solution.py:134
  53.8 59.0 %all-gather.5.cloned.1.call-done = bf16[3,1024,1024]{2,1,0:T(8,128)(2,1)} async-done(((bf16[3,128,1024]{2,1,0:T(8,128)(2,1)}), bf16[3,1024,1024]{2,1,0:T(8,128)(2,1)}) %all-gather.5.cloned.1.call-update) | async-done | bytes 6291472 | tf_op jit(solution)/shard_map/all_gather | solution.py:135
  112.8 4.7 slice_bitcast_fusion.2
  117.4 2.9 copy.73
  120.3 4.0 copy.74
  124.3 2.1 fusion.43
  136.7 2.1 fusion.42
  144.5 17.9 %all-gather.7.cloned.1.call-done = bf16[1024,1024]{1,0:T(8,128)(2,1)} async-done(((bf16[128,1024]{1,0:T(8,128)(2,1)}), bf16[1024,1024]{1,0:T(8,128)(2,1)}) %all-gather.7.cloned.1.call-update) | async-done | bytes 2097168 | tf_op jit(solution)/shard_map/all_gather | solution.py:136
  162.5 3.2 convolution_convert_fusion.10
  179.0 3.2 pad_maximum_fusion.1
  189.6 3.1 pad_maximum_fusion
  192.9 95.2 %all-gather.9.cloned.1.call-done = bf16[1024,4096]{1,0:T(8,128)(2,1)} async-done(((bf16[128,4096]{1,0:T(8,128)(2,1)}), bf16[1024,4096]{1,0:T(8,128)(2,1)}) %all-gather.9.cloned.1.call-update) | async-done | bytes 8388624 | tf_op jit(solution)/shard_map/all_gather | solution.py:139
  288.0 5.0 fusion.134
  293.1 120.1 %all-gather.11.cloned.1.call-done = bf16[4096,1024]{1,0:T(8,128)(2,1)} async-done(((bf16[512,1024]{1,0:T(8,128)(2,1)}), bf16[4096,1024]{1,0:T(8,128)(2,1)}) %all-gather.11.cloned.1.call-update) | async-done | bytes 8388624 | tf_op jit(solution)/shard_map/all_gather | solution.py:140
  413.2 6.1 fusion
  420.1 6.5 convolution_convert_fusion.3
  426.7 5.1 fusion.135
  431.8 6.5 fusion.1
  439.1 6.5 convolution_convert_fusion.2
  445.7 6.9 convolution_convert_fusion
  452.7 5.6 convolution_convert_fusion.1
  463.8 2.6 fusion.24
  466.4 2.4 fusion.32
  468.9 3.1 fusion.26
  472.0 2.5 fusion.35
  474.5 2.4 fusion.29
  477.0 3.1 fusion.25
  480.1 2.7 convolution_bitcast_fusion.5
  484.4 3.3 multiply_reduce_fusion.21
  487.7 2.6 stack.224
  492.5 6.5 convolution_bitcast_fusion.4
  500.6 3.5 multiply_reduce_fusion.2
  514.1 2.5 fusion.81
  535.0 18.9 %reduce-scatter.19.cloned.1.call-done = bf16[128,1024]{1,0:T(8,128)(2,1)} async-done(((bf16[1024,1024]{1,0:T(8,128)(2,1)}), bf16[128,1024]{1,0:T(8,128)(2,1)}) %reduce-scatter.19.cloned.1.call-update) | async-done | bytes 262160 | tf_op jit(solution)/shard_map/reduce_scatter | solution.py:310
  553.9 121.0 %reduce-scatter.17.cloned.1.call-done = bf16[3,128,1024]{2,1,0:T(8,128)(2,1)} async-done(((bf16[3,1024,1024]{2,1,0:T(8,128)(2,1)}), bf16[3,128,1024]{2,1,0:T(8,128)(2,1)}) %reduce-scatter.17.cloned.1.call-update) | async-done | bytes 786448 | tf_op jit(solution)/shard_map/reduce_scatter | solution.py:307
  674.9 121.1 %reduce-scatter.15.cloned.1.call-done = bf16[3,128,1024]{2,1,0:T(8,128)(2,1)} async-done(((bf16[3,1024,1024]{2,1,0:T(8,128)(2,1)}), bf16[3,128,1024]{2,1,0:T(8,128)(2,1)}) %reduce-scatter.15.cloned.1.call-update) | async-done | bytes 786448 | tf_op jit(solution)/shard_map/reduce_scatter | solution.py:307
  796.0 151.8 %reduce-scatter.23.cloned.1.call-done = bf16[128,4096]{1,0:T(8,128)(2,1)} async-done(((bf16[1024,4096]{1,0:T(8,128)(2,1)}), bf16[128,4096]{1,0:T(8,128)(2,1)}) %reduce-scatter.23.cloned.1.call-update) | async-done | bytes 1048592 | tf_op jit(solution)/shard_map/reduce_scatter | solution.py:202
  947.9 151.9 %reduce-scatter.25.cloned.1.call-done = bf16[128,4096]{1,0:T(8,128)(2,1)} async-done(((bf16[1024,4096]{1,0:T(8,128)(2,1)}), bf16[128,4096]{1,0:T(8,128)(2,1)}) %reduce-scatter.25.cloned.1.call-update) | async-done | bytes 1048592 | tf_op jit(solution)/shard_map/reduce_scatter | solution.py:202
  1099.8 151.7 %reduce-scatter.29.cloned.1.call-done = bf16[512,1024]{1,0:T(8,128)(2,1)} async-done(((bf16[4096,1024]{1,0:T(8,128)(2,1)}), bf16[512,1024]{1,0:T(8,128)(2,1)}) %reduce-scatter.29.cloned.1.call-update) | async-done | bytes 1048592 | tf_op jit(solution)/shard_map/reduce_scatter | solution.py:205
  1251.5 152.0 %reduce-scatter.27.cloned.1.call-done = bf16[512,1024]{1,0:T(8,128)(2,1)} async-done(((bf16[4096,1024]{1,0:T(8,128)(2,1)}), bf16[512,1024]{1,0:T(8,128)(2,1)}) %reduce-scatter.27.cloned.1.call-update) | async-done | bytes 1048592 | tf_op jit(solution)/shard_map/reduce_scatter | solution.py:205
  1404.4 2.1 fusion.99
  1410.7 40.4 %all-reduce.2 = (f32[1024]{0:T(1024)}, f32[36,36]{1,0:T(8,128)}, f32[4,9]{1,0:T(4,128)}, f32[4,1024]{1,0:T(4,128)}, f32[4,1024]{1,0:T(4,128)}) all-reduce(f32[1024]{0:T(1024)S(1)} %add.347, f32[36,36]{1,0:T(8,128)S(1)} %convolution_add_fusion.2, f32[4,9]{1,0:T(4,128)S(1)} %add.350, ...), channel_id=1, replica_groups=mesh['fsdp'=8,'replica'=4] {'fsdp','replica'}, use_global_device_ids=true, to_apply=%region_56.57 | all-reduce | flops 10548 | bytes 84384 | tf_op jit(solution)/shard_map/psum | solution.py:329
  1451.2 5.0 fusion.189
  1457.8 5.0 fusion.190
  1468.0 62.7 %reduce-scatter.33.cloned.1.call-done = bf16[128,36]{1,0:T(8,128)(2,1)} async-done(((bf16[1024,36]{1,0:T(8,128)(2,1)}), bf16[128,36]{1,0:T(8,128)(2,1)}) %reduce-scatter.33.cloned.1.call-update) | async-done | bytes 9232
  1531.5 10.7 all-reduce.3
  1542.9 110.5 %all-reduce.7.cloned.1.call-done = (bf16[3,128,1024]{2,1,0:T(8,128)(2,1)}, bf16[3,128,1024]{2,1,0:T(8,128)(2,1)}, bf16[128,1024]{1,0:T(8,128)(2,1)}, bf16[128,10...) async-done(((bf16[3,128,1024]{2,1,0:T(8,128)(2,1)}, ...) | async-done | bytes 6291472 | tf_op jit(solution)/shard_map/psum | solution.py:316
  1653.4 3.0 convert_add_fusion.2
  (554 shorter events, 110.4 us)
Async XLA Ops:
  7.2 35.5 %copy-start = (f32[36,36]{1,0:T(8,128)S(1)}, f32[36,36]{1,0:T(8,128)}, u32[]{:S(2)}) copy-start(f32[36,36]{1,0:T(8,128)} %param.20) | copy-start | bytes 15556
  7.2 105.5 %all-gather.5.cloned.1.call-start = ((), (), s32[]{:S(2)}) async-start(), calls=%async_computation.10 | async-start | bytes 7077888 | tf_op jit(solution)/shard_map/all_gather | solution.py:135
  7.9 154.5 %all-gather.7.cloned.1.call-start = ((), (), s32[]{:S(2)}) async-start(), calls=%async_computation.11 | async-start | bytes 2359296 | tf_op jit(solution)/shard_map/all_gather | solution.py:136
  8.7 279.3 %all-gather.9.cloned.1.call-start = ((), (), s32[]{:S(2)}) async-start(), calls=%async_computation.12 | async-start | bytes 9437184 | tf_op jit(solution)/shard_map/all_gather | solution.py:139
  9.4 403.7 %all-gather.11.cloned.1.call-start = ((), (), s32[]{:S(2)}) async-start(), calls=%async_computation.13 | async-start | bytes 9437184 | tf_op jit(solution)/shard_map/all_gather | solution.py:140
  10.0 525.0 %reduce-scatter.21.cloned.1.call-start = ((), (), s32[]{:S(2)}) async-start(), calls=%async_computation.17 | async-start | bytes 2359296 | tf_op jit(solution)/shard_map/reduce_scatter | solution.py:310
  38.7 5.9 copy-start.182
  38.7 7.2 copy-start.183
  40.7 7.8 copy-start.10
  40.7 7.8 copy-start.11
  42.9 7.1 copy-start.105
  53.8 75.8 %copy-start.12 = (bf16[64,4,1024]{2,0,1:T(8,128)(2,1)}, bf16[64,4,1024]{2,0,1:T(8,128)(2,1)S(1)}, u32[]{:S(2)}) copy-start(bf16[64,4,1024]{2,0,1:T(8,128)(2,1)S(1)} %get-tuple-element.160) | copy-start | bytes 1572868
  53.8 82.9 %copy-start.14 = (bf16[64,4,1024]{2,0,1:T(8,128)(2,1)}, bf16[64,4,1024]{2,0,1:T(8,128)(2,1)S(1)}, u32[]{:S(2)}) copy-start(bf16[64,4,1024]{2,0,1:T(8,128)(2,1)S(1)} %get-tuple-element.159) | copy-start | bytes 1572868
  130.4 9.8 copy-start.109
  130.4 9.8 copy-start.111
  130.4 9.8 copy-start.113
  130.4 9.8 copy-start.115
  134.1 419.8 %reduce-scatter.19.cloned.1.call-start = ((), (), s32[]{:S(2)}) async-start(), calls=%async_computation.16 | async-start | bytes 2359296 | tf_op jit(solution)/shard_map/reduce_scatter | solution.py:310
  144.5 530.5 %reduce-scatter.17.cloned.1.call-start = ((), (), s32[]{:S(2)}) async-start(), calls=%async_computation.15 | async-start | bytes 7077888 | tf_op jit(solution)/shard_map/reduce_scatter | solution.py:307
  182.2 613.8 %reduce-scatter.15.cloned.1.call-start = ((), (), s32[]{:S(2)}) async-start(), calls=%async_computation.14 | async-start | bytes 7077888 | tf_op jit(solution)/shard_map/reduce_scatter | solution.py:307
  192.7 755.2 %reduce-scatter.23.cloned.1.call-start = ((), (), s32[]{:S(2)}) async-start(), calls=%async_computation.18 | async-start | bytes 9437184 | tf_op jit(solution)/shard_map/reduce_scatter | solution.py:202
  426.7 673.1 %reduce-scatter.25.cloned.1.call-start = ((), (), s32[]{:S(2)}) async-start(), calls=%async_computation.19 | async-start | bytes 9437184 | tf_op jit(solution)/shard_map/reduce_scatter | solution.py:202
  431.8 6.5 copy-start.2
  445.7 805.8 %reduce-scatter.29.cloned.1.call-start = ((), (), s32[]{:S(2)}) async-start(), calls=%async_computation.21 | async-start | bytes 9437184 | tf_op jit(solution)/shard_map/reduce_scatter | solution.py:205
  452.6 950.8 %reduce-scatter.27.cloned.1.call-start = ((), (), s32[]{:S(2)}) async-start(), calls=%async_computation.20 | async-start | bytes 9437184 | tf_op jit(solution)/shard_map/reduce_scatter | solution.py:205
  458.3 1008.8 %reduce-scatter.31.cloned.1.call-start = ((), (), s32[]{:S(2)}) async-start(), calls=%async_computation.22 | async-start | bytes 294912
  463.8 16.2 slice-start
  466.4 5.6 copy-start.64
  468.8 5.7 copy-start.62
  472.0 8.1 slice-start.1
  492.5 6.5 copy-start.5
  492.5 6.5 copy-start.55
  492.5 6.5 copy-start.56
  492.5 7.8 copy-start.36
  492.5 7.8 copy-start.101
  504.1 10.0 copy-start.180
  504.1 10.0 copy-start.185
  504.1 10.0 copy-start.187
  505.7 7.7 copy-start.107
  516.6 17.1 %copy-start.96 = (bf16[64,1024]{1,0:T(8,128)(2,1)S(1)}, bf16[64,1024]{1,0:T(8,128)(2,1)}, u32[]{:S(2)}) copy-start(bf16[64,1024]{1,0:T(8,128)(2,1)} %get-tuple-element.73) | copy-start | bytes 393220
  516.6 17.7 %copy-start.95 = (bf16[64,1024]{1,0:T(8,128)(2,1)S(1)}, bf16[64,1024]{1,0:T(8,128)(2,1)}, u32[]{:S(2)}) copy-start(bf16[64,1024]{1,0:T(8,128)(2,1)} %get-tuple-element.72) | copy-start | bytes 393220
  516.6 1014.0 %reduce-scatter.33.cloned.1.call-start = ((), (), s32[]{:S(2)}) async-start(), calls=%async_computation.23 | async-start | bytes 294912
  516.7 18.3 %copy-start.189 = (f32[64]{0:T(128)S(1)}, f32[64]{0:T(128)}, u32[]{:S(2)}) copy-start(f32[64]{0:T(128)} %get-tuple-element.59) | copy-start | bytes 772
  518.3 1135.0 %all-reduce.7.cloned.1.call-start = ((), (), s32[]{:S(2)}) async-start(), calls=%async_computation.24 | async-start | bytes 12582912 | tf_op jit(solution)/shard_map/psum | solution.py:316
  518.4 12.6 copy-start.100
  518.4 13.3 copy-start.99
  518.4 13.9 copy-start.98
  518.4 14.6 copy-start.97
  (159 other events, 292.2 us)
Sparse Core Ops, SparseCore 0:
  10.2 102.4 all-gather.4
  114.9 47.5 all-gather.6
  164.6 123.4 all-gather.8
  290.0 123.1 all-gather.10
  417.1 66.1 reduce-scatter.20
  487.2 66.6 reduce-scatter.18
  557.5 117.3 reduce-scatter.16
  678.5 117.4 reduce-scatter.14
  799.7 148.1 reduce-scatter.22
  951.8 147.9 reduce-scatter.24
  1103.4 147.9 reduce-scatter.28
  1255.4 148.0 reduce-scatter.26
  1406.8 60.3 reduce-scatter.30
  1470.3 60.3 reduce-scatter.32
  1533.4 119.9 all-reduce.6
where the time goes:
time: 1680 us; the launch traced here: 1670 us
  waiting for transfers between devices  1340 us (80%)
  matrix products  122 us (7%)
  blocking collectives  79.7 us (5%)
  local copies, waits for them, and re-layouts  64.3 us (4%)
  other arithmetic  43.5 us (3%)
  between operations  18.2 us (1%)
    reduce_scatter x2, waiting for transfers between devices, on_device(): lax.psum_scatter(grad_up.astype(jnp.bfloat16), 'fsdp', scatter_dimension=...  304 us
    reduce_scatter x2, waiting for transfers between devices, on_device(): lax.psum_scatter(grad_down.astype(jnp.bfloat16), 'fsdp', scatter_dimensio...  304 us
    reduce_scatter x2, waiting for transfers between devices, on_device(): lax.psum_scatter(grad_projection.astype(jnp.bfloat16), 'fsdp', scatter_di...  242 us
    all_gather x1, waiting for transfers between devices, on_device(): lax.all_gather(down_weight, 'fsdp', axis=0, tiled=True)  120 us
    psum x1, waiting for transfers between devices, on_device(): lax.psum(as_sent(shards), 'replica')  111 us
    all_gather x1, waiting for transfers between devices, on_device(): lax.all_gather(up_weight, 'fsdp', axis=0, tiled=True)  95.2 us
    unnamed x17, waiting for transfers between devices  67.5 us
    all_gather x1, waiting for transfers between devices, on_device(): lax.all_gather(query_key_value, 'fsdp', axis=1, tiled=True)  59 us
  transfers between devices with their start and end apart: 15, of which 14 were waited for; matrix products, arithmetic and copies ran while one was open for 13% of the time, Pallas kernels for 0%

commit v1 on v0

--- a/solution.py
+++ b/solution.py
@@ -2,7 +2,10 @@
 
 import jax
 import jax.numpy as jnp
+import numpy as np
 from jax import lax
+from jax.experimental import pallas as pl
+from jax.experimental.pallas import tpu as pltpu
 from jax.sharding import PartitionSpec as P
 
 HEADS = 16
@@ -110,7 +113,7 @@
     micro_total = layer_stack.shape[0]
     local_seqs = layer_stack.shape[1]
     model_width = layer_stack.shape[-1]
-    groups = [(index_micro, 1) for index_micro in range(micro_total)]
+    groups = [(0, micro_total)]
     cos_table, sin_table = rotary_tables()
     output_list = []
     coef_list = []
@@ -353,9 +356,912 @@
     )
 
 
+ROWS = 128
+WIDTH = 1024
+VMEM_FULL = pl.BlockSpec(memory_space=pltpu.VMEM)
+SMEM_FULL = pl.BlockSpec(memory_space=pltpu.SMEM)
+IN_PLACE = pl.BlockSpec(memory_space=pl.ANY)
+
+
+def bits_swap(size, bit):
+    return [(index, index ^ bit) for index in range(size)]
+
+
+CORE_SWAP = bits_swap(4, 1)
+X_SWAP = bits_swap(4, 2)
+Y_SWAP = bits_swap(8, 1)
+Z_SWAP_NEAR = bits_swap(8, 2)
+Z_SWAP_FAR = bits_swap(8, 4)
+
+
+def z_pairs(moves):
+    return [(2 * src + col, 2 * dst + col) for src, dst in moves for col in range(2)]
+
+
+def pick(cond, first, second):
+    return jnp.where(cond, first, second)
+
+
+def order_two(flag, own, other, axis):
+    first = pick(flag == 0, own, other)
+    second = pick(flag == 0, other, own)
+    return jnp.concatenate([first, second], axis=axis)
+
+
+def after(value, *others):
+    return lax.optimization_barrier((value,) + others)[0]
+
+
+def gather_fsdp(piece, z, y, front):
+    up_first = lax.ppermute(piece, "fsdp", z_pairs([(0, 1), (1, 2), (2, 3)]))
+    down_first = lax.ppermute(piece, "fsdp", z_pairs([(1, 0), (2, 1), (3, 2)]))
+    side_own = lax.ppermute(piece, "fsdp", Y_SWAP)
+    early, late = front()
+    up_second = lax.ppermute(after(up_first, early), "fsdp", z_pairs([(1, 2), (2, 3)]))
+    down_second = lax.ppermute(after(down_first, early), "fsdp", z_pairs([(1, 0), (2, 1)]))
+    near = pick(z == 0, down_first, up_first)
+    side_near = lax.ppermute(near, "fsdp", Y_SWAP)
+    last = lax.ppermute(
+        after(pick(z == 2, up_second, down_second), side_own),
+        "fsdp",
+        z_pairs([(2, 3), (1, 0)]),
+    )
+    second_any = pick(z < 2, down_second, up_second)
+    inner = (z == 1) | (z == 2)
+    middle = pick(inner, down_first, second_any)
+    side_middle = lax.ppermute(after(middle, side_own), "fsdp", Y_SWAP)
+    far = pick(inner, second_any, last)
+    side_far = lax.ppermute(after(far, side_near, late), "fsdp", Y_SWAP)
+    pieces = [piece, side_own, near, side_near, middle, side_middle, far, side_far]
+    places = []
+    for z_from in (z, table([1, 0, 1, 2], z), table([2, 2, 3, 1], z), table([3, 3, 0, 0], z)):
+        places += [2 * z_from + y, 2 * z_from + 1 - y]
+    return pieces, jnp.stack(places)
+
+
+def table(values, z):
+    return jnp.asarray(values, jnp.int32)[z]
+
+
+def scatter_order(z, y):
+    places = []
+    for z_to in (table([3, 3, 0, 0], z), table([2, 2, 1, 1], z), table([1, 0, 3, 2], z), z):
+        places += [2 * z_to + 1 - y, 2 * z_to + y]
+    return jnp.stack(places)
+
+
+def wide(value):
+    return value.astype(jnp.float32)
+
+
+def scatter_fsdp(chunks, z, first_wait, beside):
+    def add(first, second):
+        return (wide(first) + wide(second)).astype(jnp.bfloat16)
+
+    came = []
+    sums = []
+    for turn in range(4):
+        sent = chunks[2 * turn]
+        if turn == 1:
+            sent = after(sent, first_wait)
+        if turn >= 2:
+            sent = after(sent, came[turn - 2])
+        came.append(lax.ppermute(sent, "fsdp", Y_SWAP))
+        sums.append(add(chunks[2 * turn + 1], came[turn]))
+    first = lax.ppermute(sums[0], "fsdp", z_pairs([(0, 1), (3, 2)]))
+    up_send = add(pick(z == 0, sums[1], sums[0]), first)
+    down_send = add(pick(z == 3, sums[1], sums[0]), first)
+    up_one = lax.ppermute(up_send, "fsdp", z_pairs([(0, 1), (1, 2)]))
+    down_one = lax.ppermute(down_send, "fsdp", z_pairs([(3, 2), (2, 1)]))
+    last_wait = beside()
+    up_two = lax.ppermute(
+        after(add(pick(z == 1, sums[1], sums[2]), up_one), last_wait),
+        "fsdp",
+        z_pairs([(0, 1), (1, 2), (2, 3)]),
+    )
+    down_two = lax.ppermute(
+        after(add(pick(z == 2, sums[1], sums[2]), down_one), last_wait),
+        "fsdp",
+        z_pairs([(3, 2), (2, 1), (1, 0)]),
+    )
+    return (wide(sums[3]) + wide(up_two) + wide(down_two)).astype(jnp.bfloat16)
+
+
+def lanes_of(shape):
+    return lax.broadcasted_iota(jnp.int32, shape, 1)
+
+
+def rows_of(shape):
+    return lax.broadcasted_iota(jnp.int32, shape, 0)
+
+
+def prepare_kernel(place, projection, out_weight, up_weight, down_weight, piece):
+    member, x, core = place[0], place[1], place[2]
+    quarter, other = 2 * x + core, 2 * x + 1 - core
+    lane = lanes_of((128, 128))
+    for index in range(8):
+        half = index % 2
+        own = up_weight[:, pl.ds(pl.multiple_of((index * 4 + quarter) * 128, 128), 128)]
+        extra = up_weight[:, pl.ds(pl.multiple_of(((index ^ 1) * 4 + other) * 128, 128), 128)]
+        taken = (lane >= 96) & (core == half)
+        piece[index // 2, :, half * 128 : half * 128 + 128] = jnp.where(
+            taken, wide(extra), wide(own)
+        ).astype(jnp.bfloat16)
+    for stream in range(3):
+        for twin in range(2):
+            tiles = [
+                wide(
+                    projection[
+                        stream,
+                        :,
+                        pl.ds(pl.multiple_of((2 * twin + low) * 256 + core * 128, 128), 128),
+                    ]
+                )
+                for low in range(2)
+            ]
+            first = jnp.where(x == 0, tiles[0], pltpu.roll(tiles[0], 64, 1))
+            second = jnp.where(x == 0, pltpu.roll(tiles[1], 64, 1), tiles[1])
+            piece[4 + stream, :, twin * 128 : twin * 128 + 128] = jnp.where(
+                lane < 64, first, second
+            ).astype(jnp.bfloat16)
+    own_row = pl.multiple_of(quarter * 128, 128)
+    other_row = pl.multiple_of(other * 128, 128)
+    head_row = pl.multiple_of(x * 64, 64)
+    for block in range(4):
+        cols = slice(block * 256, block * 256 + 256)
+        piece[7 + block, 0:96] = down_weight[pl.ds(own_row, 96), cols]
+
+        @pl.when(member % 2 == core)
+        def _():
+            piece[7 + block, 96:128] = out_weight[pl.ds(head_row, 32), cols]
+            piece[11, block * 32 : block * 32 + 32] = out_weight[pl.ds(head_row + 32, 32), cols]
+
+        @pl.when(member % 2 != core)
+        def _():
+            piece[7 + block, 96:128] = down_weight[pl.ds(own_row + 96, 32), cols]
+            piece[11, block * 32 : block * 32 + 32] = down_weight[pl.ds(other_row + 96, 32), cols]
+
+
+def front_kernel(
+    bounds,
+    stack,
+    cotangent,
+    mix_gain,
+    mix_up,
+    mix_down,
+    mix_static,
+    norm_gain,
+    norm_bias,
+    packet,
+    scaled_out,
+    stats,
+    stream_out,
+    streams,
+):
+    seqs = stack.shape[0]
+    for seq in range(seqs):
+        last = wide(stack[seq, STREAMS_IN - 1])
+        rms = lax.rsqrt(jnp.mean(last * last, axis=-1, keepdims=True) + EPSILON)
+        mixed_in = (last * rms * mix_gain[...]).astype(jnp.bfloat16)
+        hidden_pre = back_product(mixed_in, mix_up[...])
+        hidden = wide(gelu_value(hidden_pre).astype(jnp.bfloat16))
+        coef = jnp.dot(
+            hidden, mix_down[...], precision=HIGHEST, preferred_element_type=jnp.float32
+        )
+        coef = coef + mix_static[...]
+        at = slice(seq * SEQ, seq * SEQ + SEQ)
+        stats[0, at, 0:36] = coef
+        stats[1, at, 0:36] = hidden_pre
+        stats[2, at, 4:5] = rms
+        packet[4 * ROWS + seq * SEQ : 4 * ROWS + seq * SEQ + SEQ] = cotangent[at]
+
+        def mix(step, carry):
+            row = pl.multiple_of(step // 2 * 16, 16)
+            col = pl.multiple_of(step % 2 * 512, 512)
+            rows_coef = stats[0, pl.ds(seq * SEQ + row, 16), :]
+            totals = [None] * 4
+            for layer in range(STREAMS_IN):
+                value = wide(stack[seq, layer, pl.ds(row, 16), pl.ds(col, 512)])
+                for stream in range(4):
+                    at_coef = stream * STREAMS_IN + layer
+                    term = rows_coef[:, at_coef : at_coef + 1] * value
+                    totals[stream] = term if layer == 0 else totals[stream] + term
+            for stream in range(4):
+                streams[stream, pl.ds(seq * SEQ + row, 16), pl.ds(col, 512)] = totals[stream]
+            return carry
+
+        lax.fori_loop(0, 8, mix, 0)
+
+    def norm(step, carry):
+        row = pl.multiple_of(step * 16, 16)
+        for stream in range(4):
+            value = streams[stream, pl.ds(row, 16), :]
+            center = value - jnp.mean(value, axis=-1, keepdims=True)
+            inverse = lax.rsqrt(jnp.mean(center * center, axis=-1, keepdims=True) + EPSILON)
+            scaled = center * inverse
+            stats[2, pl.ds(row, 16), stream : stream + 1] = inverse
+            scaled_out[stream, pl.ds(row, 16), :] = scaled
+            packet[pl.ds(stream * ROWS + row, 16), :] = (
+                scaled * norm_gain[stream : stream + 1, :] + norm_bias[stream : stream + 1, :]
+            ).astype(jnp.bfloat16)
+            if stream == 3:
+                stream_out[pl.ds(row, 16), :] = value
+        return carry
+
+    lax.fori_loop(0, seqs * SEQ // 16, norm, 0)
+    packet[5 * ROWS :] = jnp.zeros((16, WIDTH), jnp.bfloat16)
+    row = rows_of((16, 128))
+    marks = jnp.zeros((16, 128), jnp.float32)
+    for place in range(2 * seqs):
+        marks = jnp.where(row == place, wide(bounds[place]), marks)
+    packet[5 * ROWS :, 0:128] = marks.astype(jnp.bfloat16)
+
+
+def main_kernel(
+    place,
+    origin,
+    target,
+    rope,
+    packet0,
+    packet1,
+    packet2,
+    packet3,
+    piece0,
+    piece1,
+    piece2,
+    piece3,
+    piece4,
+    piece5,
+    piece6,
+    piece7,
+    chunk0,
+    chunk1,
+    chunk2,
+    chunk3,
+    chunk4,
+    chunk5,
+    chunk6,
+    chunk7,
+    keep,
+    send,
+    acts,
+    marks,
+    up_all,
+    lin_all,
+    down_all,
+    out_all,
+    linear,
+    low_lin,
+    parts,
+    out_total,
+    norm_total,
+    sems,
+    piece_sems,
+    chunk_sems,
+):
+    core = place[2]
+    packets = (packet0, packet1, packet2, packet3)
+    pieces = (piece0, piece1, piece2, piece3, piece4, piece5, piece6, piece7)
+    chunks = (chunk0, chunk1, chunk2, chunk3, chunk4, chunk5, chunk6, chunk7)
+    copies = []
+    for block in range(4):
+        for unit in range(5):
+            copies.append(
+                pltpu.make_async_copy(
+                    packets[block].at[pl.ds(unit * ROWS, ROWS)],
+                    acts.at[unit, pl.ds(block * ROWS, ROWS)],
+                    sems.at[block, unit],
+                )
+            )
+        copies.append(
+            pltpu.make_async_copy(
+                packets[block].at[pl.ds(5 * ROWS, 16)], marks.at[block], sems.at[block, 5]
+            )
+        )
+    for index in range(8):
+        rows = pl.ds(pl.multiple_of(origin[index] * 128, 128), 128)
+        piece = pieces[index]
+        copies.append(
+            pltpu.make_async_copy(
+                piece.at[pl.ds(4, 3)], lin_all.at[:, rows], piece_sems.at[index, 0]
+            )
+        )
+        copies.append(
+            pltpu.make_async_copy(
+                piece.at[pl.ds(0, 4)], up_all.at[:, rows], piece_sems.at[index, 1]
+            )
+        )
+        copies.append(
+            pltpu.make_async_copy(
+                piece.at[pl.ds(7, 5)], down_all.at[origin[index]], piece_sems.at[index, 2]
+            )
+        )
+    for copy in copies:
+        copy.start()
+    for copy in copies:
+        copy.wait()
+    for pair in range(4):
+        even = 2 * pair + core
+        odd = 2 * pair + 1 - core
+        for block in range(4):
+            band = slice(block * 32, block * 32 + 32)
+            out_all[block, pair * 64 : pair * 64 + 32] = down_all[even, block, 96:128]
+            out_all[block, pair * 64 + 32 : pair * 64 + 64] = down_all[even, 4, band]
+            down_all[even, block, 96:128] = down_all[odd, 4, band]
+
+    for stream in range(3):
+        linear[stream] = matmul(acts[stream], lin_all[stream])
+    total = None
+    for block in range(4):
+        term = back_product(acts[4, :, block * 256 : block * 256 + 256], out_all[block])
+        total = term if total is None else total + term
+    low_lin[3] = total.astype(jnp.bfloat16)
+    cos_table = rope[0]
+    sin_left = rope[1]
+    sin_right = rope[2]
+
+    def turn(value, sign):
+        return (
+            value * cos_table
+            + pltpu.roll(value, 120, 1) * (sign * sin_left)
+            + pltpu.roll(value, 8, 1) * (sign * sin_right)
+        )
+
+    def units(block, carry):
+        row = rows_of((ROWS, ROWS))
+        lane = lanes_of((ROWS, ROWS))
+        bound = wide(marks[block])
+
+        def both(first, second):
+            by_lane = jnp.where(lane < SEQ, first, second)
+            by_row = jnp.where(row < SEQ, first, second)
+            return by_row, by_lane
+
+        start_q, start_k = both(bound[0:1, 0:128], bound[1:2, 0:128])
+        split_q, split_k = both(bound[2:3, 0:128], bound[3:4, 0:128])
+        at_q = wide(row % SEQ)
+        at_k = wide(lane % SEQ)
+        same = (row // SEQ == lane // SEQ) & ((at_q >= split_q) == (at_k >= split_k))
+        pic_q = (at_q >= start_q) & (at_q < start_q + PIC)
+        pic_k = (at_k >= start_k) & (at_k < start_k + PIC)
+        allowed = same & ((at_q >= at_k) | (pic_q & pic_k))
+        span = pl.ds(pl.multiple_of(block * ROWS, ROWS), ROWS)
+        for twin in range(2):
+            cols = slice(twin * 128, twin * 128 + 128)
+            query = turn(linear[0, span, cols], 1.0)
+            key_wide = turn(linear[1, span, cols], 1.0)
+            query_low = query.astype(jnp.bfloat16)
+            key_low = key_wide.astype(jnp.bfloat16)
+            value_low = linear[2, span, cols].astype(jnp.bfloat16)
+            grad_att = low_lin[3, span, cols]
+            grad_wide = wide(grad_att)
+            got = []
+            for head in range(2):
+                inside = (lane // 64) == head
+                query_head = jnp.where(inside, query, 0.0).astype(jnp.bfloat16)
+                grad_head = jnp.where(inside, grad_wide, 0.0).astype(jnp.bfloat16)
+                scores = back_product(query_head, key_low) * HEAD_DIM ** (-0.5)
+                scores = jnp.where(allowed, scores, -1e30)
+                exponent = jnp.exp(scores - jnp.max(scores, axis=-1, keepdims=True))
+                probs = exponent / jnp.sum(exponent, axis=-1, keepdims=True)
+                probs_low = probs.astype(jnp.bfloat16)
+                attended = matmul(probs_low, value_low)
+                grad_probs = back_product(grad_head, value_low)
+                grad_value = outer_sum(probs_low, grad_att)
+                delta = jnp.sum(probs * grad_probs, axis=-1, keepdims=True)
+                grad_scores = (probs * (grad_probs - delta)).astype(jnp.bfloat16)
+                grad_query = matmul(grad_scores, key_low)
+                grad_key = outer_sum(grad_scores, query_low)
+                got.append((attended, grad_query, grad_key, grad_value))
+            merged = [jnp.where(lane < 64, low, high) for low, high in zip(*got)]
+            scale = HEAD_DIM ** (-0.5)
+            low_lin[4, span, cols] = merged[0].astype(jnp.bfloat16)
+            low_lin[0, span, cols] = turn(merged[1] * scale, -1.0).astype(jnp.bfloat16)
+            low_lin[1, span, cols] = turn(merged[2] * scale, -1.0).astype(jnp.bfloat16)
+            low_lin[2, span, cols] = merged[3].astype(jnp.bfloat16)
+        return carry
+
+    lax.fori_loop(0, 4, units, 0)
+
+    def put(unit, value):
+        low = value.astype(jnp.bfloat16)
+        for block in range(2):
+            keep[block, unit] = low[block * ROWS : block * ROWS + ROWS]
+            send[block, unit] = low[(2 + block) * ROWS : (3 + block) * ROWS]
+
+    for block in range(4):
+        cols = slice(block * 256, block * 256 + 256)
+        out_total[:, cols] = matmul(low_lin[4], out_all[block])
+        grad = outer_sum(low_lin[4], acts[4, :, cols]).astype(jnp.bfloat16)
+        for pair in range(4):
+            even = 2 * pair + core
+            parts[even, 7 + block, 96:128] = grad[pair * 64 : pair * 64 + 32]
+            parts[even, 11, block * 32 : block * 32 + 32] = grad[pair * 64 + 32 : pair * 64 + 64]
+    for stream in range(3):
+        grad = outer_sum(acts[stream], low_lin[stream]).astype(jnp.bfloat16)
+        for index in range(8):
+            parts[index, 4 + stream] = grad[index * 128 : index * 128 + 128]
+        put(stream, back_product(low_lin[stream], lin_all[stream]))
+
+    norm_total[...] = jnp.zeros_like(norm_total)
+
+    def hidden(pair, carry):
+        up_pre = matmul(acts[3], up_all[pair])
+        bell = 0.5 * (1.0 + lax.erf(up_pre * ROOT_HALF))
+        gated = (up_pre * bell).astype(jnp.bfloat16)
+        slope = bell + up_pre * NORMAL_PEAK * jnp.exp(-0.5 * up_pre * up_pre)
+        grad_gated = None
+        for block in range(4):
+            cols = slice(block * 256, block * 256 + 256)
+            rows_down = jnp.concatenate(
+                [down_all[2 * pair, block], down_all[2 * pair + 1, block]], axis=0
+            )
+            term = back_product(acts[4, :, cols], rows_down)
+            grad_gated = term if grad_gated is None else grad_gated + term
+            out_total[:, cols] += matmul(gated, rows_down)
+        grad_pre = (grad_gated * slope).astype(jnp.bfloat16)
+        norm_total[...] += back_product(grad_pre, up_all[pair])
+        grad = outer_sum(acts[3], grad_pre).astype(jnp.bfloat16)
+        for index in range(8):
+            parts[index, pair] = grad[index * 128 : index * 128 + 128]
+        for block in range(4):
+            cols = slice(block * 256, block * 256 + 256)
+            grad = outer_sum(gated, acts[4, :, cols]).astype(jnp.bfloat16)
+            even, odd = 2 * pair + core, 2 * pair + 1 - core
+            for half in range(2):
+                parts[2 * pair + half, 7 + block, 0:96] = grad[half * 128 : half * 128 + 96]
+
+                @pl.when(core == half)
+                def _():
+                    parts[odd, 11, block * 32 : block * 32 + 32] = grad[
+                        half * 128 + 96 : half * 128 + 128
+                    ]
+
+                @pl.when(core != half)
+                def _():
+                    parts[odd, 7 + block, 96:128] = grad[half * 128 + 96 : half * 128 + 128]
+
+        return carry
+
+    lax.fori_loop(0, 4, hidden, 0)
+    sent = [
+        pltpu.make_async_copy(parts.at[target[index]], chunks[index], chunk_sems.at[index])
+        for index in range(8)
+    ]
+    for copy in sent:
+        copy.start()
+    put(3, norm_total[...])
+    put(4, out_total[...])
+    for copy in sent:
+        copy.wait()
+
+
+def back_kernel(
+    stack,
+    cotangent,
+    scaled,
+    stats,
+    stream_in,
+    keep,
+    came,
+    across,
+    mix_gain,
+    mix_up,
+    mix_down,
+    norm_gain,
+    layer_output,
+    stack_grad,
+    small,
+    grads,
+    sums,
+    coef_grad,
+):
+    seqs = stack.shape[0]
+    sums[...] = jnp.zeros_like(sums)
+    lane = lanes_of((16, 128))
+
+    def unit(step, carry):
+        row = pl.multiple_of(step * 16, 16)
+        span = pl.ds(row, 16)
+
+        def result(index):
+            return wide(keep[0, index, span]) + wide(came[0, index, span]) + wide(across[index, span])
+
+        layer_output[span] = (stream_in[span] + result(4)).astype(jnp.bfloat16)
+        for stream in range(4):
+            item = result(stream)
+            scale = scaled[stream, span]
+            moved = item * scale
+            sums[stream] += moved[:8] + moved[8:]
+            sums[4 + stream] += item[:8] + item[8:]
+            weighted = item * norm_gain[stream : stream + 1]
+            mean = jnp.mean(weighted, axis=-1, keepdims=True)
+            slant = jnp.mean(weighted * scale, axis=-1, keepdims=True)
+            grad = stats[2, span, stream : stream + 1] * (weighted - mean - scale * slant)
+            if stream == 3:
+                grad = grad + wide(cotangent[span])
+            grads[stream, span] = grad
+        return carry
+
+    lax.fori_loop(0, seqs * SEQ // 16, unit, 0)
+    for seq in range(seqs):
+
+        def coefs(step, carry):
+            row = pl.multiple_of(step * 16, 16)
+            span = pl.ds(seq * SEQ + row, 16)
+            found = jnp.zeros((16, 128), jnp.float32)
+            for layer in range(STREAMS_IN):
+                value = wide(stack[seq, layer, pl.ds(row, 16), :])
+                for stream in range(4):
+                    got = jnp.sum(grads[stream, span] * value, axis=-1, keepdims=True)
+                    found = jnp.where(lane == stream * STREAMS_IN + layer, got, found)
+            coef_grad[span] = found
+            return carry
+
+        lax.fori_loop(0, SEQ // 16, coefs, 0)
+    grad_coef = coef_grad[:, 0:36]
+    hidden_pre = stats[1, :, 0:36]
+    hidden_low = gelu_value(hidden_pre).astype(jnp.bfloat16)
+    small[...] = jnp.zeros_like(small)
+    small[0:36, WIDTH : WIDTH + 36] = lax.dot_general(
+        wide(hidden_low),
+        grad_coef,
+        (((0,), (0,)), ((), ())),
+        precision=HIGHEST,
+        preferred_element_type=jnp.float32,
+    )
+    small[36:37, WIDTH : WIDTH + 36] = jnp.sum(grad_coef, axis=0, keepdims=True)
+    grad_hidden = (
+        lax.dot_general(
+            grad_coef,
+            mix_down[...],
+            (((1,), (1,)), ((), ())),
+            precision=HIGHEST,
+            preferred_element_type=jnp.float32,
+        )
+        * gelu_slope(hidden_pre)
+    ).astype(jnp.bfloat16)
+    gain_row = jnp.zeros((8, WIDTH), jnp.float32)
+    up_part = jnp.zeros((36, WIDTH), jnp.float32)
+    for seq in range(seqs):
+        at = slice(seq * SEQ, seq * SEQ + SEQ)
+        last = wide(stack[seq, STREAMS_IN - 1])
+        rms = stats[2, at, 4:5]
+        mixed_in = (last * rms * mix_gain[...]).astype(jnp.bfloat16)
+        up_part = up_part + outer_sum(grad_hidden[at], mixed_in)
+        grad_mixed = matmul(grad_hidden[at], mix_up[...])
+        along = grad_mixed * last * rms
+        for place in range(SEQ // 8):
+            gain_row = gain_row + along[place * 8 : place * 8 + 8]
+        weighted = grad_mixed * mix_gain[...]
+        mean = jnp.mean(weighted * last, axis=-1, keepdims=True)
+        grads[4, at] = rms * (weighted - last * (rms * rms * mean))
+
+        def layers(step, carry):
+            row = pl.multiple_of(step // 2 * 16, 16)
+            cols = pl.ds(pl.multiple_of(step % 2 * 512, 512), 512)
+            span = pl.ds(seq * SEQ + row, 16)
+            rows_coef = stats[0, span, :]
+            parts = [grads[stream, span, cols] for stream in range(4)]
+            for layer in range(STREAMS_IN):
+                total = None
+                for stream in range(4):
+                    at_coef = stream * STREAMS_IN + layer
+                    term = rows_coef[:, at_coef : at_coef + 1] * parts[stream]
+                    total = term if total is None else total + term
+                if layer == STREAMS_IN - 1:
+                    total = total + grads[4, span, cols]
+                stack_grad[seq, layer, pl.ds(row, 16), cols] = total.astype(jnp.bfloat16)
+            return carry
+
+        lax.fori_loop(0, 8, layers, 0)
+    small[0:36, 0:WIDTH] = up_part
+    for place in range(8):
+        small[36 + place : 37 + place, 0:WIDTH] = jnp.sum(sums[place], axis=0, keepdims=True)
+    small[44:45, 0:WIDTH] = jnp.sum(gain_row, axis=0, keepdims=True)
+
+
+def place_kernel(place, shard0, shard1, shard2, shard3, projection, out_grad, up_grad, down_grad):
+    member, x, core = place[0], place[1], place[2]
+    shards = (shard0, shard1, shard2, shard3)
+    lane = lanes_of((128, 128))
+    for back in range(4):
+        from_x = x if back % 2 == 0 else 1 - x
+        from_core = core if back < 2 else 1 - core
+        quarter = 2 * from_x + from_core
+        own, twin = shards[back], shards[back ^ 2]
+        for index in range(8):
+            half = index % 2
+            mine = wide(own[index // 2, :, half * 128 : half * 128 + 128])
+            half_b = 1 - half
+            lent = wide(twin[index // 2, :, half_b * 128 : half_b * 128 + 128])
+            col = pl.multiple_of((index * 4 + quarter) * 128, 128)
+            up_grad[:, pl.ds(col, 128)] = jnp.where(
+                (lane >= 96) & (from_core == half), lent, mine
+            )
+        row = pl.multiple_of(quarter * 128, 128)
+        for block in range(4):
+            cols = slice(block * 256, block * 256 + 256)
+            down_grad[pl.ds(row, 96), cols] = wide(own[7 + block, 0:96])
+
+            @pl.when(member % 2 == from_core)
+            def _():
+                head_row = pl.multiple_of(from_x * 64, 64)
+                out_grad[pl.ds(head_row, 32), cols] = wide(own[7 + block, 96:128])
+                out_grad[pl.ds(head_row + 32, 32), cols] = wide(
+                    own[11, block * 32 : block * 32 + 32]
+                )
+                down_grad[pl.ds(row + 96, 32), cols] = wide(
+                    twin[11, block * 32 : block * 32 + 32]
+                )
+
+            @pl.when(member % 2 != from_core)
+            def _():
+                down_grad[pl.ds(row + 96, 32), cols] = wide(own[7 + block, 96:128])
+
+    for back in (0, 2):
+        from_core = core if back < 2 else 1 - core
+        for stream in range(3):
+            for twin in range(2):
+                tile = slice(twin * 128, twin * 128 + 128)
+                mine = wide(shards[back][4 + stream, :, tile])
+                across = wide(shards[back + 1][4 + stream, :, tile])
+                even = jnp.where(x == 0, mine, across)
+                odd = jnp.where(x == 0, across, mine)
+                first = jnp.where(lane < 64, even, pltpu.roll(odd, 64, 1))
+                second = jnp.where(lane < 64, pltpu.roll(even, 64, 1), odd)
+                for low, value in ((0, first), (1, second)):
+                    col = pl.multiple_of((2 * twin + low) * 256 + from_core * 128, 128)
+                    projection[stream, :, pl.ds(col, 128)] = value
+
+
+def call(kernel, outs, specs, out_specs, args, scratch=(), cost=None, vmem=60 << 20):
+    return pl.pallas_call(
+        kernel,
+        out_shape=outs,
+        in_specs=specs,
+        out_specs=out_specs,
+        scratch_shapes=list(scratch),
+        compiler_params=pltpu.CompilerParams(vmem_limit_bytes=vmem),
+        cost_estimate=cost,
+    )(*args)
+
+
+def shape_of(shape, dtype=jnp.bfloat16):
+    return jax.ShapeDtypeStruct(shape, dtype)
+
+
+def rope_tables():
+    half_rot = ROTARY // 2
+    step = 10000.0 ** (-2.0 * np.arange(half_rot) / ROTARY)
+    angles = np.arange(SEQ)[:, None] * step[None, :]
+    cos_table = np.ones((SEQ, HEAD_DIM))
+    left = np.zeros((SEQ, HEAD_DIM))
+    right = np.zeros((SEQ, HEAD_DIM))
+    cos_table[:, :half_rot] = np.cos(angles)
+    cos_table[:, half_rot:ROTARY] = np.cos(angles)
+    left[:, :half_rot] = -np.sin(angles)
+    right[:, half_rot:ROTARY] = np.sin(angles)
+    return np.stack([np.tile(item, (2, 2)) for item in (cos_table, left, right)]).astype(np.float32)
+
+
+def on_device_tensor(
+    layer_stack,
+    out_cotangent,
+    pic_start,
+    doc_split,
+    mix_gain,
+    mix_up,
+    mix_down,
+    mix_static,
+    norm_gain,
+    norm_bias,
+    query_key_value,
+    out_weight,
+    up_weight,
+    down_weight,
+):
+    fsdp_index = lax.axis_index("fsdp")
+    z, y = fsdp_index // 2, fsdp_index % 2
+    member = lax.axis_index("replica")
+    x, core = member // 2, member % 2
+    place = jnp.stack([fsdp_index, x, core]).astype(jnp.int32)
+    micro_total, local_seqs, _, _, width = layer_stack.shape
+    seqs = micro_total * local_seqs
+    stack = jnp.transpose(layer_stack, (0, 1, 3, 2, 4)).reshape(seqs, STREAMS_IN, SEQ, width)
+    cotangent = out_cotangent.reshape(ROWS, width)
+    gain_row = mix_gain.reshape(1, width)
+
+    up_one = mix_up.T
+    up_two = order_two(y, up_one, lax.ppermute(up_one, "fsdp", Y_SWAP), 1)
+    up_four = order_two(z % 2, up_two, lax.ppermute(up_two, "fsdp", Z_SWAP_NEAR), 1)
+    mix_up_full = order_two(z // 2, up_four, lax.ppermute(up_four, "fsdp", Z_SWAP_FAR), 1)
+
+    piece = call(
+        prepare_kernel,
+        shape_of((12, 128, 256)),
+        [SMEM_FULL] + [VMEM_FULL] * 4,
+        VMEM_FULL,
+        (place, query_key_value, out_weight, up_weight, down_weight),
+    )
+    piece = after(piece, mix_up_full)
+    bounds = jnp.concatenate([pic_start.reshape(seqs), doc_split.reshape(seqs)])
+    kept = {}
+
+    def front():
+        packet, *kept["rest"] = call(
+            front_kernel,
+            (
+                shape_of((5 * ROWS + 16, width)),
+                shape_of((4, ROWS, width), jnp.float32),
+                shape_of((3, ROWS, 128), jnp.float32),
+                shape_of((ROWS, width), jnp.float32),
+            ),
+            [SMEM_FULL] + [VMEM_FULL] * 8,
+            (VMEM_FULL,) * 4,
+            (
+                bounds,
+                stack,
+                cotangent,
+                gain_row,
+                mix_up_full,
+                mix_down,
+                mix_static.reshape(1, 36),
+                norm_gain,
+                norm_bias,
+            ),
+            scratch=[pltpu.VMEM((4, ROWS, width), jnp.float32)],
+            cost=pl.CostEstimate(flops=30 << 20, bytes_accessed=24 << 20, transcendentals=0),
+        )
+        across = lax.ppermute(packet, "replica", X_SWAP)
+        beside = lax.ppermute(packet, "replica", CORE_SWAP)
+        beside_across = lax.ppermute(across, "replica", CORE_SWAP)
+        kept["packets"] = (packet, across, beside, beside_across)
+        return packet, across
+
+    pieces, origin = gather_fsdp(piece, z, y, front)
+    packets = kept["packets"]
+    scaled, stats, stream_last = kept["rest"]
+
+    target = scatter_order(z, y)
+    results = call(
+        main_kernel,
+        (shape_of((12, 128, 256)),) * 8 + (shape_of((2, 5, ROWS, width)),) * 2,
+        [SMEM_FULL] * 3 + [VMEM_FULL] + [IN_PLACE] * 12,
+        (IN_PLACE,) * 8 + (VMEM_FULL,) * 2,
+        (place, origin, target, jnp.asarray(rope_tables())) + packets + tuple(pieces),
+        scratch=[
+            pltpu.VMEM((5, 4 * ROWS, width), jnp.bfloat16),
+            pltpu.VMEM((4, 16, width), jnp.bfloat16),
+            pltpu.VMEM((4, width, 256), jnp.bfloat16),
+            pltpu.VMEM((3, width, 256), jnp.bfloat16),
+            pltpu.VMEM((8, 5, 128, 256), jnp.bfloat16),
+            pltpu.VMEM((4, 256, 256), jnp.bfloat16),
+            pltpu.VMEM((3, 4 * ROWS, 256), jnp.float32),
+            pltpu.VMEM((5, 4 * ROWS, 256), jnp.bfloat16),
+            pltpu.VMEM((8, 12, 128, 256), jnp.bfloat16),
+            pltpu.VMEM((4 * ROWS, width), jnp.float32),
+            pltpu.VMEM((4 * ROWS, width), jnp.float32),
+            pltpu.SemaphoreType.DMA((4, 6)),
+            pltpu.SemaphoreType.DMA((8, 3)),
+            pltpu.SemaphoreType.DMA((8,)),
+        ],
+        cost=pl.CostEstimate(flops=9 << 30, bytes_accessed=24 << 20, transcendentals=0),
+    )
+    chunks, keep, send = results[:8], results[8], results[9]
+
+    came = lax.ppermute(send, "replica", CORE_SWAP)
+    sum_across = (wide(keep[1]) + wide(came[1])).astype(jnp.bfloat16)
+    came_across = lax.ppermute(sum_across, "replica", X_SWAP)
+
+    first_half = pl.BlockSpec((1, 5, ROWS, width), lambda step: (0, 0, 0, 0))
+
+    def whole(shape):
+        return pl.BlockSpec(shape, lambda step: (0,) * len(shape))
+
+    def back():
+        kept["back"] = pl.pallas_call(
+            back_kernel,
+            grid=(1,),
+            out_shape=(
+                shape_of((ROWS, width)),
+                shape_of((seqs, STREAMS_IN, SEQ, width)),
+                shape_of((48, width + 128), jnp.float32),
+            ),
+            in_specs=[
+                whole((seqs, STREAMS_IN, SEQ, width)),
+                whole((ROWS, width)),
+                whole((4, ROWS, width)),
+                whole((3, ROWS, 128)),
+                whole((ROWS, width)),
+                first_half,
+                first_half,
+                whole((5, ROWS, width)),
+                whole((1, width)),
+                whole((36, width)),
+                whole((36, 36)),
+                whole((4, width)),
+            ],
+            out_specs=(
+                whole((ROWS, width)),
+                whole((seqs, STREAMS_IN, SEQ, width)),
+                whole((48, width + 128)),
+            ),
+            scratch_shapes=[
+                pltpu.VMEM((5, ROWS, width), jnp.float32),
+                pltpu.VMEM((8, 8, width), jnp.float32),
+                pltpu.VMEM((ROWS, 128), jnp.float32),
+            ],
+            compiler_params=pltpu.CompilerParams(vmem_limit_bytes=56 << 20),
+            cost_estimate=pl.CostEstimate(flops=60 << 20, bytes_accessed=36 << 20, transcendentals=0),
+        )(
+            stack,
+            cotangent,
+            scaled,
+            stats,
+            stream_last,
+            keep,
+            came,
+            came_across,
+            gain_row,
+            mix_up_full,
+            mix_down,
+            norm_gain,
+        )
+        return kept["back"][2]
+
+    shard = scatter_fsdp(chunks, z, sum_across, back)
+    layer_output, stack_grad, small = kept["back"]
+
+    shard_across = lax.ppermute(shard, "replica", X_SWAP)
+    shard_beside = lax.ppermute(shard, "replica", CORE_SWAP)
+    shard_both = lax.ppermute(shard_across, "replica", CORE_SWAP)
+    projection_grad, out_grad, up_grad, down_grad = call(
+        place_kernel,
+        (
+            shape_of((3, 128, width), jnp.float32),
+            shape_of((128, width), jnp.float32),
+            shape_of((128, 4 * width), jnp.float32),
+            shape_of((512, width), jnp.float32),
+        ),
+        [SMEM_FULL] + [VMEM_FULL] * 4,
+        (VMEM_FULL,) * 4,
+        (place, shard, shard_across, shard_beside, shard_both),
+    )
+
+    for axis_name, perm in (
+        ("replica", CORE_SWAP),
+        ("replica", X_SWAP),
+        ("fsdp", Y_SWAP),
+        ("fsdp", Z_SWAP_NEAR),
+        ("fsdp", Z_SWAP_FAR),
+    ):
+        small = small + lax.ppermute(small, axis_name, perm)
+    mix_up_grad = lax.dynamic_slice(small, (0, 128 * fsdp_index), (36, 128)).T
+    shape = (micro_total, local_seqs, SEQ)
+    stack_grad = stack_grad.reshape(micro_total, local_seqs, STREAMS_IN, SEQ, width)
+    return (
+        layer_output.reshape(shape + (width,)),
+        stats[0, :, :36].reshape(shape + (4, STREAMS_IN)),
+        jnp.transpose(stack_grad, (0, 1, 3, 2, 4)),
+        small[44, :width],
+        mix_up_grad,
+        small[:36, width : width + 36],
+        small[36, width : width + 36].reshape(4, STREAMS_IN),
+        small[36:40, :width],
+        small[40:44, :width],
+        projection_grad,
+        out_grad,
+        up_grad,
+        down_grad,
+    )
+
+
 def solution(mesh):
+    fits = mesh.shape["fsdp"] == 8 and mesh.shape["replica"] == 4
+    body = on_device_tensor if fits else on_device
     return jax.shard_map(
-        on_device,
+        body,
         mesh=mesh,
         in_specs=(
             P(None, ("fsdp", "replica"), None, None, None),

time: 1680 us -> 315 us (0.19)
  waiting for transfers between devices: 1340 us -> 159 us
  matrix products: 122 us -> 0 us
  blocking collectives: 79.7 us -> 0 us
  Pallas kernels: 0 us -> 69.4 us
  local copies, waits for them, and re-layouts: 64.3 us -> 12.5 us
  starting transfers between devices: 1.65 us -> 53.4 us
  other arithmetic: 43.5 us -> 15.1 us
    reduce_scatter x8 -> x0, waiting for transfers between devices: 868 us -> none  [the longest x2 304 us: on_device(): lax.psum_scatter(grad_up.astype(jnp.bfloat16), 'fsdp', scatter_dimension=...]
    all_gather x4 -> x0, waiting for transfers between devices: 292 us -> none  [the longest x1 120 us: on_device(): lax.all_gather(down_weight, 'fsdp', axis=0, tiled=True)]
    ppermute x0 -> x34, waiting for transfers between devices: none -> 159 us  [the longest x5 34.2 us: on_device_tensor(): small = small + lax.ppermute(small, axis_name, perm)]
    dot_general x60 -> x0, matrix products: 122 us -> none  [the longest x14 45.2 us: back_product(): lax.dot_general(left_side, right_side, (((1,), (1,)), ((), ())), preferre...]
    psum x1 -> x0, waiting for transfers between devices: 111 us -> none  [on_device(): lax.psum(as_sent(shards), 'replica')]
    pallas_call x0 -> x5, Pallas kernels: none -> 69.4 us  [the longest x4 56.1 us: call(): pl.pallas_call(kernel, out_shape=outs, in_specs=specs, out_specs=out_spec...]
    unnamed x17 -> x0, waiting for transfers between devices: 67.5 us -> none
    ppermute x0 -> x34, starting transfers between devices: none -> 53.4 us  [the longest x5 6.65 us: on_device_tensor(): small = small + lax.ppermute(small, axis_name, perm)]
  transfers between devices with their start and end apart: 15 -> 34, of which waited for: 14 -> 21; matrix products, arithmetic and copies ran while one was open for 13% -> 7% of each run, Pallas kernels for 0% -> 8%
where the time goes in v1:
time: 315 us; the launch traced here: 314 us
  waiting for transfers between devices  159 us (50%)
  Pallas kernels  69.4 us (22%)
  starting transfers between devices  53.4 us (17%)
  other arithmetic  15.1 us (5%)
  local copies, waits for them, and re-layouts  12.5 us (4%)
  between operations  4.32 us (1%)
    pallas_call x4, Pallas kernels, call(): pl.pallas_call(kernel, out_shape=outs, in_specs=specs, out_specs=out_spec...  56.1 us
    ppermute x5, waiting for transfers between devices, on_device_tensor(): small = small + lax.ppermute(small, axis_name, perm)  34.2 us
    ppermute x4, waiting for transfers between devices, scatter_fsdp(): came.append(lax.ppermute(sent, 'fsdp', Y_SWAP))  26.6 us
    ppermute x1, waiting for transfers between devices, gather_fsdp(): side_far = lax.ppermute(after(far, side_near, late), 'fsdp', Y_SWAP)  16 us
    ppermute x1, waiting for transfers between devices, gather_fsdp(): lax.ppermute(after(down_first, early), 'fsdp', z_pairs([(1, 0), (2, 1)]))  14.8 us
    ppermute x1, waiting for transfers between devices, gather_fsdp(): lax.ppermute(after(pick(z == 2, up_second, down_second), side_own), 'fsdp...  13.9 us
    pallas_call x1, Pallas kernels, back(): pl.pallas_call(back_kernel, grid=(1,), out_shape=(shape_of((ROWS, width))...  13.4 us
    ppermute x1, waiting for transfers between devices, scatter_fsdp(): lax.ppermute(after(add(pick(z == 2, sums[1], sums[2]), down_one), last_wa...  13.3 us
  transfers between devices with their start and end apart: 34, of which 21 were waited for; matrix products, arithmetic and copies ran while one was open for 7% of the time, Pallas kernels for 8%

profile of v1, /device:TPU:0, one launch (start us, length us, event | category | flops | bytes accessed | tf_op | source)
XLA Modules:
  0.0 314.2 jit_solution(15207490390118288061)
XLA Ops:
  0.6 3.0 collective-permute-start
  3.7 1.9 collective-permute-done
  6.3 2.1 collective-permute-start.1
  8.4 1.8 collective-permute-done.1
  10.2 3.1 collective-permute-start.2
  13.9 3.2 %shard_map.301.piece0 = bf16[12,128,256]{2,1,0:T(8,128)(2,1)} custom-call(s32[3]{0:T(128)} %pad_add_fusion.1.place, bf16[3,128,1024]{2,1,0:T(8,128)(2,1)} %projection.1, bf16[128,1024]{1,0:T(8,128)(2,1)} %out_weight.1, bf16[128,4096]{1,0:T(8,128)(2,1)} %up_weight.1, bf16[512,1024]{1,0:T(8,128)(2,1)} %down_weight.1), custom_call_target="tpu_custom_call" | custom-call | tf_op jit(solution)/shard_map/pallas_call | solution.py:1019
  17.7 3.5 %collective-permute-start.8 = (bf16[12,128,256]{2,1,0:T(8,128)(2,1)}, bf16[12,128,256]{2,1,0:T(8,128)(2,1)S(1)}, u32[]{:S(2)}, u32[]{:S(2)}) collective-permute-start(bf16[12,128,256]{2,1,0:T(8,128)(2,1)} %shard_map.301.piece0), channel_id=1, source_target_pairs={{0,8},{4,12},{8,16},{12,20},{16,24},{20,28},{1,9},{5,13},{9,17},{1... | collective-permute-start | bytes 2359304 | tf_op jit(solution)/shard_map/ppermute | solution.py:396
  23.7 9.6 %shard_map.300 = (bf16[656,1024]{1,0:T(8,128)(2,1)}, f32[4,128,1024]{2,1,0:T(8,128)}, f32[3,128,128]{2,1,0:T(8,128)}, f32[128,1024]{1,0:T(8,128)}) custom-call(s32[4]{0:T(128)} %pad_add_fusion.bounds, bf16[2,9,64,1024]{3,2,1,0:T(8,128)(2,1)} %bitcast.49, bf16[128,1024]{1,0:T(8,128)(2,1)} %bitcast.51, f32[1,1024]{1,0:T(1,128)} %bitcast.53, ...), custom_call_target="tpu_custom_call" | custom-call | flops 31457280 | bytes 25165824 | tf_op jit(solution)/shard_map/pallas_call | solution.py:1019
  33.3 2.4 collective-permute-done.8
  36.4 3.5 %collective-permute-done.7 = bf16[12,128,256]{2,1,0:T(8,128)(2,1)} collective-permute-done((bf16[12,128,256]{2,1,0:T(8,128)(2,1)}, bf16[12,128,256]{2,1,0:T(8,128)(2,1)}, u32[]{:S(2)}, u32[]{:S(2)}) %collective-permute-start.7) | collective-permute-done | bytes 786464 | tf_op jit(solution)/shard_map/ppermute | solution.py:397
  41.2 1.6 collective-permute-start.6
  42.8 14.8 %collective-permute-done.10 = bf16[12,128,256]{2,1,0:T(8,128)(2,1)S(1)} collective-permute-done((bf16[12,128,256]{2,1,0:T(8,128)(2,1)}, bf16[12,128,256]{2,1,0:T(8,128)(2,1)S(1)}, u32[]{:S(2)}, u32[]{:S(2)}) %collective-permute-start.10) | collective-permute-done | bytes 786464 | tf_op jit(solution)/shard_map/ppermute | solution.py:401
  59.0 1.6 collective-permute-start.3
  60.6 13.9 %collective-permute-done.13 = bf16[12,128,256]{2,1,0:T(8,128)(2,1)} collective-permute-done((bf16[12,128,256]{2,1,0:T(8,128)(2,1)S(1)}, bf16[12,128,256]{2,1,0:T(8,128)(2,1)}, u32[]{:S(2)}, u32[]{:S(2)}) %collective-permute-start.13) | collective-permute-done | bytes 786464 | tf_op jit(solution)/shard_map/ppermute | solution.py:404
  74.4 1.6 broadcast_select_fusion.2
  76.0 1.6 collective-permute-start.9
  77.6 8.2 %collective-permute-done.3.packet1 = bf16[656,1024]{1,0:T(8,128)(2,1)} collective-permute-done((bf16[656,1024]{1,0:T(8,128)(2,1)}, bf16[656,1024]{1,0:T(8,128)(2,1)}, u32[]{:S(2)}, u32[]{:S(2)}) %collective-permute-start.3) | collective-permute-done | bytes 1343520 | tf_op jit(solution)/shard_map/ppermute | solution.py:1116
  85.9 1.5 collective-permute-start.12
  87.4 3.4 %collective-permute-done.9.piece3 = bf16[12,128,256]{2,1,0:T(8,128)(2,1)S(1)} collective-permute-done((bf16[12,128,256]{2,1,0:T(8,128)(2,1)S(1)}, bf16[12,128,256]{2,1,0:T(8,128)(2,1)S(1)}, u32[]{:S(2)}, u32[]{:S(2)}) %collective-permute-start.9) | collective-permute-done | bytes 786464 | tf_op jit(solution)/shard_map/ppermute | solution.py:403
  91.7 1.5 collective-permute-start.14
  100.8 7.0 %collective-permute-done.12.piece5 = bf16[12,128,256]{2,1,0:T(8,128)(2,1)} collective-permute-done((bf16[12,128,256]{2,1,0:T(8,128)(2,1)S(1)}, bf16[12,128,256]{2,1,0:T(8,128)(2,1)}, u32[]{:S(2)}, u32[]{:S(2)}) %collective-permute-start.12) | collective-permute-done | bytes 786464 | tf_op jit(solution)/shard_map/ppermute | solution.py:412
  107.8 16.0 %collective-permute-done.14.piece7 = bf16[12,128,256]{2,1,0:T(8,128)(2,1)} collective-permute-done((bf16[12,128,256]{2,1,0:T(8,128)(2,1)S(1)}, bf16[12,128,256]{2,1,0:T(8,128)(2,1)}, u32[]{:S(2)}, u32[]{:S(2)}) %collective-permute-start.14) | collective-permute-done | bytes 786464 | tf_op jit(solution)/shard_map/ppermute | solution.py:414
  123.8 38.2 %shard_map.302 = (bf16[12,128,256]{2,1,0:T(8,128)(2,1)}, bf16[12,128,256]{2,1,0:T(8,128)(2,1)}, bf16[12,128,256]{2,1,0:T(8,128)(2,1)}, bf16[12,128,256]{2,1,0:T(...) custom-call(s32[3]{0:T(128)} %pad_add_fusion.1.place, ...), custom_call_target="tpu_custom_call" | custom-call | flops 9663676416 | bytes 25165824 | tf_op jit(solution)/shard_map/pallas_call | solution.py:1019
  162.1 1.6 collective-permute-start.24
  163.7 18.6 %collective-permute-done.24 = bf16[12,128,256]{2,1,0:T(8,128)(2,1)S(1)} collective-permute-done((bf16[12,128,256]{2,1,0:T(8,128)(2,1)}, bf16[12,128,256]{2,1,0:T(8,128)(2,1)S(1)}, u32[]{:S(2)}, u32[]{:S(2)}) %collective-permute-start.24) | collective-permute-done | bytes 786464 | tf_op jit(solution)/shard_map/ppermute | solution.py:449
  183.6 5.0 %collective-permute-start.26 = (bf16[12,128,256]{2,1,0:T(8,128)(2,1)S(1)}, bf16[12,128,256]{2,1,0:T(8,128)(2,1)}, u32[]{:S(2)}, u32[]{:S(2)}) collective-permute-start(bf16[12,128,256]{2,1,0:T(8,128)(2,1)S(1)} %add_convert_fusion.4), channel_id=1, source_target_pairs={{0,8},{4,12},{24,16},{28,20},{1,9},{5,13},{25,17},{29,21},{2,10},{... | collective-permute-start | bytes 2359304 | tf_op jit(solution)/shard_map/ppermute | solution.py:451
  188.6 2.8 fusion.2
  191.5 1.6 collective-permute-start.22
  195.1 9.3 %collective-permute-done.26 = bf16[12,128,256]{2,1,0:T(8,128)(2,1)} collective-permute-done((bf16[12,128,256]{2,1,0:T(8,128)(2,1)S(1)}, bf16[12,128,256]{2,1,0:T(8,128)(2,1)}, u32[]{:S(2)}, u32[]{:S(2)}) %collective-permute-start.26) | collective-permute-done | bytes 786464 | tf_op jit(solution)/shard_map/ppermute | solution.py:451
  204.3 8.0 %collective-permute-done.22 = bf16[12,128,256]{2,1,0:T(8,128)(2,1)} collective-permute-done((bf16[12,128,256]{2,1,0:T(8,128)(2,1)}, bf16[12,128,256]{2,1,0:T(8,128)(2,1)}, u32[]{:S(2)}, u32[]{:S(2)}) %collective-permute-start.22) | collective-permute-done | bytes 786464 | tf_op jit(solution)/shard_map/ppermute | solution.py:449
  212.3 1.9 fusion
  215.6 2.3 fusion.1
  217.9 1.5 collective-permute-start.29
  219.4 1.5 collective-permute-start.23
  221.0 2.1 collective-permute-done.16.across
  224.1 13.4 %shard_map.303 = (bf16[128,1024]{1,0:T(8,128)(2,1)}, bf16[2,9,64,1024]{3,2,1,0:T(8,128)(2,1)}, f32[48,1152]{1,0:T(8,128)}) custom-call(bf16[2,9,64,1024]{3,2,1,0:T(8,128)(2,1)} %bitcast.50, bf16[128,1024]{1,0:T(8,128)(2,1)} %bitcast.52, f32[4,128,1024]{2,1,0:T(8,128)} %get-tuple-element.45.scaled, f32[3,128,128]{2,1,0:T(8,128)} %get-tuple-element.46.stats, ...), custom_call_target="tpu_custom_call" | custom-call | flops 62914560 | bytes 37748736 | tf_op jit(solution)/shard_map/pallas_call | solution.py:1163
  237.5 1.9 add_convert_fusion.3
  240.7 4.6 %collective-permute-start.28 = (bf16[12,128,256]{2,1,0:T(8,128)(2,1)S(1)}, bf16[12,128,256]{2,1,0:T(8,128)(2,1)S(1)}, u32[]{:S(2)}, u32[]{:S(2)}) collective-permute-start(bf16[12,128,256]{2,1,0:T(8,128)(2,1)S(1)} %get-tuple-element.71), channel_id=1, source_target_pairs={{0,8},{4,12},{8,16},{12,20},{16,24},{20,28},{1,9},{5,13},{9,17},{1... | collective-permute-start | bytes 2359304 | tf_op jit(solution)/shard_map/ppermute | solution.py:457
  245.3 13.3 %collective-permute-done.30 = bf16[12,128,256]{2,1,0:T(8,128)(2,1)S(1)} collective-permute-done((bf16[12,128,256]{2,1,0:T(8,128)(2,1)S(1)}, bf16[12,128,256]{2,1,0:T(8,128)(2,1)S(1)}, u32[]{:S(2)}, u32[]{:S(2)}) %collective-permute-start.30) | collective-permute-done | bytes 786464 | tf_op jit(solution)/shard_map/ppermute | solution.py:462
  260.3 1.6 collective-permute-start.31
  264.0 17.3 %collective-permute-done.18 = f32[48,1152]{1,0:T(8,128)S(1)} collective-permute-done((f32[48,1152]{1,0:T(8,128)S(1)}, f32[48,1152]{1,0:T(8,128)S(1)}, u32[]{:S(2)}, u32[]{:S(2)}) %collective-permute-start.18) | collective-permute-done | bytes 221216 | tf_op jit(solution)/shard_map/ppermute | solution.py:1239
  281.3 1.6 collective-permute-start.19
  282.9 4.4 %collective-permute-done.19 = f32[48,1152]{1,0:T(8,128)S(1)} collective-permute-done((f32[48,1152]{1,0:T(8,128)S(1)}, f32[48,1152]{1,0:T(8,128)S(1)}, u32[]{:S(2)}, u32[]{:S(2)}) %collective-permute-start.19) | collective-permute-done | bytes 221216 | tf_op jit(solution)/shard_map/ppermute | solution.py:1239
  287.3 2.5 collective-permute-start.20
  290.4 5.3 %collective-permute-done.20 = f32[48,1152]{1,0:T(8,128)S(1)} collective-permute-done((f32[48,1152]{1,0:T(8,128)S(1)}, f32[48,1152]{1,0:T(8,128)S(1)}, u32[]{:S(2)}, u32[]{:S(2)}) %collective-permute-start.20) | collective-permute-done | bytes 221216 | tf_op jit(solution)/shard_map/ppermute | solution.py:1239
  295.7 1.9 collective-permute-start.21
  299.3 5.7 %collective-permute-done.21 = f32[48,1152]{1,0:T(8,128)S(1)} collective-permute-done((f32[48,1152]{1,0:T(8,128)S(1)}, f32[48,1152]{1,0:T(8,128)S(1)}, u32[]{:S(2)}, u32[]{:S(2)}) %collective-permute-start.21) | collective-permute-done | bytes 221216 | tf_op jit(solution)/shard_map/ppermute | solution.py:1239
  309.1 5.1 %shard_map.304 = (f32[3,128,1024]{2,1,0:T(8,128)}, f32[128,1024]{1,0:T(8,128)}, f32[128,4096]{1,0:T(8,128)}, f32[512,1024]{1,0:T(8,128)}) custom-call(s32[3]{0:T(128)} %pad_add_fusion.1.place, bf16[12,128,256]{2,1,0:T(8,128)(2,1)} %copy-done.1, bf16[12,128,256]{2,1,0:T(8,128)(2,1)} %copy-done.10, bf16[12,128,256]{2,1,0:T(8,128)(2,1)} %copy-done.11, ...), custom_call_target="tpu_custom_call" | custom-call | tf_op jit(solution)/shard_map/pallas_call | solution.py:1019
  (112 shorter events, 30.1 us)
Async XLA Ops:
  0.6 4.9 %collective-permute-start = (bf16[36,128]{1,0:T(8,128)(2,1)}, bf16[36,128]{1,0:T(8,128)(2,1)S(1)}, u32[]{:S(2)}, u32[]{:S(2)}) collective-permute-start(bf16[36,128]{1,0:T(8,128)(2,1)} %bitcast.55), channel_id=1, source_target_pairs={{0,4},{4,0},{8,12},{12,8},{16,20},{20,16},{24,28},{28,24},{1,5},{5... | collective-permute-start | bytes 27656 | tf_op jit(solution)/shard_map/ppermute | solution.py:1076
  6.3 3.9 %collective-permute-start.1 = (bf16[36,256]{1,0:T(8,128)(2,1)S(1)}, bf16[36,256]{1,0:T(8,128)(2,1)S(1)}, u32[]{:S(2)}, u32[]{:S(2)}) collective-permute-start(bf16[36,256]{1,0:T(8,128)(2,1)S(1)} %pad_maximum_fusion.2), channel_id=1, source_target_pairs={{0,8},{4,12},{8,0},{12,4},{16,24},{20,28},{24,16},{28,20},{1,9},{5... | collective-permute-start | bytes 55304 | tf_op jit(solution)/shard_map/ppermute | solution.py:1077
  10.2 6.9 %collective-permute-start.2 = (bf16[36,512]{1,0:T(8,128)(2,1)S(1)}, bf16[36,512]{1,0:T(8,128)(2,1)S(1)}, u32[]{:S(2)}, u32[]{:S(2)}) collective-permute-start(bf16[36,512]{1,0:T(8,128)(2,1)S(1)} %pad_maximum_fusion.1), channel_id=1, source_target_pairs={{0,16},{4,20},{8,24},{12,28},{16,0},{20,4},{24,8},{28,12},{1,17},{... | collective-permute-start | bytes 110600 | tf_op jit(solution)/shard_map/ppermute | solution.py:1078
  17.1 24.1 %copy-start.4 = (bf16[12,128,256]{2,1,0:T(8,128)(2,1)S(1)}, bf16[12,128,256]{2,1,0:T(8,128)(2,1)}, u32[]{:S(2)}) copy-start(bf16[12,128,256]{2,1,0:T(8,128)(2,1)} %shard_map.301.piece0) | copy-start | bytes 2359300
  17.7 18.0 %collective-permute-start.8 = (bf16[12,128,256]{2,1,0:T(8,128)(2,1)}, bf16[12,128,256]{2,1,0:T(8,128)(2,1)S(1)}, u32[]{:S(2)}, u32[]{:S(2)}) collective-permute-start(bf16[12,128,256]{2,1,0:T(8,128)(2,1)} %shard_map.301.piece0), channel_id=1, source_target_pairs={{0,8},{4,12},{8,16},{12,20},{16,24},{20,28},{1,9},{5,13},{9,17},{1... | collective-permute-start | bytes 2359304 | tf_op jit(solution)/shard_map/ppermute | solution.py:396
  21.3 18.6 %collective-permute-start.7 = (bf16[12,128,256]{2,1,0:T(8,128)(2,1)}, bf16[12,128,256]{2,1,0:T(8,128)(2,1)}, u32[]{:S(2)}, u32[]{:S(2)}) collective-permute-start(bf16[12,128,256]{2,1,0:T(8,128)(2,1)} %shard_map.301.piece0), channel_id=1, source_target_pairs={{8,0},{12,4},{16,8},{20,12},{24,16},{28,20},{9,1},{13,5},{17,9},{2... | collective-permute-start | bytes 2359304 | tf_op jit(solution)/shard_map/ppermute | solution.py:397
  35.7 7.0 %collective-permute-start.11 = (bf16[12,128,256]{2,1,0:T(8,128)(2,1)S(1)}, bf16[12,128,256]{2,1,0:T(8,128)(2,1)S(1)}, u32[]{:S(2)}, u32[]{:S(2)}) collective-permute-start(bf16[12,128,256]{2,1,0:T(8,128)(2,1)S(1)} %collective-permute-done.8), channel_id=1, source_target_pairs={{8,16},{12,20},{16,24},{20,28},{9,17},{13,21},{17,25},{21,29},{10,... | collective-permute-start | bytes 2359304 | tf_op jit(solution)/shard_map/ppermute | solution.py:400
  39.9 17.7 %collective-permute-start.10 = (bf16[12,128,256]{2,1,0:T(8,128)(2,1)}, bf16[12,128,256]{2,1,0:T(8,128)(2,1)S(1)}, u32[]{:S(2)}, u32[]{:S(2)}) collective-permute-start(bf16[12,128,256]{2,1,0:T(8,128)(2,1)} %collective-permute-done.7), channel_id=1, source_target_pairs={{8,0},{12,4},{16,8},{20,12},{9,1},{13,5},{17,9},{21,13},{10,2},{14... | collective-permute-start | bytes 2359304 | tf_op jit(solution)/shard_map/ppermute | solution.py:401
  41.2 16.5 %collective-permute-start.6 = (bf16[12,128,256]{2,1,0:T(8,128)(2,1)S(1)}, bf16[12,128,256]{2,1,0:T(8,128)(2,1)}, u32[]{:S(2)}, u32[]{:S(2)}) collective-permute-start(bf16[12,128,256]{2,1,0:T(8,128)(2,1)S(1)} %copy-done.4), channel_id=1, source_target_pairs={{0,4},{4,0},{8,12},{12,8},{16,20},{20,16},{24,28},{28,24},{1,5},{5... | collective-permute-start | bytes 2359304 | tf_op jit(solution)/shard_map/ppermute | solution.py:398
  57.7 16.8 %collective-permute-start.13 = (bf16[12,128,256]{2,1,0:T(8,128)(2,1)S(1)}, bf16[12,128,256]{2,1,0:T(8,128)(2,1)}, u32[]{:S(2)}, u32[]{:S(2)}) collective-permute-start(bf16[12,128,256]{2,1,0:T(8,128)(2,1)S(1)} %broadcast_select_fusion), channel_id=1, source_target_pairs={{16,24},{20,28},{8,0},{12,4},{17,25},{21,29},{9,1},{13,5},{18,26},... | collective-permute-start | bytes 2359304 | tf_op jit(solution)/shard_map/ppermute | solution.py:404
  59.0 26.9 %collective-permute-start.3 = (bf16[656,1024]{1,0:T(8,128)(2,1)}, bf16[656,1024]{1,0:T(8,128)(2,1)}, u32[]{:S(2)}, u32[]{:S(2)}) collective-permute-start(bf16[656,1024]{1,0:T(8,128)(2,1)} %get-tuple-element.48.packet0), channel_id=1, source_target_pairs={{0,2},{1,3},{2,0},{3,1},{4,6},{5,7},{6,4},{7,5},{8,10},{9,11},{10,... | collective-permute-start | bytes 4030472 | tf_op jit(solution)/shard_map/ppermute | solution.py:1116
  60.5 32.7 %copy-start.23 = (s32[4]{0:T(128)S(1)}, s32[4]{0:T(128)}, u32[]{:S(2)}) copy-start(s32[4]{0:T(128)} %constant.84.clone) | copy-start | bytes 52
  60.5 34.0 %copy-start.22 = (s32[4]{0:T(128)S(1)}, s32[4]{0:T(128)}, u32[]{:S(2)}) copy-start(s32[4]{0:T(128)} %constant.85.clone) | copy-start | bytes 52
  60.5 35.2 %copy-start.21 = (s32[4]{0:T(128)S(1)}, s32[4]{0:T(128)}, u32[]{:S(2)}) copy-start(s32[4]{0:T(128)} %constant.86.clone) | copy-start | bytes 52
  60.5 36.5 %copy-start.20 = (s32[4]{0:T(128)S(1)}, s32[4]{0:T(128)}, u32[]{:S(2)}) copy-start(s32[4]{0:T(128)} %constant.87.clone) | copy-start | bytes 52
  60.5 37.7 %copy-start.19 = (s32[4]{0:T(128)S(1)}, s32[4]{0:T(128)}, u32[]{:S(2)}) copy-start(s32[4]{0:T(128)} %constant.88.clone) | copy-start | bytes 52
  76.0 14.8 %copy-start.8 = (bf16[12,128,256]{2,1,0:T(8,128)(2,1)}, bf16[12,128,256]{2,1,0:T(8,128)(2,1)S(1)}, u32[]{:S(2)}) copy-start(bf16[12,128,256]{2,1,0:T(8,128)(2,1)S(1)} %get-tuple-element.109.piece2) | copy-start | bytes 2359300
  76.0 47.7 %copy-start.6 = (bf16[12,128,256]{2,1,0:T(8,128)(2,1)}, bf16[12,128,256]{2,1,0:T(8,128)(2,1)S(1)}, u32[]{:S(2)}) copy-start(bf16[12,128,256]{2,1,0:T(8,128)(2,1)S(1)} %get-tuple-element.54.piece6) | copy-start | bytes 2359300
  76.0 47.7 %copy-start.7 = (bf16[12,128,256]{2,1,0:T(8,128)(2,1)}, bf16[12,128,256]{2,1,0:T(8,128)(2,1)S(1)}, u32[]{:S(2)}) copy-start(bf16[12,128,256]{2,1,0:T(8,128)(2,1)S(1)} %get-tuple-element.52.piece4) | copy-start | bytes 2359300
  76.0 14.8 %collective-permute-start.9 = (bf16[12,128,256]{2,1,0:T(8,128)(2,1)S(1)}, bf16[12,128,256]{2,1,0:T(8,128)(2,1)S(1)}, u32[]{:S(2)}, u32[]{:S(2)}) collective-permute-start(bf16[12,128,256]{2,1,0:T(8,128)(2,1)S(1)} %get-tuple-element.109.piece2), channel_id=1, source_target_pairs={{0,4},{4,0},{8,12},{12,8},{16,20},{20,16},{24,28},{28,24},{1,5},{5... | collective-permute-start | bytes 2359304 | tf_op jit(solution)/shard_map/ppermute | solution.py:403
  77.6 23.2 %collective-permute-start.4 = (bf16[656,1024]{1,0:T(8,128)(2,1)}, bf16[656,1024]{1,0:T(8,128)(2,1)S(1)}, u32[]{:S(2)}, u32[]{:S(2)}) collective-permute-start(bf16[656,1024]{1,0:T(8,128)(2,1)} %get-tuple-element.48.packet0), channel_id=1, source_target_pairs={{0,1},{1,0},{2,3},{3,2},{4,5},{5,4},{6,7},{7,6},{8,9},{9,8},{10,11... | collective-permute-start | bytes 4030472 | tf_op jit(solution)/shard_map/ppermute | solution.py:1117
  85.9 15.0 %collective-permute-start.5 = (bf16[656,1024]{1,0:T(8,128)(2,1)}, bf16[656,1024]{1,0:T(8,128)(2,1)}, u32[]{:S(2)}, u32[]{:S(2)}) collective-permute-start(bf16[656,1024]{1,0:T(8,128)(2,1)} %collective-permute-done.3.packet1), channel_id=1, source_target_pairs={{0,1},{1,0},{2,3},{3,2},{4,5},{5,4},{6,7},{7,6},{8,9},{9,8},{10,11... | collective-permute-start | bytes 4030472 | tf_op jit(solution)/shard_map/ppermute | solution.py:1118
  85.9 21.9 %collective-permute-start.12 = (bf16[12,128,256]{2,1,0:T(8,128)(2,1)S(1)}, bf16[12,128,256]{2,1,0:T(8,128)(2,1)}, u32[]{:S(2)}, u32[]{:S(2)}) collective-permute-start(bf16[12,128,256]{2,1,0:T(8,128)(2,1)S(1)} %get-tuple-element.52.piece4), channel_id=1, source_target_pairs={{0,4},{4,0},{8,12},{12,8},{16,20},{20,16},{24,28},{28,24},{1,5},{5... | collective-permute-start | bytes 2359304 | tf_op jit(solution)/shard_map/ppermute | solution.py:412
  91.7 32.0 %collective-permute-start.14 = (bf16[12,128,256]{2,1,0:T(8,128)(2,1)S(1)}, bf16[12,128,256]{2,1,0:T(8,128)(2,1)}, u32[]{:S(2)}, u32[]{:S(2)}) collective-permute-start(bf16[12,128,256]{2,1,0:T(8,128)(2,1)S(1)} %get-tuple-element.54.piece6), channel_id=1, source_target_pairs={{0,4},{4,0},{8,12},{12,8},{16,20},{20,16},{24,28},{28,24},{1,5},{5... | collective-permute-start | bytes 2359304 | tf_op jit(solution)/shard_map/ppermute | solution.py:414
  100.8 22.9 %copy-start.15 = (bf16[656,1024]{1,0:T(8,128)(2,1)}, bf16[656,1024]{1,0:T(8,128)(2,1)S(1)}, u32[]{:S(2)}) copy-start(bf16[656,1024]{1,0:T(8,128)(2,1)S(1)} %collective-permute-done.4.packet2) | copy-start | bytes 4030468
  162.0 26.6 %collective-permute-start.15 = (bf16[2,5,128,1024]{3,2,1,0:T(8,128)(2,1)}, bf16[2,5,128,1024]{3,2,1,0:T(8,128)(2,1)S(1)}, u32[]{:S(2)}, u32[]{:S(2)}) collective-permute-start(bf16[2,5,128,1024]{3,2,1,0:T(8,128)(2,1)} %get-tuple-element.56), channel_id=1, source_target_pairs={{0,1},{1,0},{2,3},{3,2},{4,5},{5,4},{6,7},{7,6},{8,9},{9,8},{10,11... | collective-permute-start | bytes 7864328 | tf_op jit(solution)/shard_map/ppermute | solution.py:1153
  162.1 20.2 %collective-permute-start.24 = (bf16[12,128,256]{2,1,0:T(8,128)(2,1)}, bf16[12,128,256]{2,1,0:T(8,128)(2,1)S(1)}, u32[]{:S(2)}, u32[]{:S(2)}) collective-permute-start(bf16[12,128,256]{2,1,0:T(8,128)(2,1)} %get-tuple-element.68), channel_id=1, source_target_pairs={{0,4},{4,0},{8,12},{12,8},{16,20},{20,16},{24,28},{28,24},{1,5},{5... | collective-permute-start | bytes 2359304 | tf_op jit(solution)/shard_map/ppermute | solution.py:449
  183.6 20.8 %collective-permute-start.26 = (bf16[12,128,256]{2,1,0:T(8,128)(2,1)S(1)}, bf16[12,128,256]{2,1,0:T(8,128)(2,1)}, u32[]{:S(2)}, u32[]{:S(2)}) collective-permute-start(bf16[12,128,256]{2,1,0:T(8,128)(2,1)S(1)} %add_convert_fusion.4), channel_id=1, source_target_pairs={{0,8},{4,12},{24,16},{28,20},{1,9},{5,13},{25,17},{29,21},{2,10},{... | collective-permute-start | bytes 2359304 | tf_op jit(solution)/shard_map/ppermute | solution.py:451
  188.6 23.7 %copy-start.3 = (bf16[12,128,256]{2,1,0:T(8,128)(2,1)S(1)}, bf16[12,128,256]{2,1,0:T(8,128)(2,1)}, u32[]{:S(2)}) copy-start(bf16[12,128,256]{2,1,0:T(8,128)(2,1)} %get-tuple-element.65) | copy-start | bytes 2359300
  191.5 20.9 %collective-permute-start.22 = (bf16[12,128,256]{2,1,0:T(8,128)(2,1)}, bf16[12,128,256]{2,1,0:T(8,128)(2,1)}, u32[]{:S(2)}, u32[]{:S(2)}) collective-permute-start(bf16[12,128,256]{2,1,0:T(8,128)(2,1)} %get-tuple-element.63), channel_id=1, source_target_pairs={{0,4},{4,0},{8,12},{12,8},{16,20},{20,16},{24,28},{28,24},{1,5},{5... | collective-permute-start | bytes 2359304 | tf_op jit(solution)/shard_map/ppermute | solution.py:449
  193.1 44.4 %collective-permute-start.25 = (bf16[12,128,256]{2,1,0:T(8,128)(2,1)}, bf16[12,128,256]{2,1,0:T(8,128)(2,1)S(1)}, u32[]{:S(2)}, u32[]{:S(2)}) collective-permute-start(bf16[12,128,256]{2,1,0:T(8,128)(2,1)} %get-tuple-element.69), channel_id=1, source_target_pairs={{0,4},{4,0},{8,12},{12,8},{16,20},{20,16},{24,28},{28,24},{1,5},{5... | collective-permute-start | bytes 2359304 | tf_op jit(solution)/shard_map/ppermute | solution.py:449
  193.6 29.5 %collective-permute-start.16 = (bf16[5,128,1024]{2,1,0:T(8,128)(2,1)S(1)}, bf16[5,128,1024]{2,1,0:T(8,128)(2,1)S(1)}, u32[]{:S(2)}, u32[]{:S(2)}) collective-permute-start(bf16[5,128,1024]{2,1,0:T(8,128)(2,1)S(1)} %fusion.2), channel_id=1, source_target_pairs={{0,2},{1,3},{2,0},{3,1},{4,6},{5,7},{6,4},{7,5},{8,10},{9,11},{10,... | collective-permute-start | bytes 3932168 | tf_op jit(solution)/shard_map/ppermute | solution.py:1155
  214.2 23.3 %collective-permute-start.27 = (bf16[12,128,256]{2,1,0:T(8,128)(2,1)S(1)}, bf16[12,128,256]{2,1,0:T(8,128)(2,1)S(1)}, u32[]{:S(2)}, u32[]{:S(2)}) collective-permute-start(bf16[12,128,256]{2,1,0:T(8,128)(2,1)S(1)} %get-tuple-element.103), channel_id=1, source_target_pairs={{0,8},{4,12},{8,16},{12,20},{1,9},{5,13},{9,17},{13,21},{2,10},{6,... | collective-permute-start | bytes 2359304 | tf_op jit(solution)/shard_map/ppermute | solution.py:454
  217.9 19.6 %collective-permute-start.29 = (bf16[12,128,256]{2,1,0:T(8,128)(2,1)}, bf16[12,128,256]{2,1,0:T(8,128)(2,1)}, u32[]{:S(2)}, u32[]{:S(2)}) collective-permute-start(bf16[12,128,256]{2,1,0:T(8,128)(2,1)} %fusion.1), channel_id=1, source_target_pairs={{24,16},{28,20},{16,8},{20,12},{25,17},{29,21},{17,9},{21,13},{26,... | collective-permute-start | bytes 2359304 | tf_op jit(solution)/shard_map/ppermute | solution.py:455
  219.4 25.9 %collective-permute-start.23 = (bf16[12,128,256]{2,1,0:T(8,128)(2,1)}, bf16[12,128,256]{2,1,0:T(8,128)(2,1)S(1)}, u32[]{:S(2)}, u32[]{:S(2)}) collective-permute-start(bf16[12,128,256]{2,1,0:T(8,128)(2,1)} %get-tuple-element.64), channel_id=1, source_target_pairs={{0,4},{4,0},{8,12},{12,8},{16,20},{20,16},{24,28},{28,24},{1,5},{5... | collective-permute-start | bytes 2359304 | tf_op jit(solution)/shard_map/ppermute | solution.py:449
  237.5 22.3 %copy-start.5 = (bf16[12,128,256]{2,1,0:T(8,128)(2,1)S(1)}, bf16[12,128,256]{2,1,0:T(8,128)(2,1)}, u32[]{:S(2)}) copy-start(bf16[12,128,256]{2,1,0:T(8,128)(2,1)} %get-tuple-element.60) | copy-start | bytes 2359300
  239.4 19.2 %collective-permute-start.30 = (bf16[12,128,256]{2,1,0:T(8,128)(2,1)S(1)}, bf16[12,128,256]{2,1,0:T(8,128)(2,1)S(1)}, u32[]{:S(2)}, u32[]{:S(2)}) collective-permute-start(bf16[12,128,256]{2,1,0:T(8,128)(2,1)S(1)} %get-tuple-element.72), channel_id=1, source_target_pairs={{24,16},{28,20},{16,8},{20,12},{8,0},{12,4},{25,17},{29,21},{17,9}... | collective-permute-start | bytes 2359304 | tf_op jit(solution)/shard_map/ppermute | solution.py:462
  240.7 19.1 %collective-permute-start.28 = (bf16[12,128,256]{2,1,0:T(8,128)(2,1)S(1)}, bf16[12,128,256]{2,1,0:T(8,128)(2,1)S(1)}, u32[]{:S(2)}, u32[]{:S(2)}) collective-permute-start(bf16[12,128,256]{2,1,0:T(8,128)(2,1)S(1)} %get-tuple-element.71), channel_id=1, source_target_pairs={{0,8},{4,12},{8,16},{12,20},{16,24},{20,28},{1,9},{5,13},{9,17},{1... | collective-permute-start | bytes 2359304 | tf_op jit(solution)/shard_map/ppermute | solution.py:457
  260.3 44.7 %copy-start.1 = (bf16[12,128,256]{2,1,0:T(8,128)(2,1)}, bf16[12,128,256]{2,1,0:T(8,128)(2,1)S(1)}, u32[]{:S(2)}) copy-start(bf16[12,128,256]{2,1,0:T(8,128)(2,1)S(1)} %add_convert_fusion.1.shard0) | copy-start | bytes 2359300
  260.3 29.6 %collective-permute-start.31 = (bf16[12,128,256]{2,1,0:T(8,128)(2,1)S(1)}, bf16[12,128,256]{2,1,0:T(8,128)(2,1)S(1)}, u32[]{:S(2)}, u32[]{:S(2)}) collective-permute-start(bf16[12,128,256]{2,1,0:T(8,128)(2,1)S(1)} %add_convert_fusion.1.shard0), channel_id=1, source_target_pairs={{0,2},{1,3},{2,0},{3,1},{4,6},{5,7},{6,4},{7,5},{8,10},{9,11},{10,... | collective-permute-start | bytes 2359304 | tf_op jit(solution)/shard_map/ppermute | solution.py:1216
  261.9 1.5 collective-permute-start.17
  263.4 17.9 %collective-permute-start.18 = (f32[48,1152]{1,0:T(8,128)S(1)}, f32[48,1152]{1,0:T(8,128)S(1)}, u32[]{:S(2)}, u32[]{:S(2)}) collective-permute-start(f32[48,1152]{1,0:T(8,128)S(1)} %add.136), channel_id=1, source_target_pairs={{0,2},{1,3},{2,0},{3,1},{4,6},{5,7},{6,4},{7,5},{8,10},{9,11},{10,... | collective-permute-start | bytes 663560 | tf_op jit(solution)/shard_map/ppermute | solution.py:1239
  281.3 6.0 %collective-permute-start.19 = (f32[48,1152]{1,0:T(8,128)S(1)}, f32[48,1152]{1,0:T(8,128)S(1)}, u32[]{:S(2)}, u32[]{:S(2)}) collective-permute-start(f32[48,1152]{1,0:T(8,128)S(1)} %add.137), channel_id=1, source_target_pairs={{0,4},{4,0},{8,12},{12,8},{16,20},{20,16},{24,28},{28,24},{1,5},{5... | collective-permute-start | bytes 663560 | tf_op jit(solution)/shard_map/ppermute | solution.py:1239
  287.3 8.4 %collective-permute-start.20 = (f32[48,1152]{1,0:T(8,128)S(1)}, f32[48,1152]{1,0:T(8,128)S(1)}, u32[]{:S(2)}, u32[]{:S(2)}) collective-permute-start(f32[48,1152]{1,0:T(8,128)S(1)} %add.138), channel_id=1, source_target_pairs={{0,8},{4,12},{8,0},{12,4},{16,24},{20,28},{24,16},{28,20},{1,9},{5... | collective-permute-start | bytes 663560 | tf_op jit(solution)/shard_map/ppermute | solution.py:1239
  289.9 18.3 %collective-permute-start.32 = (bf16[12,128,256]{2,1,0:T(8,128)(2,1)S(1)}, bf16[12,128,256]{2,1,0:T(8,128)(2,1)S(1)}, u32[]{:S(2)}, u32[]{:S(2)}) collective-permute-start(bf16[12,128,256]{2,1,0:T(8,128)(2,1)S(1)} %add_convert_fusion.1.shard0), channel_id=1, source_target_pairs={{0,1},{1,0},{2,3},{3,2},{4,5},{5,4},{6,7},{7,6},{8,9},{9,8},{10,11... | collective-permute-start | bytes 2359304 | tf_op jit(solution)/shard_map/ppermute | solution.py:1217
  289.9 18.3 %copy-start.10 = (bf16[12,128,256]{2,1,0:T(8,128)(2,1)}, bf16[12,128,256]{2,1,0:T(8,128)(2,1)S(1)}, u32[]{:S(2)}) copy-start(bf16[12,128,256]{2,1,0:T(8,128)(2,1)S(1)} %collective-permute-done.31.shard1) | copy-start | bytes 2359300
  289.9 18.3 %collective-permute-start.33 = (bf16[12,128,256]{2,1,0:T(8,128)(2,1)S(1)}, bf16[12,128,256]{2,1,0:T(8,128)(2,1)}, u32[]{:S(2)}, u32[]{:S(2)}) collective-permute-start(bf16[12,128,256]{2,1,0:T(8,128)(2,1)S(1)} %collective-permute-done.31.shard1), channel_id=1, source_target_pairs={{0,1},{1,0},{2,3},{3,2},{4,5},{5,4},{6,7},{7,6},{8,9},{9,8},{10,11... | collective-permute-start | bytes 2359304 | tf_op jit(solution)/shard_map/ppermute | solution.py:1218
  295.7 9.3 %collective-permute-start.21 = (f32[48,1152]{1,0:T(8,128)S(1)}, f32[48,1152]{1,0:T(8,128)S(1)}, u32[]{:S(2)}, u32[]{:S(2)}) collective-permute-start(f32[48,1152]{1,0:T(8,128)S(1)} %add.139), channel_id=1, source_target_pairs={{0,16},{4,20},{8,24},{12,28},{16,0},{20,4},{24,8},{28,12},{1,17},{... | collective-permute-start | bytes 663560 | tf_op jit(solution)/shard_map/ppermute | solution.py:1239
  (10 other events, 55.4 us)

commit v2 on v1

--- a/solution.py
+++ b/solution.py
@@ -392,49 +392,64 @@
     return lax.optimization_barrier((value,) + others)[0]
 
 
-def gather_fsdp(piece, z, y, front):
-    up_first = lax.ppermute(piece, "fsdp", z_pairs([(0, 1), (1, 2), (2, 3)]))
-    down_first = lax.ppermute(piece, "fsdp", z_pairs([(1, 0), (2, 1), (3, 2)]))
-    side_own = lax.ppermute(piece, "fsdp", Y_SWAP)
+Z_NEAR = z_pairs([(0, 1), (1, 0), (2, 3), (3, 2)])
+Z_MIDDLE = z_pairs([(0, 0), (1, 2), (2, 1), (3, 3)])
+
+
+def fsdp_move(value, pairs):
+    return lax.ppermute(value, "fsdp", pairs)
+
+
+def gather_fsdp(piece, z, front):
+    inner = (z == 1) | (z == 2)
+    near = fsdp_move(piece, Z_NEAR)
+    middle = fsdp_move(piece, Z_MIDDLE)
+    side_own = fsdp_move(piece, Y_SWAP)
     early, late = front()
-    up_second = lax.ppermute(after(up_first, early), "fsdp", z_pairs([(1, 2), (2, 3)]))
-    down_second = lax.ppermute(after(down_first, early), "fsdp", z_pairs([(1, 0), (2, 1)]))
-    near = pick(z == 0, down_first, up_first)
-    side_near = lax.ppermute(near, "fsdp", Y_SWAP)
-    last = lax.ppermute(
-        after(pick(z == 2, up_second, down_second), side_own),
-        "fsdp",
-        z_pairs([(2, 3), (1, 0)]),
-    )
-    second_any = pick(z < 2, down_second, up_second)
-    inner = (z == 1) | (z == 2)
-    middle = pick(inner, down_first, second_any)
-    side_middle = lax.ppermute(after(middle, side_own), "fsdp", Y_SWAP)
-    far = pick(inner, second_any, last)
-    side_far = lax.ppermute(after(far, side_near, late), "fsdp", Y_SWAP)
-    pieces = [piece, side_own, near, side_near, middle, side_middle, far, side_far]
+    side_near = fsdp_move(near, Y_SWAP)
+    middle_near = fsdp_move(after(near, early, side_own), Z_MIDDLE)
+    near_middle = fsdp_move(after(middle, early, side_own), Z_NEAR)
+    third = pick(inner, middle, near_middle)
+    near_twice = fsdp_move(after(middle_near, side_near, third), Z_NEAR)
+    side_third = fsdp_move(after(third, late), Y_SWAP)
+    last = pick(inner, middle_near, near_twice)
+    side_last = fsdp_move(after(last, side_third), Y_SWAP)
+    return [piece, side_own, near, side_near, third, side_third, last, side_last]
+
+
+def position():
+    member, partner = lax.axis_index("fsdp"), lax.axis_index("replica")
+    return member // 2, member % 2, partner // 2, partner % 2
+
+
+def table(values, z):
+    found = jnp.int32(values[0])
+    for index in range(1, 4):
+        found = jnp.where(z == index, jnp.int32(values[index]), found)
+    return found
+
+
+def gather_order(z, y):
     places = []
-    for z_from in (z, table([1, 0, 1, 2], z), table([2, 2, 3, 1], z), table([3, 3, 0, 0], z)):
+    for z_from in (z, table([1, 0, 3, 2], z), table([2, 2, 1, 1], z), table([3, 3, 0, 0], z)):
         places += [2 * z_from + y, 2 * z_from + 1 - y]
-    return pieces, jnp.stack(places)
-
-
-def table(values, z):
-    return jnp.asarray(values, jnp.int32)[z]
+    return places
 
 
 def scatter_order(z, y):
     places = []
     for z_to in (table([3, 3, 0, 0], z), table([2, 2, 1, 1], z), table([1, 0, 3, 2], z), z):
         places += [2 * z_to + 1 - y, 2 * z_to + y]
-    return jnp.stack(places)
+    return places
 
 
 def wide(value):
     return value.astype(jnp.float32)
 
 
-def scatter_fsdp(chunks, z, first_wait, beside):
+def scatter_fsdp(chunks, z, first_wait, second_wait, beside):
+    inner = (z == 1) | (z == 2)
+
     def add(first, second):
         return (wide(first) + wide(second)).astype(jnp.bfloat16)
 
@@ -442,29 +457,20 @@
     sums = []
     for turn in range(4):
         sent = chunks[2 * turn]
-        if turn == 1:
-            sent = after(sent, first_wait)
         if turn >= 2:
             sent = after(sent, came[turn - 2])
-        came.append(lax.ppermute(sent, "fsdp", Y_SWAP))
-        sums.append(add(chunks[2 * turn + 1], came[turn]))
-    first = lax.ppermute(sums[0], "fsdp", z_pairs([(0, 1), (3, 2)]))
-    up_send = add(pick(z == 0, sums[1], sums[0]), first)
-    down_send = add(pick(z == 3, sums[1], sums[0]), first)
-    up_one = lax.ppermute(up_send, "fsdp", z_pairs([(0, 1), (1, 2)]))
-    down_one = lax.ppermute(down_send, "fsdp", z_pairs([(3, 2), (2, 1)]))
+        came.append(fsdp_move(sent, Y_SWAP))
+        held = chunks[2 * turn + 1]
+        sums.append(add(after(held, first_wait) if turn == 0 else held, came[turn]))
+    far = fsdp_move(sums[0], Z_NEAR)
+    far = fsdp_move(after(add(sums[0], far), second_wait), Z_MIDDLE)
+    second = fsdp_move(after(sums[1], second_wait), Z_NEAR)
     last_wait = beside()
-    up_two = lax.ppermute(
-        after(add(pick(z == 1, sums[1], sums[2]), up_one), last_wait),
-        "fsdp",
-        z_pairs([(0, 1), (1, 2), (2, 3)]),
-    )
-    down_two = lax.ppermute(
-        after(add(pick(z == 2, sums[1], sums[2]), down_one), last_wait),
-        "fsdp",
-        z_pairs([(3, 2), (2, 1), (1, 0)]),
-    )
-    return (wide(sums[3]) + wide(up_two) + wide(down_two)).astype(jnp.bfloat16)
+    last = add(sums[2], jnp.where(inner, wide(far), 0.0))
+    last = fsdp_move(after(last, last_wait), Z_NEAR)
+    second = fsdp_move(after(add(sums[1], second), last_wait), Z_MIDDLE)
+    total = wide(sums[3]) + wide(last) + jnp.where(inner, wide(second), 0.0)
+    return total.astype(jnp.bfloat16)
 
 
 def lanes_of(shape):
@@ -475,8 +481,8 @@
     return lax.broadcasted_iota(jnp.int32, shape, 0)
 
 
-def prepare_kernel(place, projection, out_weight, up_weight, down_weight, piece):
-    member, x, core = place[0], place[1], place[2]
+def prepare_kernel(projection, out_weight, up_weight, down_weight, piece):
+    _, member_parity, x, core = position()
     quarter, other = 2 * x + core, 2 * x + 1 - core
     lane = lanes_of((128, 128))
     for index in range(8):
@@ -511,12 +517,12 @@
         cols = slice(block * 256, block * 256 + 256)
         piece[7 + block, 0:96] = down_weight[pl.ds(own_row, 96), cols]
 
-        @pl.when(member % 2 == core)
+        @pl.when(member_parity == core)
         def _():
             piece[7 + block, 96:128] = out_weight[pl.ds(head_row, 32), cols]
             piece[11, block * 32 : block * 32 + 32] = out_weight[pl.ds(head_row + 32, 32), cols]
 
-        @pl.when(member % 2 != core)
+        @pl.when(member_parity != core)
         def _():
             piece[7 + block, 96:128] = down_weight[pl.ds(own_row + 96, 32), cols]
             piece[11, block * 32 : block * 32 + 32] = down_weight[pl.ds(other_row + 96, 32), cols]
@@ -527,7 +533,10 @@
     stack,
     cotangent,
     mix_gain,
-    mix_up,
+    up_own,
+    up_one,
+    up_two,
+    up_three,
     mix_down,
     mix_static,
     norm_gain,
@@ -536,9 +545,16 @@
     scaled_out,
     stats,
     stream_out,
+    mix_up,
     streams,
 ):
     seqs = stack.shape[0]
+    z, y, _, _ = position()
+    for step, part in enumerate((up_own, up_one, up_two, up_three)):
+        z_from = (z + step) % 4
+        for half, col in enumerate((y, 1 - y)):
+            lanes = pl.ds(pl.multiple_of((2 * z_from + col) * 128, 128), 128)
+            mix_up[:, lanes] = part[:, half * 128 : half * 128 + 128]
     for seq in range(seqs):
         last = wide(stack[seq, STREAMS_IN - 1])
         rms = lax.rsqrt(jnp.mean(last * last, axis=-1, keepdims=True) + EPSILON)
@@ -598,9 +614,6 @@
 
 
 def main_kernel(
-    place,
-    origin,
-    target,
     rope,
     packet0,
     packet1,
@@ -628,77 +641,104 @@
     marks,
     up_all,
     lin_all,
-    down_all,
-    out_all,
+    rhs_all,
+    spare,
+    lhs_all,
+    grad_pre,
     linear,
-    low_lin,
+    grad_att,
+    grad_lin,
     parts,
-    out_total,
-    norm_total,
-    sems,
+    tokens,
+    packet_sems,
     piece_sems,
     chunk_sems,
+    token_sems,
 ):
-    core = place[2]
+    z, y, _, core = position()
+    origin = gather_order(z, y)
+    target = scatter_order(z, y)
     packets = (packet0, packet1, packet2, packet3)
     pieces = (piece0, piece1, piece2, piece3, piece4, piece5, piece6, piece7)
     chunks = (chunk0, chunk1, chunk2, chunk3, chunk4, chunk5, chunk6, chunk7)
-    copies = []
+    member_rows = [pl.ds(pl.multiple_of(place * 128, 128), 128) for place in origin]
+
+    def unit_copies(unit):
+        return [
+            pltpu.make_async_copy(
+                packets[block].at[pl.ds(unit * ROWS, ROWS)],
+                acts.at[unit, pl.ds(block * ROWS, ROWS)],
+                packet_sems.at[block, unit],
+            )
+            for block in range(4)
+        ]
+
+    first = unit_copies(0) + unit_copies(1) + unit_copies(2)
+    for index in range(8):
+        first.append(
+            pltpu.make_async_copy(
+                pieces[index].at[pl.ds(4, 3)],
+                lin_all.at[:, member_rows[index]],
+                piece_sems.at[index, 0],
+            )
+        )
+    second = unit_copies(4)
     for block in range(4):
-        for unit in range(5):
-            copies.append(
+        second.append(
+            pltpu.make_async_copy(
+                packets[block].at[pl.ds(5 * ROWS, 16)], marks.at[block], packet_sems.at[block, 5]
+            )
+        )
+    for index in range(8):
+        for block in range(4):
+            second.append(
                 pltpu.make_async_copy(
-                    packets[block].at[pl.ds(unit * ROWS, ROWS)],
-                    acts.at[unit, pl.ds(block * ROWS, ROWS)],
-                    sems.at[block, unit],
+                    pieces[index].at[7 + block],
+                    rhs_all.at[member_rows[index], pl.ds(block * 256, 256)],
+                    piece_sems.at[index, 1 + block],
                 )
             )
-        copies.append(
+        second.append(
             pltpu.make_async_copy(
-                packets[block].at[pl.ds(5 * ROWS, 16)], marks.at[block], sems.at[block, 5]
+                pieces[index].at[11], spare.at[origin[index]], piece_sems.at[index, 5]
             )
         )
+    third = unit_copies(3)
     for index in range(8):
-        rows = pl.ds(pl.multiple_of(origin[index] * 128, 128), 128)
-        piece = pieces[index]
-        copies.append(
-            pltpu.make_async_copy(
-                piece.at[pl.ds(4, 3)], lin_all.at[:, rows], piece_sems.at[index, 0]
+        for block in range(4):
+            third.append(
+                pltpu.make_async_copy(
+                    pieces[index].at[block],
+                    up_all.at[member_rows[index], pl.ds(block * 256, 256)],
+                    piece_sems.at[index, 6 + block],
+                )
             )
-        )
-        copies.append(
-            pltpu.make_async_copy(
-                piece.at[pl.ds(0, 4)], up_all.at[:, rows], piece_sems.at[index, 1]
-            )
-        )
-        copies.append(
-            pltpu.make_async_copy(
-                piece.at[pl.ds(7, 5)], down_all.at[origin[index]], piece_sems.at[index, 2]
-            )
-        )
-    for copy in copies:
+    for copy in first + second + third:
         copy.start()
-    for copy in copies:
+    for copy in first:
+        copy.wait()
+    for stream in range(3):
+        linear[stream] = matmul(acts[stream], lin_all[stream])
+    for copy in second:
         copy.wait()
     for pair in range(4):
         even = 2 * pair + core
         odd = 2 * pair + 1 - core
+        tail = pl.ds(pl.multiple_of(even * 128 + 96, 32), 32)
+        first_rows = slice(WIDTH + pair * 64, WIDTH + pair * 64 + 32)
+        last_rows = slice(WIDTH + pair * 64 + 32, WIDTH + pair * 64 + 64)
         for block in range(4):
             band = slice(block * 32, block * 32 + 32)
-            out_all[block, pair * 64 : pair * 64 + 32] = down_all[even, block, 96:128]
-            out_all[block, pair * 64 + 32 : pair * 64 + 64] = down_all[even, 4, band]
-            down_all[even, block, 96:128] = down_all[odd, 4, band]
-
-    for stream in range(3):
-        linear[stream] = matmul(acts[stream], lin_all[stream])
-    total = None
-    for block in range(4):
-        term = back_product(acts[4, :, block * 256 : block * 256 + 256], out_all[block])
-        total = term if total is None else total + term
-    low_lin[3] = total.astype(jnp.bfloat16)
+            cols = slice(block * 256, block * 256 + 256)
+            rhs_all[first_rows, cols] = rhs_all[tail, cols]
+            rhs_all[last_rows, cols] = spare[even, band]
+            rhs_all[tail, cols] = spare[odd, band]
+
+    grad_att[...] = back_product(acts[4], rhs_all[WIDTH:, :]).astype(jnp.bfloat16)
     cos_table = rope[0]
     sin_left = rope[1]
     sin_right = rope[2]
+    scale = HEAD_DIM ** (-0.5)
 
     def turn(value, sign):
         return (
@@ -712,10 +752,8 @@
         lane = lanes_of((ROWS, ROWS))
         bound = wide(marks[block])
 
-        def both(first, second):
-            by_lane = jnp.where(lane < SEQ, first, second)
-            by_row = jnp.where(row < SEQ, first, second)
-            return by_row, by_lane
+        def both(low, high):
+            return jnp.where(row < SEQ, low, high), jnp.where(lane < SEQ, low, high)
 
         start_q, start_k = both(bound[0:1, 0:128], bound[1:2, 0:128])
         split_q, split_k = both(bound[2:3, 0:128], bound[3:4, 0:128])
@@ -724,114 +762,138 @@
         same = (row // SEQ == lane // SEQ) & ((at_q >= split_q) == (at_k >= split_k))
         pic_q = (at_q >= start_q) & (at_q < start_q + PIC)
         pic_k = (at_k >= start_k) & (at_k < start_k + PIC)
-        allowed = same & ((at_q >= at_k) | (pic_q & pic_k))
+        penalty = jnp.where(same & ((at_q >= at_k) | (pic_q & pic_k)), 0.0, -1e30)
         span = pl.ds(pl.multiple_of(block * ROWS, ROWS), ROWS)
-        for twin in range(2):
-            cols = slice(twin * 128, twin * 128 + 128)
-            query = turn(linear[0, span, cols], 1.0)
-            key_wide = turn(linear[1, span, cols], 1.0)
-            query_low = query.astype(jnp.bfloat16)
-            key_low = key_wide.astype(jnp.bfloat16)
-            value_low = linear[2, span, cols].astype(jnp.bfloat16)
-            grad_att = low_lin[3, span, cols]
-            grad_wide = wide(grad_att)
-            got = []
-            for head in range(2):
-                inside = (lane // 64) == head
-                query_head = jnp.where(inside, query, 0.0).astype(jnp.bfloat16)
-                grad_head = jnp.where(inside, grad_wide, 0.0).astype(jnp.bfloat16)
-                scores = back_product(query_head, key_low) * HEAD_DIM ** (-0.5)
-                scores = jnp.where(allowed, scores, -1e30)
-                exponent = jnp.exp(scores - jnp.max(scores, axis=-1, keepdims=True))
-                probs = exponent / jnp.sum(exponent, axis=-1, keepdims=True)
-                probs_low = probs.astype(jnp.bfloat16)
-                attended = matmul(probs_low, value_low)
-                grad_probs = back_product(grad_head, value_low)
-                grad_value = outer_sum(probs_low, grad_att)
-                delta = jnp.sum(probs * grad_probs, axis=-1, keepdims=True)
-                grad_scores = (probs * (grad_probs - delta)).astype(jnp.bfloat16)
-                grad_query = matmul(grad_scores, key_low)
-                grad_key = outer_sum(grad_scores, query_low)
-                got.append((attended, grad_query, grad_key, grad_value))
-            merged = [jnp.where(lane < 64, low, high) for low, high in zip(*got)]
-            scale = HEAD_DIM ** (-0.5)
-            low_lin[4, span, cols] = merged[0].astype(jnp.bfloat16)
-            low_lin[0, span, cols] = turn(merged[1] * scale, -1.0).astype(jnp.bfloat16)
-            low_lin[1, span, cols] = turn(merged[2] * scale, -1.0).astype(jnp.bfloat16)
-            low_lin[2, span, cols] = merged[3].astype(jnp.bfloat16)
+        twins = [slice(twin * 128, twin * 128 + 128) for twin in range(2)]
+        heads = [(twin, head) for twin in range(2) for head in range(2)]
+        query = [turn(linear[0, span, cols], 1.0) for cols in twins]
+        query_low = [item.astype(jnp.bfloat16) for item in query]
+        key_low = [turn(linear[1, span, cols], 1.0).astype(jnp.bfloat16) for cols in twins]
+        value_low = [linear[2, span, cols].astype(jnp.bfloat16) for cols in twins]
+        grad_low = [grad_att[span, cols] for cols in twins]
+
+        def only(item, head):
+            return jnp.where(lane // 64 == head, wide(item), 0.0).astype(jnp.bfloat16)
+
+        scores = [
+            back_product(only(query[twin], head), key_low[twin]) * scale + penalty
+            for twin, head in heads
+        ]
+        grad_probs = [
+            back_product(only(grad_low[twin], head), value_low[twin]) for twin, head in heads
+        ]
+        exponent = [jnp.exp(item - jnp.max(item, axis=-1, keepdims=True)) for item in scores]
+        probs = [item / jnp.sum(item, axis=-1, keepdims=True) for item in exponent]
+        probs_low = [item.astype(jnp.bfloat16) for item in probs]
+        grad_scores = [
+            (prob * (grad - jnp.sum(prob * grad, axis=-1, keepdims=True))).astype(jnp.bfloat16)
+            for prob, grad in zip(probs, grad_probs)
+        ]
+        attended = [matmul(probs_low[i], value_low[heads[i][0]]) for i in range(4)]
+        grad_value = [outer_sum(probs_low[i], grad_low[heads[i][0]]) for i in range(4)]
+        grad_query = [matmul(grad_scores[i], key_low[heads[i][0]]) for i in range(4)]
+        grad_key = [outer_sum(grad_scores[i], query_low[heads[i][0]]) for i in range(4)]
+
+        def merge(items, twin):
+            return jnp.where(lane < 64, items[2 * twin], items[2 * twin + 1])
+
+        for twin, cols in enumerate(twins):
+            side = slice(WIDTH + twin * 128, WIDTH + twin * 128 + 128)
+            lhs_all[span, side] = merge(attended, twin).astype(jnp.bfloat16)
+            grad_lin[0, span, cols] = turn(merge(grad_query, twin) * scale, -1.0).astype(
+                jnp.bfloat16
+            )
+            grad_lin[1, span, cols] = turn(merge(grad_key, twin) * scale, -1.0).astype(
+                jnp.bfloat16
+            )
+            grad_lin[2, span, cols] = merge(grad_value, twin).astype(jnp.bfloat16)
         return carry
 
     lax.fori_loop(0, 4, units, 0)
 
-    def put(unit, value):
-        low = value.astype(jnp.bfloat16)
-        for block in range(2):
-            keep[block, unit] = low[block * ROWS : block * ROWS + ROWS]
-            send[block, unit] = low[(2 + block) * ROWS : (3 + block) * ROWS]
-
+    for copy in third:
+        copy.wait()
+
+    def hidden(pair, carry):
+        cols = pl.ds(pl.multiple_of(pair * 256, 256), 256)
+        up_pre = matmul(acts[3], up_all[:, cols])
+        bell = 0.5 * (1.0 + lax.erf(up_pre * ROOT_HALF))
+        slope = bell + up_pre * NORMAL_PEAK * jnp.exp(-0.5 * up_pre * up_pre)
+        lhs_all[:, cols] = (up_pre * bell).astype(jnp.bfloat16)
+        grad_gated = back_product(acts[4], rhs_all[cols, :])
+        grad_pre[:, cols] = (grad_gated * slope).astype(jnp.bfloat16)
+        return carry
+
+    lax.fori_loop(0, 4, hidden, 0)
+
+    def weights(index, carry):
+        cols = pl.ds(pl.multiple_of(index * 128, 128), 128)
+        grad = outer_sum(acts[3, :, cols], grad_pre[...]).astype(jnp.bfloat16)
+        for block in range(4):
+            parts[index, block] = grad[:, block * 256 : block * 256 + 256]
+        for stream in range(3):
+            parts[index, 4 + stream] = outer_sum(acts[stream, :, cols], grad_lin[stream]).astype(
+                jnp.bfloat16
+            )
+        grad = outer_sum(lhs_all[:, cols], acts[4]).astype(jnp.bfloat16)
+        other = index + 1 - 2 * (index % 2)
+        for block in range(4):
+            part = grad[:, block * 256 : block * 256 + 256]
+            parts[index, 7 + block, 0:96] = part[0:96]
+
+            @pl.when(index % 2 == core)
+            def _():
+                parts[other, 11, block * 32 : block * 32 + 32] = part[96:128]
+
+            @pl.when(index % 2 != core)
+            def _():
+                parts[index, 7 + block, 96:128] = part[96:128]
+
+        return carry
+
+    lax.fori_loop(0, 8, weights, 0)
+    grad = outer_sum(lhs_all[:, WIDTH:], acts[4]).astype(jnp.bfloat16)
     for block in range(4):
-        cols = slice(block * 256, block * 256 + 256)
-        out_total[:, cols] = matmul(low_lin[4], out_all[block])
-        grad = outer_sum(low_lin[4], acts[4, :, cols]).astype(jnp.bfloat16)
+        part = grad[:, block * 256 : block * 256 + 256]
         for pair in range(4):
             even = 2 * pair + core
-            parts[even, 7 + block, 96:128] = grad[pair * 64 : pair * 64 + 32]
-            parts[even, 11, block * 32 : block * 32 + 32] = grad[pair * 64 + 32 : pair * 64 + 64]
-    for stream in range(3):
-        grad = outer_sum(acts[stream], low_lin[stream]).astype(jnp.bfloat16)
-        for index in range(8):
-            parts[index, 4 + stream] = grad[index * 128 : index * 128 + 128]
-        put(stream, back_product(low_lin[stream], lin_all[stream]))
-
-    norm_total[...] = jnp.zeros_like(norm_total)
-
-    def hidden(pair, carry):
-        up_pre = matmul(acts[3], up_all[pair])
-        bell = 0.5 * (1.0 + lax.erf(up_pre * ROOT_HALF))
-        gated = (up_pre * bell).astype(jnp.bfloat16)
-        slope = bell + up_pre * NORMAL_PEAK * jnp.exp(-0.5 * up_pre * up_pre)
-        grad_gated = None
-        for block in range(4):
-            cols = slice(block * 256, block * 256 + 256)
-            rows_down = jnp.concatenate(
-                [down_all[2 * pair, block], down_all[2 * pair + 1, block]], axis=0
-            )
-            term = back_product(acts[4, :, cols], rows_down)
-            grad_gated = term if grad_gated is None else grad_gated + term
-            out_total[:, cols] += matmul(gated, rows_down)
-        grad_pre = (grad_gated * slope).astype(jnp.bfloat16)
-        norm_total[...] += back_product(grad_pre, up_all[pair])
-        grad = outer_sum(acts[3], grad_pre).astype(jnp.bfloat16)
-        for index in range(8):
-            parts[index, pair] = grad[index * 128 : index * 128 + 128]
-        for block in range(4):
-            cols = slice(block * 256, block * 256 + 256)
-            grad = outer_sum(gated, acts[4, :, cols]).astype(jnp.bfloat16)
-            even, odd = 2 * pair + core, 2 * pair + 1 - core
-            for half in range(2):
-                parts[2 * pair + half, 7 + block, 0:96] = grad[half * 128 : half * 128 + 96]
-
-                @pl.when(core == half)
-                def _():
-                    parts[odd, 11, block * 32 : block * 32 + 32] = grad[
-                        half * 128 + 96 : half * 128 + 128
-                    ]
-
-                @pl.when(core != half)
-                def _():
-                    parts[odd, 7 + block, 96:128] = grad[half * 128 + 96 : half * 128 + 128]
-
-        return carry
-
-    lax.fori_loop(0, 4, hidden, 0)
+            parts[even, 7 + block, 96:128] = part[pair * 64 : pair * 64 + 32]
+            parts[even, 11, block * 32 : block * 32 + 32] = part[pair * 64 + 32 : pair * 64 + 64]
     sent = [
         pltpu.make_async_copy(parts.at[target[index]], chunks[index], chunk_sems.at[index])
         for index in range(8)
     ]
     for copy in sent:
         copy.start()
-    put(3, norm_total[...])
-    put(4, out_total[...])
+
+    def put(unit, cols, value):
+        low = value.astype(jnp.bfloat16)
+        for half in range(2):
+            for block in range(2):
+                at = (2 * half + block) * ROWS
+                tokens[half, block, unit, :, cols] = low[at : at + ROWS]
+
+    def ship(unit):
+        for half, ref in enumerate((keep, send)):
+            copy = pltpu.make_async_copy(
+                tokens.at[half, :, unit], ref.at[:, unit], token_sems.at[half, unit]
+            )
+            copy.start()
+            sent.append(copy)
+
+    for stream in range(3):
+        put(stream, slice(0, WIDTH), back_product(grad_lin[stream], lin_all[stream]))
+        ship(stream)
+
+    def feed(block, carry):
+        cols = pl.ds(pl.multiple_of(block * 256, 256), 256)
+        put(3, cols, back_product(grad_pre[...], up_all[cols, :]))
+        put(4, cols, matmul(lhs_all[...], rhs_all[:, cols]))
+        return carry
+
+    lax.fori_loop(0, 4, feed, 0)
+    ship(3)
+    ship(4)
     for copy in sent:
         copy.wait()
 
@@ -851,10 +913,13 @@
     norm_gain,
     layer_output,
     stack_grad,
-    small,
+    small_own,
+    small_other,
+    coefficients,
     grads,
     sums,
     coef_grad,
+    small,
 ):
     seqs = stack.shape[0]
     sums[...] = jnp.zeros_like(sums)
@@ -902,6 +967,12 @@
     grad_coef = coef_grad[:, 0:36]
     hidden_pre = stats[1, :, 0:36]
     hidden_low = gelu_value(hidden_pre).astype(jnp.bfloat16)
+    for seq in range(seqs):
+        turned = stats[0, seq * SEQ : seq * SEQ + SEQ, :].T
+        for stream in range(4):
+            for layer in range(STREAMS_IN):
+                at = stream * STREAMS_IN + layer
+                coefficients[seq, layer, stream : stream + 1] = turned[at : at + 1]
     small[...] = jnp.zeros_like(small)
     small[0:36, WIDTH : WIDTH + 36] = lax.dot_general(
         wide(hidden_low),
@@ -959,10 +1030,42 @@
     for place in range(8):
         small[36 + place : 37 + place, 0:WIDTH] = jnp.sum(sums[place], axis=0, keepdims=True)
     small[44:45, 0:WIDTH] = jnp.sum(gain_row, axis=0, keepdims=True)
-
-
-def place_kernel(place, shard0, shard1, shard2, shard3, projection, out_grad, up_grad, down_grad):
-    member, x, core = place[0], place[1], place[2]
+    _, _, _, core = position()
+    small_own[...] = small[pl.ds(pl.multiple_of(core * 24, 8), 24), :]
+    small_other[...] = small[pl.ds(pl.multiple_of(24 - core * 24, 8), 24), :]
+
+
+def place_kernel(
+    shard0,
+    shard1,
+    shard2,
+    shard3,
+    small_own,
+    small_other,
+    projection,
+    out_grad,
+    up_grad,
+    down_grad,
+    mix_gain_grad,
+    mix_up_grad,
+    mix_down_grad,
+    mix_static_grad,
+    gain_grad,
+    bias_grad,
+    small,
+):
+    z, member_parity, x, core = position()
+    small[pl.ds(pl.multiple_of(core * 24, 8), 24), :] = small_own[...]
+    small[pl.ds(pl.multiple_of(24 - core * 24, 8), 24), :] = small_other[...]
+    lanes = pl.ds(pl.multiple_of((2 * z + member_parity) * 128, 128), 128)
+    mix_up_grad[...] = small[0:36, lanes]
+    gain_grad[...] = small[36:40, 0:WIDTH]
+    bias_grad[...] = small[40:44, 0:WIDTH]
+    mix_gain_grad[...] = small[44:45, 0:WIDTH]
+    mix_down_grad[...] = small[0:36, WIDTH : WIDTH + 36]
+    for stream in range(4):
+        at = WIDTH + stream * STREAMS_IN
+        mix_static_grad[stream : stream + 1] = small[36:37, at : at + STREAMS_IN]
     shards = (shard0, shard1, shard2, shard3)
     lane = lanes_of((128, 128))
     for back in range(4):
@@ -984,7 +1087,7 @@
             cols = slice(block * 256, block * 256 + 256)
             down_grad[pl.ds(row, 96), cols] = wide(own[7 + block, 0:96])
 
-            @pl.when(member % 2 == from_core)
+            @pl.when(member_parity == from_core)
             def _():
                 head_row = pl.multiple_of(from_x * 64, 64)
                 out_grad[pl.ds(head_row, 32), cols] = wide(own[7 + block, 96:128])
@@ -995,7 +1098,7 @@
                     twin[11, block * 32 : block * 32 + 32]
                 )
 
-            @pl.when(member % 2 != from_core)
+            @pl.when(member_parity != from_core)
             def _():
                 down_grad[pl.ds(row + 96, 32), cols] = wide(own[7 + block, 96:128])
 
@@ -1061,30 +1164,27 @@
     up_weight,
     down_weight,
 ):
-    fsdp_index = lax.axis_index("fsdp")
-    z, y = fsdp_index // 2, fsdp_index % 2
-    member = lax.axis_index("replica")
-    x, core = member // 2, member % 2
-    place = jnp.stack([fsdp_index, x, core]).astype(jnp.int32)
+    z, y, _, _ = position()
     micro_total, local_seqs, _, _, width = layer_stack.shape
     seqs = micro_total * local_seqs
     stack = jnp.transpose(layer_stack, (0, 1, 3, 2, 4)).reshape(seqs, STREAMS_IN, SEQ, width)
     cotangent = out_cotangent.reshape(ROWS, width)
     gain_row = mix_gain.reshape(1, width)
 
-    up_one = mix_up.T
-    up_two = order_two(y, up_one, lax.ppermute(up_one, "fsdp", Y_SWAP), 1)
-    up_four = order_two(z % 2, up_two, lax.ppermute(up_two, "fsdp", Z_SWAP_NEAR), 1)
-    mix_up_full = order_two(z // 2, up_four, lax.ppermute(up_four, "fsdp", Z_SWAP_FAR), 1)
-
     piece = call(
         prepare_kernel,
         shape_of((12, 128, 256)),
-        [SMEM_FULL] + [VMEM_FULL] * 4,
+        [VMEM_FULL] * 4,
         VMEM_FULL,
-        (place, query_key_value, out_weight, up_weight, down_weight),
+        (query_key_value, out_weight, up_weight, down_weight),
     )
-    piece = after(piece, mix_up_full)
+    up_own = mix_up.T
+    up_pair = jnp.concatenate([up_own, after(lax.ppermute(up_own, "fsdp", Y_SWAP), piece)], axis=1)
+    ups = [up_pair] + [
+        lax.ppermute(up_pair, "fsdp", z_pairs([((step + to) % 4, to) for to in range(4)]))
+        for step in (1, 2, 3)
+    ]
+    piece = after(piece, *ups)
     bounds = jnp.concatenate([pic_start.reshape(seqs), doc_split.reshape(seqs)])
     kept = {}
 
@@ -1096,22 +1196,22 @@
                 shape_of((4, ROWS, width), jnp.float32),
                 shape_of((3, ROWS, 128), jnp.float32),
                 shape_of((ROWS, width), jnp.float32),
+                shape_of((36, width)),
             ),
-            [SMEM_FULL] + [VMEM_FULL] * 8,
-            (VMEM_FULL,) * 4,
+            [SMEM_FULL] + [VMEM_FULL] * 11,
+            (VMEM_FULL,) * 5,
             (
                 bounds,
                 stack,
                 cotangent,
                 gain_row,
-                mix_up_full,
+                *ups,
                 mix_down,
                 mix_static.reshape(1, 36),
                 norm_gain,
                 norm_bias,
             ),
             scratch=[pltpu.VMEM((4, ROWS, width), jnp.float32)],
-            cost=pl.CostEstimate(flops=30 << 20, bytes_accessed=24 << 20, transcendentals=0),
         )
         across = lax.ppermute(packet, "replica", X_SWAP)
         beside = lax.ppermute(packet, "replica", CORE_SWAP)
@@ -1119,34 +1219,35 @@
         kept["packets"] = (packet, across, beside, beside_across)
         return packet, across
 
-    pieces, origin = gather_fsdp(piece, z, y, front)
+    pieces = gather_fsdp(piece, z, front)
     packets = kept["packets"]
-    scaled, stats, stream_last = kept["rest"]
-
-    target = scatter_order(z, y)
+    scaled, stats, stream_last, mix_up_full = kept["rest"]
+
     results = call(
         main_kernel,
         (shape_of((12, 128, 256)),) * 8 + (shape_of((2, 5, ROWS, width)),) * 2,
-        [SMEM_FULL] * 3 + [VMEM_FULL] + [IN_PLACE] * 12,
-        (IN_PLACE,) * 8 + (VMEM_FULL,) * 2,
-        (place, origin, target, jnp.asarray(rope_tables())) + packets + tuple(pieces),
+        [VMEM_FULL] + [IN_PLACE] * 12,
+        (IN_PLACE,) * 10,
+        (jnp.asarray(rope_tables()),) + packets + tuple(pieces),
         scratch=[
             pltpu.VMEM((5, 4 * ROWS, width), jnp.bfloat16),
             pltpu.VMEM((4, 16, width), jnp.bfloat16),
-            pltpu.VMEM((4, width, 256), jnp.bfloat16),
+            pltpu.VMEM((width, width), jnp.bfloat16),
             pltpu.VMEM((3, width, 256), jnp.bfloat16),
-            pltpu.VMEM((8, 5, 128, 256), jnp.bfloat16),
-            pltpu.VMEM((4, 256, 256), jnp.bfloat16),
+            pltpu.VMEM((width + 256, width), jnp.bfloat16),
+            pltpu.VMEM((8, 128, 256), jnp.bfloat16),
+            pltpu.VMEM((4 * ROWS, width + 256), jnp.bfloat16),
+            pltpu.VMEM((4 * ROWS, width), jnp.bfloat16),
             pltpu.VMEM((3, 4 * ROWS, 256), jnp.float32),
-            pltpu.VMEM((5, 4 * ROWS, 256), jnp.bfloat16),
+            pltpu.VMEM((4 * ROWS, 256), jnp.bfloat16),
+            pltpu.VMEM((3, 4 * ROWS, 256), jnp.bfloat16),
             pltpu.VMEM((8, 12, 128, 256), jnp.bfloat16),
-            pltpu.VMEM((4 * ROWS, width), jnp.float32),
-            pltpu.VMEM((4 * ROWS, width), jnp.float32),
+            pltpu.VMEM((2, 2, 5, ROWS, width), jnp.bfloat16),
             pltpu.SemaphoreType.DMA((4, 6)),
-            pltpu.SemaphoreType.DMA((8, 3)),
+            pltpu.SemaphoreType.DMA((8, 10)),
             pltpu.SemaphoreType.DMA((8,)),
+            pltpu.SemaphoreType.DMA((2, 5)),
         ],
-        cost=pl.CostEstimate(flops=9 << 30, bytes_accessed=24 << 20, transcendentals=0),
     )
     chunks, keep, send = results[:8], results[8], results[9]
 
@@ -1166,7 +1267,9 @@
             out_shape=(
                 shape_of((ROWS, width)),
                 shape_of((seqs, STREAMS_IN, SEQ, width)),
-                shape_of((48, width + 128), jnp.float32),
+                shape_of((24, width + 128), jnp.float32),
+                shape_of((24, width + 128), jnp.float32),
+                shape_of((seqs, STREAMS_IN, 4, SEQ), jnp.float32),
             ),
             in_specs=[
                 whole((seqs, STREAMS_IN, SEQ, width)),
@@ -1185,15 +1288,17 @@
             out_specs=(
                 whole((ROWS, width)),
                 whole((seqs, STREAMS_IN, SEQ, width)),
-                whole((48, width + 128)),
+                whole((24, width + 128)),
+                whole((24, width + 128)),
+                whole((seqs, STREAMS_IN, 4, SEQ)),
             ),
             scratch_shapes=[
                 pltpu.VMEM((5, ROWS, width), jnp.float32),
                 pltpu.VMEM((8, 8, width), jnp.float32),
                 pltpu.VMEM((ROWS, 128), jnp.float32),
+                pltpu.VMEM((48, width + 128), jnp.float32),
             ],
             compiler_params=pltpu.CompilerParams(vmem_limit_bytes=56 << 20),
-            cost_estimate=pl.CostEstimate(flops=60 << 20, bytes_accessed=36 << 20, transcendentals=0),
         )(
             stack,
             cotangent,
@@ -1210,46 +1315,51 @@
         )
         return kept["back"][2]
 
-    shard = scatter_fsdp(chunks, z, sum_across, back)
-    layer_output, stack_grad, small = kept["back"]
-
+    shard = scatter_fsdp(chunks, z, sum_across, came_across, back)
+    layer_output, stack_grad, small, small_other, coefficients = kept["back"]
+
+    small = small + lax.ppermute(small_other, "replica", CORE_SWAP)
+    small = small + lax.ppermute(small, "replica", X_SWAP)
+    shard = after(shard, small)
     shard_across = lax.ppermute(shard, "replica", X_SWAP)
     shard_beside = lax.ppermute(shard, "replica", CORE_SWAP)
-    shard_both = lax.ppermute(shard_across, "replica", CORE_SWAP)
-    projection_grad, out_grad, up_grad, down_grad = call(
+    for perm in (Y_SWAP, Z_SWAP_NEAR, Z_SWAP_FAR):
+        small = small + lax.ppermute(small, "fsdp", perm)
+    small_beside = lax.ppermute(small, "replica", CORE_SWAP)
+    shard_both = lax.ppermute(after(shard_across, small), "replica", CORE_SWAP)
+    owned = call(
         place_kernel,
         (
             shape_of((3, 128, width), jnp.float32),
             shape_of((128, width), jnp.float32),
             shape_of((128, 4 * width), jnp.float32),
             shape_of((512, width), jnp.float32),
+            shape_of((1, width), jnp.float32),
+            shape_of((36, 128), jnp.float32),
+            shape_of((36, 36), jnp.float32),
+            shape_of((4, STREAMS_IN), jnp.float32),
+            shape_of((4, width), jnp.float32),
+            shape_of((4, width), jnp.float32),
         ),
-        [SMEM_FULL] + [VMEM_FULL] * 4,
-        (VMEM_FULL,) * 4,
-        (place, shard, shard_across, shard_beside, shard_both),
+        [VMEM_FULL] * 6,
+        (VMEM_FULL,) * 10,
+        (shard, shard_across, shard_beside, shard_both, small, small_beside),
+        scratch=[pltpu.VMEM((48, width + 128), jnp.float32)],
     )
-
-    for axis_name, perm in (
-        ("replica", CORE_SWAP),
-        ("replica", X_SWAP),
-        ("fsdp", Y_SWAP),
-        ("fsdp", Z_SWAP_NEAR),
-        ("fsdp", Z_SWAP_FAR),
-    ):
-        small = small + lax.ppermute(small, axis_name, perm)
-    mix_up_grad = lax.dynamic_slice(small, (0, 128 * fsdp_index), (36, 128)).T
+    projection_grad, out_grad, up_grad, down_grad, *small_grads = owned
     shape = (micro_total, local_seqs, SEQ)
     stack_grad = stack_grad.reshape(micro_total, local_seqs, STREAMS_IN, SEQ, width)
+    coefficients = coefficients.reshape(micro_total, local_seqs, STREAMS_IN, 4, SEQ)
     return (
         layer_output.reshape(shape + (width,)),
-        stats[0, :, :36].reshape(shape + (4, STREAMS_IN)),
+        jnp.transpose(coefficients, (0, 1, 4, 3, 2)),
         jnp.transpose(stack_grad, (0, 1, 3, 2, 4)),
-        small[44, :width],
-        mix_up_grad,
-        small[:36, width : width + 36],
-        small[36, width : width + 36].reshape(4, STREAMS_IN),
-        small[36:40, :width],
-        small[40:44, :width],
+        small_grads[0].reshape(width),
+        small_grads[1].T,
+        small_grads[2],
+        small_grads[3],
+        small_grads[4],
+        small_grads[5],
         projection_grad,
         out_grad,
         up_grad,

time: 315 us -> 238 us (0.76)
  waiting for transfers between devices: 159 us -> 118 us
  Pallas kernels: 69.4 us -> 57.6 us
  other arithmetic: 15.1 us -> 6.49 us
  local copies, waits for them, and re-layouts: 12.5 us -> 5.51 us
  starting transfers between devices: 53.4 us -> 48.8 us
    ppermute x27 -> x29, waiting for transfers between devices: 149 us -> 106 us  [the longest x18 84.8 us: fsdp_move(): return lax.ppermute(value, 'fsdp', pairs)]
    pallas_call x4, Pallas kernels: 56.1 us -> 44 us  [call(): pl.pallas_call(kernel, out_shape=outs, in_specs=specs, out_specs=out_spec...]
    convert_element_type x4 -> x5, other arithmetic: 7.46 us -> 1.23 us  [add(): return (wide(first) + wide(second)).astype(jnp.bfloat16)]
    ppermute x27 -> x29, starting transfers between devices: 48.8 us -> 43.7 us  [the longest x18 26.2 us: fsdp_move(): return lax.ppermute(value, 'fsdp', pairs)]
    ppermute x1, waiting for transfers between devices: 0.01 us -> 4.64 us  [on_device_tensor(): came = lax.ppermute(send, 'replica', CORE_SWAP)]
  transfers between devices with their start and end apart: 34 -> 36, of which waited for: 21 -> 22; matrix products, arithmetic and copies ran while one was open for 7% -> 3% of each run, Pallas kernels for 8% -> 11%
where the time goes in v2:
time: 238 us; the launch traced here: 237 us
  waiting for transfers between devices  118 us (50%)
  Pallas kernels  57.6 us (24%)
  starting transfers between devices  48.8 us (21%)
  other arithmetic  6.49 us (3%)
  local copies, waits for them, and re-layouts  5.51 us (2%)
    ppermute x18, waiting for transfers between devices, fsdp_move(): return lax.ppermute(value, 'fsdp', pairs)  84.8 us
    pallas_call x4, Pallas kernels, call(): pl.pallas_call(kernel, out_shape=outs, in_specs=specs, out_specs=out_spec...  44 us
    ppermute x18, starting transfers between devices, fsdp_move(): return lax.ppermute(value, 'fsdp', pairs)  26.2 us
    pallas_call x1, Pallas kernels, back(): pl.pallas_call(back_kernel, grid=(1,), out_shape=(shape_of((ROWS, width))...  13.6 us
    ppermute x3, waiting for transfers between devices, on_device_tensor(): small = small + lax.ppermute(small, 'fsdp', perm)  10.7 us
    ppermute x1, waiting for transfers between devices, front(): across = lax.ppermute(packet, 'replica', X_SWAP)  7.09 us
    ppermute x3, starting transfers between devices, on_device_tensor(): small = small + lax.ppermute(small, 'fsdp', perm)  6.73 us
    ppermute x3, starting transfers between devices, on_device_tensor(): lax.ppermute(up_pair, 'fsdp', z_pairs([((step + to) % 4, to) for to in ra...  5.57 us
  transfers between devices with their start and end apart: 36, of which 22 were waited for; matrix products, arithmetic and copies ran while one was open for 3% of the time, Pallas kernels for 11%

profile of v2, /device:TPU:0, one launch (start us, length us, event | category | flops | bytes accessed | tf_op | source)
XLA Modules:
  0.0 237.2 jit_solution(11810936177425545697)
XLA Ops:
  0.7 3.0 %collective-permute-start = (bf16[36,128]{1,0:T(8,128)(2,1)}, bf16[36,128]{1,0:T(8,128)(2,1)S(1)}, u32[]{:S(2)}, u32[]{:S(2)}) collective-permute-start(bf16[36,128]{1,0:T(8,128)(2,1)} %bitcast.33), channel_id=1, source_target_pairs={{0,4},{4,0},{8,12},{12,8},{16,20},{20,16},{24,28},{28,24},{1,5},{5... | collective-permute-start | bytes 27656 | tf_op jit(solution)/shard_map/ppermute | solution.py:1182
  3.7 3.2 %shard_map.246.piece0 = bf16[12,128,256]{2,1,0:T(8,128)(2,1)} custom-call(bf16[3,128,1024]{2,1,0:T(8,128)(2,1)} %projection.1, bf16[128,1024]{1,0:T(8,128)(2,1)} %out_weight.1, bf16[128,4096]{1,0:T(8,128)(2,1)} %up_weight.1, bf16[512,1024]{1,0:T(8,128)(2,1)} %down_weight.1), custom_call_target="tpu_custom_call" | custom-call | tf_op jit(solution)/shard_map/pallas_call | solution.py:1122
  6.9 1.6 collective-permute-start.3
  8.6 2.6 %collective-permute-start.2 = (bf16[36,256]{1,0:T(8,128)(2,1)S(1)}, bf16[36,256]{1,0:T(8,128)(2,1)S(1)}, u32[]{:S(2)}, u32[]{:S(2)}) collective-permute-start(bf16[36,256]{1,0:T(8,128)(2,1)S(1)} %pad_maximum_fusion.up_own), channel_id=1, source_target_pairs={{16,0},{20,4},{24,8},{28,12},{0,16},{4,20},{8,24},{12,28},{17,1},{... | collective-permute-start | bytes 55304 | tf_op jit(solution)/shard_map/ppermute | solution.py:1184
  11.2 1.3 collective-permute-start.1
  13.3 1.7 collective-permute-done.1.up_one
  14.9 7.4 %collective-permute-start.10 = (bf16[12,128,256]{2,1,0:T(8,128)(2,1)}, bf16[12,128,256]{2,1,0:T(8,128)(2,1)}, u32[]{:S(2)}, u32[]{:S(2)}) collective-permute-start(bf16[12,128,256]{2,1,0:T(8,128)(2,1)} %shard_map.246.piece0), channel_id=1, source_target_pairs={{0,0},{4,4},{8,16},{12,20},{16,8},{20,12},{24,24},{28,28},{1,1},{5... | collective-permute-start | bytes 2359304 | tf_op jit(solution)/shard_map/ppermute | solution.py:400
  24.3 9.6 %shard_map.247 = (bf16[656,1024]{1,0:T(8,128)(2,1)}, f32[4,128,1024]{2,1,0:T(8,128)}, f32[3,128,128]{2,1,0:T(8,128)}, f32[128,1024]{1,0:T(8,128)}, bf16[36,1024]{1,0:T(8,128)(2,1)}) custom-call(s32[4]{0:T(128)} %pad_add_fusion.bounds, bf16[2,9,64,1024]{3,2,1,0:T(8,128)(2,1)} %bitcast.27, bf16[128,1024]{1,0:T(8,128)(2,1)} %bitcast.29, f32[1,1024]{1,0:T(1,128)} %bitcast.31, ...), custom_call_target="tpu_custom_call" | custom-call | tf_op jit(solution)/shard_map/pallas_call | solution.py:1122
  33.9 6.3 %collective-permute-done.7.piece1 = bf16[12,128,256]{2,1,0:T(8,128)(2,1)S(1)} collective-permute-done((bf16[12,128,256]{2,1,0:T(8,128)(2,1)}, bf16[12,128,256]{2,1,0:T(8,128)(2,1)S(1)}, u32[]{:S(2)}, u32[]{:S(2)}) %collective-permute-start.7) | collective-permute-done | bytes 786464 | tf_op jit(solution)/shard_map/ppermute | solution.py:400
  40.2 1.5 collective-permute-start.4
  41.7 1.4 collective-permute-start.9
  43.1 1.5 collective-permute-start.13
  44.6 12.8 %collective-permute-done.11 = bf16[12,128,256]{2,1,0:T(8,128)(2,1)} collective-permute-done((bf16[12,128,256]{2,1,0:T(8,128)(2,1)}, bf16[12,128,256]{2,1,0:T(8,128)(2,1)}, u32[]{:S(2)}, u32[]{:S(2)}) %collective-permute-start.11) | collective-permute-done | bytes 786464 | tf_op jit(solution)/shard_map/ppermute | solution.py:400
  57.5 1.2 broadcast_select_fusion.1.piece4
  58.7 3.3 %collective-permute-start.14 = (bf16[12,128,256]{2,1,0:T(8,128)(2,1)}, bf16[12,128,256]{2,1,0:T(8,128)(2,1)S(1)}, u32[]{:S(2)}, u32[]{:S(2)}) collective-permute-start(bf16[12,128,256]{2,1,0:T(8,128)(2,1)} %collective-permute-done.13), channel_id=1, source_target_pairs={{0,8},{4,12},{8,0},{12,4},{16,24},{20,28},{24,16},{28,20},{1,9},{5... | collective-permute-start | bytes 2359304 | tf_op jit(solution)/shard_map/ppermute | solution.py:400
  62.1 7.1 %collective-permute-done.4.packet1 = bf16[656,1024]{1,0:T(8,128)(2,1)} collective-permute-done((bf16[656,1024]{1,0:T(8,128)(2,1)}, bf16[656,1024]{1,0:T(8,128)(2,1)}, u32[]{:S(2)}, u32[]{:S(2)}) %collective-permute-start.4) | collective-permute-done | bytes 1343520 | tf_op jit(solution)/shard_map/ppermute | solution.py:1216
  70.2 5.2 %collective-permute-done.14 = bf16[12,128,256]{2,1,0:T(8,128)(2,1)S(1)} collective-permute-done((bf16[12,128,256]{2,1,0:T(8,128)(2,1)}, bf16[12,128,256]{2,1,0:T(8,128)(2,1)S(1)}, u32[]{:S(2)}, u32[]{:S(2)}) %collective-permute-start.14) | collective-permute-done | bytes 786464 | tf_op jit(solution)/shard_map/ppermute | solution.py:400
  75.5 11.4 %collective-permute-done.12.piece5 = bf16[12,128,256]{2,1,0:T(8,128)(2,1)S(1)} collective-permute-done((bf16[12,128,256]{2,1,0:T(8,128)(2,1)S(1)}, bf16[12,128,256]{2,1,0:T(8,128)(2,1)S(1)}, u32[]{:S(2)}, u32[]{:S(2)}) %collective-permute-start.12) | collective-permute-done | bytes 786464 | tf_op jit(solution)/shard_map/ppermute | solution.py:400
  87.4 1.1 copy-done.5
  88.4 1.1 copy-done.6
  89.5 12.3 %collective-permute-done.15.piece7 = bf16[12,128,256]{2,1,0:T(8,128)(2,1)S(1)} collective-permute-done((bf16[12,128,256]{2,1,0:T(8,128)(2,1)S(1)}, bf16[12,128,256]{2,1,0:T(8,128)(2,1)S(1)}, u32[]{:S(2)}, u32[]{:S(2)}) %collective-permute-start.15) | collective-permute-done | bytes 786464 | tf_op jit(solution)/shard_map/ppermute | solution.py:400
  101.8 0.9 copy-done.11
  102.7 26.0 %shard_map.248 = (bf16[12,128,256]{2,1,0:T(8,128)(2,1)}, bf16[12,128,256]{2,1,0:T(8,128)(2,1)}, bf16[12,128,256]{2,1,0:T(8,128)(2,1)}, bf16[12,128,256]{2,1,0:T(...) custom-call(f32[3,128,128]{2,1,0:T(8,128)} %constant.26.clone.rope, ...), custom_call_target="tpu_custom_call" | custom-call | tf_op jit(solution)/shard_map/pallas_call | solution.py:1122
  129.3 4.6 %collective-permute-done.16.came = bf16[2,5,128,1024]{3,2,1,0:T(8,128)(2,1)S(1)} collective-permute-done((bf16[2,5,128,1024]{3,2,1,0:T(8,128)(2,1)}, bf16[2,5,128,1024]{3,2,1,0:T(8,128)(2,1)S(1)}, u32[]{:S(2)}, u32[]{:S(2)}) %collective-permute-start.16) | collective-permute-done | bytes 2621472 | tf_op jit(solution)/shard_map/ppermute | solution.py:1254
  133.9 2.8 %fusion = bf16[5,128,1024]{2,1,0:T(8,128)(2,1)S(1)} fusion(bf16[2,5,128,1024]{3,2,1,0:T(8,128)(2,1)S(1)} %collective-permute-done.16.came, bf16[2,5,128,1024]{3,2,1,0:T(8,128)(2,1)} %get-tuple-element.70.keep), kind=kLoop, calls=%fused_computation.9 | loop fusion | flops 2621440 | bytes 3932160 | tf_op jit(solution)/shard_map/convert_element_type | solution.py:1255
  136.8 1.6 collective-permute-start.17
  138.3 10.7 %collective-permute-done.20 = bf16[12,128,256]{2,1,0:T(8,128)(2,1)S(1)} collective-permute-done((bf16[12,128,256]{2,1,0:T(8,128)(2,1)}, bf16[12,128,256]{2,1,0:T(8,128)(2,1)S(1)}, u32[]{:S(2)}, u32[]{:S(2)}) %collective-permute-start.20) | collective-permute-done | bytes 786464 | tf_op jit(solution)/shard_map/ppermute | solution.py:400
  149.2 1.5 collective-permute-start.22
  151.2 1.6 collective-permute-start.21
  152.8 15.6 %collective-permute-done.22 = bf16[12,128,256]{2,1,0:T(8,128)(2,1)S(1)} collective-permute-done((bf16[12,128,256]{2,1,0:T(8,128)(2,1)S(1)}, bf16[12,128,256]{2,1,0:T(8,128)(2,1)S(1)}, u32[]{:S(2)}, u32[]{:S(2)}) %collective-permute-start.22) | collective-permute-done | bytes 786464 | tf_op jit(solution)/shard_map/ppermute | solution.py:400
  168.7 1.0 collective-permute-start.23
  169.7 1.6 collective-permute-done.18
  171.5 2.5 %collective-permute-start.25 = (bf16[12,128,256]{2,1,0:T(8,128)(2,1)S(1)}, bf16[12,128,256]{2,1,0:T(8,128)(2,1)S(1)}, u32[]{:S(2)}, u32[]{:S(2)}) collective-permute-start(bf16[12,128,256]{2,1,0:T(8,128)(2,1)S(1)} %add_convert_fusion.3), channel_id=1, source_target_pairs={{0,8},{4,12},{8,0},{12,4},{16,24},{20,28},{24,16},{28,20},{1,9},{5... | collective-permute-start | bytes 2359304 | tf_op jit(solution)/shard_map/ppermute | solution.py:400
  174.2 13.6 %shard_map.249 = (bf16[128,1024]{1,0:T(8,128)(2,1)}, bf16[2,9,64,1024]{3,2,1,0:T(8,128)(2,1)}, f32[24,1152]{1,0:T(8,128)}, f32[24,1152]{1,0:T(8,128)}, f32[2,9,4,64]{3,2,1,0:T(4,128)}) custom-call(bf16[2,9,64,1024]{3,2,1,0:T(8,128)(2,1)} %bitcast.28, bf16[128,1024]{1,0:T(8,128)(2,1)} %bitcast.30, f32[4,128,1024]{2,1,0:T(8,128)} %get-tuple-element.60.scaled, ...), custom_call_target="tpu_custom_call" | custom-call | tf_op jit(solution)/shard_map/pallas_call | solution.py:1264
  188.5 2.3 collective-permute-start.24
  191.9 1.3 collective-permute-done.27
  193.2 1.6 collective-permute-start.28
  194.7 3.6 %collective-permute-done.28 = f32[24,1152]{1,0:T(8,128)S(1)} collective-permute-done((f32[24,1152]{1,0:T(8,128)S(1)}, f32[24,1152]{1,0:T(8,128)S(1)}, u32[]{:S(2)}, u32[]{:S(2)}) %collective-permute-start.28) | collective-permute-done | bytes 110624 | tf_op jit(solution)/shard_map/ppermute | solution.py:1322
  198.4 4.9 %collective-permute-done.19 = bf16[12,128,256]{2,1,0:T(8,128)(2,1)S(1)} collective-permute-done((bf16[12,128,256]{2,1,0:T(8,128)(2,1)S(1)}, bf16[12,128,256]{2,1,0:T(8,128)(2,1)S(1)}, u32[]{:S(2)}, u32[]{:S(2)}) %collective-permute-start.19) | collective-permute-done | bytes 786464 | tf_op jit(solution)/shard_map/ppermute | solution.py:400
  203.3 3.7 %collective-permute-done.24 = bf16[12,128,256]{2,1,0:T(8,128)(2,1)S(1)} collective-permute-done((bf16[12,128,256]{2,1,0:T(8,128)(2,1)S(1)}, bf16[12,128,256]{2,1,0:T(8,128)(2,1)S(1)}, u32[]{:S(2)}, u32[]{:S(2)}) %collective-permute-start.24) | collective-permute-done | bytes 786464 | tf_op jit(solution)/shard_map/ppermute | solution.py:400
  207.5 1.4 collective-permute-start.29
  209.3 4.3 %collective-permute-done.31 = f32[24,1152]{1,0:T(8,128)S(1)} collective-permute-done((f32[24,1152]{1,0:T(8,128)S(1)}, f32[24,1152]{1,0:T(8,128)S(1)}, u32[]{:S(2)}, u32[]{:S(2)}) %collective-permute-start.31) | collective-permute-done | bytes 110624 | tf_op jit(solution)/shard_map/ppermute | solution.py:1327
  213.7 4.1 %collective-permute-start.32 = (f32[24,1152]{1,0:T(8,128)S(1)}, f32[24,1152]{1,0:T(8,128)S(1)}, u32[]{:S(2)}, u32[]{:S(2)}) collective-permute-start(f32[24,1152]{1,0:T(8,128)S(1)} %add.59), channel_id=1, source_target_pairs={{0,8},{4,12},{8,0},{12,4},{16,24},{20,28},{24,16},{28,20},{1,9},{5... | collective-permute-start | bytes 331784 | tf_op jit(solution)/shard_map/ppermute | solution.py:1327
  217.7 2.9 %collective-permute-done.32 = f32[24,1152]{1,0:T(8,128)S(1)} collective-permute-done((f32[24,1152]{1,0:T(8,128)S(1)}, f32[24,1152]{1,0:T(8,128)S(1)}, u32[]{:S(2)}, u32[]{:S(2)}) %collective-permute-start.32) | collective-permute-done | bytes 110624 | tf_op jit(solution)/shard_map/ppermute | solution.py:1327
  220.7 2.2 collective-permute-start.33
  222.9 3.5 %collective-permute-done.33 = f32[24,1152]{1,0:T(8,128)S(1)} collective-permute-done((f32[24,1152]{1,0:T(8,128)S(1)}, f32[24,1152]{1,0:T(8,128)S(1)}, u32[]{:S(2)}, u32[]{:S(2)}) %collective-permute-start.33) | collective-permute-done | bytes 110624 | tf_op jit(solution)/shard_map/ppermute | solution.py:1327
  227.1 3.0 %collective-permute-done.35.small_other = f32[24,1152]{1,0:T(8,128)S(1)} collective-permute-done((f32[24,1152]{1,0:T(8,128)S(1)}, f32[24,1152]{1,0:T(8,128)S(1)}, u32[]{:S(2)}, u32[]{:S(2)}) %collective-permute-start.35) | collective-permute-done | bytes 110624 | tf_op jit(solution)/shard_map/ppermute | solution.py:1328
  231.9 5.2 %shard_map.250 = (f32[3,128,1024]{2,1,0:T(8,128)}, f32[128,1024]{1,0:T(8,128)}, f32[128,4096]{1,0:T(8,128)}, f32[512,1024]{1,0:T(8,128)}, f32[1,1024]{1,0:T(1,12...) custom-call(bf16[12,128,256]{2,1,0:T(8,128)(2,1)} %copy-done.3, ...), custom_call_target="tpu_custom_call" | custom-call | tf_op jit(solution)/shard_map/pallas_call | solution.py:1122
  (112 shorter events, 11.3 us)
Async XLA Ops:
  0.7 22.4 %copy-start.27 = (f32[4,9]{1,0:T(4,128)S(1)}, f32[4,9]{1,0:T(4,128)}, u32[]{:S(2)}) copy-start(f32[4,9]{1,0:T(4,128)} %param.22) | copy-start | bytes 436
  0.7 23.0 %copy-start.31 = (s32[2,1]{0,1:T(1,128)S(1)}, s32[2,1]{0,1:T(1,128)}, u32[]{:S(2)}) copy-start(s32[2,1]{0,1:T(1,128)} %param.18) | copy-start | bytes 28
  0.7 23.0 %copy-start.32 = (s32[2,1]{0,1:T(1,128)S(1)}, s32[2,1]{0,1:T(1,128)}, u32[]{:S(2)}) copy-start(s32[2,1]{0,1:T(1,128)} %param.17) | copy-start | bytes 28
  0.7 6.2 %collective-permute-start = (bf16[36,128]{1,0:T(8,128)(2,1)}, bf16[36,128]{1,0:T(8,128)(2,1)S(1)}, u32[]{:S(2)}, u32[]{:S(2)}) collective-permute-start(bf16[36,128]{1,0:T(8,128)(2,1)} %bitcast.33), channel_id=1, source_target_pairs={{0,4},{4,0},{8,12},{12,8},{16,20},{20,16},{24,28},{28,24},{1,5},{5... | collective-permute-start | bytes 27656 | tf_op jit(solution)/shard_map/ppermute | solution.py:1182
  6.9 17.3 %copy-start.22 = (bf16[36,256]{1,0:T(8,128)(2,1)}, bf16[36,256]{1,0:T(8,128)(2,1)S(1)}, u32[]{:S(2)}) copy-start(bf16[36,256]{1,0:T(8,128)(2,1)S(1)} %pad_maximum_fusion.up_own) | copy-start | bytes 55300
  6.9 5.9 %collective-permute-start.3 = (bf16[36,256]{1,0:T(8,128)(2,1)S(1)}, bf16[36,256]{1,0:T(8,128)(2,1)S(1)}, u32[]{:S(2)}, u32[]{:S(2)}) collective-permute-start(bf16[36,256]{1,0:T(8,128)(2,1)S(1)} %pad_maximum_fusion.up_own), channel_id=1, source_target_pairs={{24,0},{28,4},{0,8},{4,12},{8,16},{12,20},{16,24},{20,28},{25,1},{... | collective-permute-start | bytes 55304 | tf_op jit(solution)/shard_map/ppermute | solution.py:1184
  8.6 4.7 %collective-permute-start.2 = (bf16[36,256]{1,0:T(8,128)(2,1)S(1)}, bf16[36,256]{1,0:T(8,128)(2,1)S(1)}, u32[]{:S(2)}, u32[]{:S(2)}) collective-permute-start(bf16[36,256]{1,0:T(8,128)(2,1)S(1)} %pad_maximum_fusion.up_own), channel_id=1, source_target_pairs={{16,0},{20,4},{24,8},{28,12},{0,16},{4,20},{8,24},{12,28},{17,1},{... | collective-permute-start | bytes 55304 | tf_op jit(solution)/shard_map/ppermute | solution.py:1184
  11.2 3.8 %collective-permute-start.1 = (bf16[36,256]{1,0:T(8,128)(2,1)S(1)}, bf16[36,256]{1,0:T(8,128)(2,1)S(1)}, u32[]{:S(2)}, u32[]{:S(2)}) collective-permute-start(bf16[36,256]{1,0:T(8,128)(2,1)S(1)} %pad_maximum_fusion.up_own), channel_id=1, source_target_pairs={{8,0},{12,4},{16,8},{20,12},{24,16},{28,20},{0,24},{4,28},{9,1},{1... | collective-permute-start | bytes 55304 | tf_op jit(solution)/shard_map/ppermute | solution.py:1184
  14.9 18.9 %collective-permute-start.10 = (bf16[12,128,256]{2,1,0:T(8,128)(2,1)}, bf16[12,128,256]{2,1,0:T(8,128)(2,1)}, u32[]{:S(2)}, u32[]{:S(2)}) collective-permute-start(bf16[12,128,256]{2,1,0:T(8,128)(2,1)} %shard_map.246.piece0), channel_id=1, source_target_pairs={{0,0},{4,4},{8,16},{12,20},{16,8},{20,12},{24,24},{28,28},{1,1},{5... | collective-permute-start | bytes 2359304 | tf_op jit(solution)/shard_map/ppermute | solution.py:400
  22.4 17.8 %collective-permute-start.7 = (bf16[12,128,256]{2,1,0:T(8,128)(2,1)}, bf16[12,128,256]{2,1,0:T(8,128)(2,1)S(1)}, u32[]{:S(2)}, u32[]{:S(2)}) collective-permute-start(bf16[12,128,256]{2,1,0:T(8,128)(2,1)} %shard_map.246.piece0), channel_id=1, source_target_pairs={{0,4},{4,0},{8,12},{12,8},{16,20},{20,16},{24,28},{28,24},{1,5},{5... | collective-permute-start | bytes 2359304 | tf_op jit(solution)/shard_map/ppermute | solution.py:400
  23.1 18.6 %collective-permute-start.8 = (bf16[12,128,256]{2,1,0:T(8,128)(2,1)}, bf16[12,128,256]{2,1,0:T(8,128)(2,1)S(1)}, u32[]{:S(2)}, u32[]{:S(2)}) collective-permute-start(bf16[12,128,256]{2,1,0:T(8,128)(2,1)} %shard_map.246.piece0), channel_id=1, source_target_pairs={{0,8},{4,12},{8,0},{12,4},{16,24},{20,28},{24,16},{28,20},{1,9},{5... | collective-permute-start | bytes 2359304 | tf_op jit(solution)/shard_map/ppermute | solution.py:400
  33.9 35.8 %copy-start.4 = (bf16[656,1024]{1,0:T(8,128)(2,1)S(1)}, bf16[656,1024]{1,0:T(8,128)(2,1)}, u32[]{:S(2)}) copy-start(bf16[656,1024]{1,0:T(8,128)(2,1)} %get-tuple-element.63.packet0) | copy-start | bytes 4030468
  40.2 35.3 %copy-start.8 = (bf16[12,128,256]{2,1,0:T(8,128)(2,1)}, bf16[12,128,256]{2,1,0:T(8,128)(2,1)S(1)}, u32[]{:S(2)}) copy-start(bf16[12,128,256]{2,1,0:T(8,128)(2,1)S(1)} %collective-permute-done.7.piece1) | copy-start | bytes 2359300
  40.2 17.3 %collective-permute-start.11 = (bf16[12,128,256]{2,1,0:T(8,128)(2,1)}, bf16[12,128,256]{2,1,0:T(8,128)(2,1)}, u32[]{:S(2)}, u32[]{:S(2)}) collective-permute-start(bf16[12,128,256]{2,1,0:T(8,128)(2,1)} %collective-permute-done.10), channel_id=1, source_target_pairs={{0,8},{4,12},{8,0},{12,4},{16,24},{20,28},{24,16},{28,20},{1,9},{5... | collective-permute-start | bytes 2359304 | tf_op jit(solution)/shard_map/ppermute | solution.py:400
  40.2 28.9 %collective-permute-start.4 = (bf16[656,1024]{1,0:T(8,128)(2,1)}, bf16[656,1024]{1,0:T(8,128)(2,1)}, u32[]{:S(2)}, u32[]{:S(2)}) collective-permute-start(bf16[656,1024]{1,0:T(8,128)(2,1)} %get-tuple-element.63.packet0), channel_id=1, source_target_pairs={{0,2},{1,3},{2,0},{3,1},{4,6},{5,7},{6,4},{7,5},{8,10},{9,11},{10,... | collective-permute-start | bytes 4030472 | tf_op jit(solution)/shard_map/ppermute | solution.py:1216
  41.7 28.5 %copy-start.9 = (bf16[12,128,256]{2,1,0:T(8,128)(2,1)}, bf16[12,128,256]{2,1,0:T(8,128)(2,1)S(1)}, u32[]{:S(2)}) copy-start(bf16[12,128,256]{2,1,0:T(8,128)(2,1)S(1)} %collective-permute-done.8.piece2) | copy-start | bytes 2359300
  41.7 17.0 %collective-permute-start.9 = (bf16[12,128,256]{2,1,0:T(8,128)(2,1)S(1)}, bf16[12,128,256]{2,1,0:T(8,128)(2,1)}, u32[]{:S(2)}, u32[]{:S(2)}) collective-permute-start(bf16[12,128,256]{2,1,0:T(8,128)(2,1)S(1)} %collective-permute-done.8.piece2), channel_id=1, source_target_pairs={{0,4},{4,0},{8,12},{12,8},{16,20},{20,16},{24,28},{28,24},{1,5},{5... | collective-permute-start | bytes 2359304 | tf_op jit(solution)/shard_map/ppermute | solution.py:400
  43.1 15.6 %collective-permute-start.13 = (bf16[12,128,256]{2,1,0:T(8,128)(2,1)S(1)}, bf16[12,128,256]{2,1,0:T(8,128)(2,1)}, u32[]{:S(2)}, u32[]{:S(2)}) collective-permute-start(bf16[12,128,256]{2,1,0:T(8,128)(2,1)S(1)} %collective-permute-done.8.piece2), channel_id=1, source_target_pairs={{0,0},{4,4},{8,16},{12,20},{16,8},{20,12},{24,24},{28,28},{1,1},{5... | collective-permute-start | bytes 2359304 | tf_op jit(solution)/shard_map/ppermute | solution.py:400
  58.7 43.1 %copy-start.1 = (bf16[12,128,256]{2,1,0:T(8,128)(2,1)}, bf16[12,128,256]{2,1,0:T(8,128)(2,1)S(1)}, u32[]{:S(2)}) copy-start(bf16[12,128,256]{2,1,0:T(8,128)(2,1)S(1)} %broadcast_select_fusion.1.piece4) | copy-start | bytes 2359300
  58.7 16.6 %collective-permute-start.14 = (bf16[12,128,256]{2,1,0:T(8,128)(2,1)}, bf16[12,128,256]{2,1,0:T(8,128)(2,1)S(1)}, u32[]{:S(2)}, u32[]{:S(2)}) collective-permute-start(bf16[12,128,256]{2,1,0:T(8,128)(2,1)} %collective-permute-done.13), channel_id=1, source_target_pairs={{0,8},{4,12},{8,0},{12,4},{16,24},{20,28},{24,16},{28,20},{1,9},{5... | collective-permute-start | bytes 2359304 | tf_op jit(solution)/shard_map/ppermute | solution.py:400
  69.2 17.7 %collective-permute-start.12 = (bf16[12,128,256]{2,1,0:T(8,128)(2,1)S(1)}, bf16[12,128,256]{2,1,0:T(8,128)(2,1)S(1)}, u32[]{:S(2)}, u32[]{:S(2)}) collective-permute-start(bf16[12,128,256]{2,1,0:T(8,128)(2,1)S(1)} %broadcast_select_fusion.1.piece4), channel_id=1, source_target_pairs={{0,4},{4,0},{8,12},{12,8},{16,20},{20,16},{24,28},{28,24},{1,5},{5... | collective-permute-start | bytes 2359304 | tf_op jit(solution)/shard_map/ppermute | solution.py:400
  69.7 17.7 %collective-permute-start.5 = (bf16[656,1024]{1,0:T(8,128)(2,1)S(1)}, bf16[656,1024]{1,0:T(8,128)(2,1)S(1)}, u32[]{:S(2)}, u32[]{:S(2)}) collective-permute-start(bf16[656,1024]{1,0:T(8,128)(2,1)S(1)} %copy-done.4), channel_id=1, source_target_pairs={{0,1},{1,0},{2,3},{3,2},{4,5},{5,4},{6,7},{7,6},{8,9},{9,8},{10,11... | collective-permute-start | bytes 4030472 | tf_op jit(solution)/shard_map/ppermute | solution.py:1217
  69.7 18.8 %collective-permute-start.6 = (bf16[656,1024]{1,0:T(8,128)(2,1)}, bf16[656,1024]{1,0:T(8,128)(2,1)S(1)}, u32[]{:S(2)}, u32[]{:S(2)}) collective-permute-start(bf16[656,1024]{1,0:T(8,128)(2,1)} %collective-permute-done.4.packet1), channel_id=1, source_target_pairs={{0,1},{1,0},{2,3},{3,2},{4,5},{5,4},{6,7},{7,6},{8,9},{9,8},{10,11... | collective-permute-start | bytes 4030472 | tf_op jit(solution)/shard_map/ppermute | solution.py:1218
  75.5 26.3 %copy-start.2 = (bf16[12,128,256]{2,1,0:T(8,128)(2,1)}, bf16[12,128,256]{2,1,0:T(8,128)(2,1)S(1)}, u32[]{:S(2)}) copy-start(bf16[12,128,256]{2,1,0:T(8,128)(2,1)S(1)} %broadcast_select_fusion.piece6) | copy-start | bytes 2359300
  86.9 14.9 %collective-permute-start.15 = (bf16[12,128,256]{2,1,0:T(8,128)(2,1)S(1)}, bf16[12,128,256]{2,1,0:T(8,128)(2,1)S(1)}, u32[]{:S(2)}, u32[]{:S(2)}) collective-permute-start(bf16[12,128,256]{2,1,0:T(8,128)(2,1)S(1)} %broadcast_select_fusion.piece6), channel_id=1, source_target_pairs={{0,4},{4,0},{8,12},{12,8},{16,20},{20,16},{24,28},{28,24},{1,5},{5... | collective-permute-start | bytes 2359304 | tf_op jit(solution)/shard_map/ppermute | solution.py:400
  128.7 5.2 %collective-permute-start.16 = (bf16[2,5,128,1024]{3,2,1,0:T(8,128)(2,1)}, bf16[2,5,128,1024]{3,2,1,0:T(8,128)(2,1)S(1)}, u32[]{:S(2)}, u32[]{:S(2)}) collective-permute-start(bf16[2,5,128,1024]{3,2,1,0:T(8,128)(2,1)} %get-tuple-element.71), channel_id=1, source_target_pairs={{0,1},{1,0},{2,3},{3,2},{4,5},{5,4},{6,7},{7,6},{8,9},{9,8},{10,11... | collective-permute-start | bytes 7864328 | tf_op jit(solution)/shard_map/ppermute | solution.py:1254
  128.8 20.2 %collective-permute-start.20 = (bf16[12,128,256]{2,1,0:T(8,128)(2,1)}, bf16[12,128,256]{2,1,0:T(8,128)(2,1)S(1)}, u32[]{:S(2)}, u32[]{:S(2)}) collective-permute-start(bf16[12,128,256]{2,1,0:T(8,128)(2,1)} %get-tuple-element.82), channel_id=1, source_target_pairs={{0,4},{4,0},{8,12},{12,8},{16,20},{20,16},{24,28},{28,24},{1,5},{5... | collective-permute-start | bytes 2359304 | tf_op jit(solution)/shard_map/ppermute | solution.py:400
  136.8 31.9 %collective-permute-start.17 = (bf16[5,128,1024]{2,1,0:T(8,128)(2,1)S(1)}, bf16[5,128,1024]{2,1,0:T(8,128)(2,1)S(1)}, u32[]{:S(2)}, u32[]{:S(2)}) collective-permute-start(bf16[5,128,1024]{2,1,0:T(8,128)(2,1)S(1)} %fusion), channel_id=1, source_target_pairs={{0,2},{1,3},{2,0},{3,1},{4,6},{5,7},{6,4},{7,5},{8,10},{9,11},{10,... | collective-permute-start | bytes 3932168 | tf_op jit(solution)/shard_map/ppermute | solution.py:1256
  149.2 22.0 %copy-start.13 = (bf16[12,128,256]{2,1,0:T(8,128)(2,1)S(1)}, bf16[12,128,256]{2,1,0:T(8,128)(2,1)}, u32[]{:S(2)}) copy-start(bf16[12,128,256]{2,1,0:T(8,128)(2,1)} %get-tuple-element.89) | copy-start | bytes 2359300
  149.2 19.2 %collective-permute-start.22 = (bf16[12,128,256]{2,1,0:T(8,128)(2,1)S(1)}, bf16[12,128,256]{2,1,0:T(8,128)(2,1)S(1)}, u32[]{:S(2)}, u32[]{:S(2)}) collective-permute-start(bf16[12,128,256]{2,1,0:T(8,128)(2,1)S(1)} %add_convert_fusion.6), channel_id=1, source_target_pairs={{0,8},{4,12},{8,0},{12,4},{16,24},{20,28},{24,16},{28,20},{1,9},{5... | collective-permute-start | bytes 2359304 | tf_op jit(solution)/shard_map/ppermute | solution.py:400
  150.8 20.5 %collective-permute-start.18 = (bf16[12,128,256]{2,1,0:T(8,128)(2,1)S(1)}, bf16[12,128,256]{2,1,0:T(8,128)(2,1)S(1)}, u32[]{:S(2)}, u32[]{:S(2)}) collective-permute-start(bf16[12,128,256]{2,1,0:T(8,128)(2,1)S(1)} %copy-done.29), channel_id=1, source_target_pairs={{0,4},{4,0},{8,12},{12,8},{16,20},{20,16},{24,28},{28,24},{1,5},{5... | collective-permute-start | bytes 2359304 | tf_op jit(solution)/shard_map/ppermute | solution.py:400
  151.2 36.9 %collective-permute-start.21 = (bf16[12,128,256]{2,1,0:T(8,128)(2,1)}, bf16[12,128,256]{2,1,0:T(8,128)(2,1)S(1)}, u32[]{:S(2)}, u32[]{:S(2)}) collective-permute-start(bf16[12,128,256]{2,1,0:T(8,128)(2,1)} %get-tuple-element.83), channel_id=1, source_target_pairs={{0,4},{4,0},{8,12},{12,8},{16,20},{20,16},{24,28},{28,24},{1,5},{5... | collective-permute-start | bytes 2359304 | tf_op jit(solution)/shard_map/ppermute | solution.py:400
  168.7 19.4 %collective-permute-start.23 = (bf16[12,128,256]{2,1,0:T(8,128)(2,1)S(1)}, bf16[12,128,256]{2,1,0:T(8,128)(2,1)S(1)}, u32[]{:S(2)}, u32[]{:S(2)}) collective-permute-start(bf16[12,128,256]{2,1,0:T(8,128)(2,1)S(1)} %add_convert_fusion.5), channel_id=1, source_target_pairs={{0,0},{4,4},{8,16},{12,20},{16,8},{20,12},{24,24},{28,28},{1,1},{5... | collective-permute-start | bytes 2359304 | tf_op jit(solution)/shard_map/ppermute | solution.py:400
  171.5 19.4 %collective-permute-start.25 = (bf16[12,128,256]{2,1,0:T(8,128)(2,1)S(1)}, bf16[12,128,256]{2,1,0:T(8,128)(2,1)S(1)}, u32[]{:S(2)}, u32[]{:S(2)}) collective-permute-start(bf16[12,128,256]{2,1,0:T(8,128)(2,1)S(1)} %add_convert_fusion.3), channel_id=1, source_target_pairs={{0,8},{4,12},{8,0},{12,4},{16,24},{20,28},{24,16},{28,20},{1,9},{5... | collective-permute-start | bytes 2359304 | tf_op jit(solution)/shard_map/ppermute | solution.py:400
  173.9 29.4 %collective-permute-start.19 = (bf16[12,128,256]{2,1,0:T(8,128)(2,1)S(1)}, bf16[12,128,256]{2,1,0:T(8,128)(2,1)S(1)}, u32[]{:S(2)}, u32[]{:S(2)}) collective-permute-start(bf16[12,128,256]{2,1,0:T(8,128)(2,1)S(1)} %copy-done.28), channel_id=1, source_target_pairs={{0,4},{4,0},{8,12},{12,8},{16,20},{20,16},{24,28},{28,24},{1,5},{5... | collective-permute-start | bytes 2359304 | tf_op jit(solution)/shard_map/ppermute | solution.py:400
  188.5 18.5 %copy-start.12 = (bf16[12,128,256]{2,1,0:T(8,128)(2,1)S(1)}, bf16[12,128,256]{2,1,0:T(8,128)(2,1)}, u32[]{:S(2)}) copy-start(bf16[12,128,256]{2,1,0:T(8,128)(2,1)} %get-tuple-element.76) | copy-start | bytes 2359300
  188.5 18.5 %collective-permute-start.24 = (bf16[12,128,256]{2,1,0:T(8,128)(2,1)S(1)}, bf16[12,128,256]{2,1,0:T(8,128)(2,1)S(1)}, u32[]{:S(2)}, u32[]{:S(2)}) collective-permute-start(bf16[12,128,256]{2,1,0:T(8,128)(2,1)S(1)} %add_convert_fusion.4), channel_id=1, source_target_pairs={{0,8},{4,12},{8,0},{12,4},{16,24},{20,28},{24,16},{28,20},{1,9},{5... | collective-permute-start | bytes 2359304 | tf_op jit(solution)/shard_map/ppermute | solution.py:400
  191.1 15.9 %collective-permute-start.26 = (bf16[12,128,256]{2,1,0:T(8,128)(2,1)S(1)}, bf16[12,128,256]{2,1,0:T(8,128)(2,1)S(1)}, u32[]{:S(2)}, u32[]{:S(2)}) collective-permute-start(bf16[12,128,256]{2,1,0:T(8,128)(2,1)S(1)} %add_convert_fusion.2), channel_id=1, source_target_pairs={{0,0},{4,4},{8,16},{12,20},{16,8},{20,12},{24,24},{28,28},{1,1},{5... | collective-permute-start | bytes 2359304 | tf_op jit(solution)/shard_map/ppermute | solution.py:400
  191.8 1.4 collective-permute-start.27
  193.2 5.2 %collective-permute-start.28 = (f32[24,1152]{1,0:T(8,128)S(1)}, f32[24,1152]{1,0:T(8,128)S(1)}, u32[]{:S(2)}, u32[]{:S(2)}) collective-permute-start(f32[24,1152]{1,0:T(8,128)S(1)} %add.57), channel_id=1, source_target_pairs={{0,2},{1,3},{2,0},{3,1},{4,6},{5,7},{6,4},{7,5},{8,10},{9,11},{10,... | collective-permute-start | bytes 331784 | tf_op jit(solution)/shard_map/ppermute | solution.py:1322
  207.5 22.6 %copy-start.3 = (bf16[12,128,256]{2,1,0:T(8,128)(2,1)}, bf16[12,128,256]{2,1,0:T(8,128)(2,1)S(1)}, u32[]{:S(2)}) copy-start(bf16[12,128,256]{2,1,0:T(8,128)(2,1)S(1)} %add_convert_fusion.1.shard0) | copy-start | bytes 2359300
  207.5 19.0 %collective-permute-start.29 = (bf16[12,128,256]{2,1,0:T(8,128)(2,1)S(1)}, bf16[12,128,256]{2,1,0:T(8,128)(2,1)S(1)}, u32[]{:S(2)}, u32[]{:S(2)}) collective-permute-start(bf16[12,128,256]{2,1,0:T(8,128)(2,1)S(1)} %add_convert_fusion.1.shard0), channel_id=1, source_target_pairs={{0,2},{1,3},{2,0},{3,1},{4,6},{5,7},{6,4},{7,5},{8,10},{9,11},{10,... | collective-permute-start | bytes 2359304 | tf_op jit(solution)/shard_map/ppermute | solution.py:1324
  208.9 4.7 %collective-permute-start.31 = (f32[24,1152]{1,0:T(8,128)S(1)}, f32[24,1152]{1,0:T(8,128)S(1)}, u32[]{:S(2)}, u32[]{:S(2)}) collective-permute-start(f32[24,1152]{1,0:T(8,128)S(1)} %add.58), channel_id=1, source_target_pairs={{0,4},{4,0},{8,12},{12,8},{16,20},{20,16},{24,28},{28,24},{1,5},{5... | collective-permute-start | bytes 331784 | tf_op jit(solution)/shard_map/ppermute | solution.py:1327
  213.7 7.0 %collective-permute-start.32 = (f32[24,1152]{1,0:T(8,128)S(1)}, f32[24,1152]{1,0:T(8,128)S(1)}, u32[]{:S(2)}, u32[]{:S(2)}) collective-permute-start(f32[24,1152]{1,0:T(8,128)S(1)} %add.59), channel_id=1, source_target_pairs={{0,8},{4,12},{8,0},{12,4},{16,24},{20,28},{24,16},{28,20},{1,9},{5... | collective-permute-start | bytes 331784 | tf_op jit(solution)/shard_map/ppermute | solution.py:1327
  220.7 5.7 %collective-permute-start.33 = (f32[24,1152]{1,0:T(8,128)S(1)}, f32[24,1152]{1,0:T(8,128)S(1)}, u32[]{:S(2)}, u32[]{:S(2)}) collective-permute-start(f32[24,1152]{1,0:T(8,128)S(1)} %add.60), channel_id=1, source_target_pairs={{0,16},{4,20},{8,24},{12,28},{16,0},{20,4},{24,8},{28,12},{1,17},{... | collective-permute-start | bytes 331784 | tf_op jit(solution)/shard_map/ppermute | solution.py:1327
  226.4 3.6 %collective-permute-start.30 = (bf16[12,128,256]{2,1,0:T(8,128)(2,1)S(1)}, bf16[12,128,256]{2,1,0:T(8,128)(2,1)S(1)}, u32[]{:S(2)}, u32[]{:S(2)}) collective-permute-start(bf16[12,128,256]{2,1,0:T(8,128)(2,1)S(1)} %add_convert_fusion.1.shard0), channel_id=1, source_target_pairs={{0,1},{1,0},{2,3},{3,2},{4,5},{5,4},{6,7},{7,6},{8,9},{9,8},{10,11... | collective-permute-start | bytes 2359304 | tf_op jit(solution)/shard_map/ppermute | solution.py:1325
  226.5 3.5 %collective-permute-start.34 = (bf16[12,128,256]{2,1,0:T(8,128)(2,1)S(1)}, bf16[12,128,256]{2,1,0:T(8,128)(2,1)S(1)}, u32[]{:S(2)}, u32[]{:S(2)}) collective-permute-start(bf16[12,128,256]{2,1,0:T(8,128)(2,1)S(1)} %collective-permute-done.29.shard1), channel_id=1, source_target_pairs={{0,1},{1,0},{2,3},{3,2},{4,5},{5,4},{6,7},{7,6},{8,9},{9,8},{10,11... | collective-permute-start | bytes 2359304 | tf_op jit(solution)/shard_map/ppermute | solution.py:1329
  227.0 3.1 %collective-permute-start.35 = (f32[24,1152]{1,0:T(8,128)S(1)}, f32[24,1152]{1,0:T(8,128)S(1)}, u32[]{:S(2)}, u32[]{:S(2)}) collective-permute-start(f32[24,1152]{1,0:T(8,128)S(1)} %add.61.small_own), channel_id=1, source_target_pairs={{0,1},{1,0},{2,3},{3,2},{4,5},{5,4},{6,7},{7,6},{8,9},{9,8},{10,11... | collective-permute-start | bytes 331784 | tf_op jit(solution)/shard_map/ppermute | solution.py:1328
  (21 other events, 117.1 us)

commit v3 on v2

--- a/solution.py
+++ b/solution.py
@@ -393,28 +393,46 @@
 
 
 Z_NEAR = z_pairs([(0, 1), (1, 0), (2, 3), (3, 2)])
-Z_MIDDLE = z_pairs([(0, 0), (1, 2), (2, 1), (3, 3)])
+Z_MIDDLE = [
+    (index, (index ^ 1) if index // 8 in (0, 3) else (24 - index // 8 * 8 + index % 8))
+    for index in range(32)
+]
 
 
 def fsdp_move(value, pairs):
-    return lax.ppermute(value, "fsdp", pairs)
+    return lax.ppermute(value, "fsdp" if len(pairs) == 8 else ("fsdp", "replica"), pairs)
+
+
+PART = 7
 
 
 def gather_fsdp(piece, z, front):
     inner = (z == 1) | (z == 2)
     near = fsdp_move(piece, Z_NEAR)
     middle = fsdp_move(piece, Z_MIDDLE)
-    side_own = fsdp_move(piece, Y_SWAP)
+    side = fsdp_move(piece, Y_SWAP)
     early, late = front()
-    side_near = fsdp_move(near, Y_SWAP)
-    middle_near = fsdp_move(after(near, early, side_own), Z_MIDDLE)
-    near_middle = fsdp_move(after(middle, early, side_own), Z_NEAR)
-    third = pick(inner, middle, near_middle)
-    near_twice = fsdp_move(after(middle_near, side_near, third), Z_NEAR)
-    side_third = fsdp_move(after(third, late), Y_SWAP)
-    last = pick(inner, middle_near, near_twice)
-    side_last = fsdp_move(after(last, side_third), Y_SWAP)
-    return [piece, side_own, near, side_near, third, side_third, last, side_last]
+    middle_near = fsdp_move(after(near, *early, side), Z_MIDDLE)
+    turned = fsdp_move(after(pick(inner, middle, side), *early), Z_NEAR)
+    side_two = fsdp_move(pick(inner, middle, near), Y_SWAP)
+    third = pick(inner, middle_near, turned)
+    near_twice = fsdp_move(after(middle_near, side_two, third), Z_NEAR)
+    side_three = fsdp_move(third, Y_SWAP)
+    over_z = fsdp_move(side_three[:PART], Z_NEAR)
+    over_y = fsdp_move(after(near_twice[PART:], side_three, *late), Y_SWAP)
+    return [
+        piece,
+        side,
+        near,
+        middle,
+        middle_near,
+        turned,
+        near_twice,
+        side_two,
+        side_three,
+        over_z,
+        over_y,
+    ]
 
 
 def position():
@@ -437,40 +455,49 @@
 
 
 def scatter_order(z, y):
-    places = []
-    for z_to in (table([3, 3, 0, 0], z), table([2, 2, 1, 1], z), table([1, 0, 3, 2], z), z):
-        places += [2 * z_to + 1 - y, 2 * z_to + y]
-    return places
+    others = (table([3, 0, 3, 0], z), table([2, 3, 0, 1], z), table([1, 2, 1, 2], z), z)
+    own = (table([3, 3, 0, 0], z), table([2, 2, 1, 1], z), table([1, 0, 3, 2], z), z)
+    return [2 * z_to + 1 - y for z_to in others] + [2 * z_to + y for z_to in own]
 
 
 def wide(value):
     return value.astype(jnp.float32)
 
 
-def scatter_fsdp(chunks, z, first_wait, second_wait, beside):
+def scatter_fsdp(chunks, z, first_wait, beside):
     inner = (z == 1) | (z == 2)
-
-    def add(first, second):
-        return (wide(first) + wide(second)).astype(jnp.bfloat16)
-
-    came = []
-    sums = []
-    for turn in range(4):
-        sent = chunks[2 * turn]
-        if turn >= 2:
-            sent = after(sent, came[turn - 2])
-        came.append(fsdp_move(sent, Y_SWAP))
-        held = chunks[2 * turn + 1]
-        sums.append(add(after(held, first_wait) if turn == 0 else held, came[turn]))
-    far = fsdp_move(sums[0], Z_NEAR)
-    far = fsdp_move(after(add(sums[0], far), second_wait), Z_MIDDLE)
-    second = fsdp_move(after(sums[1], second_wait), Z_NEAR)
-    last_wait = beside()
-    last = add(sums[2], jnp.where(inner, wide(far), 0.0))
-    last = fsdp_move(after(last, last_wait), Z_NEAR)
-    second = fsdp_move(after(add(sums[1], second), last_wait), Z_MIDDLE)
-    total = wide(sums[3]) + wide(last) + jnp.where(inner, wide(second), 0.0)
-    return total.astype(jnp.bfloat16)
+    side_low, side_high, side_one, side_two, side_own, last, third, near, own = chunks
+
+    def low(value):
+        return value.astype(jnp.bfloat16)
+
+    def only(cond, value):
+        return jnp.where(cond, wide(value), 0.0)
+
+    over_y = fsdp_move(side_high, Y_SWAP)
+    over_z = fsdp_move(side_low, Z_NEAR)
+    over_z = jnp.pad(only(inner, over_z), ((0, 12 - PART), (0, 0), (0, 0)))
+    back_one = fsdp_move(low(wide(after(side_one, first_wait)) + over_z), Y_SWAP)
+    over_y = jnp.pad(wide(over_y), ((PART, 0), (0, 0), (0, 0)))
+    back_far = fsdp_move(low(wide(last) + over_y), Z_NEAR)
+    back_two = fsdp_move(after(side_two, first_wait), Y_SWAP)
+    to_middle = low(wide(last) + wide(back_one) + wide(back_far))
+    to_near = low(
+        jnp.where(
+            inner,
+            wide(jnp.concatenate([side_low, side_high])),
+            wide(third) + wide(back_one),
+        )
+    )
+    middle_one = fsdp_move(to_middle, Z_MIDDLE)
+    near_one = fsdp_move(to_near, Z_NEAR)
+    back_own = fsdp_move(low(wide(side_own) + only(z % 3 == 0, near_one)), Y_SWAP)
+    to_near = low(wide(near) + jnp.where(inner, wide(middle_one), wide(back_two)))
+    to_middle = low(wide(third) + wide(back_two) + wide(near_one))
+    to_near, to_middle, _ = lax.optimization_barrier((to_near, to_middle, beside()))
+    near_two = fsdp_move(to_near, Z_NEAR)
+    middle_two = fsdp_move(to_middle, Z_MIDDLE)
+    return low(wide(own) + wide(back_own) + wide(near_two) + only(inner, middle_two))
 
 
 def lanes_of(shape):
@@ -531,7 +558,6 @@
 def front_kernel(
     bounds,
     stack,
-    cotangent,
     mix_gain,
     up_own,
     up_one,
@@ -569,7 +595,6 @@
         stats[0, at, 0:36] = coef
         stats[1, at, 0:36] = hidden_pre
         stats[2, at, 4:5] = rms
-        packet[4 * ROWS + seq * SEQ : 4 * ROWS + seq * SEQ + SEQ] = cotangent[at]
 
         def mix(step, carry):
             row = pl.multiple_of(step // 2 * 16, 16)
@@ -605,12 +630,12 @@
         return carry
 
     lax.fori_loop(0, seqs * SEQ // 16, norm, 0)
-    packet[5 * ROWS :] = jnp.zeros((16, WIDTH), jnp.bfloat16)
+    packet[4 * ROWS :] = jnp.zeros((16, WIDTH), jnp.bfloat16)
     row = rows_of((16, 128))
     marks = jnp.zeros((16, 128), jnp.float32)
     for place in range(2 * seqs):
         marks = jnp.where(row == place, wide(bounds[place]), marks)
-    packet[5 * ROWS :, 0:128] = marks.astype(jnp.bfloat16)
+    packet[4 * ROWS :, 0:128] = marks.astype(jnp.bfloat16)
 
 
 def main_kernel(
@@ -619,6 +644,10 @@
     packet1,
     packet2,
     packet3,
+    cotangent0,
+    cotangent1,
+    cotangent2,
+    cotangent3,
     piece0,
     piece1,
     piece2,
@@ -627,7 +656,11 @@
     piece5,
     piece6,
     piece7,
-    chunk0,
+    piece8,
+    piece9,
+    piece10,
+    chunk_low,
+    chunk_high,
     chunk1,
     chunk2,
     chunk3,
@@ -659,8 +692,21 @@
     origin = gather_order(z, y)
     target = scatter_order(z, y)
     packets = (packet0, packet1, packet2, packet3)
-    pieces = (piece0, piece1, piece2, piece3, piece4, piece5, piece6, piece7)
-    chunks = (chunk0, chunk1, chunk2, chunk3, chunk4, chunk5, chunk6, chunk7)
+    cotangents = (cotangent0, cotangent1, cotangent2, cotangent3)
+    piece, side, near, middle, middle_near, turned = piece0, piece1, piece2, piece3, piece4, piece5
+    near_twice, side_two, side_three, over_z, over_y = piece6, piece7, piece8, piece9, piece10
+    inner = (z == 1) | (z == 2)
+    sources = (
+        (piece, piece),
+        (side, side),
+        (near, near),
+        (turned, side_two),
+        (middle, turned),
+        (side_two, side_three),
+        (middle_near, near_twice),
+        (side_three, None),
+    )
+    chunks = (chunk1, chunk2, chunk3, chunk4, chunk5, chunk6, chunk7)
     member_rows = [pl.ds(pl.multiple_of(place * 128, 128), 128) for place in origin]
 
     def unit_copies(unit):
@@ -673,48 +719,79 @@
             for block in range(4)
         ]
 
+    def piece_copies(index, ref, tail_ref):
+        rows = member_rows[index]
+        down = 7 if tail_ref is ref else 0
+        found = [
+            pltpu.make_async_copy(
+                ref.at[pl.ds(4, 3)], lin_all.at[:, rows], piece_sems.at[index, 0]
+            )
+        ]
+        for block in range(4):
+            cols = pl.ds(block * 256, 256)
+            found.append(
+                pltpu.make_async_copy(
+                    tail_ref.at[down + block], rhs_all.at[rows, cols], piece_sems.at[index, 1 + block]
+                )
+            )
+        found.append(
+            pltpu.make_async_copy(
+                tail_ref.at[down + 4], spare.at[origin[index]], piece_sems.at[index, 5]
+            )
+        )
+        for block in range(4):
+            found.append(
+                pltpu.make_async_copy(
+                    ref.at[block],
+                    up_all.at[rows, pl.ds(block * 256, 256)],
+                    piece_sems.at[index, 6 + block],
+                )
+            )
+        return found
+
     first = unit_copies(0) + unit_copies(1) + unit_copies(2)
-    for index in range(8):
-        first.append(
-            pltpu.make_async_copy(
-                pieces[index].at[pl.ds(4, 3)],
-                lin_all.at[:, member_rows[index]],
-                piece_sems.at[index, 0],
-            )
-        )
-    second = unit_copies(4)
+    second = [
+        pltpu.make_async_copy(
+            cotangents[block],
+            acts.at[4, pl.ds(block * ROWS, ROWS)],
+            packet_sems.at[block, 4],
+        )
+        for block in range(4)
+    ]
     for block in range(4):
         second.append(
             pltpu.make_async_copy(
-                packets[block].at[pl.ds(5 * ROWS, 16)], marks.at[block], packet_sems.at[block, 5]
+                packets[block].at[pl.ds(4 * ROWS, 16)], marks.at[block], packet_sems.at[block, 5]
             )
         )
-    for index in range(8):
-        for block in range(4):
-            second.append(
-                pltpu.make_async_copy(
-                    pieces[index].at[7 + block],
-                    rhs_all.at[member_rows[index], pl.ds(block * 256, 256)],
-                    piece_sems.at[index, 1 + block],
-                )
-            )
-        second.append(
-            pltpu.make_async_copy(
-                pieces[index].at[11], spare.at[origin[index]], piece_sems.at[index, 5]
-            )
-        )
     third = unit_copies(3)
-    for index in range(8):
-        for block in range(4):
-            third.append(
-                pltpu.make_async_copy(
-                    pieces[index].at[block],
-                    up_all.at[member_rows[index], pl.ds(block * 256, 256)],
-                    piece_sems.at[index, 6 + block],
-                )
-            )
     for copy in first + second + third:
         copy.start()
+    for index, (for_inner, for_ends) in enumerate(sources):
+        copies = piece_copies(index, for_inner, for_inner)
+        first.append(copies[0])
+        second += copies[1:6]
+        third += copies[6:]
+        if for_inner is for_ends:
+            for copy in copies:
+                copy.start()
+            continue
+        ends = (
+            piece_copies(index, over_z, over_y)
+            if for_ends is None
+            else piece_copies(index, for_ends, for_ends)
+        )
+
+        @pl.when(inner)
+        def _():
+            for copy in copies:
+                copy.start()
+
+        @pl.when(jnp.logical_not(inner))
+        def _():
+            for copy in ends:
+                copy.start()
+
     for copy in first:
         copy.wait()
     for stream in range(3):
@@ -860,8 +937,15 @@
             parts[even, 7 + block, 96:128] = part[pair * 64 : pair * 64 + 32]
             parts[even, 11, block * 32 : block * 32 + 32] = part[pair * 64 + 32 : pair * 64 + 64]
     sent = [
-        pltpu.make_async_copy(parts.at[target[index]], chunks[index], chunk_sems.at[index])
-        for index in range(8)
+        pltpu.make_async_copy(
+            parts.at[target[0], pl.ds(0, PART)], chunk_low, chunk_sems.at[0]
+        ),
+        pltpu.make_async_copy(
+            parts.at[target[0], pl.ds(PART, 12 - PART)], chunk_high, chunk_sems.at[8]
+        ),
+    ] + [
+        pltpu.make_async_copy(parts.at[target[index]], chunks[index - 1], chunk_sems.at[index])
+        for index in range(1, 8)
     ]
     for copy in sent:
         copy.start()
@@ -903,7 +987,6 @@
     cotangent,
     scaled,
     stats,
-    stream_in,
     keep,
     came,
     across,
@@ -911,7 +994,6 @@
     mix_up,
     mix_down,
     norm_gain,
-    layer_output,
     stack_grad,
     small_own,
     small_other,
@@ -932,7 +1014,6 @@
         def result(index):
             return wide(keep[0, index, span]) + wide(came[0, index, span]) + wide(across[index, span])
 
-        layer_output[span] = (stream_in[span] + result(4)).astype(jnp.bfloat16)
         for stream in range(4):
             item = result(stream)
             scale = scaled[stream, span]
@@ -1187,23 +1268,29 @@
     piece = after(piece, *ups)
     bounds = jnp.concatenate([pic_start.reshape(seqs), doc_split.reshape(seqs)])
     kept = {}
+    grad_across = lax.ppermute(cotangent, "replica", X_SWAP)
+    grad_packets = (
+        cotangent,
+        grad_across,
+        lax.ppermute(cotangent, "replica", CORE_SWAP),
+        lax.ppermute(grad_across, "replica", CORE_SWAP),
+    )
 
     def front():
         packet, *kept["rest"] = call(
             front_kernel,
             (
-                shape_of((5 * ROWS + 16, width)),
+                shape_of((4 * ROWS + 16, width)),
                 shape_of((4, ROWS, width), jnp.float32),
                 shape_of((3, ROWS, 128), jnp.float32),
                 shape_of((ROWS, width), jnp.float32),
                 shape_of((36, width)),
             ),
-            [SMEM_FULL] + [VMEM_FULL] * 11,
+            [SMEM_FULL] + [VMEM_FULL] * 10,
             (VMEM_FULL,) * 5,
             (
                 bounds,
                 stack,
-                cotangent,
                 gain_row,
                 *ups,
                 mix_down,
@@ -1217,7 +1304,7 @@
         beside = lax.ppermute(packet, "replica", CORE_SWAP)
         beside_across = lax.ppermute(across, "replica", CORE_SWAP)
         kept["packets"] = (packet, across, beside, beside_across)
-        return packet, across
+        return (packet, grad_across), (across,)
 
     pieces = gather_fsdp(piece, z, front)
     packets = kept["packets"]
@@ -1225,10 +1312,12 @@
 
     results = call(
         main_kernel,
-        (shape_of((12, 128, 256)),) * 8 + (shape_of((2, 5, ROWS, width)),) * 2,
-        [VMEM_FULL] + [IN_PLACE] * 12,
-        (IN_PLACE,) * 10,
-        (jnp.asarray(rope_tables()),) + packets + tuple(pieces),
+        (shape_of((PART, 128, 256)), shape_of((12 - PART, 128, 256)))
+        + (shape_of((12, 128, 256)),) * 7
+        + (shape_of((2, 5, ROWS, width)),) * 2,
+        [VMEM_FULL] + [IN_PLACE] * 19,
+        (IN_PLACE,) * 11,
+        (jnp.asarray(rope_tables()),) + packets + grad_packets + tuple(pieces),
         scratch=[
             pltpu.VMEM((5, 4 * ROWS, width), jnp.bfloat16),
             pltpu.VMEM((4, 16, width), jnp.bfloat16),
@@ -1245,17 +1334,22 @@
             pltpu.VMEM((2, 2, 5, ROWS, width), jnp.bfloat16),
             pltpu.SemaphoreType.DMA((4, 6)),
             pltpu.SemaphoreType.DMA((8, 10)),
-            pltpu.SemaphoreType.DMA((8,)),
+            pltpu.SemaphoreType.DMA((9,)),
             pltpu.SemaphoreType.DMA((2, 5)),
         ],
     )
-    chunks, keep, send = results[:8], results[8], results[9]
+    chunks, keep, send = results[:9], results[9], results[10]
 
     came = lax.ppermute(send, "replica", CORE_SWAP)
-    sum_across = (wide(keep[1]) + wide(came[1])).astype(jnp.bfloat16)
+    sum_across = (wide(keep[1, :4]) + wide(came[1, :4])).astype(jnp.bfloat16)
     came_across = lax.ppermute(sum_across, "replica", X_SWAP)
-
-    first_half = pl.BlockSpec((1, 5, ROWS, width), lambda step: (0, 0, 0, 0))
+    out_across = (wide(keep[1, 4]) + wide(came[1, 4])).astype(jnp.bfloat16)
+    out_across = lax.ppermute(after(out_across, came_across), "replica", X_SWAP)
+    layer_output = (
+        stream_last + wide(keep[0, 4]) + wide(came[0, 4]) + wide(out_across)
+    ).astype(jnp.bfloat16)
+
+    first_half = pl.BlockSpec((1, 4, ROWS, width), lambda step: (0, 0, 0, 0))
 
     def whole(shape):
         return pl.BlockSpec(shape, lambda step: (0,) * len(shape))
@@ -1265,7 +1359,6 @@
             back_kernel,
             grid=(1,),
             out_shape=(
-                shape_of((ROWS, width)),
                 shape_of((seqs, STREAMS_IN, SEQ, width)),
                 shape_of((24, width + 128), jnp.float32),
                 shape_of((24, width + 128), jnp.float32),
@@ -1276,17 +1369,15 @@
                 whole((ROWS, width)),
                 whole((4, ROWS, width)),
                 whole((3, ROWS, 128)),
-                whole((ROWS, width)),
                 first_half,
                 first_half,
-                whole((5, ROWS, width)),
+                whole((4, ROWS, width)),
                 whole((1, width)),
                 whole((36, width)),
                 whole((36, 36)),
                 whole((4, width)),
             ],
             out_specs=(
-                whole((ROWS, width)),
                 whole((seqs, STREAMS_IN, SEQ, width)),
                 whole((24, width + 128)),
                 whole((24, width + 128)),
@@ -1304,7 +1395,6 @@
             cotangent,
             scaled,
             stats,
-            stream_last,
             keep,
             came,
             came_across,
@@ -1313,14 +1403,14 @@
             mix_down,
             norm_gain,
         )
-        return kept["back"][2]
-
-    shard = scatter_fsdp(chunks, z, sum_across, came_across, back)
-    layer_output, stack_grad, small, small_other, coefficients = kept["back"]
+        return kept["back"][1]
+
+    shard = scatter_fsdp(chunks, z, sum_across, back)
+    stack_grad, small, small_other, coefficients = kept["back"]
 
     small = small + lax.ppermute(small_other, "replica", CORE_SWAP)
     small = small + lax.ppermute(small, "replica", X_SWAP)
-    shard = after(shard, small)
+    shard = after(shard, small, out_across)
     shard_across = lax.ppermute(shard, "replica", X_SWAP)
     shard_beside = lax.ppermute(shard, "replica", CORE_SWAP)
     for perm in (Y_SWAP, Z_SWAP_NEAR, Z_SWAP_FAR):

time: 238 us -> 223 us (0.937)
  starting transfers between devices: 48.8 us -> 36.6 us
  waiting for transfers between devices: 118 us -> 107 us
  other arithmetic: 6.49 us -> 13.7 us
    ppermute x18 -> x24, starting transfers between devices: 26.2 us -> 17.9 us  [the longest x20 14.8 us: fsdp_move(): lax.ppermute(value, 'fsdp' if len(pairs) == 8 else ('fsdp', 'replica'), p...]
    convert_element_type x7 -> x8, other arithmetic: 4.52 us -> 12.7 us  [the longest x5 6.27 us: low(): return value.astype(jnp.bfloat16)]
    ppermute x1, waiting for transfers between devices: 4.64 us -> 0.01 us  [on_device_tensor(): came = lax.ppermute(send, 'replica', CORE_SWAP)]
    ppermute x18 -> x24, waiting for transfers between devices: 84.8 us -> 81.4 us  [the longest x20 79.9 us: fsdp_move(): lax.ppermute(value, 'fsdp' if len(pairs) == 8 else ('fsdp', 'replica'), p...]
    ppermute x1, waiting for transfers between devices: 7.09 us -> 3.72 us  [front(): across = lax.ppermute(packet, 'replica', X_SWAP)]
    ppermute x1, waiting for transfers between devices: 0.01 us -> 3.01 us  [on_device_tensor(): came_across = lax.ppermute(sum_across, 'replica', X_SWAP)]
    unnamed x66 -> x94, local copies, waits for them, and re-layouts: 4.91 us -> 5.32 us
  transfers between devices with their start and end apart: 36 -> 42, of which waited for: 22 -> 24; matrix products, arithmetic and copies ran while one was open for 3% -> 5% of each run, Pallas kernels for 11% -> 11%
where the time goes in v3:
time: 223 us; the launch traced here: 222 us
  waiting for transfers between devices  107 us (48%)
  Pallas kernels  57.7 us (26%)
  starting transfers between devices  36.6 us (16%)
  other arithmetic  13.7 us (6%)
  local copies, waits for them, and re-layouts  5.97 us (3%)
    ppermute x20, waiting for transfers between devices, fsdp_move(): lax.ppermute(value, 'fsdp' if len(pairs) == 8 else ('fsdp', 'replica'), p...  79.9 us
    pallas_call x4, Pallas kernels, call(): pl.pallas_call(kernel, out_shape=outs, in_specs=specs, out_specs=out_spec...  44.8 us
    ppermute x20, starting transfers between devices, fsdp_move(): lax.ppermute(value, 'fsdp' if len(pairs) == 8 else ('fsdp', 'replica'), p...  14.8 us
    pallas_call x1, Pallas kernels, back(): pl.pallas_call(back_kernel, grid=(1,), out_shape=(shape_of((seqs, STREAMS...  13 us
    ppermute x3, waiting for transfers between devices, on_device_tensor(): small = small + lax.ppermute(small, 'fsdp', perm)  10.9 us
    convert_element_type x5, other arithmetic, low(): return value.astype(jnp.bfloat16)  6.27 us
    ppermute x3, starting transfers between devices, on_device_tensor(): small = small + lax.ppermute(small, 'fsdp', perm)  5.7 us
    ppermute x3, starting transfers between devices, on_device_tensor(): lax.ppermute(up_pair, 'fsdp', z_pairs([((step + to) % 4, to) for to in ra...  5.57 us
  transfers between devices with their start and end apart: 42, of which 24 were waited for; matrix products, arithmetic and copies ran while one was open for 5% of the time, Pallas kernels for 11%

profile of v3, /device:TPU:0, one launch (start us, length us, event | category | flops | bytes accessed | tf_op | source)
XLA Modules:
  0.0 222.2 jit_solution(15487054113816929054)
XLA Ops:
  0.7 3.0 %collective-permute-start = (bf16[36,128]{1,0:T(8,128)(2,1)}, bf16[36,128]{1,0:T(8,128)(2,1)S(1)}, u32[]{:S(2)}, u32[]{:S(2)}) collective-permute-start(bf16[36,128]{1,0:T(8,128)(2,1)} %bitcast.46), channel_id=1, source_target_pairs={{0,4},{4,0},{8,12},{12,8},{16,20},{20,16},{24,28},{28,24},{1,5},{5... | collective-permute-start | bytes 27656 | tf_op jit(solution)/shard_map/ppermute | solution.py:1263
  3.7 3.2 %shard_map.246.piece0 = bf16[12,128,256]{2,1,0:T(8,128)(2,1)} custom-call(bf16[3,128,1024]{2,1,0:T(8,128)(2,1)} %projection.1, bf16[128,1024]{1,0:T(8,128)(2,1)} %out_weight.1, bf16[128,4096]{1,0:T(8,128)(2,1)} %up_weight.1, bf16[512,1024]{1,0:T(8,128)(2,1)} %down_weight.1), custom_call_target="tpu_custom_call" | custom-call | tf_op jit(solution)/shard_map/pallas_call | solution.py:1203
  6.9 1.6 collective-permute-start.3
  8.6 2.6 %collective-permute-start.2 = (bf16[36,256]{1,0:T(8,128)(2,1)S(1)}, bf16[36,256]{1,0:T(8,128)(2,1)S(1)}, u32[]{:S(2)}, u32[]{:S(2)}) collective-permute-start(bf16[36,256]{1,0:T(8,128)(2,1)S(1)} %pad_maximum_fusion.up_own), channel_id=1, source_target_pairs={{16,0},{20,4},{24,8},{28,12},{0,16},{4,20},{8,24},{12,28},{17,1},{... | collective-permute-start | bytes 55304 | tf_op jit(solution)/shard_map/ppermute | solution.py:1265
  11.1 1.3 collective-permute-start.1
  13.2 1.7 collective-permute-done.1.up_one
  14.9 1.5 collective-permute-start.11
  17.2 1.5 collective-permute-start.7
  19.9 9.4 %shard_map.247 = (bf16[528,1024]{1,0:T(8,128)(2,1)}, f32[4,128,1024]{2,1,0:T(8,128)}, f32[3,128,128]{2,1,0:T(8,128)}, f32[128,1024]{1,0:T(8,128)}, bf16[36,1024]{1,0:T(8,128)(2,1)}) custom-call(s32[4]{0:T(128)} %pad_add_fusion.bounds, bf16[2,9,64,1024]{3,2,1,0:T(8,128)(2,1)} %bitcast.37, f32[1,1024]{1,0:T(1,128)} %bitcast.44, bf16[36,256]{1,0:T(8,128)(2,1)} %copy-done.37, ...), custom_call_target="tpu_custom_call" | custom-call | tf_op jit(solution)/shard_map/pallas_call | solution.py:1203
  29.3 5.8 %collective-permute-done.11.piece2 = bf16[12,128,256]{2,1,0:T(8,128)(2,1)S(1)} collective-permute-done((bf16[12,128,256]{2,1,0:T(8,128)(2,1)}, bf16[12,128,256]{2,1,0:T(8,128)(2,1)S(1)}, u32[]{:S(2)}, u32[]{:S(2)}) %collective-permute-start.11) | collective-permute-done | bytes 786464 | tf_op jit(solution)/shard_map/ppermute | solution.py:403
  36.7 4.1 %collective-permute-start.14 = (bf16[12,128,256]{2,1,0:T(8,128)(2,1)S(1)}, bf16[12,128,256]{2,1,0:T(8,128)(2,1)S(1)}, u32[]{:S(2)}, u32[]{:S(2)}) collective-permute-start(bf16[12,128,256]{2,1,0:T(8,128)(2,1)S(1)} %get-tuple-element.61), channel_id=1, source_target_pairs={{0,8},{4,12},{8,0},{12,4},{16,24},{20,28},{24,16},{28,20},{1,9},{5... | collective-permute-start | bytes 2359304 | tf_op jit(solution)/shard_map/ppermute | solution.py:403
  40.8 1.5 collective-permute-start.4
  43.0 14.6 %collective-permute-done.14.piece5 = bf16[12,128,256]{2,1,0:T(8,128)(2,1)S(1)} collective-permute-done((bf16[12,128,256]{2,1,0:T(8,128)(2,1)S(1)}, bf16[12,128,256]{2,1,0:T(8,128)(2,1)S(1)}, u32[]{:S(2)}, u32[]{:S(2)}) %collective-permute-start.14) | collective-permute-done | bytes 786464 | tf_op jit(solution)/shard_map/ppermute | solution.py:403
  58.5 3.2 %collective-permute-done.15.piece7 = bf16[12,128,256]{2,1,0:T(8,128)(2,1)S(1)} collective-permute-done((bf16[12,128,256]{2,1,0:T(8,128)(2,1)S(1)}, bf16[12,128,256]{2,1,0:T(8,128)(2,1)S(1)}, u32[]{:S(2)}, u32[]{:S(2)}) %collective-permute-start.15) | collective-permute-done | bytes 786464 | tf_op jit(solution)/shard_map/ppermute | solution.py:403
  61.7 3.7 %collective-permute-done.4.packet1 = bf16[528,1024]{1,0:T(8,128)(2,1)S(1)} collective-permute-done((bf16[528,1024]{1,0:T(8,128)(2,1)S(1)}, bf16[528,1024]{1,0:T(8,128)(2,1)S(1)}, u32[]{:S(2)}, u32[]{:S(2)}) %collective-permute-start.4) | collective-permute-done | bytes 1081376 | tf_op jit(solution)/shard_map/ppermute | solution.py:1303
  65.9 11.2 %collective-permute-done.17.piece8 = bf16[12,128,256]{2,1,0:T(8,128)(2,1)S(1)} collective-permute-done((bf16[12,128,256]{2,1,0:T(8,128)(2,1)S(1)}, bf16[12,128,256]{2,1,0:T(8,128)(2,1)S(1)}, u32[]{:S(2)}, u32[]{:S(2)}) %collective-permute-start.17) | collective-permute-done | bytes 786464 | tf_op jit(solution)/shard_map/ppermute | solution.py:403
  78.5 1.5 collective-permute-done.9.cotangent3
  80.0 1.0 copy-done.13
  81.0 4.8 %collective-permute-done.19.piece10 = bf16[5,128,256]{2,1,0:T(8,128)(2,1)S(1)} collective-permute-done((bf16[5,128,256]{2,1,0:T(8,128)(2,1)S(1)}, bf16[5,128,256]{2,1,0:T(8,128)(2,1)S(1)}, u32[]{:S(2)}, u32[]{:S(2)}) %collective-permute-start.19) | collective-permute-done | bytes 327712 | tf_op jit(solution)/shard_map/ppermute | solution.py:403
  85.8 2.8 %collective-permute-done.18.piece9 = bf16[7,128,256]{2,1,0:T(8,128)(2,1)} collective-permute-done((bf16[7,128,256]{2,1,0:T(8,128)(2,1)S(1)}, bf16[7,128,256]{2,1,0:T(8,128)(2,1)}, u32[]{:S(2)}, u32[]{:S(2)}) %collective-permute-start.18) | collective-permute-done | bytes 458784 | tf_op jit(solution)/shard_map/ppermute | solution.py:403
  88.6 27.0 %shard_map.248 = (bf16[7,128,256]{2,1,0:T(8,128)(2,1)}, bf16[5,128,256]{2,1,0:T(8,128)(2,1)}, bf16[12,128,256]{2,1,0:T(8,128)(2,1)}, bf16[12,128,256]{2,1,0:T(8,...) custom-call(f32[3,128,128]{2,1,0:T(8,128)} %constant.39.clone.rope, ...), custom_call_target="tpu_custom_call" | custom-call | tf_op jit(solution)/shard_map/pallas_call | solution.py:1203
  116.7 9.3 %collective-permute-done.27 = bf16[5,128,256]{2,1,0:T(8,128)(2,1)S(1)} collective-permute-done((bf16[5,128,256]{2,1,0:T(8,128)(2,1)}, bf16[5,128,256]{2,1,0:T(8,128)(2,1)S(1)}, u32[]{:S(2)}, u32[]{:S(2)}) %collective-permute-start.27) | collective-permute-done | bytes 327712 | tf_op jit(solution)/shard_map/ppermute | solution.py:403
  126.0 1.2 fusion.7
  127.6 1.7 collective-permute-done.23
  129.3 3.5 %fusion.10 = bf16[4,128,1024]{2,1,0:T(8,128)(2,1)} fusion(bf16[2,5,128,1024]{3,2,1,0:T(8,128)(2,1)S(1)} %collective-permute-done.20.came, bf16[2,5,128,1024]{3,2,1,0:T(8,128)(2,1)} %get-tuple-element.64.keep), kind=kLoop, calls=%fused_computation.20 | loop fusion | flops 2097152 | bytes 3145728 | tf_op jit(solution)/shard_map/convert_element_type | solution.py:1344
  133.0 1.6 collective-permute-start.24
  135.1 11.2 %collective-permute-done.28 = bf16[12,128,256]{2,1,0:T(8,128)(2,1)S(1)} collective-permute-done((bf16[12,128,256]{2,1,0:T(8,128)(2,1)S(1)}, bf16[12,128,256]{2,1,0:T(8,128)(2,1)S(1)}, u32[]{:S(2)}, u32[]{:S(2)}) %collective-permute-start.28) | collective-permute-done | bytes 786464 | tf_op jit(solution)/shard_map/ppermute | solution.py:403
  146.4 7.2 %collective-permute-done.24 = bf16[12,128,256]{2,1,0:T(8,128)(2,1)S(1)} collective-permute-done((bf16[12,128,256]{2,1,0:T(8,128)(2,1)S(1)}, bf16[12,128,256]{2,1,0:T(8,128)(2,1)S(1)}, u32[]{:S(2)}, u32[]{:S(2)}) %collective-permute-start.24) | collective-permute-done | bytes 786464 | tf_op jit(solution)/shard_map/ppermute | solution.py:403
  153.6 1.8 fusion.1
  155.7 3.0 %collective-permute-done.21.across = bf16[4,128,1024]{2,1,0:T(8,128)(2,1)S(1)} collective-permute-done((bf16[4,128,1024]{2,1,0:T(8,128)(2,1)}, bf16[4,128,1024]{2,1,0:T(8,128)(2,1)S(1)}, u32[]{:S(2)}, u32[]{:S(2)}) %collective-permute-start.21) | collective-permute-done | bytes 1048608 | tf_op jit(solution)/shard_map/ppermute | solution.py:1345
  159.7 13.0 %shard_map.249 = (bf16[2,9,64,1024]{3,2,1,0:T(8,128)(2,1)}, f32[24,1152]{1,0:T(8,128)}, f32[24,1152]{1,0:T(8,128)}, f32[2,9,4,64]{3,2,1,0:T(4,128)}) custom-call(bf16[2,9,64,1024]{3,2,1,0:T(8,128)(2,1)} %bitcast.38, bf16[128,1024]{1,0:T(8,128)(2,1)} %bitcast.40, f32[4,128,1024]{2,1,0:T(8,128)} %get-tuple-element.67.scaled, ...), custom_call_target="tpu_custom_call" | custom-call | tf_op jit(solution)/shard_map/pallas_call | solution.py:1358
  172.7 2.6 %fusion.3 = (bf16[12,128,256]{2,1,0:T(8,128)(2,1)S(1)}, bf16[12,128,256]{2,1,0:T(8,128)(2,1)S(1)}, bf16[12,128,256]{2,1,0:T(8,128)(2,1)S(1)}) fusion(bf16[12,128,256]{2,1,0:T(8,128)(2,1)} %collective-permute-done.25, bf16[12,128,256]{2,1,0:T(8,128)(2,1)S(1)} %copy-done.24, pred[]{:T(512)S(6)} %eq.15, bf16[12,128,256]{2,1,0:T(8,128)(2,1)} %collective-permute-done.30, ...), kind=kLoop, calls=%fused_computation.11 | loop fusion | flops 5898240 | bytes 7077890 | tf_op jit(solution)/shard_map/convert_element_type | solution.py:472
  176.1 1.3 collective-permute-start.31
  177.9 1.9 collective-permute-done.33
  179.9 1.1 collective-permute-start.34
  181.0 1.1 fusion.13
  182.1 1.0 collective-permute-start.22
  183.1 2.3 %collective-permute-done.34 = f32[24,1152]{1,0:T(8,128)S(1)} collective-permute-done((f32[24,1152]{1,0:T(8,128)S(1)}, f32[24,1152]{1,0:T(8,128)S(1)}, u32[]{:S(2)}, u32[]{:S(2)}) %collective-permute-start.34) | collective-permute-done | bytes 110624 | tf_op jit(solution)/shard_map/ppermute | solution.py:1412
  185.5 7.4 %collective-permute-done.26 = bf16[12,128,256]{2,1,0:T(8,128)(2,1)S(1)} collective-permute-done((bf16[12,128,256]{2,1,0:T(8,128)(2,1)S(1)}, bf16[12,128,256]{2,1,0:T(8,128)(2,1)S(1)}, u32[]{:S(2)}, u32[]{:S(2)}) %collective-permute-start.26) | collective-permute-done | bytes 786464 | tf_op jit(solution)/shard_map/ppermute | solution.py:403
  194.7 1.1 collective-permute-start.37
  195.8 3.6 %collective-permute-done.37 = f32[24,1152]{1,0:T(8,128)S(1)} collective-permute-done((f32[24,1152]{1,0:T(8,128)S(1)}, f32[24,1152]{1,0:T(8,128)S(1)}, u32[]{:S(2)}, u32[]{:S(2)}) %collective-permute-start.37) | collective-permute-done | bytes 110624 | tf_op jit(solution)/shard_map/ppermute | solution.py:1417
  199.4 2.4 %collective-permute-start.38 = (f32[24,1152]{1,0:T(8,128)S(1)}, f32[24,1152]{1,0:T(8,128)S(1)}, u32[]{:S(2)}, u32[]{:S(2)}) collective-permute-start(f32[24,1152]{1,0:T(8,128)S(1)} %add.97), channel_id=1, source_target_pairs={{0,8},{4,12},{8,0},{12,4},{16,24},{20,28},{24,16},{28,20},{1,9},{5... | collective-permute-start | bytes 331784 | tf_op jit(solution)/shard_map/ppermute | solution.py:1417
  201.8 3.8 %collective-permute-done.38 = f32[24,1152]{1,0:T(8,128)S(1)} collective-permute-done((f32[24,1152]{1,0:T(8,128)S(1)}, f32[24,1152]{1,0:T(8,128)S(1)}, u32[]{:S(2)}, u32[]{:S(2)}) %collective-permute-start.38) | collective-permute-done | bytes 110624 | tf_op jit(solution)/shard_map/ppermute | solution.py:1417
  205.6 2.2 %collective-permute-start.39 = (f32[24,1152]{1,0:T(8,128)S(1)}, f32[24,1152]{1,0:T(8,128)S(1)}, u32[]{:S(2)}, u32[]{:S(2)}) collective-permute-start(f32[24,1152]{1,0:T(8,128)S(1)} %add.98), channel_id=1, source_target_pairs={{0,16},{4,20},{8,24},{12,28},{16,0},{20,4},{24,8},{28,12},{1,17},{... | collective-permute-start | bytes 331784 | tf_op jit(solution)/shard_map/ppermute | solution.py:1417
  207.8 3.5 %collective-permute-done.39 = f32[24,1152]{1,0:T(8,128)S(1)} collective-permute-done((f32[24,1152]{1,0:T(8,128)S(1)}, f32[24,1152]{1,0:T(8,128)S(1)}, u32[]{:S(2)}, u32[]{:S(2)}) %collective-permute-start.39) | collective-permute-done | bytes 110624 | tf_op jit(solution)/shard_map/ppermute | solution.py:1417
  212.0 1.9 fusion.12
  213.9 1.1 collective-permute-done.41.small_other
  216.8 5.2 %shard_map.250 = (f32[3,128,1024]{2,1,0:T(8,128)}, f32[128,1024]{1,0:T(8,128)}, f32[128,4096]{1,0:T(8,128)}, f32[512,1024]{1,0:T(8,128)}, f32[1,1024]{1,0:T(1,12...) custom-call(bf16[12,128,256]{2,1,0:T(8,128)(2,1)} %copy-done.6, ...), custom_call_target="tpu_custom_call" | custom-call | tf_op jit(solution)/shard_map/pallas_call | solution.py:1203
  (156 shorter events, 16.8 us)
Async XLA Ops:
  0.7 6.2 %collective-permute-start = (bf16[36,128]{1,0:T(8,128)(2,1)}, bf16[36,128]{1,0:T(8,128)(2,1)S(1)}, u32[]{:S(2)}, u32[]{:S(2)}) collective-permute-start(bf16[36,128]{1,0:T(8,128)(2,1)} %bitcast.46), channel_id=1, source_target_pairs={{0,4},{4,0},{8,12},{12,8},{16,20},{20,16},{24,28},{28,24},{1,5},{5... | collective-permute-start | bytes 27656 | tf_op jit(solution)/shard_map/ppermute | solution.py:1263
  6.9 5.9 %collective-permute-start.3 = (bf16[36,256]{1,0:T(8,128)(2,1)S(1)}, bf16[36,256]{1,0:T(8,128)(2,1)S(1)}, u32[]{:S(2)}, u32[]{:S(2)}) collective-permute-start(bf16[36,256]{1,0:T(8,128)(2,1)S(1)} %pad_maximum_fusion.up_own), channel_id=1, source_target_pairs={{24,0},{28,4},{0,8},{4,12},{8,16},{12,20},{16,24},{20,28},{25,1},{... | collective-permute-start | bytes 55304 | tf_op jit(solution)/shard_map/ppermute | solution.py:1265
  8.6 4.7 %collective-permute-start.2 = (bf16[36,256]{1,0:T(8,128)(2,1)S(1)}, bf16[36,256]{1,0:T(8,128)(2,1)S(1)}, u32[]{:S(2)}, u32[]{:S(2)}) collective-permute-start(bf16[36,256]{1,0:T(8,128)(2,1)S(1)} %pad_maximum_fusion.up_own), channel_id=1, source_target_pairs={{16,0},{20,4},{24,8},{28,12},{0,16},{4,20},{8,24},{12,28},{17,1},{... | collective-permute-start | bytes 55304 | tf_op jit(solution)/shard_map/ppermute | solution.py:1265
  11.1 3.8 %collective-permute-start.1 = (bf16[36,256]{1,0:T(8,128)(2,1)S(1)}, bf16[36,256]{1,0:T(8,128)(2,1)S(1)}, u32[]{:S(2)}, u32[]{:S(2)}) collective-permute-start(bf16[36,256]{1,0:T(8,128)(2,1)S(1)} %pad_maximum_fusion.up_own), channel_id=1, source_target_pairs={{8,0},{12,4},{16,8},{20,12},{24,16},{28,20},{0,24},{4,28},{9,1},{1... | collective-permute-start | bytes 55304 | tf_op jit(solution)/shard_map/ppermute | solution.py:1265
  14.9 14.4 %collective-permute-start.12 = (bf16[12,128,256]{2,1,0:T(8,128)(2,1)}, bf16[12,128,256]{2,1,0:T(8,128)(2,1)S(1)}, u32[]{:S(2)}, u32[]{:S(2)}) collective-permute-start(bf16[12,128,256]{2,1,0:T(8,128)(2,1)} %shard_map.246.piece0), channel_id=1, source_target_pairs={{0,1},{1,0},{2,3},{3,2},{4,5},{5,4},{6,7},{7,6},{8,16},{9,17},{10,... | collective-permute-start | bytes 2359304 | tf_op jit(solution)/shard_map/ppermute | solution.py:403
  14.9 20.2 %collective-permute-start.11 = (bf16[12,128,256]{2,1,0:T(8,128)(2,1)}, bf16[12,128,256]{2,1,0:T(8,128)(2,1)S(1)}, u32[]{:S(2)}, u32[]{:S(2)}) collective-permute-start(bf16[12,128,256]{2,1,0:T(8,128)(2,1)} %shard_map.246.piece0), channel_id=1, source_target_pairs={{0,8},{4,12},{8,0},{12,4},{16,24},{20,28},{24,16},{28,20},{1,9},{5... | collective-permute-start | bytes 2359304 | tf_op jit(solution)/shard_map/ppermute | solution.py:403
  16.5 18.6 %collective-permute-start.10 = (bf16[12,128,256]{2,1,0:T(8,128)(2,1)}, bf16[12,128,256]{2,1,0:T(8,128)(2,1)S(1)}, u32[]{:S(2)}, u32[]{:S(2)}) collective-permute-start(bf16[12,128,256]{2,1,0:T(8,128)(2,1)} %shard_map.246.piece0), channel_id=1, source_target_pairs={{0,4},{4,0},{8,12},{12,8},{16,20},{20,16},{24,28},{28,24},{1,5},{5... | collective-permute-start | bytes 2359304 | tf_op jit(solution)/shard_map/ppermute | solution.py:403
  17.2 18.8 %collective-permute-start.7 = (bf16[128,1024]{1,0:T(8,128)(2,1)S(1)}, bf16[128,1024]{1,0:T(8,128)(2,1)S(1)}, u32[]{:S(2)}, u32[]{:S(2)}) collective-permute-start(bf16[128,1024]{1,0:T(8,128)(2,1)S(1)} %bitcast.41), channel_id=1, source_target_pairs={{0,2},{1,3},{2,0},{3,1},{4,6},{5,7},{6,4},{7,5},{8,10},{9,11},{10,... | collective-permute-start | bytes 786440 | tf_op jit(solution)/shard_map/ppermute | solution.py:1271
  36.0 29.4 %copy-start.17 = (bf16[2,1,64,1024]{3,2,1,0:T(8,128)(2,1)S(1)}, bf16[2,1,64,1024]{3,2,1,0:T(8,128)(2,1)}, u32[]{:S(2)}) copy-start(bf16[2,1,64,1024]{3,2,1,0:T(8,128)(2,1)} %param.16) | copy-start | bytes 786436
  36.7 6.3 %collective-permute-start.13 = (bf16[12,128,256]{2,1,0:T(8,128)(2,1)S(1)}, bf16[12,128,256]{2,1,0:T(8,128)(2,1)S(1)}, u32[]{:S(2)}, u32[]{:S(2)}) collective-permute-start(bf16[12,128,256]{2,1,0:T(8,128)(2,1)S(1)} %collective-permute-done.11.piece2), channel_id=1, source_target_pairs={{0,1},{1,0},{2,3},{3,2},{4,5},{5,4},{6,7},{7,6},{8,16},{9,17},{10,... | collective-permute-start | bytes 2359304 | tf_op jit(solution)/shard_map/ppermute | solution.py:403
  36.7 20.9 %collective-permute-start.14 = (bf16[12,128,256]{2,1,0:T(8,128)(2,1)S(1)}, bf16[12,128,256]{2,1,0:T(8,128)(2,1)S(1)}, u32[]{:S(2)}, u32[]{:S(2)}) collective-permute-start(bf16[12,128,256]{2,1,0:T(8,128)(2,1)S(1)} %get-tuple-element.61), channel_id=1, source_target_pairs={{0,8},{4,12},{8,0},{12,4},{16,24},{20,28},{24,16},{28,20},{1,9},{5... | collective-permute-start | bytes 2359304 | tf_op jit(solution)/shard_map/ppermute | solution.py:403
  40.8 24.6 %collective-permute-start.4 = (bf16[528,1024]{1,0:T(8,128)(2,1)S(1)}, bf16[528,1024]{1,0:T(8,128)(2,1)S(1)}, u32[]{:S(2)}, u32[]{:S(2)}) collective-permute-start(bf16[528,1024]{1,0:T(8,128)(2,1)S(1)} %copy-done.11), channel_id=1, source_target_pairs={{0,2},{1,3},{2,0},{3,1},{4,6},{5,7},{6,4},{7,5},{8,10},{9,11},{10,... | collective-permute-start | bytes 3244040 | tf_op jit(solution)/shard_map/ppermute | solution.py:1303
  42.3 36.1 %copy-start.32 = (bf16[128,1024]{1,0:T(8,128)(2,1)S(1)}, bf16[128,1024]{1,0:T(8,128)(2,1)}, u32[]{:S(2)}) copy-start(bf16[128,1024]{1,0:T(8,128)(2,1)} %copy-done.31) | copy-start | bytes 786436
  42.3 19.4 %collective-permute-start.15 = (bf16[12,128,256]{2,1,0:T(8,128)(2,1)S(1)}, bf16[12,128,256]{2,1,0:T(8,128)(2,1)S(1)}, u32[]{:S(2)}, u32[]{:S(2)}) collective-permute-start(bf16[12,128,256]{2,1,0:T(8,128)(2,1)S(1)} %get-tuple-element.117), channel_id=1, source_target_pairs={{0,4},{4,0},{8,12},{12,8},{16,20},{20,16},{24,28},{28,24},{1,5},{5... | collective-permute-start | bytes 2359304 | tf_op jit(solution)/shard_map/ppermute | solution.py:403
  43.0 34.2 %copy-start.1 = (bf16[12,128,256]{2,1,0:T(8,128)(2,1)}, bf16[12,128,256]{2,1,0:T(8,128)(2,1)S(1)}, u32[]{:S(2)}) copy-start(bf16[12,128,256]{2,1,0:T(8,128)(2,1)S(1)} %collective-permute-done.13.piece4) | copy-start | bytes 2359300
  57.7 19.4 %collective-permute-start.17 = (bf16[12,128,256]{2,1,0:T(8,128)(2,1)S(1)}, bf16[12,128,256]{2,1,0:T(8,128)(2,1)S(1)}, u32[]{:S(2)}, u32[]{:S(2)}) collective-permute-start(bf16[12,128,256]{2,1,0:T(8,128)(2,1)S(1)} %broadcast_select_fusion), channel_id=1, source_target_pairs={{0,4},{4,0},{8,12},{12,8},{16,20},{20,16},{24,28},{28,24},{1,5},{5... | collective-permute-start | bytes 2359304 | tf_op jit(solution)/shard_map/ppermute | solution.py:403
  61.7 26.9 %copy-start.18 = (bf16[12,128,256]{2,1,0:T(8,128)(2,1)}, bf16[12,128,256]{2,1,0:T(8,128)(2,1)S(1)}, u32[]{:S(2)}) copy-start(bf16[12,128,256]{2,1,0:T(8,128)(2,1)S(1)} %collective-permute-done.15.piece7) | copy-start | bytes 2359300
  61.7 15.9 %collective-permute-start.16 = (bf16[12,128,256]{2,1,0:T(8,128)(2,1)S(1)}, bf16[12,128,256]{2,1,0:T(8,128)(2,1)S(1)}, u32[]{:S(2)}, u32[]{:S(2)}) collective-permute-start(bf16[12,128,256]{2,1,0:T(8,128)(2,1)S(1)} %collective-permute-done.13.piece4), channel_id=1, source_target_pairs={{0,8},{4,12},{8,0},{12,4},{16,24},{20,28},{24,16},{28,20},{1,9},{5... | collective-permute-start | bytes 2359304 | tf_op jit(solution)/shard_map/ppermute | solution.py:403
  61.7 18.3 %collective-permute-start.5 = (bf16[528,1024]{1,0:T(8,128)(2,1)S(1)}, bf16[528,1024]{1,0:T(8,128)(2,1)S(1)}, u32[]{:S(2)}, u32[]{:S(2)}) collective-permute-start(bf16[528,1024]{1,0:T(8,128)(2,1)S(1)} %copy-done.11), channel_id=1, source_target_pairs={{0,1},{1,0},{2,3},{3,2},{4,5},{5,4},{6,7},{7,6},{8,9},{9,8},{10,11... | collective-permute-start | bytes 3244040 | tf_op jit(solution)/shard_map/ppermute | solution.py:1304
  65.4 14.6 %collective-permute-start.6 = (bf16[528,1024]{1,0:T(8,128)(2,1)S(1)}, bf16[528,1024]{1,0:T(8,128)(2,1)S(1)}, u32[]{:S(2)}, u32[]{:S(2)}) collective-permute-start(bf16[528,1024]{1,0:T(8,128)(2,1)S(1)} %collective-permute-done.4.packet1), channel_id=1, source_target_pairs={{0,1},{1,0},{2,3},{3,2},{4,5},{5,4},{6,7},{7,6},{8,9},{9,8},{10,11... | collective-permute-start | bytes 3244040 | tf_op jit(solution)/shard_map/ppermute | solution.py:1305
  65.4 13.0 %collective-permute-start.8 = (bf16[128,1024]{1,0:T(8,128)(2,1)S(1)}, bf16[128,1024]{1,0:T(8,128)(2,1)S(1)}, u32[]{:S(2)}, u32[]{:S(2)}) collective-permute-start(bf16[128,1024]{1,0:T(8,128)(2,1)S(1)} %bitcast.42), channel_id=1, source_target_pairs={{0,1},{1,0},{2,3},{3,2},{4,5},{5,4},{6,7},{7,6},{8,9},{9,8},{10,11... | collective-permute-start | bytes 786440 | tf_op jit(solution)/shard_map/ppermute | solution.py:1275
  77.2 11.3 %collective-permute-start.18 = (bf16[7,128,256]{2,1,0:T(8,128)(2,1)S(1)}, bf16[7,128,256]{2,1,0:T(8,128)(2,1)}, u32[]{:S(2)}, u32[]{:S(2)}) collective-permute-start(bf16[7,128,256]{2,1,0:T(8,128)(2,1)S(1)} %slice.32), channel_id=1, source_target_pairs={{0,8},{4,12},{8,0},{12,4},{16,24},{20,28},{24,16},{28,20},{1,9},{5... | collective-permute-start | bytes 1376264 | tf_op jit(solution)/shard_map/ppermute | solution.py:403
  77.6 8.2 %collective-permute-start.19 = (bf16[5,128,256]{2,1,0:T(8,128)(2,1)S(1)}, bf16[5,128,256]{2,1,0:T(8,128)(2,1)S(1)}, u32[]{:S(2)}, u32[]{:S(2)}) collective-permute-start(bf16[5,128,256]{2,1,0:T(8,128)(2,1)S(1)} %slice.33), channel_id=1, source_target_pairs={{0,4},{4,0},{8,12},{12,8},{16,20},{20,16},{24,28},{28,24},{1,5},{5... | collective-permute-start | bytes 983048 | tf_op jit(solution)/shard_map/ppermute | solution.py:403
  78.4 1.6 collective-permute-start.9
  115.6 13.8 %collective-permute-start.20 = (bf16[2,5,128,1024]{3,2,1,0:T(8,128)(2,1)}, bf16[2,5,128,1024]{3,2,1,0:T(8,128)(2,1)S(1)}, u32[]{:S(2)}, u32[]{:S(2)}) collective-permute-start(bf16[2,5,128,1024]{3,2,1,0:T(8,128)(2,1)} %get-tuple-element.65), channel_id=1, source_target_pairs={{0,1},{1,0},{2,3},{3,2},{4,5},{5,4},{6,7},{7,6},{8,9},{9,8},{10,11... | collective-permute-start | bytes 7864328 | tf_op jit(solution)/shard_map/ppermute | solution.py:1343
  115.6 10.3 %collective-permute-start.27 = (bf16[5,128,256]{2,1,0:T(8,128)(2,1)}, bf16[5,128,256]{2,1,0:T(8,128)(2,1)S(1)}, u32[]{:S(2)}, u32[]{:S(2)}) collective-permute-start(bf16[5,128,256]{2,1,0:T(8,128)(2,1)} %get-tuple-element.75), channel_id=1, source_target_pairs={{0,4},{4,0},{8,12},{12,8},{16,20},{20,16},{24,28},{28,24},{1,5},{5... | collective-permute-start | bytes 983048 | tf_op jit(solution)/shard_map/ppermute | solution.py:403
  116.4 12.8 %collective-permute-start.23 = (bf16[7,128,256]{2,1,0:T(8,128)(2,1)}, bf16[7,128,256]{2,1,0:T(8,128)(2,1)S(1)}, u32[]{:S(2)}, u32[]{:S(2)}) collective-permute-start(bf16[7,128,256]{2,1,0:T(8,128)(2,1)} %get-tuple-element.74), channel_id=1, source_target_pairs={{0,8},{4,12},{8,0},{12,4},{16,24},{20,28},{24,16},{28,20},{1,9},{5... | collective-permute-start | bytes 1376264 | tf_op jit(solution)/shard_map/ppermute | solution.py:403
  127.2 19.2 %collective-permute-start.28 = (bf16[12,128,256]{2,1,0:T(8,128)(2,1)S(1)}, bf16[12,128,256]{2,1,0:T(8,128)(2,1)S(1)}, u32[]{:S(2)}, u32[]{:S(2)}) collective-permute-start(bf16[12,128,256]{2,1,0:T(8,128)(2,1)S(1)} %fusion.7), channel_id=1, source_target_pairs={{0,8},{4,12},{8,0},{12,4},{16,24},{20,28},{24,16},{28,20},{1,9},{5... | collective-permute-start | bytes 2359304 | tf_op jit(solution)/shard_map/ppermute | solution.py:403
  132.8 20.7 %copy-start.27 = (bf16[7,128,256]{2,1,0:T(8,128)(2,1)S(1)}, bf16[7,128,256]{2,1,0:T(8,128)(2,1)}, u32[]{:S(2)}) copy-start(bf16[7,128,256]{2,1,0:T(8,128)(2,1)} %get-tuple-element.74) | copy-start | bytes 1376260
  133.0 20.6 %collective-permute-start.24 = (bf16[12,128,256]{2,1,0:T(8,128)(2,1)S(1)}, bf16[12,128,256]{2,1,0:T(8,128)(2,1)S(1)}, u32[]{:S(2)}, u32[]{:S(2)}) collective-permute-start(bf16[12,128,256]{2,1,0:T(8,128)(2,1)S(1)} %add_convert_fusion.2), channel_id=1, source_target_pairs={{0,4},{4,0},{8,12},{12,8},{16,20},{20,16},{24,28},{28,24},{1,5},{5... | collective-permute-start | bytes 2359304 | tf_op jit(solution)/shard_map/ppermute | solution.py:403
  134.6 24.1 %collective-permute-start.21 = (bf16[4,128,1024]{2,1,0:T(8,128)(2,1)}, bf16[4,128,1024]{2,1,0:T(8,128)(2,1)S(1)}, u32[]{:S(2)}, u32[]{:S(2)}) collective-permute-start(bf16[4,128,1024]{2,1,0:T(8,128)(2,1)} %fusion.10), channel_id=1, source_target_pairs={{0,2},{1,3},{2,0},{3,1},{4,6},{5,7},{6,4},{7,5},{8,10},{9,11},{10,... | collective-permute-start | bytes 3145736 | tf_op jit(solution)/shard_map/ppermute | solution.py:1345
  134.6 38.0 %collective-permute-start.30 = (bf16[12,128,256]{2,1,0:T(8,128)(2,1)S(1)}, bf16[12,128,256]{2,1,0:T(8,128)(2,1)}, u32[]{:S(2)}, u32[]{:S(2)}) collective-permute-start(bf16[12,128,256]{2,1,0:T(8,128)(2,1)S(1)} %copy-done.43), channel_id=1, source_target_pairs={{0,4},{4,0},{8,12},{12,8},{16,20},{20,16},{24,28},{28,24},{1,5},{5... | collective-permute-start | bytes 2359304 | tf_op jit(solution)/shard_map/ppermute | solution.py:403
  155.4 17.2 %collective-permute-start.25 = (bf16[12,128,256]{2,1,0:T(8,128)(2,1)}, bf16[12,128,256]{2,1,0:T(8,128)(2,1)}, u32[]{:S(2)}, u32[]{:S(2)}) collective-permute-start(bf16[12,128,256]{2,1,0:T(8,128)(2,1)} %get-tuple-element.115), channel_id=1, source_target_pairs={{0,8},{4,12},{8,0},{12,4},{16,24},{20,28},{24,16},{28,20},{1,9},{5... | collective-permute-start | bytes 2359304 | tf_op jit(solution)/shard_map/ppermute | solution.py:403
  155.7 17.0 %collective-permute-start.29 = (bf16[12,128,256]{2,1,0:T(8,128)(2,1)}, bf16[12,128,256]{2,1,0:T(8,128)(2,1)}, u32[]{:S(2)}, u32[]{:S(2)}) collective-permute-start(bf16[12,128,256]{2,1,0:T(8,128)(2,1)} %get-tuple-element.116), channel_id=1, source_target_pairs={{0,1},{1,0},{2,3},{3,2},{4,5},{5,4},{6,7},{7,6},{8,16},{9,17},{10,... | collective-permute-start | bytes 2359304 | tf_op jit(solution)/shard_map/ppermute | solution.py:403
  175.3 17.5 %collective-permute-start.26 = (bf16[12,128,256]{2,1,0:T(8,128)(2,1)S(1)}, bf16[12,128,256]{2,1,0:T(8,128)(2,1)S(1)}, u32[]{:S(2)}, u32[]{:S(2)}) collective-permute-start(bf16[12,128,256]{2,1,0:T(8,128)(2,1)S(1)} %get-tuple-element.112), channel_id=1, source_target_pairs={{0,4},{4,0},{8,12},{12,8},{16,20},{20,16},{24,28},{28,24},{1,5},{5... | collective-permute-start | bytes 2359304 | tf_op jit(solution)/shard_map/ppermute | solution.py:403
  176.1 17.5 %collective-permute-start.31 = (bf16[12,128,256]{2,1,0:T(8,128)(2,1)S(1)}, bf16[12,128,256]{2,1,0:T(8,128)(2,1)S(1)}, u32[]{:S(2)}, u32[]{:S(2)}) collective-permute-start(bf16[12,128,256]{2,1,0:T(8,128)(2,1)S(1)} %get-tuple-element.84), channel_id=1, source_target_pairs={{0,8},{4,12},{8,0},{12,4},{16,24},{20,28},{24,16},{28,20},{1,9},{5... | collective-permute-start | bytes 2359304 | tf_op jit(solution)/shard_map/ppermute | solution.py:403
  177.4 16.2 %collective-permute-start.32 = (bf16[12,128,256]{2,1,0:T(8,128)(2,1)S(1)}, bf16[12,128,256]{2,1,0:T(8,128)(2,1)S(1)}, u32[]{:S(2)}, u32[]{:S(2)}) collective-permute-start(bf16[12,128,256]{2,1,0:T(8,128)(2,1)S(1)} %get-tuple-element.85), channel_id=1, source_target_pairs={{0,1},{1,0},{2,3},{3,2},{4,5},{5,4},{6,7},{7,6},{8,16},{9,17},{10,... | collective-permute-start | bytes 2359304 | tf_op jit(solution)/shard_map/ppermute | solution.py:403
  177.4 2.4 %collective-permute-start.33 = (f32[24,1152]{1,0:T(8,128)S(1)}, f32[24,1152]{1,0:T(8,128)S(1)}, u32[]{:S(2)}, u32[]{:S(2)}) collective-permute-start(f32[24,1152]{1,0:T(8,128)S(1)} %copy-done.44), channel_id=1, source_target_pairs={{0,1},{1,0},{2,3},{3,2},{4,5},{5,4},{6,7},{7,6},{8,9},{9,8},{10,11... | collective-permute-start | bytes 331784 | tf_op jit(solution)/shard_map/ppermute | solution.py:1411
  179.9 5.6 %collective-permute-start.34 = (f32[24,1152]{1,0:T(8,128)S(1)}, f32[24,1152]{1,0:T(8,128)S(1)}, u32[]{:S(2)}, u32[]{:S(2)}) collective-permute-start(f32[24,1152]{1,0:T(8,128)S(1)} %add.95), channel_id=1, source_target_pairs={{0,2},{1,3},{2,0},{3,1},{4,6},{5,7},{6,4},{7,5},{8,10},{9,11},{10,... | collective-permute-start | bytes 331784 | tf_op jit(solution)/shard_map/ppermute | solution.py:1412
  182.1 12.0 %collective-permute-start.22 = (bf16[128,1024]{1,0:T(8,128)(2,1)S(1)}, bf16[128,1024]{1,0:T(8,128)(2,1)S(1)}, u32[]{:S(2)}, u32[]{:S(2)}) collective-permute-start(bf16[128,1024]{1,0:T(8,128)(2,1)S(1)} %fusion.13), channel_id=1, source_target_pairs={{0,2},{1,3},{2,0},{3,1},{4,6},{5,7},{6,4},{7,5},{8,10},{9,11},{10,... | collective-permute-start | bytes 786440 | tf_op jit(solution)/shard_map/ppermute | solution.py:1347
  194.1 20.9 %copy-start.6 = (bf16[12,128,256]{2,1,0:T(8,128)(2,1)}, bf16[12,128,256]{2,1,0:T(8,128)(2,1)S(1)}, u32[]{:S(2)}) copy-start(bf16[12,128,256]{2,1,0:T(8,128)(2,1)S(1)} %add_convert_fusion.1.shard0) | copy-start | bytes 2359300
  194.1 17.3 %collective-permute-start.35 = (bf16[12,128,256]{2,1,0:T(8,128)(2,1)S(1)}, bf16[12,128,256]{2,1,0:T(8,128)(2,1)S(1)}, u32[]{:S(2)}, u32[]{:S(2)}) collective-permute-start(bf16[12,128,256]{2,1,0:T(8,128)(2,1)S(1)} %add_convert_fusion.1.shard0), channel_id=1, source_target_pairs={{0,2},{1,3},{2,0},{3,1},{4,6},{5,7},{6,4},{7,5},{8,10},{9,11},{10,... | collective-permute-start | bytes 2359304 | tf_op jit(solution)/shard_map/ppermute | solution.py:1414
  194.7 4.7 %collective-permute-start.37 = (f32[24,1152]{1,0:T(8,128)S(1)}, f32[24,1152]{1,0:T(8,128)S(1)}, u32[]{:S(2)}, u32[]{:S(2)}) collective-permute-start(f32[24,1152]{1,0:T(8,128)S(1)} %add.96), channel_id=1, source_target_pairs={{0,4},{4,0},{8,12},{12,8},{16,20},{20,16},{24,28},{28,24},{1,5},{5... | collective-permute-start | bytes 331784 | tf_op jit(solution)/shard_map/ppermute | solution.py:1417
  199.4 6.1 %collective-permute-start.38 = (f32[24,1152]{1,0:T(8,128)S(1)}, f32[24,1152]{1,0:T(8,128)S(1)}, u32[]{:S(2)}, u32[]{:S(2)}) collective-permute-start(f32[24,1152]{1,0:T(8,128)S(1)} %add.97), channel_id=1, source_target_pairs={{0,8},{4,12},{8,0},{12,4},{16,24},{20,28},{24,16},{28,20},{1,9},{5... | collective-permute-start | bytes 331784 | tf_op jit(solution)/shard_map/ppermute | solution.py:1417
  205.6 5.7 %collective-permute-start.39 = (f32[24,1152]{1,0:T(8,128)S(1)}, f32[24,1152]{1,0:T(8,128)S(1)}, u32[]{:S(2)}, u32[]{:S(2)}) collective-permute-start(f32[24,1152]{1,0:T(8,128)S(1)} %add.98), channel_id=1, source_target_pairs={{0,16},{4,20},{8,24},{12,28},{16,0},{20,4},{24,8},{28,12},{1,17},{... | collective-permute-start | bytes 331784 | tf_op jit(solution)/shard_map/ppermute | solution.py:1417
  211.3 3.6 %collective-permute-start.36 = (bf16[12,128,256]{2,1,0:T(8,128)(2,1)S(1)}, bf16[12,128,256]{2,1,0:T(8,128)(2,1)S(1)}, u32[]{:S(2)}, u32[]{:S(2)}) collective-permute-start(bf16[12,128,256]{2,1,0:T(8,128)(2,1)S(1)} %add_convert_fusion.1.shard0), channel_id=1, source_target_pairs={{0,1},{1,0},{2,3},{3,2},{4,5},{5,4},{6,7},{7,6},{8,9},{9,8},{10,11... | collective-permute-start | bytes 2359304 | tf_op jit(solution)/shard_map/ppermute | solution.py:1415
  211.4 3.5 %collective-permute-start.40 = (bf16[12,128,256]{2,1,0:T(8,128)(2,1)S(1)}, bf16[12,128,256]{2,1,0:T(8,128)(2,1)S(1)}, u32[]{:S(2)}, u32[]{:S(2)}) collective-permute-start(bf16[12,128,256]{2,1,0:T(8,128)(2,1)S(1)} %collective-permute-done.35.shard1), channel_id=1, source_target_pairs={{0,1},{1,0},{2,3},{3,2},{4,5},{5,4},{6,7},{7,6},{8,9},{9,8},{10,11... | collective-permute-start | bytes 2359304 | tf_op jit(solution)/shard_map/ppermute | solution.py:1419
  211.9 3.1 %collective-permute-start.41 = (f32[24,1152]{1,0:T(8,128)S(1)}, f32[24,1152]{1,0:T(8,128)S(1)}, u32[]{:S(2)}, u32[]{:S(2)}) collective-permute-start(f32[24,1152]{1,0:T(8,128)S(1)} %add.99.small_own), channel_id=1, source_target_pairs={{0,1},{1,0},{2,3},{3,2},{4,5},{5,4},{6,7},{7,6},{8,9},{9,8},{10,11... | collective-permute-start | bytes 331784 | tf_op jit(solution)/shard_map/ppermute | solution.py:1418
  (41 other events, 370.6 us)

commit v4 on v3

--- a/solution.py
+++ b/solution.py
@@ -474,12 +474,12 @@
     def only(cond, value):
         return jnp.where(cond, wide(value), 0.0)
 
-    over_y = fsdp_move(side_high, Y_SWAP)
-    over_z = fsdp_move(side_low, Z_NEAR)
-    over_z = jnp.pad(only(inner, over_z), ((0, 12 - PART), (0, 0), (0, 0)))
-    back_one = fsdp_move(low(wide(after(side_one, first_wait)) + over_z), Y_SWAP)
-    over_y = jnp.pad(wide(over_y), ((PART, 0), (0, 0), (0, 0)))
-    back_far = fsdp_move(low(wide(last) + over_y), Z_NEAR)
+    over_z = fsdp_move(side_high, Z_NEAR)
+    over_y = fsdp_move(side_low, Y_SWAP)
+    over_z = jnp.pad(only(inner, over_z), ((PART, 0), (0, 0), (0, 0)))
+    back_one = fsdp_move(low(wide(side_one) + over_z), Y_SWAP)
+    over_y = jnp.pad(wide(over_y), ((0, 12 - PART), (0, 0), (0, 0)))
+    back_far = fsdp_move(low(wide(after(last, first_wait)) + over_y), Z_NEAR)
     back_two = fsdp_move(after(side_two, first_wait), Y_SWAP)
     to_middle = low(wide(last) + wide(back_one) + wide(back_far))
     to_near = low(
@@ -668,14 +668,17 @@
     chunk5,
     chunk6,
     chunk7,
-    keep,
-    send,
+    keep_own,
+    keep_far,
+    send_norm,
+    keep_out,
+    send_out,
     acts,
     marks,
     up_all,
     lin_all,
-    rhs_all,
-    spare,
+    down_all,
+    out_rows,
     lhs_all,
     grad_pre,
     linear,
@@ -722,32 +725,17 @@
     def piece_copies(index, ref, tail_ref):
         rows = member_rows[index]
         down = 7 if tail_ref is ref else 0
-        found = [
+        return [
             pltpu.make_async_copy(
                 ref.at[pl.ds(4, 3)], lin_all.at[:, rows], piece_sems.at[index, 0]
-            )
+            ),
+            pltpu.make_async_copy(
+                tail_ref.at[pl.ds(down, 5)], down_all.at[origin[index]], piece_sems.at[index, 1]
+            ),
+            pltpu.make_async_copy(
+                ref.at[pl.ds(0, 4)], up_all.at[:, rows], piece_sems.at[index, 2]
+            ),
         ]
-        for block in range(4):
-            cols = pl.ds(block * 256, 256)
-            found.append(
-                pltpu.make_async_copy(
-                    tail_ref.at[down + block], rhs_all.at[rows, cols], piece_sems.at[index, 1 + block]
-                )
-            )
-        found.append(
-            pltpu.make_async_copy(
-                tail_ref.at[down + 4], spare.at[origin[index]], piece_sems.at[index, 5]
-            )
-        )
-        for block in range(4):
-            found.append(
-                pltpu.make_async_copy(
-                    ref.at[block],
-                    up_all.at[rows, pl.ds(block * 256, 256)],
-                    piece_sems.at[index, 6 + block],
-                )
-            )
-        return found
 
     first = unit_copies(0) + unit_copies(1) + unit_copies(2)
     second = [
@@ -770,8 +758,8 @@
     for index, (for_inner, for_ends) in enumerate(sources):
         copies = piece_copies(index, for_inner, for_inner)
         first.append(copies[0])
-        second += copies[1:6]
-        third += copies[6:]
+        second.append(copies[1])
+        third.append(copies[2])
         if for_inner is for_ends:
             for copy in copies:
                 copy.start()
@@ -801,17 +789,14 @@
     for pair in range(4):
         even = 2 * pair + core
         odd = 2 * pair + 1 - core
-        tail = pl.ds(pl.multiple_of(even * 128 + 96, 32), 32)
-        first_rows = slice(WIDTH + pair * 64, WIDTH + pair * 64 + 32)
-        last_rows = slice(WIDTH + pair * 64 + 32, WIDTH + pair * 64 + 64)
         for block in range(4):
             band = slice(block * 32, block * 32 + 32)
             cols = slice(block * 256, block * 256 + 256)
-            rhs_all[first_rows, cols] = rhs_all[tail, cols]
-            rhs_all[last_rows, cols] = spare[even, band]
-            rhs_all[tail, cols] = spare[odd, band]
-
-    grad_att[...] = back_product(acts[4], rhs_all[WIDTH:, :]).astype(jnp.bfloat16)
+            out_rows[pair * 64 : pair * 64 + 32, cols] = down_all[even, block, 96:128]
+            out_rows[pair * 64 + 32 : pair * 64 + 64, cols] = down_all[even, 4, band]
+            down_all[even, block, 96:128] = down_all[odd, 4, band]
+
+    grad_att[...] = back_product(acts[4], out_rows[...]).astype(jnp.bfloat16)
     cos_table = rope[0]
     sin_left = rope[1]
     sin_right = rope[2]
@@ -893,11 +878,17 @@
 
     def hidden(pair, carry):
         cols = pl.ds(pl.multiple_of(pair * 256, 256), 256)
-        up_pre = matmul(acts[3], up_all[:, cols])
+        up_pre = matmul(acts[3], up_all[pair])
         bell = 0.5 * (1.0 + lax.erf(up_pre * ROOT_HALF))
         slope = bell + up_pre * NORMAL_PEAK * jnp.exp(-0.5 * up_pre * up_pre)
         lhs_all[:, cols] = (up_pre * bell).astype(jnp.bfloat16)
-        grad_gated = back_product(acts[4], rhs_all[cols, :])
+        rows_down = jnp.concatenate(
+            [
+                jnp.concatenate([down_all[2 * pair + half, block] for block in range(4)], axis=1)
+                for half in range(2)
+            ]
+        )
+        grad_gated = back_product(acts[4], rows_down)
         grad_pre[:, cols] = (grad_gated * slope).astype(jnp.bfloat16)
         return carry
 
@@ -958,10 +949,16 @@
                 tokens[half, block, unit, :, cols] = low[at : at + ROWS]
 
     def ship(unit):
-        for half, ref in enumerate((keep, send)):
-            copy = pltpu.make_async_copy(
-                tokens.at[half, :, unit], ref.at[:, unit], token_sems.at[half, unit]
+        if unit < 4:
+            routes = (
+                (tokens.at[0, 0, unit], keep_own.at[unit]),
+                (tokens.at[0, 1, unit], keep_far.at[unit]),
+                (tokens.at[1, :, unit], send_norm.at[:, unit]),
             )
+        else:
+            routes = ((tokens.at[0, :, unit], keep_out), (tokens.at[1, :, unit], send_out))
+        for place, (source, goal) in enumerate(routes):
+            copy = pltpu.make_async_copy(source, goal, token_sems.at[place, unit])
             copy.start()
             sent.append(copy)
 
@@ -971,8 +968,10 @@
 
     def feed(block, carry):
         cols = pl.ds(pl.multiple_of(block * 256, 256), 256)
-        put(3, cols, back_product(grad_pre[...], up_all[cols, :]))
-        put(4, cols, matmul(lhs_all[...], rhs_all[:, cols]))
+        rows_up = jnp.concatenate([up_all[part, cols] for part in range(4)], axis=1)
+        put(3, cols, back_product(grad_pre[...], rows_up))
+        right = [down_all[index, block] for index in range(8)] + [out_rows[:, cols]]
+        put(4, cols, matmul(lhs_all[...], jnp.concatenate(right)))
         return carry
 
     lax.fori_loop(0, 4, feed, 0)
@@ -1012,7 +1011,7 @@
         span = pl.ds(row, 16)
 
         def result(index):
-            return wide(keep[0, index, span]) + wide(came[0, index, span]) + wide(across[index, span])
+            return wide(keep[index, span]) + wide(came[0, index, span]) + wide(across[index, span])
 
         for stream in range(4):
             item = result(stream)
@@ -1314,17 +1313,19 @@
         main_kernel,
         (shape_of((PART, 128, 256)), shape_of((12 - PART, 128, 256)))
         + (shape_of((12, 128, 256)),) * 7
-        + (shape_of((2, 5, ROWS, width)),) * 2,
+        + (shape_of((4, ROWS, width)),) * 2
+        + (shape_of((2, 4, ROWS, width)),)
+        + (shape_of((2, ROWS, width)),) * 2,
         [VMEM_FULL] + [IN_PLACE] * 19,
-        (IN_PLACE,) * 11,
+        (IN_PLACE,) * 14,
         (jnp.asarray(rope_tables()),) + packets + grad_packets + tuple(pieces),
         scratch=[
             pltpu.VMEM((5, 4 * ROWS, width), jnp.bfloat16),
             pltpu.VMEM((4, 16, width), jnp.bfloat16),
-            pltpu.VMEM((width, width), jnp.bfloat16),
+            pltpu.VMEM((4, width, 256), jnp.bfloat16),
             pltpu.VMEM((3, width, 256), jnp.bfloat16),
-            pltpu.VMEM((width + 256, width), jnp.bfloat16),
-            pltpu.VMEM((8, 128, 256), jnp.bfloat16),
+            pltpu.VMEM((8, 5, 128, 256), jnp.bfloat16),
+            pltpu.VMEM((256, width), jnp.bfloat16),
             pltpu.VMEM((4 * ROWS, width + 256), jnp.bfloat16),
             pltpu.VMEM((4 * ROWS, width), jnp.bfloat16),
             pltpu.VMEM((3, 4 * ROWS, 256), jnp.float32),
@@ -1333,20 +1334,22 @@
             pltpu.VMEM((8, 12, 128, 256), jnp.bfloat16),
             pltpu.VMEM((2, 2, 5, ROWS, width), jnp.bfloat16),
             pltpu.SemaphoreType.DMA((4, 6)),
-            pltpu.SemaphoreType.DMA((8, 10)),
+            pltpu.SemaphoreType.DMA((8, 3)),
             pltpu.SemaphoreType.DMA((9,)),
-            pltpu.SemaphoreType.DMA((2, 5)),
+            pltpu.SemaphoreType.DMA((3, 5)),
         ],
     )
-    chunks, keep, send = results[:9], results[9], results[10]
-
-    came = lax.ppermute(send, "replica", CORE_SWAP)
-    sum_across = (wide(keep[1, :4]) + wide(came[1, :4])).astype(jnp.bfloat16)
+    chunks = results[:9]
+    keep_own, keep_far, send_norm, keep_out, send_out = results[9:]
+
+    came = lax.ppermute(send_norm, "replica", CORE_SWAP)
+    sum_across = (wide(keep_far) + wide(came[1])).astype(jnp.bfloat16)
     came_across = lax.ppermute(sum_across, "replica", X_SWAP)
-    out_across = (wide(keep[1, 4]) + wide(came[1, 4])).astype(jnp.bfloat16)
+    out_came = lax.ppermute(after(send_out, sum_across), "replica", CORE_SWAP)
+    out_across = (wide(keep_out[1]) + wide(out_came[1])).astype(jnp.bfloat16)
     out_across = lax.ppermute(after(out_across, came_across), "replica", X_SWAP)
     layer_output = (
-        stream_last + wide(keep[0, 4]) + wide(came[0, 4]) + wide(out_across)
+        stream_last + wide(keep_out[0]) + wide(out_came[0]) + wide(out_across)
     ).astype(jnp.bfloat16)
 
     first_half = pl.BlockSpec((1, 4, ROWS, width), lambda step: (0, 0, 0, 0))
@@ -1369,7 +1372,7 @@
                 whole((ROWS, width)),
                 whole((4, ROWS, width)),
                 whole((3, ROWS, 128)),
-                first_half,
+                whole((4, ROWS, width)),
                 first_half,
                 whole((4, ROWS, width)),
                 whole((1, width)),
@@ -1395,7 +1398,7 @@
             cotangent,
             scaled,
             stats,
-            keep,
+            keep_own,
             came,
             came_across,
             gain_row,

time: 223 us -> 218 us (0.978)
  other arithmetic: 13.7 us -> 9.04 us
    ppermute x20, waiting for transfers between devices: 79.9 us -> 75.3 us  [fsdp_move(): lax.ppermute(value, 'fsdp' if len(pairs) == 8 else ('fsdp', 'replica'), p...]
    convert_element_type x3, other arithmetic: 6.47 us -> 2.32 us  [the longest x1 1.4 us: on_device_tensor(): sum_across = (wide(keep_far) + wide(came[1])).astype(jnp.bfloat16)]
    unnamed x94 -> x96, local copies, waits for them, and re-layouts: 5.32 us -> 5.88 us
  transfers between devices with their start and end apart: 42 -> 43, of which waited for: 24 -> 23; matrix products, arithmetic and copies ran while one was open for 5% -> 4% of each run, Pallas kernels for 11% -> 12%
where the time goes in v4:
time: 218 us; the launch traced here: 217 us
  waiting for transfers between devices  106 us (49%)
  Pallas kernels  56.8 us (26%)
  starting transfers between devices  37.4 us (17%)
  other arithmetic  9.04 us (4%)
  local copies, waits for them, and re-layouts  6.53 us (3%)
    ppermute x20, waiting for transfers between devices, fsdp_move(): lax.ppermute(value, 'fsdp' if len(pairs) == 8 else ('fsdp', 'replica'), p...  75.3 us
    pallas_call x4, Pallas kernels, call(): pl.pallas_call(kernel, out_shape=outs, in_specs=specs, out_specs=out_spec...  43.7 us
    ppermute x20, starting transfers between devices, fsdp_move(): lax.ppermute(value, 'fsdp' if len(pairs) == 8 else ('fsdp', 'replica'), p...  15.7 us
    pallas_call x1, Pallas kernels, back(): pl.pallas_call(back_kernel, grid=(1,), out_shape=(shape_of((seqs, STREAMS...  13.1 us
    ppermute x3, waiting for transfers between devices, on_device_tensor(): small = small + lax.ppermute(small, 'fsdp', perm)  11.1 us
    unnamed x96, local copies, waits for them, and re-layouts  5.88 us
    convert_element_type x5, other arithmetic, low(): return value.astype(jnp.bfloat16)  5.74 us
    ppermute x3, starting transfers between devices, on_device_tensor(): lax.ppermute(up_pair, 'fsdp', z_pairs([((step + to) % 4, to) for to in ra...  5.57 us
  transfers between devices with their start and end apart: 43, of which 23 were waited for; matrix products, arithmetic and copies ran while one was open for 4% of the time, Pallas kernels for 12%

profile of v4, /device:TPU:0, one launch (start us, length us, event | category | flops | bytes accessed | tf_op | source)
XLA Modules:
  0.0 217.3 jit_solution(9375260958668121548)
XLA Ops:
  0.7 3.0 %collective-permute-start = (bf16[36,128]{1,0:T(8,128)(2,1)}, bf16[36,128]{1,0:T(8,128)(2,1)S(1)}, u32[]{:S(2)}, u32[]{:S(2)}) collective-permute-start(bf16[36,128]{1,0:T(8,128)(2,1)} %bitcast.49), channel_id=1, source_target_pairs={{0,4},{4,0},{8,12},{12,8},{16,20},{20,16},{24,28},{28,24},{1,5},{5... | collective-permute-start | bytes 27656 | tf_op jit(solution)/shard_map/ppermute | solution.py:1262
  3.7 3.2 %shard_map.246.piece0 = bf16[12,128,256]{2,1,0:T(8,128)(2,1)} custom-call(bf16[3,128,1024]{2,1,0:T(8,128)(2,1)} %projection.1, bf16[128,1024]{1,0:T(8,128)(2,1)} %out_weight.1, bf16[128,4096]{1,0:T(8,128)(2,1)} %up_weight.1, bf16[512,1024]{1,0:T(8,128)(2,1)} %down_weight.1), custom_call_target="tpu_custom_call" | custom-call | tf_op jit(solution)/shard_map/pallas_call | solution.py:1202
  7.0 1.6 collective-permute-start.3
  8.6 2.6 %collective-permute-start.2 = (bf16[36,256]{1,0:T(8,128)(2,1)S(1)}, bf16[36,256]{1,0:T(8,128)(2,1)S(1)}, u32[]{:S(2)}, u32[]{:S(2)}) collective-permute-start(bf16[36,256]{1,0:T(8,128)(2,1)S(1)} %pad_maximum_fusion.up_own), channel_id=1, source_target_pairs={{16,0},{20,4},{24,8},{28,12},{0,16},{4,20},{8,24},{12,28},{17,1},{... | collective-permute-start | bytes 55304 | tf_op jit(solution)/shard_map/ppermute | solution.py:1264
  11.2 1.3 collective-permute-start.1
  13.3 1.7 collective-permute-done.1.up_one
  15.0 1.5 collective-permute-start.11
  17.2 1.5 collective-permute-start.7
  19.9 9.4 %shard_map.247 = (bf16[528,1024]{1,0:T(8,128)(2,1)}, f32[4,128,1024]{2,1,0:T(8,128)}, f32[3,128,128]{2,1,0:T(8,128)}, f32[128,1024]{1,0:T(8,128)}, bf16[36,1024]{1,0:T(8,128)(2,1)}) custom-call(s32[4]{0:T(128)} %pad_add_fusion.bounds, bf16[2,9,64,1024]{3,2,1,0:T(8,128)(2,1)} %bitcast.40, f32[1,1024]{1,0:T(1,128)} %bitcast.47, bf16[36,256]{1,0:T(8,128)(2,1)} %copy-done.38, ...), custom_call_target="tpu_custom_call" | custom-call | tf_op jit(solution)/shard_map/pallas_call | solution.py:1202
  29.3 5.8 %collective-permute-done.11.piece2 = bf16[12,128,256]{2,1,0:T(8,128)(2,1)S(1)} collective-permute-done((bf16[12,128,256]{2,1,0:T(8,128)(2,1)}, bf16[12,128,256]{2,1,0:T(8,128)(2,1)S(1)}, u32[]{:S(2)}, u32[]{:S(2)}) %collective-permute-start.11) | collective-permute-done | bytes 786464 | tf_op jit(solution)/shard_map/ppermute | solution.py:403
  36.3 3.9 %collective-permute-start.14 = (bf16[12,128,256]{2,1,0:T(8,128)(2,1)S(1)}, bf16[12,128,256]{2,1,0:T(8,128)(2,1)S(1)}, u32[]{:S(2)}, u32[]{:S(2)}) collective-permute-start(bf16[12,128,256]{2,1,0:T(8,128)(2,1)S(1)} %get-tuple-element.65), channel_id=1, source_target_pairs={{0,8},{4,12},{8,0},{12,4},{16,24},{20,28},{24,16},{28,20},{1,9},{5... | collective-permute-start | bytes 2359304 | tf_op jit(solution)/shard_map/ppermute | solution.py:403
  40.2 1.5 collective-permute-start.4
  42.4 14.6 %collective-permute-done.14.piece5 = bf16[12,128,256]{2,1,0:T(8,128)(2,1)S(1)} collective-permute-done((bf16[12,128,256]{2,1,0:T(8,128)(2,1)S(1)}, bf16[12,128,256]{2,1,0:T(8,128)(2,1)S(1)}, u32[]{:S(2)}, u32[]{:S(2)}) %collective-permute-start.14) | collective-permute-done | bytes 786464 | tf_op jit(solution)/shard_map/ppermute | solution.py:403
  57.8 3.2 %collective-permute-done.15.piece7 = bf16[12,128,256]{2,1,0:T(8,128)(2,1)S(1)} collective-permute-done((bf16[12,128,256]{2,1,0:T(8,128)(2,1)S(1)}, bf16[12,128,256]{2,1,0:T(8,128)(2,1)S(1)}, u32[]{:S(2)}, u32[]{:S(2)}) %collective-permute-start.15) | collective-permute-done | bytes 786464 | tf_op jit(solution)/shard_map/ppermute | solution.py:403
  61.1 3.7 %collective-permute-done.4.packet1 = bf16[528,1024]{1,0:T(8,128)(2,1)S(1)} collective-permute-done((bf16[528,1024]{1,0:T(8,128)(2,1)S(1)}, bf16[528,1024]{1,0:T(8,128)(2,1)S(1)}, u32[]{:S(2)}, u32[]{:S(2)}) %collective-permute-start.4) | collective-permute-done | bytes 1081376 | tf_op jit(solution)/shard_map/ppermute | solution.py:1302
  65.3 11.2 %collective-permute-done.17.piece8 = bf16[12,128,256]{2,1,0:T(8,128)(2,1)S(1)} collective-permute-done((bf16[12,128,256]{2,1,0:T(8,128)(2,1)S(1)}, bf16[12,128,256]{2,1,0:T(8,128)(2,1)S(1)}, u32[]{:S(2)}, u32[]{:S(2)}) %collective-permute-start.17) | collective-permute-done | bytes 786464 | tf_op jit(solution)/shard_map/ppermute | solution.py:403
  77.8 1.5 collective-permute-done.9.cotangent3
  79.4 1.0 copy-done.13
  80.3 4.8 %collective-permute-done.19.piece10 = bf16[5,128,256]{2,1,0:T(8,128)(2,1)S(1)} collective-permute-done((bf16[5,128,256]{2,1,0:T(8,128)(2,1)S(1)}, bf16[5,128,256]{2,1,0:T(8,128)(2,1)S(1)}, u32[]{:S(2)}, u32[]{:S(2)}) %collective-permute-start.19) | collective-permute-done | bytes 327712 | tf_op jit(solution)/shard_map/ppermute | solution.py:403
  85.1 2.7 %collective-permute-done.18.piece9 = bf16[7,128,256]{2,1,0:T(8,128)(2,1)S(1)} collective-permute-done((bf16[7,128,256]{2,1,0:T(8,128)(2,1)S(1)}, bf16[7,128,256]{2,1,0:T(8,128)(2,1)S(1)}, u32[]{:S(2)}, u32[]{:S(2)}) %collective-permute-start.18) | collective-permute-done | bytes 458784 | tf_op jit(solution)/shard_map/ppermute | solution.py:403
  88.6 25.9 %shard_map.248 = (bf16[7,128,256]{2,1,0:T(8,128)(2,1)}, bf16[5,128,256]{2,1,0:T(8,128)(2,1)}, bf16[12,128,256]{2,1,0:T(8,128)(2,1)}, bf16[12,128,256]{2,1,0:T(8,...) custom-call(f32[3,128,128]{2,1,0:T(8,128)} %constant.39.clone.rope, ...), custom_call_target="tpu_custom_call" | custom-call | tf_op jit(solution)/shard_map/pallas_call | solution.py:1202
  115.5 9.5 %collective-permute-done.24 = bf16[5,128,256]{2,1,0:T(8,128)(2,1)S(1)} collective-permute-done((bf16[5,128,256]{2,1,0:T(8,128)(2,1)}, bf16[5,128,256]{2,1,0:T(8,128)(2,1)S(1)}, u32[]{:S(2)}, u32[]{:S(2)}) %collective-permute-start.24) | collective-permute-done | bytes 327712 | tf_op jit(solution)/shard_map/ppermute | solution.py:403
  125.0 1.2 add_convert_fusion.2
  127.0 1.4 fusion
  128.9 1.3 collective-permute-start.29
  130.8 16.0 %collective-permute-done.25 = bf16[12,128,256]{2,1,0:T(8,128)(2,1)S(1)} collective-permute-done((bf16[12,128,256]{2,1,0:T(8,128)(2,1)S(1)}, bf16[12,128,256]{2,1,0:T(8,128)(2,1)S(1)}, u32[]{:S(2)}, u32[]{:S(2)}) %collective-permute-start.25) | collective-permute-done | bytes 786464 | tf_op jit(solution)/shard_map/ppermute | solution.py:403
  146.8 1.0 collective-permute-done.29
  147.8 1.8 fusion.2
  150.4 3.7 %collective-permute-done.22.across = bf16[4,128,1024]{2,1,0:T(8,128)(2,1)S(1)} collective-permute-done((bf16[4,128,1024]{2,1,0:T(8,128)(2,1)}, bf16[4,128,1024]{2,1,0:T(8,128)(2,1)S(1)}, u32[]{:S(2)}, u32[]{:S(2)}) %collective-permute-start.22) | collective-permute-done | bytes 1048608 | tf_op jit(solution)/shard_map/ppermute | solution.py:1347
  154.1 1.0 copy-done.16
  155.1 13.1 %shard_map.249 = (bf16[2,9,64,1024]{3,2,1,0:T(8,128)(2,1)}, f32[24,1152]{1,0:T(8,128)}, f32[24,1152]{1,0:T(8,128)}, f32[2,9,4,64]{3,2,1,0:T(4,128)}) custom-call(bf16[2,9,64,1024]{3,2,1,0:T(8,128)(2,1)} %bitcast.41, bf16[128,1024]{1,0:T(8,128)(2,1)} %bitcast.43, f32[4,128,1024]{2,1,0:T(8,128)} %get-tuple-element.74.scaled, ...), custom_call_target="tpu_custom_call" | custom-call | tf_op jit(solution)/shard_map/pallas_call | solution.py:1361
  168.3 2.0 fusion.6
  170.3 1.1 collective-permute-start.27
  171.5 1.6 collective-permute-start.32
  173.7 2.6 %collective-permute-done.34 = f32[24,1152]{1,0:T(8,128)S(1)} collective-permute-done((f32[24,1152]{1,0:T(8,128)S(1)}, f32[24,1152]{1,0:T(8,128)S(1)}, u32[]{:S(2)}, u32[]{:S(2)}) %collective-permute-start.34) | collective-permute-done | bytes 110624 | tf_op jit(solution)/shard_map/ppermute | solution.py:1414
  176.3 1.3 collective-permute-start.35
  177.7 0.9 collective-permute-start.23
  178.5 3.7 %collective-permute-done.35 = f32[24,1152]{1,0:T(8,128)S(1)} collective-permute-done((f32[24,1152]{1,0:T(8,128)S(1)}, f32[24,1152]{1,0:T(8,128)S(1)}, u32[]{:S(2)}, u32[]{:S(2)}) %collective-permute-start.35) | collective-permute-done | bytes 110624 | tf_op jit(solution)/shard_map/ppermute | solution.py:1415
  182.3 5.3 %collective-permute-done.27 = bf16[12,128,256]{2,1,0:T(8,128)(2,1)S(1)} collective-permute-done((bf16[12,128,256]{2,1,0:T(8,128)(2,1)S(1)}, bf16[12,128,256]{2,1,0:T(8,128)(2,1)S(1)}, u32[]{:S(2)}, u32[]{:S(2)}) %collective-permute-start.27) | collective-permute-done | bytes 786464 | tf_op jit(solution)/shard_map/ppermute | solution.py:403
  187.6 1.2 collective-permute-done.32
  190.6 4.1 %collective-permute-done.38 = f32[24,1152]{1,0:T(8,128)S(1)} collective-permute-done((f32[24,1152]{1,0:T(8,128)S(1)}, f32[24,1152]{1,0:T(8,128)S(1)}, u32[]{:S(2)}, u32[]{:S(2)}) %collective-permute-start.38) | collective-permute-done | bytes 110624 | tf_op jit(solution)/shard_map/ppermute | solution.py:1420
  194.7 2.4 %collective-permute-start.39 = (f32[24,1152]{1,0:T(8,128)S(1)}, f32[24,1152]{1,0:T(8,128)S(1)}, u32[]{:S(2)}, u32[]{:S(2)}) collective-permute-start(f32[24,1152]{1,0:T(8,128)S(1)} %add.96), channel_id=1, source_target_pairs={{0,8},{4,12},{8,0},{12,4},{16,24},{20,28},{24,16},{28,20},{1,9},{5... | collective-permute-start | bytes 331784 | tf_op jit(solution)/shard_map/ppermute | solution.py:1420
  197.1 3.7 %collective-permute-done.39 = f32[24,1152]{1,0:T(8,128)S(1)} collective-permute-done((f32[24,1152]{1,0:T(8,128)S(1)}, f32[24,1152]{1,0:T(8,128)S(1)}, u32[]{:S(2)}, u32[]{:S(2)}) %collective-permute-start.39) | collective-permute-done | bytes 110624 | tf_op jit(solution)/shard_map/ppermute | solution.py:1420
  200.8 2.3 %collective-permute-start.40 = (f32[24,1152]{1,0:T(8,128)S(1)}, f32[24,1152]{1,0:T(8,128)S(1)}, u32[]{:S(2)}, u32[]{:S(2)}) collective-permute-start(f32[24,1152]{1,0:T(8,128)S(1)} %add.97), channel_id=1, source_target_pairs={{0,16},{4,20},{8,24},{12,28},{16,0},{20,4},{24,8},{28,12},{1,17},{... | collective-permute-start | bytes 331784 | tf_op jit(solution)/shard_map/ppermute | solution.py:1420
  203.1 3.4 %collective-permute-done.40 = f32[24,1152]{1,0:T(8,128)S(1)} collective-permute-done((f32[24,1152]{1,0:T(8,128)S(1)}, f32[24,1152]{1,0:T(8,128)S(1)}, u32[]{:S(2)}, u32[]{:S(2)}) %collective-permute-start.40) | collective-permute-done | bytes 110624 | tf_op jit(solution)/shard_map/ppermute | solution.py:1420
  208.1 2.1 collective-permute-done.42.small_other
  211.1 0.9 copy-done.23
  212.0 5.2 %shard_map.250 = (f32[3,128,1024]{2,1,0:T(8,128)}, f32[128,1024]{1,0:T(8,128)}, f32[128,4096]{1,0:T(8,128)}, f32[512,1024]{1,0:T(8,128)}, f32[1,1024]{1,0:T(1,12...) custom-call(bf16[12,128,256]{2,1,0:T(8,128)(2,1)} %copy-done.6, ...), custom_call_target="tpu_custom_call" | custom-call | tf_op jit(solution)/shard_map/pallas_call | solution.py:1202
  (160 shorter events, 16.4 us)
Async XLA Ops:
  0.7 6.2 %collective-permute-start = (bf16[36,128]{1,0:T(8,128)(2,1)}, bf16[36,128]{1,0:T(8,128)(2,1)S(1)}, u32[]{:S(2)}, u32[]{:S(2)}) collective-permute-start(bf16[36,128]{1,0:T(8,128)(2,1)} %bitcast.49), channel_id=1, source_target_pairs={{0,4},{4,0},{8,12},{12,8},{16,20},{20,16},{24,28},{28,24},{1,5},{5... | collective-permute-start | bytes 27656 | tf_op jit(solution)/shard_map/ppermute | solution.py:1262
  7.0 5.9 %collective-permute-start.3 = (bf16[36,256]{1,0:T(8,128)(2,1)S(1)}, bf16[36,256]{1,0:T(8,128)(2,1)S(1)}, u32[]{:S(2)}, u32[]{:S(2)}) collective-permute-start(bf16[36,256]{1,0:T(8,128)(2,1)S(1)} %pad_maximum_fusion.up_own), channel_id=1, source_target_pairs={{24,0},{28,4},{0,8},{4,12},{8,16},{12,20},{16,24},{20,28},{25,1},{... | collective-permute-start | bytes 55304 | tf_op jit(solution)/shard_map/ppermute | solution.py:1264
  8.6 4.7 %collective-permute-start.2 = (bf16[36,256]{1,0:T(8,128)(2,1)S(1)}, bf16[36,256]{1,0:T(8,128)(2,1)S(1)}, u32[]{:S(2)}, u32[]{:S(2)}) collective-permute-start(bf16[36,256]{1,0:T(8,128)(2,1)S(1)} %pad_maximum_fusion.up_own), channel_id=1, source_target_pairs={{16,0},{20,4},{24,8},{28,12},{0,16},{4,20},{8,24},{12,28},{17,1},{... | collective-permute-start | bytes 55304 | tf_op jit(solution)/shard_map/ppermute | solution.py:1264
  11.2 3.8 %collective-permute-start.1 = (bf16[36,256]{1,0:T(8,128)(2,1)S(1)}, bf16[36,256]{1,0:T(8,128)(2,1)S(1)}, u32[]{:S(2)}, u32[]{:S(2)}) collective-permute-start(bf16[36,256]{1,0:T(8,128)(2,1)S(1)} %pad_maximum_fusion.up_own), channel_id=1, source_target_pairs={{8,0},{12,4},{16,8},{20,12},{24,16},{28,20},{0,24},{4,28},{9,1},{1... | collective-permute-start | bytes 55304 | tf_op jit(solution)/shard_map/ppermute | solution.py:1264
  15.0 14.3 %collective-permute-start.12 = (bf16[12,128,256]{2,1,0:T(8,128)(2,1)}, bf16[12,128,256]{2,1,0:T(8,128)(2,1)S(1)}, u32[]{:S(2)}, u32[]{:S(2)}) collective-permute-start(bf16[12,128,256]{2,1,0:T(8,128)(2,1)} %shard_map.246.piece0), channel_id=1, source_target_pairs={{0,1},{1,0},{2,3},{3,2},{4,5},{5,4},{6,7},{7,6},{8,16},{9,17},{10,... | collective-permute-start | bytes 2359304 | tf_op jit(solution)/shard_map/ppermute | solution.py:403
  15.0 20.2 %collective-permute-start.11 = (bf16[12,128,256]{2,1,0:T(8,128)(2,1)}, bf16[12,128,256]{2,1,0:T(8,128)(2,1)S(1)}, u32[]{:S(2)}, u32[]{:S(2)}) collective-permute-start(bf16[12,128,256]{2,1,0:T(8,128)(2,1)} %shard_map.246.piece0), channel_id=1, source_target_pairs={{0,8},{4,12},{8,0},{12,4},{16,24},{20,28},{24,16},{28,20},{1,9},{5... | collective-permute-start | bytes 2359304 | tf_op jit(solution)/shard_map/ppermute | solution.py:403
  16.5 18.6 %collective-permute-start.10 = (bf16[12,128,256]{2,1,0:T(8,128)(2,1)}, bf16[12,128,256]{2,1,0:T(8,128)(2,1)S(1)}, u32[]{:S(2)}, u32[]{:S(2)}) collective-permute-start(bf16[12,128,256]{2,1,0:T(8,128)(2,1)} %shard_map.246.piece0), channel_id=1, source_target_pairs={{0,4},{4,0},{8,12},{12,8},{16,20},{20,16},{24,28},{28,24},{1,5},{5... | collective-permute-start | bytes 2359304 | tf_op jit(solution)/shard_map/ppermute | solution.py:403
  17.2 18.9 %collective-permute-start.7 = (bf16[128,1024]{1,0:T(8,128)(2,1)S(1)}, bf16[128,1024]{1,0:T(8,128)(2,1)S(1)}, u32[]{:S(2)}, u32[]{:S(2)}) collective-permute-start(bf16[128,1024]{1,0:T(8,128)(2,1)S(1)} %bitcast.44), channel_id=1, source_target_pairs={{0,2},{1,3},{2,0},{3,1},{4,6},{5,7},{6,4},{7,5},{8,10},{9,11},{10,... | collective-permute-start | bytes 786440 | tf_op jit(solution)/shard_map/ppermute | solution.py:1270
  36.0 28.8 %copy-start.18 = (bf16[2,1,64,1024]{3,2,1,0:T(8,128)(2,1)S(1)}, bf16[2,1,64,1024]{3,2,1,0:T(8,128)(2,1)}, u32[]{:S(2)}) copy-start(bf16[2,1,64,1024]{3,2,1,0:T(8,128)(2,1)} %param.16) | copy-start | bytes 786436
  36.0 41.7 %copy-start.33 = (bf16[128,1024]{1,0:T(8,128)(2,1)}, bf16[128,1024]{1,0:T(8,128)(2,1)S(1)}, u32[]{:S(2)}) copy-start(bf16[128,1024]{1,0:T(8,128)(2,1)S(1)} %collective-permute-done.7.cotangent1) | copy-start | bytes 786436
  36.3 6.1 %collective-permute-start.13 = (bf16[12,128,256]{2,1,0:T(8,128)(2,1)S(1)}, bf16[12,128,256]{2,1,0:T(8,128)(2,1)S(1)}, u32[]{:S(2)}, u32[]{:S(2)}) collective-permute-start(bf16[12,128,256]{2,1,0:T(8,128)(2,1)S(1)} %collective-permute-done.11.piece2), channel_id=1, source_target_pairs={{0,1},{1,0},{2,3},{3,2},{4,5},{5,4},{6,7},{7,6},{8,16},{9,17},{10,... | collective-permute-start | bytes 2359304 | tf_op jit(solution)/shard_map/ppermute | solution.py:403
  36.3 20.7 %collective-permute-start.14 = (bf16[12,128,256]{2,1,0:T(8,128)(2,1)S(1)}, bf16[12,128,256]{2,1,0:T(8,128)(2,1)S(1)}, u32[]{:S(2)}, u32[]{:S(2)}) collective-permute-start(bf16[12,128,256]{2,1,0:T(8,128)(2,1)S(1)} %get-tuple-element.65), channel_id=1, source_target_pairs={{0,8},{4,12},{8,0},{12,4},{16,24},{20,28},{24,16},{28,20},{1,9},{5... | collective-permute-start | bytes 2359304 | tf_op jit(solution)/shard_map/ppermute | solution.py:403
  40.2 24.6 %collective-permute-start.4 = (bf16[528,1024]{1,0:T(8,128)(2,1)S(1)}, bf16[528,1024]{1,0:T(8,128)(2,1)S(1)}, u32[]{:S(2)}, u32[]{:S(2)}) collective-permute-start(bf16[528,1024]{1,0:T(8,128)(2,1)S(1)} %copy-done.11), channel_id=1, source_target_pairs={{0,2},{1,3},{2,0},{3,1},{4,6},{5,7},{6,4},{7,5},{8,10},{9,11},{10,... | collective-permute-start | bytes 3244040 | tf_op jit(solution)/shard_map/ppermute | solution.py:1302
  41.7 19.4 %collective-permute-start.15 = (bf16[12,128,256]{2,1,0:T(8,128)(2,1)S(1)}, bf16[12,128,256]{2,1,0:T(8,128)(2,1)S(1)}, u32[]{:S(2)}, u32[]{:S(2)}) collective-permute-start(bf16[12,128,256]{2,1,0:T(8,128)(2,1)S(1)} %get-tuple-element.125), channel_id=1, source_target_pairs={{0,4},{4,0},{8,12},{12,8},{16,20},{20,16},{24,28},{28,24},{1,5},{5... | collective-permute-start | bytes 2359304 | tf_op jit(solution)/shard_map/ppermute | solution.py:403
  42.4 34.2 %copy-start.1 = (bf16[12,128,256]{2,1,0:T(8,128)(2,1)}, bf16[12,128,256]{2,1,0:T(8,128)(2,1)S(1)}, u32[]{:S(2)}) copy-start(bf16[12,128,256]{2,1,0:T(8,128)(2,1)S(1)} %collective-permute-done.13.piece4) | copy-start | bytes 2359300
  57.1 19.4 %collective-permute-start.17 = (bf16[12,128,256]{2,1,0:T(8,128)(2,1)S(1)}, bf16[12,128,256]{2,1,0:T(8,128)(2,1)S(1)}, u32[]{:S(2)}, u32[]{:S(2)}) collective-permute-start(bf16[12,128,256]{2,1,0:T(8,128)(2,1)S(1)} %broadcast_select_fusion), channel_id=1, source_target_pairs={{0,4},{4,0},{8,12},{12,8},{16,20},{20,16},{24,28},{28,24},{1,5},{5... | collective-permute-start | bytes 2359304 | tf_op jit(solution)/shard_map/ppermute | solution.py:403
  61.1 26.8 %copy-start.19 = (bf16[12,128,256]{2,1,0:T(8,128)(2,1)}, bf16[12,128,256]{2,1,0:T(8,128)(2,1)S(1)}, u32[]{:S(2)}) copy-start(bf16[12,128,256]{2,1,0:T(8,128)(2,1)S(1)} %collective-permute-done.15.piece7) | copy-start | bytes 2359300
  61.1 15.9 %collective-permute-start.16 = (bf16[12,128,256]{2,1,0:T(8,128)(2,1)S(1)}, bf16[12,128,256]{2,1,0:T(8,128)(2,1)S(1)}, u32[]{:S(2)}, u32[]{:S(2)}) collective-permute-start(bf16[12,128,256]{2,1,0:T(8,128)(2,1)S(1)} %collective-permute-done.13.piece4), channel_id=1, source_target_pairs={{0,8},{4,12},{8,0},{12,4},{16,24},{20,28},{24,16},{28,20},{1,9},{5... | collective-permute-start | bytes 2359304 | tf_op jit(solution)/shard_map/ppermute | solution.py:403
  61.1 18.3 %collective-permute-start.5 = (bf16[528,1024]{1,0:T(8,128)(2,1)S(1)}, bf16[528,1024]{1,0:T(8,128)(2,1)S(1)}, u32[]{:S(2)}, u32[]{:S(2)}) collective-permute-start(bf16[528,1024]{1,0:T(8,128)(2,1)S(1)} %copy-done.11), channel_id=1, source_target_pairs={{0,1},{1,0},{2,3},{3,2},{4,5},{5,4},{6,7},{7,6},{8,9},{9,8},{10,11... | collective-permute-start | bytes 3244040 | tf_op jit(solution)/shard_map/ppermute | solution.py:1303
  64.8 14.6 %collective-permute-start.6 = (bf16[528,1024]{1,0:T(8,128)(2,1)S(1)}, bf16[528,1024]{1,0:T(8,128)(2,1)S(1)}, u32[]{:S(2)}, u32[]{:S(2)}) collective-permute-start(bf16[528,1024]{1,0:T(8,128)(2,1)S(1)} %collective-permute-done.4.packet1), channel_id=1, source_target_pairs={{0,1},{1,0},{2,3},{3,2},{4,5},{5,4},{6,7},{7,6},{8,9},{9,8},{10,11... | collective-permute-start | bytes 3244040 | tf_op jit(solution)/shard_map/ppermute | solution.py:1304
  64.8 12.9 %collective-permute-start.8 = (bf16[128,1024]{1,0:T(8,128)(2,1)S(1)}, bf16[128,1024]{1,0:T(8,128)(2,1)S(1)}, u32[]{:S(2)}, u32[]{:S(2)}) collective-permute-start(bf16[128,1024]{1,0:T(8,128)(2,1)S(1)} %bitcast.45), channel_id=1, source_target_pairs={{0,1},{1,0},{2,3},{3,2},{4,5},{5,4},{6,7},{7,6},{8,9},{9,8},{10,11... | collective-permute-start | bytes 786440 | tf_op jit(solution)/shard_map/ppermute | solution.py:1274
  76.6 11.2 %collective-permute-start.18 = (bf16[7,128,256]{2,1,0:T(8,128)(2,1)S(1)}, bf16[7,128,256]{2,1,0:T(8,128)(2,1)S(1)}, u32[]{:S(2)}, u32[]{:S(2)}) collective-permute-start(bf16[7,128,256]{2,1,0:T(8,128)(2,1)S(1)} %slice.28), channel_id=1, source_target_pairs={{0,8},{4,12},{8,0},{12,4},{16,24},{20,28},{24,16},{28,20},{1,9},{5... | collective-permute-start | bytes 1376264 | tf_op jit(solution)/shard_map/ppermute | solution.py:403
  77.0 8.2 %collective-permute-start.19 = (bf16[5,128,256]{2,1,0:T(8,128)(2,1)S(1)}, bf16[5,128,256]{2,1,0:T(8,128)(2,1)S(1)}, u32[]{:S(2)}, u32[]{:S(2)}) collective-permute-start(bf16[5,128,256]{2,1,0:T(8,128)(2,1)S(1)} %slice.29), channel_id=1, source_target_pairs={{0,4},{4,0},{8,12},{12,8},{16,20},{20,16},{24,28},{28,24},{1,5},{5... | collective-permute-start | bytes 983048 | tf_op jit(solution)/shard_map/ppermute | solution.py:403
  77.7 1.6 collective-permute-start.9
  114.6 12.5 %collective-permute-start.20 = (bf16[2,4,128,1024]{3,2,1,0:T(8,128)(2,1)}, bf16[2,4,128,1024]{3,2,1,0:T(8,128)(2,1)S(1)}, u32[]{:S(2)}, u32[]{:S(2)}) collective-permute-start(bf16[2,4,128,1024]{3,2,1,0:T(8,128)(2,1)} %get-tuple-element.71), channel_id=1, source_target_pairs={{0,1},{1,0},{2,3},{3,2},{4,5},{5,4},{6,7},{7,6},{8,9},{9,8},{10,11... | collective-permute-start | bytes 6291464 | tf_op jit(solution)/shard_map/ppermute | solution.py:1345
  114.6 10.3 %collective-permute-start.24 = (bf16[5,128,256]{2,1,0:T(8,128)(2,1)}, bf16[5,128,256]{2,1,0:T(8,128)(2,1)S(1)}, u32[]{:S(2)}, u32[]{:S(2)}) collective-permute-start(bf16[5,128,256]{2,1,0:T(8,128)(2,1)} %get-tuple-element.83), channel_id=1, source_target_pairs={{0,8},{4,12},{8,0},{12,4},{16,24},{20,28},{24,16},{28,20},{1,9},{5... | collective-permute-start | bytes 983048 | tf_op jit(solution)/shard_map/ppermute | solution.py:403
  114.7 14.0 %collective-permute-start.28 = (bf16[7,128,256]{2,1,0:T(8,128)(2,1)}, bf16[7,128,256]{2,1,0:T(8,128)(2,1)S(1)}, u32[]{:S(2)}, u32[]{:S(2)}) collective-permute-start(bf16[7,128,256]{2,1,0:T(8,128)(2,1)} %get-tuple-element.82), channel_id=1, source_target_pairs={{0,4},{4,0},{8,12},{12,8},{16,20},{20,16},{24,28},{28,24},{1,5},{5... | collective-permute-start | bytes 1376264 | tf_op jit(solution)/shard_map/ppermute | solution.py:403
  126.3 20.5 %collective-permute-start.25 = (bf16[12,128,256]{2,1,0:T(8,128)(2,1)S(1)}, bf16[12,128,256]{2,1,0:T(8,128)(2,1)S(1)}, u32[]{:S(2)}, u32[]{:S(2)}) collective-permute-start(bf16[12,128,256]{2,1,0:T(8,128)(2,1)S(1)} %add_convert_fusion.2), channel_id=1, source_target_pairs={{0,4},{4,0},{8,12},{12,8},{16,20},{20,16},{24,28},{28,24},{1,5},{5... | collective-permute-start | bytes 2359304 | tf_op jit(solution)/shard_map/ppermute | solution.py:403
  128.9 18.9 %collective-permute-start.29 = (bf16[12,128,256]{2,1,0:T(8,128)(2,1)S(1)}, bf16[12,128,256]{2,1,0:T(8,128)(2,1)S(1)}, u32[]{:S(2)}, u32[]{:S(2)}) collective-permute-start(bf16[12,128,256]{2,1,0:T(8,128)(2,1)S(1)} %add_convert_fusion.1), channel_id=1, source_target_pairs={{0,8},{4,12},{8,0},{12,4},{16,24},{20,28},{24,16},{28,20},{1,9},{5... | collective-permute-start | bytes 2359304 | tf_op jit(solution)/shard_map/ppermute | solution.py:403
  130.2 23.9 %collective-permute-start.22 = (bf16[4,128,1024]{2,1,0:T(8,128)(2,1)}, bf16[4,128,1024]{2,1,0:T(8,128)(2,1)S(1)}, u32[]{:S(2)}, u32[]{:S(2)}) collective-permute-start(bf16[4,128,1024]{2,1,0:T(8,128)(2,1)} %fusion), channel_id=1, source_target_pairs={{0,2},{1,3},{2,0},{3,1},{4,6},{5,7},{6,4},{7,5},{8,10},{9,11},{10,... | collective-permute-start | bytes 3145736 | tf_op jit(solution)/shard_map/ppermute | solution.py:1347
  130.2 38.0 %collective-permute-start.31 = (bf16[12,128,256]{2,1,0:T(8,128)(2,1)}, bf16[12,128,256]{2,1,0:T(8,128)(2,1)S(1)}, u32[]{:S(2)}, u32[]{:S(2)}) collective-permute-start(bf16[12,128,256]{2,1,0:T(8,128)(2,1)} %get-tuple-element.90), channel_id=1, source_target_pairs={{0,4},{4,0},{8,12},{12,8},{16,20},{20,16},{24,28},{28,24},{1,5},{5... | collective-permute-start | bytes 2359304 | tf_op jit(solution)/shard_map/ppermute | solution.py:403
  149.6 18.6 %collective-permute-start.26 = (bf16[12,128,256]{2,1,0:T(8,128)(2,1)}, bf16[12,128,256]{2,1,0:T(8,128)(2,1)S(1)}, u32[]{:S(2)}, u32[]{:S(2)}) collective-permute-start(bf16[12,128,256]{2,1,0:T(8,128)(2,1)} %get-tuple-element.123), channel_id=1, source_target_pairs={{0,8},{4,12},{8,0},{12,4},{16,24},{20,28},{24,16},{28,20},{1,9},{5... | collective-permute-start | bytes 2359304 | tf_op jit(solution)/shard_map/ppermute | solution.py:403
  150.4 17.8 %collective-permute-start.30 = (bf16[12,128,256]{2,1,0:T(8,128)(2,1)}, bf16[12,128,256]{2,1,0:T(8,128)(2,1)}, u32[]{:S(2)}, u32[]{:S(2)}) collective-permute-start(bf16[12,128,256]{2,1,0:T(8,128)(2,1)} %get-tuple-element.124), channel_id=1, source_target_pairs={{0,1},{1,0},{2,3},{3,2},{4,5},{5,4},{6,7},{7,6},{8,16},{9,17},{10,... | collective-permute-start | bytes 2359304 | tf_op jit(solution)/shard_map/ppermute | solution.py:403
  170.3 17.2 %collective-permute-start.27 = (bf16[12,128,256]{2,1,0:T(8,128)(2,1)S(1)}, bf16[12,128,256]{2,1,0:T(8,128)(2,1)S(1)}, u32[]{:S(2)}, u32[]{:S(2)}) collective-permute-start(bf16[12,128,256]{2,1,0:T(8,128)(2,1)S(1)} %get-tuple-element.120), channel_id=1, source_target_pairs={{0,4},{4,0},{8,12},{12,8},{16,20},{20,16},{24,28},{28,24},{1,5},{5... | collective-permute-start | bytes 2359304 | tf_op jit(solution)/shard_map/ppermute | solution.py:403
  171.5 17.3 %collective-permute-start.32 = (bf16[12,128,256]{2,1,0:T(8,128)(2,1)S(1)}, bf16[12,128,256]{2,1,0:T(8,128)(2,1)S(1)}, u32[]{:S(2)}, u32[]{:S(2)}) collective-permute-start(bf16[12,128,256]{2,1,0:T(8,128)(2,1)S(1)} %get-tuple-element.92), channel_id=1, source_target_pairs={{0,8},{4,12},{8,0},{12,4},{16,24},{20,28},{24,16},{28,20},{1,9},{5... | collective-permute-start | bytes 2359304 | tf_op jit(solution)/shard_map/ppermute | solution.py:403
  173.1 15.7 %collective-permute-start.33 = (bf16[12,128,256]{2,1,0:T(8,128)(2,1)S(1)}, bf16[12,128,256]{2,1,0:T(8,128)(2,1)S(1)}, u32[]{:S(2)}, u32[]{:S(2)}) collective-permute-start(bf16[12,128,256]{2,1,0:T(8,128)(2,1)S(1)} %get-tuple-element.93), channel_id=1, source_target_pairs={{0,1},{1,0},{2,3},{3,2},{4,5},{5,4},{6,7},{7,6},{8,16},{9,17},{10,... | collective-permute-start | bytes 2359304 | tf_op jit(solution)/shard_map/ppermute | solution.py:403
  173.1 4.5 %collective-permute-start.21 = (bf16[2,128,1024]{2,1,0:T(8,128)(2,1)S(1)}, bf16[2,128,1024]{2,1,0:T(8,128)(2,1)S(1)}, u32[]{:S(2)}, u32[]{:S(2)}) collective-permute-start(bf16[2,128,1024]{2,1,0:T(8,128)(2,1)S(1)} %copy-done.44), channel_id=1, source_target_pairs={{0,1},{1,0},{2,3},{3,2},{4,5},{5,4},{6,7},{7,6},{8,9},{9,8},{10,11... | collective-permute-start | bytes 1572872 | tf_op jit(solution)/shard_map/ppermute | solution.py:1348
  173.6 2.7 %collective-permute-start.34 = (f32[24,1152]{1,0:T(8,128)S(1)}, f32[24,1152]{1,0:T(8,128)S(1)}, u32[]{:S(2)}, u32[]{:S(2)}) collective-permute-start(f32[24,1152]{1,0:T(8,128)S(1)} %copy-done.45), channel_id=1, source_target_pairs={{0,1},{1,0},{2,3},{3,2},{4,5},{5,4},{6,7},{7,6},{8,9},{9,8},{10,11... | collective-permute-start | bytes 331784 | tf_op jit(solution)/shard_map/ppermute | solution.py:1414
  176.3 6.0 %collective-permute-start.35 = (f32[24,1152]{1,0:T(8,128)S(1)}, f32[24,1152]{1,0:T(8,128)S(1)}, u32[]{:S(2)}, u32[]{:S(2)}) collective-permute-start(f32[24,1152]{1,0:T(8,128)S(1)} %add.94), channel_id=1, source_target_pairs={{0,2},{1,3},{2,0},{3,1},{4,6},{5,7},{6,4},{7,5},{8,10},{9,11},{10,... | collective-permute-start | bytes 331784 | tf_op jit(solution)/shard_map/ppermute | solution.py:1415
  177.7 11.6 %collective-permute-start.23 = (bf16[128,1024]{1,0:T(8,128)(2,1)S(1)}, bf16[128,1024]{1,0:T(8,128)(2,1)S(1)}, u32[]{:S(2)}, u32[]{:S(2)}) collective-permute-start(bf16[128,1024]{1,0:T(8,128)(2,1)S(1)} %fusion.12), channel_id=1, source_target_pairs={{0,2},{1,3},{2,0},{3,1},{4,6},{5,7},{6,4},{7,5},{8,10},{9,11},{10,... | collective-permute-start | bytes 786440 | tf_op jit(solution)/shard_map/ppermute | solution.py:1350
  189.3 20.9 %copy-start.6 = (bf16[12,128,256]{2,1,0:T(8,128)(2,1)}, bf16[12,128,256]{2,1,0:T(8,128)(2,1)S(1)}, u32[]{:S(2)}) copy-start(bf16[12,128,256]{2,1,0:T(8,128)(2,1)S(1)} %add_convert_fusion.shard0) | copy-start | bytes 2359300
  189.3 17.3 %collective-permute-start.36 = (bf16[12,128,256]{2,1,0:T(8,128)(2,1)S(1)}, bf16[12,128,256]{2,1,0:T(8,128)(2,1)S(1)}, u32[]{:S(2)}, u32[]{:S(2)}) collective-permute-start(bf16[12,128,256]{2,1,0:T(8,128)(2,1)S(1)} %add_convert_fusion.shard0), channel_id=1, source_target_pairs={{0,2},{1,3},{2,0},{3,1},{4,6},{5,7},{6,4},{7,5},{8,10},{9,11},{10,... | collective-permute-start | bytes 2359304 | tf_op jit(solution)/shard_map/ppermute | solution.py:1417
  189.9 4.7 %collective-permute-start.38 = (f32[24,1152]{1,0:T(8,128)S(1)}, f32[24,1152]{1,0:T(8,128)S(1)}, u32[]{:S(2)}, u32[]{:S(2)}) collective-permute-start(f32[24,1152]{1,0:T(8,128)S(1)} %add.95), channel_id=1, source_target_pairs={{0,4},{4,0},{8,12},{12,8},{16,20},{20,16},{24,28},{28,24},{1,5},{5... | collective-permute-start | bytes 331784 | tf_op jit(solution)/shard_map/ppermute | solution.py:1420
  194.7 6.1 %collective-permute-start.39 = (f32[24,1152]{1,0:T(8,128)S(1)}, f32[24,1152]{1,0:T(8,128)S(1)}, u32[]{:S(2)}, u32[]{:S(2)}) collective-permute-start(f32[24,1152]{1,0:T(8,128)S(1)} %add.96), channel_id=1, source_target_pairs={{0,8},{4,12},{8,0},{12,4},{16,24},{20,28},{24,16},{28,20},{1,9},{5... | collective-permute-start | bytes 331784 | tf_op jit(solution)/shard_map/ppermute | solution.py:1420
  200.8 5.7 %collective-permute-start.40 = (f32[24,1152]{1,0:T(8,128)S(1)}, f32[24,1152]{1,0:T(8,128)S(1)}, u32[]{:S(2)}, u32[]{:S(2)}) collective-permute-start(f32[24,1152]{1,0:T(8,128)S(1)} %add.97), channel_id=1, source_target_pairs={{0,16},{4,20},{8,24},{12,28},{16,0},{20,4},{24,8},{28,12},{1,17},{... | collective-permute-start | bytes 331784 | tf_op jit(solution)/shard_map/ppermute | solution.py:1420
  206.5 3.6 %collective-permute-start.37 = (bf16[12,128,256]{2,1,0:T(8,128)(2,1)S(1)}, bf16[12,128,256]{2,1,0:T(8,128)(2,1)S(1)}, u32[]{:S(2)}, u32[]{:S(2)}) collective-permute-start(bf16[12,128,256]{2,1,0:T(8,128)(2,1)S(1)} %add_convert_fusion.shard0), channel_id=1, source_target_pairs={{0,1},{1,0},{2,3},{3,2},{4,5},{5,4},{6,7},{7,6},{8,9},{9,8},{10,11... | collective-permute-start | bytes 2359304 | tf_op jit(solution)/shard_map/ppermute | solution.py:1418
  206.6 3.5 %collective-permute-start.41 = (bf16[12,128,256]{2,1,0:T(8,128)(2,1)S(1)}, bf16[12,128,256]{2,1,0:T(8,128)(2,1)S(1)}, u32[]{:S(2)}, u32[]{:S(2)}) collective-permute-start(bf16[12,128,256]{2,1,0:T(8,128)(2,1)S(1)} %collective-permute-done.36.shard1), channel_id=1, source_target_pairs={{0,1},{1,0},{2,3},{3,2},{4,5},{5,4},{6,7},{7,6},{8,9},{9,8},{10,11... | collective-permute-start | bytes 2359304 | tf_op jit(solution)/shard_map/ppermute | solution.py:1422
  207.1 3.1 %collective-permute-start.42 = (f32[24,1152]{1,0:T(8,128)S(1)}, f32[24,1152]{1,0:T(8,128)S(1)}, u32[]{:S(2)}, u32[]{:S(2)}) collective-permute-start(f32[24,1152]{1,0:T(8,128)S(1)} %add.98.small_own), channel_id=1, source_target_pairs={{0,1},{1,0},{2,3},{3,2},{4,5},{5,4},{6,7},{7,6},{8,9},{9,8},{10,11... | collective-permute-start | bytes 331784 | tf_op jit(solution)/shard_map/ppermute | solution.py:1421
  (43 other events, 387.0 us)

commit v5 on v4

--- a/solution.py
+++ b/solution.py
@@ -1257,6 +1257,7 @@
         [VMEM_FULL] * 4,
         VMEM_FULL,
         (query_key_value, out_weight, up_weight, down_weight),
+        vmem=60 << 20,
     )
     up_own = mix_up.T
     up_pair = jnp.concatenate([up_own, after(lax.ppermute(up_own, "fsdp", Y_SWAP), piece)], axis=1)
@@ -1298,6 +1299,7 @@
                 norm_bias,
             ),
             scratch=[pltpu.VMEM((4, ROWS, width), jnp.float32)],
+            vmem=36 << 20,
         )
         across = lax.ppermute(packet, "replica", X_SWAP)
         beside = lax.ppermute(packet, "replica", CORE_SWAP)
@@ -1338,6 +1340,7 @@
             pltpu.SemaphoreType.DMA((9,)),
             pltpu.SemaphoreType.DMA((3, 5)),
         ],
+        vmem=38 << 20,
     )
     chunks = results[:9]
     keep_own, keep_far, send_norm, keep_out, send_out = results[9:]
@@ -1438,6 +1441,7 @@
         (VMEM_FULL,) * 10,
         (shard, shard_across, shard_beside, shard_both, small, small_beside),
         scratch=[pltpu.VMEM((48, width + 128), jnp.float32)],
+        vmem=14 << 20,
     )
     projection_grad, out_grad, up_grad, down_grad, *small_grads = owned
     shape = (micro_total, local_seqs, SEQ)

time: 218 us -> 211 us (0.968)
  Pallas kernels: 56.8 us -> 50.1 us
  local copies, waits for them, and re-layouts: 6.53 us -> 0.87 us
  starting transfers between devices: 37.4 us -> 42 us
    pallas_call x4, Pallas kernels: 43.7 us -> 37.2 us  [call(): pl.pallas_call(kernel, out_shape=outs, in_specs=specs, out_specs=out_spec...]
    unnamed x96 -> x58, local copies, waits for them, and re-layouts: 5.88 us -> 0.73 us
    ppermute x20, starting transfers between devices: 15.7 us -> 18.9 us  [fsdp_move(): lax.ppermute(value, 'fsdp' if len(pairs) == 8 else ('fsdp', 'replica'), p...]
  transfers between devices with their start and end apart: 43 -> 43, of which waited for: 23 -> 24; matrix products, arithmetic and copies ran while one was open for 4% -> 4% of each run, Pallas kernels for 12% -> 11%
where the time goes in v5:
time: 211 us
  waiting for transfers between devices  107 us (51%)
  Pallas kernels  50.1 us (24%)
  starting transfers between devices  42 us (20%)
  other arithmetic  9.87 us (5%)
    ppermute x20, waiting for transfers between devices, fsdp_move(): lax.ppermute(value, 'fsdp' if len(pairs) == 8 else ('fsdp', 'replica'), p...  74.4 us
    pallas_call x4, Pallas kernels, call(): pl.pallas_call(kernel, out_shape=outs, in_specs=specs, out_specs=out_spec...  37.2 us
    ppermute x20, starting transfers between devices, fsdp_move(): lax.ppermute(value, 'fsdp' if len(pairs) == 8 else ('fsdp', 'replica'), p...  18.9 us
    pallas_call x1, Pallas kernels, back(): pl.pallas_call(back_kernel, grid=(1,), out_shape=(shape_of((seqs, STREAMS...  12.9 us
    ppermute x3, waiting for transfers between devices, on_device_tensor(): small = small + lax.ppermute(small, 'fsdp', perm)  12.2 us
    ppermute x3, starting transfers between devices, on_device_tensor(): lax.ppermute(up_pair, 'fsdp', z_pairs([((step + to) % 4, to) for to in ra...  5.57 us
    convert_element_type x5, other arithmetic, low(): return value.astype(jnp.bfloat16)  4.82 us
    ppermute x3, starting transfers between devices, on_device_tensor(): small = small + lax.ppermute(small, 'fsdp', perm)  4.73 us
  transfers between devices with their start and end apart: 43, of which 24 were waited for; matrix products, arithmetic and copies ran while one was open for 4% of the time, Pallas kernels for 11%

profile of v5, /device:TPU:0, one launch (start us, length us, event | category | flops | bytes accessed | tf_op | source)
XLA Modules:
  0.0 210.8 jit_solution(5554177287899845441)
XLA Ops:
  0.7 3.0 %collective-permute-start = (bf16[36,128]{1,0:T(8,128)(2,1)}, bf16[36,128]{1,0:T(8,128)(2,1)S(1)}, u32[]{:S(2)}, u32[]{:S(2)}) collective-permute-start(bf16[36,128]{1,0:T(8,128)(2,1)} %bitcast.49), channel_id=1, source_target_pairs={{0,4},{4,0},{8,12},{12,8},{16,20},{20,16},{24,28},{28,24},{1,5},{5... | collective-permute-start | bytes 27656 | tf_op jit(solution)/shard_map/ppermute | solution.py:1263
  3.8 3.1 %shard_map.246.piece0 = bf16[12,128,256]{2,1,0:T(8,128)(2,1)} custom-call(bf16[3,128,1024]{2,1,0:T(8,128)(2,1)} %projection.1, bf16[128,1024]{1,0:T(8,128)(2,1)} %out_weight.1, bf16[128,4096]{1,0:T(8,128)(2,1)} %up_weight.1, bf16[512,1024]{1,0:T(8,128)(2,1)} %down_weight.1), custom_call_target="tpu_custom_call" | custom-call | tf_op jit(solution)/shard_map/pallas_call | solution.py:1202
  6.9 1.6 collective-permute-start.3
  8.5 2.6 %collective-permute-start.2 = (bf16[36,256]{1,0:T(8,128)(2,1)S(1)}, bf16[36,256]{1,0:T(8,128)(2,1)S(1)}, u32[]{:S(2)}, u32[]{:S(2)}) collective-permute-start(bf16[36,256]{1,0:T(8,128)(2,1)S(1)} %pad_maximum_fusion.up_own), channel_id=1, source_target_pairs={{16,0},{20,4},{24,8},{28,12},{0,16},{4,20},{8,24},{12,28},{17,1},{... | collective-permute-start | bytes 55304 | tf_op jit(solution)/shard_map/ppermute | solution.py:1265
  11.1 1.3 collective-permute-start.1
  13.2 1.7 collective-permute-done.1.up_one
  14.9 1.5 collective-permute-start.11
  17.1 1.5 collective-permute-start.7
  19.5 6.3 %shard_map.247 = (bf16[528,1024]{1,0:T(8,128)(2,1)S(1)}, f32[4,128,1024]{2,1,0:T(8,128)S(1)}, f32[3,128,128]{2,1,0:T(8,128)S(1)}, f32[128,1024]{1,0:T(8,128)S(1)}, bf16[36,1024]{1,0:T(8,128)(2,1)S(1)}) custom-call(s32[4]{0:T(128)S(1)} %pad_add_fusion.bounds, bf16[2,9,64,1024]{3,2,1,0:T(8,128)(2,1)S(1)} %bitcast.41, f32[1,1024]{1,0:T(1,128)S(1)} %bitcast.47, ...), custom_call_target="tpu_custom_call" | custom-call | tf_op jit(solution)/shard_map/pallas_call | solution.py:1202
  26.4 8.8 %collective-permute-done.11.piece2 = bf16[12,128,256]{2,1,0:T(8,128)(2,1)} collective-permute-done((bf16[12,128,256]{2,1,0:T(8,128)(2,1)}, bf16[12,128,256]{2,1,0:T(8,128)(2,1)}, u32[]{:S(2)}, u32[]{:S(2)}) %collective-permute-start.11) | collective-permute-done | bytes 786464 | tf_op jit(solution)/shard_map/ppermute | solution.py:403
  35.2 1.5 broadcast_select_fusion.1
  36.8 2.7 %collective-permute-start.14 = (bf16[12,128,256]{2,1,0:T(8,128)(2,1)S(1)}, bf16[12,128,256]{2,1,0:T(8,128)(2,1)S(1)}, u32[]{:S(2)}, u32[]{:S(2)}) collective-permute-start(bf16[12,128,256]{2,1,0:T(8,128)(2,1)S(1)} %get-tuple-element.65), channel_id=1, source_target_pairs={{0,8},{4,12},{8,0},{12,4},{16,24},{20,28},{24,16},{28,20},{1,9},{5... | collective-permute-start | bytes 2359304 | tf_op jit(solution)/shard_map/ppermute | solution.py:403
  39.5 1.5 collective-permute-start.4
  41.8 15.0 %collective-permute-done.14.piece5 = bf16[12,128,256]{2,1,0:T(8,128)(2,1)S(1)} collective-permute-done((bf16[12,128,256]{2,1,0:T(8,128)(2,1)S(1)}, bf16[12,128,256]{2,1,0:T(8,128)(2,1)S(1)}, u32[]{:S(2)}, u32[]{:S(2)}) %collective-permute-start.14) | collective-permute-done | bytes 786464 | tf_op jit(solution)/shard_map/ppermute | solution.py:403
  57.7 1.9 collective-permute-done.15.piece7
  60.4 3.8 %collective-permute-done.4.packet1 = bf16[528,1024]{1,0:T(8,128)(2,1)S(1)} collective-permute-done((bf16[528,1024]{1,0:T(8,128)(2,1)S(1)}, bf16[528,1024]{1,0:T(8,128)(2,1)S(1)}, u32[]{:S(2)}, u32[]{:S(2)}) %collective-permute-start.4) | collective-permute-done | bytes 1081376 | tf_op jit(solution)/shard_map/ppermute | solution.py:1304
  64.7 11.2 %collective-permute-done.17.piece8 = bf16[12,128,256]{2,1,0:T(8,128)(2,1)S(1)} collective-permute-done((bf16[12,128,256]{2,1,0:T(8,128)(2,1)S(1)}, bf16[12,128,256]{2,1,0:T(8,128)(2,1)S(1)}, u32[]{:S(2)}, u32[]{:S(2)}) %collective-permute-start.17) | collective-permute-done | bytes 786464 | tf_op jit(solution)/shard_map/ppermute | solution.py:403
  77.5 1.7 collective-permute-done.9.cotangent3
  79.3 5.0 %collective-permute-done.19.piece10 = bf16[5,128,256]{2,1,0:T(8,128)(2,1)S(1)} collective-permute-done((bf16[5,128,256]{2,1,0:T(8,128)(2,1)S(1)}, bf16[5,128,256]{2,1,0:T(8,128)(2,1)S(1)}, u32[]{:S(2)}, u32[]{:S(2)}) %collective-permute-start.19) | collective-permute-done | bytes 327712 | tf_op jit(solution)/shard_map/ppermute | solution.py:403
  84.3 2.7 %collective-permute-done.18.piece9 = bf16[7,128,256]{2,1,0:T(8,128)(2,1)S(1)} collective-permute-done((bf16[7,128,256]{2,1,0:T(8,128)(2,1)S(1)}, bf16[7,128,256]{2,1,0:T(8,128)(2,1)S(1)}, u32[]{:S(2)}, u32[]{:S(2)}) %collective-permute-start.18) | collective-permute-done | bytes 458784 | tf_op jit(solution)/shard_map/ppermute | solution.py:403
  87.1 24.4 %shard_map.248 = (bf16[7,128,256]{2,1,0:T(8,128)(2,1)S(1)}, bf16[5,128,256]{2,1,0:T(8,128)(2,1)S(1)}, bf16[12,128,256]{2,1,0:T(8,128)(2,1)S(1)}, bf16[12,128,256...) custom-call(f32[3,128,128]{2,1,0:T(8,128)S(1)} %copy-done.11, ...), custom_call_target="tpu_custom_call" | custom-call | tf_op jit(solution)/shard_map/pallas_call | solution.py:1202
  112.8 9.0 %collective-permute-done.24 = bf16[5,128,256]{2,1,0:T(8,128)(2,1)S(1)} collective-permute-done((bf16[5,128,256]{2,1,0:T(8,128)(2,1)S(1)}, bf16[5,128,256]{2,1,0:T(8,128)(2,1)S(1)}, u32[]{:S(2)}, u32[]{:S(2)}) %collective-permute-start.24) | collective-permute-done | bytes 327712 | tf_op jit(solution)/shard_map/ppermute | solution.py:403
  121.9 0.8 collective-permute-start.25
  122.8 1.7 fusion
  125.0 2.3 %collective-permute-start.29 = (bf16[12,128,256]{2,1,0:T(8,128)(2,1)S(1)}, bf16[12,128,256]{2,1,0:T(8,128)(2,1)S(1)}, u32[]{:S(2)}, u32[]{:S(2)}) collective-permute-start(bf16[12,128,256]{2,1,0:T(8,128)(2,1)S(1)} %add_convert_fusion.1), channel_id=1, source_target_pairs={{0,8},{4,12},{8,0},{12,4},{16,24},{20,28},{24,16},{28,20},{1,9},{5... | collective-permute-start | bytes 2359304 | tf_op jit(solution)/shard_map/ppermute | solution.py:403
  127.6 1.0 collective-permute-start.31
  128.6 13.8 %collective-permute-done.25 = bf16[12,128,256]{2,1,0:T(8,128)(2,1)S(1)} collective-permute-done((bf16[12,128,256]{2,1,0:T(8,128)(2,1)S(1)}, bf16[12,128,256]{2,1,0:T(8,128)(2,1)S(1)}, u32[]{:S(2)}, u32[]{:S(2)}) %collective-permute-start.25) | collective-permute-done | bytes 786464 | tf_op jit(solution)/shard_map/ppermute | solution.py:403
  142.5 1.1 collective-permute-done.29
  143.6 1.8 fusion.2
  145.4 1.7 collective-permute-start.26
  147.1 3.9 %collective-permute-done.22.across = bf16[4,128,1024]{2,1,0:T(8,128)(2,1)} collective-permute-done((bf16[4,128,1024]{2,1,0:T(8,128)(2,1)}, bf16[4,128,1024]{2,1,0:T(8,128)(2,1)}, u32[]{:S(2)}, u32[]{:S(2)}) %collective-permute-start.22) | collective-permute-done | bytes 1048608 | tf_op jit(solution)/shard_map/ppermute | solution.py:1350
  150.9 12.9 %shard_map.249 = (bf16[2,9,64,1024]{3,2,1,0:T(8,128)(2,1)}, f32[24,1152]{1,0:T(8,128)}, f32[24,1152]{1,0:T(8,128)}, f32[2,9,4,64]{3,2,1,0:T(4,128)}) custom-call(bf16[2,9,64,1024]{3,2,1,0:T(8,128)(2,1)} %bitcast.40, bf16[128,1024]{1,0:T(8,128)(2,1)} %bitcast.42, f32[4,128,1024]{2,1,0:T(8,128)} %copy-done.2, f32[3,128,128]{2,1,0:T(8,128)} %copy-done.12, ...), custom_call_target="tpu_custom_call" | custom-call | tf_op jit(solution)/shard_map/pallas_call | solution.py:1364
  163.9 2.3 %fusion.6 = (bf16[12,128,256]{2,1,0:T(8,128)(2,1)S(1)}, bf16[12,128,256]{2,1,0:T(8,128)(2,1)S(1)}, bf16[12,128,256]{2,1,0:T(8,128)(2,1)S(1)}) fusion(bf16[12,128,256]{2,1,0:T(8,128)(2,1)} %collective-permute-done.26, bf16[12,128,256]{2,1,0:T(8,128)(2,1)S(1)} %get-tuple-element.81, pred[]{:T(512)S(6)} %eq.15, ...), kind=kLoop, calls=%fused_computation.13 | loop fusion | flops 5898240 | bytes 7077890 | tf_op jit(solution)/shard_map/convert_element_type | solution.py:472
  166.2 0.9 collective-permute-start.27
  167.2 2.0 collective-permute-start.32
  169.8 2.6 %collective-permute-done.34 = f32[24,1152]{1,0:T(8,128)S(1)} collective-permute-done((f32[24,1152]{1,0:T(8,128)S(1)}, f32[24,1152]{1,0:T(8,128)S(1)}, u32[]{:S(2)}, u32[]{:S(2)}) %collective-permute-start.34) | collective-permute-done | bytes 110624 | tf_op jit(solution)/shard_map/ppermute | solution.py:1417
  172.4 2.2 %collective-permute-start.35 = (f32[24,1152]{1,0:T(8,128)S(1)}, f32[24,1152]{1,0:T(8,128)S(1)}, u32[]{:S(2)}, u32[]{:S(2)}) collective-permute-start(f32[24,1152]{1,0:T(8,128)S(1)} %add.94), channel_id=1, source_target_pairs={{0,2},{1,3},{2,0},{3,1},{4,6},{5,7},{6,4},{7,5},{8,10},{9,11},{10,... | collective-permute-start | bytes 331784 | tf_op jit(solution)/shard_map/ppermute | solution.py:1418
  174.8 3.7 %collective-permute-done.35 = f32[24,1152]{1,0:T(8,128)S(1)} collective-permute-done((f32[24,1152]{1,0:T(8,128)S(1)}, f32[24,1152]{1,0:T(8,128)S(1)}, u32[]{:S(2)}, u32[]{:S(2)}) %collective-permute-start.35) | collective-permute-done | bytes 110624 | tf_op jit(solution)/shard_map/ppermute | solution.py:1418
  178.4 4.7 %collective-permute-done.27 = bf16[12,128,256]{2,1,0:T(8,128)(2,1)S(1)} collective-permute-done((bf16[12,128,256]{2,1,0:T(8,128)(2,1)S(1)}, bf16[12,128,256]{2,1,0:T(8,128)(2,1)S(1)}, u32[]{:S(2)}, u32[]{:S(2)}) %collective-permute-start.27) | collective-permute-done | bytes 786464 | tf_op jit(solution)/shard_map/ppermute | solution.py:403
  184.4 2.5 %collective-permute-start.36 = (bf16[12,128,256]{2,1,0:T(8,128)(2,1)S(1)}, bf16[12,128,256]{2,1,0:T(8,128)(2,1)S(1)}, u32[]{:S(2)}, u32[]{:S(2)}) collective-permute-start(bf16[12,128,256]{2,1,0:T(8,128)(2,1)S(1)} %add_convert_fusion.shard0), channel_id=1, source_target_pairs={{0,2},{1,3},{2,0},{3,1},{4,6},{5,7},{6,4},{7,5},{8,10},{9,11},{10,... | collective-permute-start | bytes 2359304 | tf_op jit(solution)/shard_map/ppermute | solution.py:1420
  187.2 4.4 %collective-permute-done.38 = f32[24,1152]{1,0:T(8,128)S(1)} collective-permute-done((f32[24,1152]{1,0:T(8,128)S(1)}, f32[24,1152]{1,0:T(8,128)S(1)}, u32[]{:S(2)}, u32[]{:S(2)}) %collective-permute-start.38) | collective-permute-done | bytes 110624 | tf_op jit(solution)/shard_map/ppermute | solution.py:1423
  191.6 1.8 collective-permute-start.39
  193.4 3.4 %collective-permute-done.39 = f32[24,1152]{1,0:T(8,128)S(1)} collective-permute-done((f32[24,1152]{1,0:T(8,128)S(1)}, f32[24,1152]{1,0:T(8,128)S(1)}, u32[]{:S(2)}, u32[]{:S(2)}) %collective-permute-start.39) | collective-permute-done | bytes 110624 | tf_op jit(solution)/shard_map/ppermute | solution.py:1423
  196.9 2.5 %collective-permute-start.40 = (f32[24,1152]{1,0:T(8,128)S(1)}, f32[24,1152]{1,0:T(8,128)S(1)}, u32[]{:S(2)}, u32[]{:S(2)}) collective-permute-start(f32[24,1152]{1,0:T(8,128)S(1)} %add.97), channel_id=1, source_target_pairs={{0,16},{4,20},{8,24},{12,28},{16,0},{20,4},{24,8},{28,12},{1,17},{... | collective-permute-start | bytes 331784 | tf_op jit(solution)/shard_map/ppermute | solution.py:1423
  199.4 4.4 %collective-permute-done.40 = f32[24,1152]{1,0:T(8,128)S(1)} collective-permute-done((f32[24,1152]{1,0:T(8,128)S(1)}, f32[24,1152]{1,0:T(8,128)S(1)}, u32[]{:S(2)}, u32[]{:S(2)}) %collective-permute-start.40) | collective-permute-done | bytes 110624 | tf_op jit(solution)/shard_map/ppermute | solution.py:1423
  204.5 0.9 fusion.11
  205.3 2.1 collective-permute-done.42.small_other
  207.4 3.4 %shard_map.250 = (f32[3,128,1024]{2,1,0:T(8,128)}, f32[128,1024]{1,0:T(8,128)}, f32[128,4096]{1,0:T(8,128)}, f32[512,1024]{1,0:T(8,128)}, f32[1,1024]{1,0:T(1,12...) custom-call(bf16[12,128,256]{2,1,0:T(8,128)(2,1)S(1)} %add_convert_fus, ...), custom_call_target="tpu_custom_call" | custom-call | tf_op jit(solution)/shard_map/pallas_call | solution.py:1202
  (122 shorter events, 13.0 us)
Async XLA Ops:
  0.7 6.2 %collective-permute-start = (bf16[36,128]{1,0:T(8,128)(2,1)}, bf16[36,128]{1,0:T(8,128)(2,1)S(1)}, u32[]{:S(2)}, u32[]{:S(2)}) collective-permute-start(bf16[36,128]{1,0:T(8,128)(2,1)} %bitcast.49), channel_id=1, source_target_pairs={{0,4},{4,0},{8,12},{12,8},{16,20},{20,16},{24,28},{28,24},{1,5},{5... | collective-permute-start | bytes 27656 | tf_op jit(solution)/shard_map/ppermute | solution.py:1263
  6.9 5.9 %collective-permute-start.3 = (bf16[36,256]{1,0:T(8,128)(2,1)S(1)}, bf16[36,256]{1,0:T(8,128)(2,1)S(1)}, u32[]{:S(2)}, u32[]{:S(2)}) collective-permute-start(bf16[36,256]{1,0:T(8,128)(2,1)S(1)} %pad_maximum_fusion.up_own), channel_id=1, source_target_pairs={{24,0},{28,4},{0,8},{4,12},{8,16},{12,20},{16,24},{20,28},{25,1},{... | collective-permute-start | bytes 55304 | tf_op jit(solution)/shard_map/ppermute | solution.py:1265
  8.5 4.7 %collective-permute-start.2 = (bf16[36,256]{1,0:T(8,128)(2,1)S(1)}, bf16[36,256]{1,0:T(8,128)(2,1)S(1)}, u32[]{:S(2)}, u32[]{:S(2)}) collective-permute-start(bf16[36,256]{1,0:T(8,128)(2,1)S(1)} %pad_maximum_fusion.up_own), channel_id=1, source_target_pairs={{16,0},{20,4},{24,8},{28,12},{0,16},{4,20},{8,24},{12,28},{17,1},{... | collective-permute-start | bytes 55304 | tf_op jit(solution)/shard_map/ppermute | solution.py:1265
  11.1 3.8 %collective-permute-start.1 = (bf16[36,256]{1,0:T(8,128)(2,1)S(1)}, bf16[36,256]{1,0:T(8,128)(2,1)S(1)}, u32[]{:S(2)}, u32[]{:S(2)}) collective-permute-start(bf16[36,256]{1,0:T(8,128)(2,1)S(1)} %pad_maximum_fusion.up_own), channel_id=1, source_target_pairs={{8,0},{12,4},{16,8},{20,12},{24,16},{28,20},{0,24},{4,28},{9,1},{1... | collective-permute-start | bytes 55304 | tf_op jit(solution)/shard_map/ppermute | solution.py:1265
  14.9 11.5 %collective-permute-start.12 = (bf16[12,128,256]{2,1,0:T(8,128)(2,1)}, bf16[12,128,256]{2,1,0:T(8,128)(2,1)S(1)}, u32[]{:S(2)}, u32[]{:S(2)}) collective-permute-start(bf16[12,128,256]{2,1,0:T(8,128)(2,1)} %shard_map.246.piece0), channel_id=1, source_target_pairs={{0,1},{1,0},{2,3},{3,2},{4,5},{5,4},{6,7},{7,6},{8,16},{9,17},{10,... | collective-permute-start | bytes 2359304 | tf_op jit(solution)/shard_map/ppermute | solution.py:403
  14.9 20.3 %collective-permute-start.11 = (bf16[12,128,256]{2,1,0:T(8,128)(2,1)}, bf16[12,128,256]{2,1,0:T(8,128)(2,1)}, u32[]{:S(2)}, u32[]{:S(2)}) collective-permute-start(bf16[12,128,256]{2,1,0:T(8,128)(2,1)} %shard_map.246.piece0), channel_id=1, source_target_pairs={{0,8},{4,12},{8,0},{12,4},{16,24},{20,28},{24,16},{28,20},{1,9},{5... | collective-permute-start | bytes 2359304 | tf_op jit(solution)/shard_map/ppermute | solution.py:403
  16.4 18.8 %collective-permute-start.10 = (bf16[12,128,256]{2,1,0:T(8,128)(2,1)}, bf16[12,128,256]{2,1,0:T(8,128)(2,1)}, u32[]{:S(2)}, u32[]{:S(2)}) collective-permute-start(bf16[12,128,256]{2,1,0:T(8,128)(2,1)} %shard_map.246.piece0), channel_id=1, source_target_pairs={{0,4},{4,0},{8,12},{12,8},{16,20},{20,16},{24,28},{28,24},{1,5},{5... | collective-permute-start | bytes 2359304 | tf_op jit(solution)/shard_map/ppermute | solution.py:403
  17.1 19.6 %collective-permute-start.7 = (bf16[128,1024]{1,0:T(8,128)(2,1)S(1)}, bf16[128,1024]{1,0:T(8,128)(2,1)}, u32[]{:S(2)}, u32[]{:S(2)}) collective-permute-start(bf16[128,1024]{1,0:T(8,128)(2,1)S(1)} %bitcast.43), channel_id=1, source_target_pairs={{0,2},{1,3},{2,0},{3,1},{4,6},{5,7},{6,4},{7,5},{8,10},{9,11},{10,... | collective-permute-start | bytes 786440 | tf_op jit(solution)/shard_map/ppermute | solution.py:1271
  26.4 33.9 %copy-start.3 = (bf16[528,1024]{1,0:T(8,128)(2,1)}, bf16[528,1024]{1,0:T(8,128)(2,1)S(1)}, u32[]{:S(2)}) copy-start(bf16[528,1024]{1,0:T(8,128)(2,1)S(1)} %get-tuple-element.62.packet0) | copy-start | bytes 3244036
  36.7 5.0 %collective-permute-start.13 = (bf16[12,128,256]{2,1,0:T(8,128)(2,1)}, bf16[12,128,256]{2,1,0:T(8,128)(2,1)S(1)}, u32[]{:S(2)}, u32[]{:S(2)}) collective-permute-start(bf16[12,128,256]{2,1,0:T(8,128)(2,1)} %collective-permute-done.11.piece2), channel_id=1, source_target_pairs={{0,1},{1,0},{2,3},{3,2},{4,5},{5,4},{6,7},{7,6},{8,16},{9,17},{10,... | collective-permute-start | bytes 2359304 | tf_op jit(solution)/shard_map/ppermute | solution.py:403
  36.8 20.0 %collective-permute-start.14 = (bf16[12,128,256]{2,1,0:T(8,128)(2,1)S(1)}, bf16[12,128,256]{2,1,0:T(8,128)(2,1)S(1)}, u32[]{:S(2)}, u32[]{:S(2)}) collective-permute-start(bf16[12,128,256]{2,1,0:T(8,128)(2,1)S(1)} %get-tuple-element.65), channel_id=1, source_target_pairs={{0,8},{4,12},{8,0},{12,4},{16,24},{20,28},{24,16},{28,20},{1,9},{5... | collective-permute-start | bytes 2359304 | tf_op jit(solution)/shard_map/ppermute | solution.py:403
  39.5 24.6 %collective-permute-start.4 = (bf16[528,1024]{1,0:T(8,128)(2,1)S(1)}, bf16[528,1024]{1,0:T(8,128)(2,1)S(1)}, u32[]{:S(2)}, u32[]{:S(2)}) collective-permute-start(bf16[528,1024]{1,0:T(8,128)(2,1)S(1)} %get-tuple-element.62.packet0), channel_id=1, source_target_pairs={{0,2},{1,3},{2,0},{3,1},{4,6},{5,7},{6,4},{7,5},{8,10},{9,11},{10,... | collective-permute-start | bytes 3244040 | tf_op jit(solution)/shard_map/ppermute | solution.py:1304
  41.0 46.0 %copy-start.1 = (bf16[12,128,256]{2,1,0:T(8,128)(2,1)S(1)}, bf16[12,128,256]{2,1,0:T(8,128)(2,1)}, u32[]{:S(2)}) copy-start(bf16[12,128,256]{2,1,0:T(8,128)(2,1)} %shard_map.246.piece0) | copy-start | bytes 2359300
  41.0 46.0 %copy-start.11 = (f32[3,128,128]{2,1,0:T(8,128)S(1)}, f32[3,128,128]{2,1,0:T(8,128)}, u32[]{:S(2)}) copy-start(f32[3,128,128]{2,1,0:T(8,128)} %constant.39.clone.rope) | copy-start | bytes 589828
  41.0 18.5 %collective-permute-start.15 = (bf16[12,128,256]{2,1,0:T(8,128)(2,1)S(1)}, bf16[12,128,256]{2,1,0:T(8,128)(2,1)S(1)}, u32[]{:S(2)}, u32[]{:S(2)}) collective-permute-start(bf16[12,128,256]{2,1,0:T(8,128)(2,1)S(1)} %get-tuple-element.125), channel_id=1, source_target_pairs={{0,4},{4,0},{8,12},{12,8},{16,20},{20,16},{24,28},{28,24},{1,5},{5... | collective-permute-start | bytes 2359304 | tf_op jit(solution)/shard_map/ppermute | solution.py:403
  56.9 19.0 %collective-permute-start.17 = (bf16[12,128,256]{2,1,0:T(8,128)(2,1)S(1)}, bf16[12,128,256]{2,1,0:T(8,128)(2,1)S(1)}, u32[]{:S(2)}, u32[]{:S(2)}) collective-permute-start(bf16[12,128,256]{2,1,0:T(8,128)(2,1)S(1)} %broadcast_select_fusion), channel_id=1, source_target_pairs={{0,4},{4,0},{8,12},{12,8},{16,20},{20,16},{24,28},{28,24},{1,5},{5... | collective-permute-start | bytes 2359304 | tf_op jit(solution)/shard_map/ppermute | solution.py:403
  59.6 17.1 %collective-permute-start.16 = (bf16[12,128,256]{2,1,0:T(8,128)(2,1)S(1)}, bf16[12,128,256]{2,1,0:T(8,128)(2,1)S(1)}, u32[]{:S(2)}, u32[]{:S(2)}) collective-permute-start(bf16[12,128,256]{2,1,0:T(8,128)(2,1)S(1)} %collective-permute-done.13.piece4), channel_id=1, source_target_pairs={{0,8},{4,12},{8,0},{12,4},{16,24},{20,28},{24,16},{28,20},{1,9},{5... | collective-permute-start | bytes 2359304 | tf_op jit(solution)/shard_map/ppermute | solution.py:403
  60.4 18.9 %collective-permute-start.5 = (bf16[528,1024]{1,0:T(8,128)(2,1)S(1)}, bf16[528,1024]{1,0:T(8,128)(2,1)S(1)}, u32[]{:S(2)}, u32[]{:S(2)}) collective-permute-start(bf16[528,1024]{1,0:T(8,128)(2,1)S(1)} %get-tuple-element.62.packet0), channel_id=1, source_target_pairs={{0,1},{1,0},{2,3},{3,2},{4,5},{5,4},{6,7},{7,6},{8,9},{9,8},{10,11... | collective-permute-start | bytes 3244040 | tf_op jit(solution)/shard_map/ppermute | solution.py:1305
  64.2 22.9 %copy-start.21 = (bf16[528,1024]{1,0:T(8,128)(2,1)}, bf16[528,1024]{1,0:T(8,128)(2,1)S(1)}, u32[]{:S(2)}) copy-start(bf16[528,1024]{1,0:T(8,128)(2,1)S(1)} %collective-permute-done.4.packet1) | copy-start | bytes 3244036
  64.2 15.1 %collective-permute-start.6 = (bf16[528,1024]{1,0:T(8,128)(2,1)S(1)}, bf16[528,1024]{1,0:T(8,128)(2,1)S(1)}, u32[]{:S(2)}, u32[]{:S(2)}) collective-permute-start(bf16[528,1024]{1,0:T(8,128)(2,1)S(1)} %collective-permute-done.4.packet1), channel_id=1, source_target_pairs={{0,1},{1,0},{2,3},{3,2},{4,5},{5,4},{6,7},{7,6},{8,9},{9,8},{10,11... | collective-permute-start | bytes 3244040 | tf_op jit(solution)/shard_map/ppermute | solution.py:1306
  64.2 13.4 %collective-permute-start.8 = (bf16[128,1024]{1,0:T(8,128)(2,1)S(1)}, bf16[128,1024]{1,0:T(8,128)(2,1)S(1)}, u32[]{:S(2)}, u32[]{:S(2)}) collective-permute-start(bf16[128,1024]{1,0:T(8,128)(2,1)S(1)} %bitcast.44), channel_id=1, source_target_pairs={{0,1},{1,0},{2,3},{3,2},{4,5},{5,4},{6,7},{7,6},{8,9},{9,8},{10,11... | collective-permute-start | bytes 786440 | tf_op jit(solution)/shard_map/ppermute | solution.py:1275
  75.9 11.1 %collective-permute-start.18 = (bf16[7,128,256]{2,1,0:T(8,128)(2,1)S(1)}, bf16[7,128,256]{2,1,0:T(8,128)(2,1)S(1)}, u32[]{:S(2)}, u32[]{:S(2)}) collective-permute-start(bf16[7,128,256]{2,1,0:T(8,128)(2,1)S(1)} %slice.28), channel_id=1, source_target_pairs={{0,8},{4,12},{8,0},{12,4},{16,24},{20,28},{24,16},{28,20},{1,9},{5... | collective-permute-start | bytes 1376264 | tf_op jit(solution)/shard_map/ppermute | solution.py:403
  76.7 7.6 %collective-permute-start.19 = (bf16[5,128,256]{2,1,0:T(8,128)(2,1)S(1)}, bf16[5,128,256]{2,1,0:T(8,128)(2,1)S(1)}, u32[]{:S(2)}, u32[]{:S(2)}) collective-permute-start(bf16[5,128,256]{2,1,0:T(8,128)(2,1)S(1)} %slice.29), channel_id=1, source_target_pairs={{0,4},{4,0},{8,12},{12,8},{16,20},{20,16},{24,28},{28,24},{1,5},{5... | collective-permute-start | bytes 983048 | tf_op jit(solution)/shard_map/ppermute | solution.py:403
  77.5 1.7 collective-permute-start.9
  111.5 11.2 %collective-permute-start.20 = (bf16[2,4,128,1024]{3,2,1,0:T(8,128)(2,1)}, bf16[2,4,128,1024]{3,2,1,0:T(8,128)(2,1)S(1)}, u32[]{:S(2)}, u32[]{:S(2)}) collective-permute-start(bf16[2,4,128,1024]{3,2,1,0:T(8,128)(2,1)} %get-tuple-element.71), channel_id=1, source_target_pairs={{0,1},{1,0},{2,3},{3,2},{4,5},{5,4},{6,7},{7,6},{8,9},{9,8},{10,11... | collective-permute-start | bytes 6291464 | tf_op jit(solution)/shard_map/ppermute | solution.py:1348
  111.6 10.1 %collective-permute-start.24 = (bf16[5,128,256]{2,1,0:T(8,128)(2,1)S(1)}, bf16[5,128,256]{2,1,0:T(8,128)(2,1)S(1)}, u32[]{:S(2)}, u32[]{:S(2)}) collective-permute-start(bf16[5,128,256]{2,1,0:T(8,128)(2,1)S(1)} %get-tuple-element.83), channel_id=1, source_target_pairs={{0,8},{4,12},{8,0},{12,4},{16,24},{20,28},{24,16},{28,20},{1,9},{5... | collective-permute-start | bytes 983048 | tf_op jit(solution)/shard_map/ppermute | solution.py:403
  112.0 12.9 %collective-permute-start.28 = (bf16[7,128,256]{2,1,0:T(8,128)(2,1)S(1)}, bf16[7,128,256]{2,1,0:T(8,128)(2,1)S(1)}, u32[]{:S(2)}, u32[]{:S(2)}) collective-permute-start(bf16[7,128,256]{2,1,0:T(8,128)(2,1)S(1)} %get-tuple-element.82), channel_id=1, source_target_pairs={{0,4},{4,0},{8,12},{12,8},{16,20},{20,16},{24,28},{28,24},{1,5},{5... | collective-permute-start | bytes 1376264 | tf_op jit(solution)/shard_map/ppermute | solution.py:403
  121.9 20.5 %collective-permute-start.25 = (bf16[12,128,256]{2,1,0:T(8,128)(2,1)S(1)}, bf16[12,128,256]{2,1,0:T(8,128)(2,1)S(1)}, u32[]{:S(2)}, u32[]{:S(2)}) collective-permute-start(bf16[12,128,256]{2,1,0:T(8,128)(2,1)S(1)} %add_convert_fusion.2), channel_id=1, source_target_pairs={{0,4},{4,0},{8,12},{12,8},{16,20},{20,16},{24,28},{28,24},{1,5},{5... | collective-permute-start | bytes 2359304 | tf_op jit(solution)/shard_map/ppermute | solution.py:403
  125.0 18.6 %collective-permute-start.29 = (bf16[12,128,256]{2,1,0:T(8,128)(2,1)S(1)}, bf16[12,128,256]{2,1,0:T(8,128)(2,1)S(1)}, u32[]{:S(2)}, u32[]{:S(2)}) collective-permute-start(bf16[12,128,256]{2,1,0:T(8,128)(2,1)S(1)} %add_convert_fusion.1), channel_id=1, source_target_pairs={{0,8},{4,12},{8,0},{12,4},{16,24},{20,28},{24,16},{28,20},{1,9},{5... | collective-permute-start | bytes 2359304 | tf_op jit(solution)/shard_map/ppermute | solution.py:403
  127.3 23.7 %collective-permute-start.22 = (bf16[4,128,1024]{2,1,0:T(8,128)(2,1)}, bf16[4,128,1024]{2,1,0:T(8,128)(2,1)}, u32[]{:S(2)}, u32[]{:S(2)}) collective-permute-start(bf16[4,128,1024]{2,1,0:T(8,128)(2,1)} %fusion), channel_id=1, source_target_pairs={{0,2},{1,3},{2,0},{3,1},{4,6},{5,7},{6,4},{7,5},{8,10},{9,11},{10,... | collective-permute-start | bytes 3145736 | tf_op jit(solution)/shard_map/ppermute | solution.py:1350
  127.6 36.3 %collective-permute-start.31 = (bf16[12,128,256]{2,1,0:T(8,128)(2,1)}, bf16[12,128,256]{2,1,0:T(8,128)(2,1)S(1)}, u32[]{:S(2)}, u32[]{:S(2)}) collective-permute-start(bf16[12,128,256]{2,1,0:T(8,128)(2,1)} %get-tuple-element.90), channel_id=1, source_target_pairs={{0,4},{4,0},{8,12},{12,8},{16,20},{20,16},{24,28},{28,24},{1,5},{5... | collective-permute-start | bytes 2359304 | tf_op jit(solution)/shard_map/ppermute | solution.py:403
  145.4 18.5 %collective-permute-start.26 = (bf16[12,128,256]{2,1,0:T(8,128)(2,1)}, bf16[12,128,256]{2,1,0:T(8,128)(2,1)}, u32[]{:S(2)}, u32[]{:S(2)}) collective-permute-start(bf16[12,128,256]{2,1,0:T(8,128)(2,1)} %get-tuple-element.123), channel_id=1, source_target_pairs={{0,8},{4,12},{8,0},{12,4},{16,24},{20,28},{24,16},{28,20},{1,9},{5... | collective-permute-start | bytes 2359304 | tf_op jit(solution)/shard_map/ppermute | solution.py:403
  147.1 16.8 %collective-permute-start.30 = (bf16[12,128,256]{2,1,0:T(8,128)(2,1)}, bf16[12,128,256]{2,1,0:T(8,128)(2,1)}, u32[]{:S(2)}, u32[]{:S(2)}) collective-permute-start(bf16[12,128,256]{2,1,0:T(8,128)(2,1)} %get-tuple-element.124), channel_id=1, source_target_pairs={{0,1},{1,0},{2,3},{3,2},{4,5},{5,4},{6,7},{7,6},{8,16},{9,17},{10,... | collective-permute-start | bytes 2359304 | tf_op jit(solution)/shard_map/ppermute | solution.py:403
  166.2 16.9 %collective-permute-start.27 = (bf16[12,128,256]{2,1,0:T(8,128)(2,1)S(1)}, bf16[12,128,256]{2,1,0:T(8,128)(2,1)S(1)}, u32[]{:S(2)}, u32[]{:S(2)}) collective-permute-start(bf16[12,128,256]{2,1,0:T(8,128)(2,1)S(1)} %get-tuple-element.120), channel_id=1, source_target_pairs={{0,4},{4,0},{8,12},{12,8},{16,20},{20,16},{24,28},{28,24},{1,5},{5... | collective-permute-start | bytes 2359304 | tf_op jit(solution)/shard_map/ppermute | solution.py:403
  167.2 16.7 %collective-permute-start.32 = (bf16[12,128,256]{2,1,0:T(8,128)(2,1)S(1)}, bf16[12,128,256]{2,1,0:T(8,128)(2,1)S(1)}, u32[]{:S(2)}, u32[]{:S(2)}) collective-permute-start(bf16[12,128,256]{2,1,0:T(8,128)(2,1)S(1)} %get-tuple-element.92), channel_id=1, source_target_pairs={{0,8},{4,12},{8,0},{12,4},{16,24},{20,28},{24,16},{28,20},{1,9},{5... | collective-permute-start | bytes 2359304 | tf_op jit(solution)/shard_map/ppermute | solution.py:403
  169.2 14.7 %collective-permute-start.33 = (bf16[12,128,256]{2,1,0:T(8,128)(2,1)S(1)}, bf16[12,128,256]{2,1,0:T(8,128)(2,1)S(1)}, u32[]{:S(2)}, u32[]{:S(2)}) collective-permute-start(bf16[12,128,256]{2,1,0:T(8,128)(2,1)S(1)} %get-tuple-element.93), channel_id=1, source_target_pairs={{0,1},{1,0},{2,3},{3,2},{4,5},{5,4},{6,7},{7,6},{8,16},{9,17},{10,... | collective-permute-start | bytes 2359304 | tf_op jit(solution)/shard_map/ppermute | solution.py:403
  169.2 5.4 %collective-permute-start.21 = (bf16[2,128,1024]{2,1,0:T(8,128)(2,1)S(1)}, bf16[2,128,1024]{2,1,0:T(8,128)(2,1)S(1)}, u32[]{:S(2)}, u32[]{:S(2)}) collective-permute-start(bf16[2,128,1024]{2,1,0:T(8,128)(2,1)S(1)} %copy-done.19), channel_id=1, source_target_pairs={{0,1},{1,0},{2,3},{3,2},{4,5},{5,4},{6,7},{7,6},{8,9},{9,8},{10,11... | collective-permute-start | bytes 1572872 | tf_op jit(solution)/shard_map/ppermute | solution.py:1351
  169.7 2.7 %collective-permute-start.34 = (f32[24,1152]{1,0:T(8,128)S(1)}, f32[24,1152]{1,0:T(8,128)S(1)}, u32[]{:S(2)}, u32[]{:S(2)}) collective-permute-start(f32[24,1152]{1,0:T(8,128)S(1)} %copy-done.28), channel_id=1, source_target_pairs={{0,1},{1,0},{2,3},{3,2},{4,5},{5,4},{6,7},{7,6},{8,9},{9,8},{10,11... | collective-permute-start | bytes 331784 | tf_op jit(solution)/shard_map/ppermute | solution.py:1417
  172.4 6.0 %collective-permute-start.35 = (f32[24,1152]{1,0:T(8,128)S(1)}, f32[24,1152]{1,0:T(8,128)S(1)}, u32[]{:S(2)}, u32[]{:S(2)}) collective-permute-start(f32[24,1152]{1,0:T(8,128)S(1)} %add.94), channel_id=1, source_target_pairs={{0,2},{1,3},{2,0},{3,1},{4,6},{5,7},{6,4},{7,5},{8,10},{9,11},{10,... | collective-permute-start | bytes 331784 | tf_op jit(solution)/shard_map/ppermute | solution.py:1418
  174.7 9.7 %collective-permute-start.23 = (bf16[128,1024]{1,0:T(8,128)(2,1)S(1)}, bf16[128,1024]{1,0:T(8,128)(2,1)S(1)}, u32[]{:S(2)}, u32[]{:S(2)}) collective-permute-start(bf16[128,1024]{1,0:T(8,128)(2,1)S(1)} %fusion.12), channel_id=1, source_target_pairs={{0,2},{1,3},{2,0},{3,1},{4,6},{5,7},{6,4},{7,5},{8,10},{9,11},{10,... | collective-permute-start | bytes 786440 | tf_op jit(solution)/shard_map/ppermute | solution.py:1353
  183.9 20.6 %copy-start.8 = (f32[128,1024]{1,0:T(8,128)S(1)}, f32[128,1024]{1,0:T(8,128)}, u32[]{:S(2)}) copy-start(f32[128,1024]{1,0:T(8,128)} %copy-done.7) | copy-start | bytes 1572868
  184.4 19.5 %collective-permute-start.36 = (bf16[12,128,256]{2,1,0:T(8,128)(2,1)S(1)}, bf16[12,128,256]{2,1,0:T(8,128)(2,1)S(1)}, u32[]{:S(2)}, u32[]{:S(2)}) collective-permute-start(bf16[12,128,256]{2,1,0:T(8,128)(2,1)S(1)} %add_convert_fusion.shard0), channel_id=1, source_target_pairs={{0,2},{1,3},{2,0},{3,1},{4,6},{5,7},{6,4},{7,5},{8,10},{9,11},{10,... | collective-permute-start | bytes 2359304 | tf_op jit(solution)/shard_map/ppermute | solution.py:1420
  186.8 4.7 %collective-permute-start.38 = (f32[24,1152]{1,0:T(8,128)S(1)}, f32[24,1152]{1,0:T(8,128)S(1)}, u32[]{:S(2)}, u32[]{:S(2)}) collective-permute-start(f32[24,1152]{1,0:T(8,128)S(1)} %add.95), channel_id=1, source_target_pairs={{0,4},{4,0},{8,12},{12,8},{16,20},{20,16},{24,28},{28,24},{1,5},{5... | collective-permute-start | bytes 331784 | tf_op jit(solution)/shard_map/ppermute | solution.py:1423
  191.6 5.3 %collective-permute-start.39 = (f32[24,1152]{1,0:T(8,128)S(1)}, f32[24,1152]{1,0:T(8,128)S(1)}, u32[]{:S(2)}, u32[]{:S(2)}) collective-permute-start(f32[24,1152]{1,0:T(8,128)S(1)} %add.96), channel_id=1, source_target_pairs={{0,8},{4,12},{8,0},{12,4},{16,24},{20,28},{24,16},{28,20},{1,9},{5... | collective-permute-start | bytes 331784 | tf_op jit(solution)/shard_map/ppermute | solution.py:1423
  196.9 6.9 %collective-permute-start.40 = (f32[24,1152]{1,0:T(8,128)S(1)}, f32[24,1152]{1,0:T(8,128)S(1)}, u32[]{:S(2)}, u32[]{:S(2)}) collective-permute-start(f32[24,1152]{1,0:T(8,128)S(1)} %add.97), channel_id=1, source_target_pairs={{0,16},{4,20},{8,24},{12,28},{16,0},{20,4},{24,8},{28,12},{1,17},{... | collective-permute-start | bytes 331784 | tf_op jit(solution)/shard_map/ppermute | solution.py:1423
  203.8 3.6 %collective-permute-start.37 = (bf16[12,128,256]{2,1,0:T(8,128)(2,1)S(1)}, bf16[12,128,256]{2,1,0:T(8,128)(2,1)S(1)}, u32[]{:S(2)}, u32[]{:S(2)}) collective-permute-start(bf16[12,128,256]{2,1,0:T(8,128)(2,1)S(1)} %add_convert_fusion.shard0), channel_id=1, source_target_pairs={{0,1},{1,0},{2,3},{3,2},{4,5},{5,4},{6,7},{7,6},{8,9},{9,8},{10,11... | collective-permute-start | bytes 2359304 | tf_op jit(solution)/shard_map/ppermute | solution.py:1421
  203.9 3.6 %collective-permute-start.41 = (bf16[12,128,256]{2,1,0:T(8,128)(2,1)S(1)}, bf16[12,128,256]{2,1,0:T(8,128)(2,1)S(1)}, u32[]{:S(2)}, u32[]{:S(2)}) collective-permute-start(bf16[12,128,256]{2,1,0:T(8,128)(2,1)S(1)} %collective-permute-done.36.shard1), channel_id=1, source_target_pairs={{0,1},{1,0},{2,3},{3,2},{4,5},{5,4},{6,7},{7,6},{8,9},{9,8},{10,11... | collective-permute-start | bytes 2359304 | tf_op jit(solution)/shard_map/ppermute | solution.py:1425
  204.4 3.1 %collective-permute-start.42 = (f32[24,1152]{1,0:T(8,128)S(1)}, f32[24,1152]{1,0:T(8,128)S(1)}, u32[]{:S(2)}, u32[]{:S(2)}) collective-permute-start(f32[24,1152]{1,0:T(8,128)S(1)} %add.98.small_own), channel_id=1, source_target_pairs={{0,1},{1,0},{2,3},{3,2},{4,5},{5,4},{6,7},{7,6},{8,9},{9,8},{10,11... | collective-permute-start | bytes 331784 | tf_op jit(solution)/shard_map/ppermute | solution.py:1424
  (24 other events, 268.6 us)

commit v6 on v5

--- a/solution.py
+++ b/solution.py
@@ -575,8 +575,8 @@
     streams,
 ):
     seqs = stack.shape[0]
-    z, y, _, _ = position()
-    for step, part in enumerate((up_own, up_one, up_two, up_three)):
+    z, y, _, core = position()
+    for step, part in ((0, up_own), (1 + 2 * core, up_one), (2, up_two), (3 - 2 * core, up_three)):
         z_from = (z + step) % 4
         for half, col in enumerate((y, 1 - y)):
             lanes = pl.ds(pl.multiple_of((2 * z_from + col) * 128, 128), 128)
@@ -894,32 +894,35 @@
 
     lax.fori_loop(0, 4, hidden, 0)
 
-    def weights(index, carry):
-        cols = pl.ds(pl.multiple_of(index * 128, 128), 128)
+    def weights(pair, carry):
+        cols = pl.ds(pl.multiple_of(pair * 256, 256), 256)
+        halves = (slice(0, 128), slice(128, 256))
         grad = outer_sum(acts[3, :, cols], grad_pre[...]).astype(jnp.bfloat16)
         for block in range(4):
-            parts[index, block] = grad[:, block * 256 : block * 256 + 256]
+            for half, rows in enumerate(halves):
+                parts[2 * pair + half, block] = grad[rows, block * 256 : block * 256 + 256]
         for stream in range(3):
-            parts[index, 4 + stream] = outer_sum(acts[stream, :, cols], grad_lin[stream]).astype(
-                jnp.bfloat16
-            )
+            grad = outer_sum(acts[stream, :, cols], grad_lin[stream]).astype(jnp.bfloat16)
+            for half, rows in enumerate(halves):
+                parts[2 * pair + half, 4 + stream] = grad[rows]
         grad = outer_sum(lhs_all[:, cols], acts[4]).astype(jnp.bfloat16)
-        other = index + 1 - 2 * (index % 2)
-        for block in range(4):
-            part = grad[:, block * 256 : block * 256 + 256]
-            parts[index, 7 + block, 0:96] = part[0:96]
-
-            @pl.when(index % 2 == core)
-            def _():
-                parts[other, 11, block * 32 : block * 32 + 32] = part[96:128]
-
-            @pl.when(index % 2 != core)
-            def _():
-                parts[index, 7 + block, 96:128] = part[96:128]
+        for half in range(2):
+            index, other = 2 * pair + half, 2 * pair + 1 - half
+            for block in range(4):
+                part = grad[half * 128 : half * 128 + 128, block * 256 : block * 256 + 256]
+                parts[index, 7 + block, 0:96] = part[0:96]
+
+                @pl.when(core == half)
+                def _():
+                    parts[other, 11, block * 32 : block * 32 + 32] = part[96:128]
+
+                @pl.when(core != half)
+                def _():
+                    parts[index, 7 + block, 96:128] = part[96:128]
 
         return carry
 
-    lax.fori_loop(0, 8, weights, 0)
+    lax.fori_loop(0, 4, weights, 0)
     grad = outer_sum(lhs_all[:, WIDTH:], acts[4]).astype(jnp.bfloat16)
     for block in range(4):
         part = grad[:, block * 256 : block * 256 + 256]
@@ -1261,11 +1264,15 @@
     )
     up_own = mix_up.T
     up_pair = jnp.concatenate([up_own, after(lax.ppermute(up_own, "fsdp", Y_SWAP), piece)], axis=1)
-    ups = [up_pair] + [
-        lax.ppermute(up_pair, "fsdp", z_pairs([((step + to) % 4, to) for to in range(4)]))
-        for step in (1, 2, 3)
-    ]
+    up_one = fsdp_move(
+        up_pair,
+        [((index + 8 + index % 2 * 16) % 32, index) for index in range(32)],
+    )
+    up_two = fsdp_move(up_pair, Z_SWAP_FAR)
+    ups = (up_pair, up_one, up_two)
     piece = after(piece, *ups)
+    up_three = lax.ppermute(up_one, "replica", CORE_SWAP)
+    ups += (up_three,)
     bounds = jnp.concatenate([pic_start.reshape(seqs), doc_split.reshape(seqs)])
     kept = {}
     grad_across = lax.ppermute(cotangent, "replica", X_SWAP)
@@ -1416,10 +1423,11 @@
 
     small = small + lax.ppermute(small_other, "replica", CORE_SWAP)
     small = small + lax.ppermute(small, "replica", X_SWAP)
+    small = small + lax.ppermute(small, "fsdp", Y_SWAP)
     shard = after(shard, small, out_across)
     shard_across = lax.ppermute(shard, "replica", X_SWAP)
     shard_beside = lax.ppermute(shard, "replica", CORE_SWAP)
-    for perm in (Y_SWAP, Z_SWAP_NEAR, Z_SWAP_FAR):
+    for perm in (Z_SWAP_NEAR, Z_SWAP_FAR):
         small = small + lax.ppermute(small, "fsdp", perm)
     small_beside = lax.ppermute(small, "replica", CORE_SWAP)
     shard_both = lax.ppermute(after(shard_across, small), "replica", CORE_SWAP)

time: 211 us -> 207 us (0.981)
  waiting for transfers between devices: 107 us -> 103 us
    ppermute x3 -> x2, waiting for transfers between devices: 12.2 us -> 6.15 us  [on_device_tensor(): small = small + lax.ppermute(small, 'fsdp', perm)]
    ppermute x1, waiting for transfers between devices: 0.01 us -> 4.82 us  [on_device_tensor(): shard_across = lax.ppermute(shard, 'replica', X_SWAP)]
    ppermute x3 -> x2, starting transfers between devices: 5.57 us -> 0.98 us  [the longest x1 0.98 us: on_device_tensor(): small = small + lax.ppermute(small, 'fsdp', Y_SWAP)]
    ppermute x20 -> x22, starting transfers between devices: 18.9 us -> 22.4 us  [fsdp_move(): lax.ppermute(value, 'fsdp' if len(pairs) == 8 else ('fsdp', 'replica'), p...]
    ppermute x20 -> x22, waiting for transfers between devices: 74.4 us -> 70.9 us  [fsdp_move(): lax.ppermute(value, 'fsdp' if len(pairs) == 8 else ('fsdp', 'replica'), p...]
    ppermute x3 -> x2, waiting for transfers between devices: 2.43 us -> 5.41 us  [the longest x1 5.07 us: on_device_tensor(): small = small + lax.ppermute(small, 'fsdp', Y_SWAP)]
    ppermute x3 -> x2, starting transfers between devices: 4.73 us -> 5.22 us  [on_device_tensor(): small = small + lax.ppermute(small, 'fsdp', perm)]
where the time goes in v6:
time: 207 us
  waiting for transfers between devices  103 us (50%)
  Pallas kernels  49.3 us (24%)
  starting transfers between devices  42.6 us (21%)
  other arithmetic  9.19 us (4%)
    ppermute x22, waiting for transfers between devices, fsdp_move(): lax.ppermute(value, 'fsdp' if len(pairs) == 8 else ('fsdp', 'replica'), p...  70.9 us
    pallas_call x4, Pallas kernels, call(): pl.pallas_call(kernel, out_shape=outs, in_specs=specs, out_specs=out_spec...  36.4 us
    ppermute x22, starting transfers between devices, fsdp_move(): lax.ppermute(value, 'fsdp' if len(pairs) == 8 else ('fsdp', 'replica'), p...  22.4 us
    pallas_call x1, Pallas kernels, back(): pl.pallas_call(back_kernel, grid=(1,), out_shape=(shape_of((seqs, STREAMS...  12.9 us
    ppermute x2, waiting for transfers between devices, on_device_tensor(): small = small + lax.ppermute(small, 'fsdp', perm)  6.15 us
    ppermute x2, starting transfers between devices, on_device_tensor(): small = small + lax.ppermute(small, 'fsdp', perm)  5.22 us
    ppermute x1, waiting for transfers between devices, on_device_tensor(): small = small + lax.ppermute(small, 'fsdp', Y_SWAP)  5.07 us
    convert_element_type x5, other arithmetic, low(): return value.astype(jnp.bfloat16)  4.82 us
  transfers between devices with their start and end apart: 43, of which 24 were waited for; matrix products, arithmetic and copies ran while one was open for 4% of the time, Pallas kernels for 11%

profile of v6, /device:TPU:0, one launch (start us, length us, event | category | flops | bytes accessed | tf_op | source)
XLA Modules:
  0.0 207.2 jit_solution(7689010553960039378)
XLA Ops:
  0.7 3.0 %collective-permute-start = (bf16[36,128]{1,0:T(8,128)(2,1)}, bf16[36,128]{1,0:T(8,128)(2,1)S(1)}, u32[]{:S(2)}, u32[]{:S(2)}) collective-permute-start(bf16[36,128]{1,0:T(8,128)(2,1)} %bitcast.49), channel_id=1, source_target_pairs={{0,4},{4,0},{8,12},{12,8},{16,20},{20,16},{24,28},{28,24},{1,5},{5... | collective-permute-start | bytes 27656 | tf_op jit(solution)/shard_map/ppermute | solution.py:1266
  3.8 3.1 %shard_map.246.piece0 = bf16[12,128,256]{2,1,0:T(8,128)(2,1)} custom-call(bf16[3,128,1024]{2,1,0:T(8,128)(2,1)} %projection.1, bf16[128,1024]{1,0:T(8,128)(2,1)} %out_weight.1, bf16[128,4096]{1,0:T(8,128)(2,1)} %up_weight.1, bf16[512,1024]{1,0:T(8,128)(2,1)} %down_weight.1), custom_call_target="tpu_custom_call" | custom-call | tf_op jit(solution)/shard_map/pallas_call | solution.py:1205
  6.9 2.7 %collective-permute-start.2 = (bf16[36,256]{1,0:T(8,128)(2,1)S(1)}, bf16[36,256]{1,0:T(8,128)(2,1)S(1)}, u32[]{:S(2)}, u32[]{:S(2)}) collective-permute-start(bf16[36,256]{1,0:T(8,128)(2,1)S(1)} %pad_maximum_fusion.up_own), channel_id=1, source_target_pairs={{0,16},{4,20},{8,24},{12,28},{16,0},{20,4},{24,8},{28,12},{1,17},{... | collective-permute-start | bytes 55304 | tf_op jit(solution)/shard_map/ppermute | solution.py:403
  9.6 1.3 collective-permute-start.1
  11.7 1.9 collective-permute-done.1.up_one
  13.6 1.4 collective-permute-start.11
  15.8 1.5 collective-permute-start.7
  18.5 6.3 %shard_map.247 = (bf16[528,1024]{1,0:T(8,128)(2,1)S(1)}, f32[4,128,1024]{2,1,0:T(8,128)S(1)}, f32[3,128,128]{2,1,0:T(8,128)S(1)}, f32[128,1024]{1,0:T(8,128)S(1)}, bf16[36,1024]{1,0:T(8,128)(2,1)S(1)}) custom-call(s32[4]{0:T(128)S(1)} %pad_add_fusion.bounds, bf16[2,9,64,1024]{3,2,1,0:T(8,128)(2,1)S(1)} %bitcast.41, f32[1,1024]{1,0:T(1,128)S(1)} %bitcast.47, ...), custom_call_target="tpu_custom_call" | custom-call | tf_op jit(solution)/shard_map/pallas_call | solution.py:1205
  25.4 8.5 %collective-permute-done.11.piece2 = bf16[12,128,256]{2,1,0:T(8,128)(2,1)} collective-permute-done((bf16[12,128,256]{2,1,0:T(8,128)(2,1)}, bf16[12,128,256]{2,1,0:T(8,128)(2,1)}, u32[]{:S(2)}, u32[]{:S(2)}) %collective-permute-start.11) | collective-permute-done | bytes 786464 | tf_op jit(solution)/shard_map/ppermute | solution.py:403
  33.9 1.5 broadcast_select_fusion.1
  35.5 2.4 %collective-permute-start.14 = (bf16[12,128,256]{2,1,0:T(8,128)(2,1)S(1)}, bf16[12,128,256]{2,1,0:T(8,128)(2,1)S(1)}, u32[]{:S(2)}, u32[]{:S(2)}) collective-permute-start(bf16[12,128,256]{2,1,0:T(8,128)(2,1)S(1)} %get-tuple-element.65), channel_id=1, source_target_pairs={{0,8},{4,12},{8,0},{12,4},{16,24},{20,28},{24,16},{28,20},{1,9},{5... | collective-permute-start | bytes 2359304 | tf_op jit(solution)/shard_map/ppermute | solution.py:403
  37.9 1.5 collective-permute-start.4
  40.1 15.3 %collective-permute-done.14.piece5 = bf16[12,128,256]{2,1,0:T(8,128)(2,1)S(1)} collective-permute-done((bf16[12,128,256]{2,1,0:T(8,128)(2,1)S(1)}, bf16[12,128,256]{2,1,0:T(8,128)(2,1)S(1)}, u32[]{:S(2)}, u32[]{:S(2)}) %collective-permute-start.14) | collective-permute-done | bytes 786464 | tf_op jit(solution)/shard_map/ppermute | solution.py:403
  56.3 1.0 collective-permute-done.15.piece7
  57.4 1.9 collective-permute-start.16
  59.3 3.1 %collective-permute-done.4.packet1 = bf16[528,1024]{1,0:T(8,128)(2,1)S(1)} collective-permute-done((bf16[528,1024]{1,0:T(8,128)(2,1)S(1)}, bf16[528,1024]{1,0:T(8,128)(2,1)S(1)}, u32[]{:S(2)}, u32[]{:S(2)}) %collective-permute-start.4) | collective-permute-done | bytes 1081376 | tf_op jit(solution)/shard_map/ppermute | solution.py:1311
  63.0 11.3 %collective-permute-done.17.piece8 = bf16[12,128,256]{2,1,0:T(8,128)(2,1)S(1)} collective-permute-done((bf16[12,128,256]{2,1,0:T(8,128)(2,1)S(1)}, bf16[12,128,256]{2,1,0:T(8,128)(2,1)S(1)}, u32[]{:S(2)}, u32[]{:S(2)}) %collective-permute-start.17) | collective-permute-done | bytes 786464 | tf_op jit(solution)/shard_map/ppermute | solution.py:403
  76.2 1.7 collective-permute-done.9.cotangent3
  78.0 5.1 %collective-permute-done.19.piece10 = bf16[5,128,256]{2,1,0:T(8,128)(2,1)S(1)} collective-permute-done((bf16[5,128,256]{2,1,0:T(8,128)(2,1)S(1)}, bf16[5,128,256]{2,1,0:T(8,128)(2,1)S(1)}, u32[]{:S(2)}, u32[]{:S(2)}) %collective-permute-start.19) | collective-permute-done | bytes 327712 | tf_op jit(solution)/shard_map/ppermute | solution.py:403
  83.1 2.2 %collective-permute-done.18.piece9 = bf16[7,128,256]{2,1,0:T(8,128)(2,1)S(1)} collective-permute-done((bf16[7,128,256]{2,1,0:T(8,128)(2,1)S(1)}, bf16[7,128,256]{2,1,0:T(8,128)(2,1)S(1)}, u32[]{:S(2)}, u32[]{:S(2)}) %collective-permute-start.18) | collective-permute-done | bytes 458784 | tf_op jit(solution)/shard_map/ppermute | solution.py:403
  85.3 23.6 %shard_map.248 = (bf16[7,128,256]{2,1,0:T(8,128)(2,1)S(1)}, bf16[5,128,256]{2,1,0:T(8,128)(2,1)S(1)}, bf16[12,128,256]{2,1,0:T(8,128)(2,1)S(1)}, bf16[12,128,256...) custom-call(f32[3,128,128]{2,1,0:T(8,128)S(1)} %copy-done.11, ...), custom_call_target="tpu_custom_call" | custom-call | tf_op jit(solution)/shard_map/pallas_call | solution.py:1205
  109.0 1.2 collective-permute-start.24
  110.9 8.2 %collective-permute-done.24 = bf16[5,128,256]{2,1,0:T(8,128)(2,1)S(1)} collective-permute-done((bf16[5,128,256]{2,1,0:T(8,128)(2,1)S(1)}, bf16[5,128,256]{2,1,0:T(8,128)(2,1)S(1)}, u32[]{:S(2)}, u32[]{:S(2)}) %collective-permute-start.24) | collective-permute-done | bytes 327712 | tf_op jit(solution)/shard_map/ppermute | solution.py:403
  120.2 1.7 fusion
  121.8 1.7 collective-permute-done.28
  123.7 1.0 collective-permute-start.29
  124.7 1.5 collective-permute-start.22
  126.9 13.5 %collective-permute-done.25 = bf16[12,128,256]{2,1,0:T(8,128)(2,1)S(1)} collective-permute-done((bf16[12,128,256]{2,1,0:T(8,128)(2,1)S(1)}, bf16[12,128,256]{2,1,0:T(8,128)(2,1)S(1)}, u32[]{:S(2)}, u32[]{:S(2)}) %collective-permute-start.25) | collective-permute-done | bytes 786464 | tf_op jit(solution)/shard_map/ppermute | solution.py:403
  140.4 1.3 collective-permute-done.29
  141.7 1.8 fusion.2
  144.5 3.9 %collective-permute-done.22.across = bf16[4,128,1024]{2,1,0:T(8,128)(2,1)} collective-permute-done((bf16[4,128,1024]{2,1,0:T(8,128)(2,1)}, bf16[4,128,1024]{2,1,0:T(8,128)(2,1)}, u32[]{:S(2)}, u32[]{:S(2)}) %collective-permute-start.22) | collective-permute-done | bytes 1048608 | tf_op jit(solution)/shard_map/ppermute | solution.py:1357
  148.3 12.9 %shard_map.249 = (bf16[2,9,64,1024]{3,2,1,0:T(8,128)(2,1)}, f32[24,1152]{1,0:T(8,128)}, f32[24,1152]{1,0:T(8,128)}, f32[2,9,4,64]{3,2,1,0:T(4,128)}) custom-call(bf16[2,9,64,1024]{3,2,1,0:T(8,128)(2,1)} %bitcast.40, bf16[128,1024]{1,0:T(8,128)(2,1)} %bitcast.42, f32[4,128,1024]{2,1,0:T(8,128)} %copy-done.2, f32[3,128,128]{2,1,0:T(8,128)} %copy-done.12, ...), custom_call_target="tpu_custom_call" | custom-call | tf_op jit(solution)/shard_map/pallas_call | solution.py:1371
  161.3 2.3 %fusion.6 = (bf16[12,128,256]{2,1,0:T(8,128)(2,1)S(1)}, bf16[12,128,256]{2,1,0:T(8,128)(2,1)S(1)}, bf16[12,128,256]{2,1,0:T(8,128)(2,1)S(1)}) fusion(bf16[12,128,256]{2,1,0:T(8,128)(2,1)} %collective-permute-done.26, bf16[12,128,256]{2,1,0:T(8,128)(2,1)S(1)} %get-tuple-element.81, pred[]{:T(512)S(6)} %eq.15, ...), kind=kLoop, calls=%fused_computation.13 | loop fusion | flops 5898240 | bytes 7077890 | tf_op jit(solution)/shard_map/convert_element_type | solution.py:472
  164.5 2.2 %collective-permute-start.32 = (bf16[12,128,256]{2,1,0:T(8,128)(2,1)S(1)}, bf16[12,128,256]{2,1,0:T(8,128)(2,1)S(1)}, u32[]{:S(2)}, u32[]{:S(2)}) collective-permute-start(bf16[12,128,256]{2,1,0:T(8,128)(2,1)S(1)} %get-tuple-element.92), channel_id=1, source_target_pairs={{0,8},{4,12},{8,0},{12,4},{16,24},{20,28},{24,16},{28,20},{1,9},{5... | collective-permute-start | bytes 2359304 | tf_op jit(solution)/shard_map/ppermute | solution.py:403
  167.3 2.6 %collective-permute-done.34 = f32[24,1152]{1,0:T(8,128)S(1)} collective-permute-done((f32[24,1152]{1,0:T(8,128)S(1)}, f32[24,1152]{1,0:T(8,128)S(1)}, u32[]{:S(2)}, u32[]{:S(2)}) %collective-permute-start.34) | collective-permute-done | bytes 110624 | tf_op jit(solution)/shard_map/ppermute | solution.py:1424
  169.9 2.2 %collective-permute-start.35 = (f32[24,1152]{1,0:T(8,128)S(1)}, f32[24,1152]{1,0:T(8,128)S(1)}, u32[]{:S(2)}, u32[]{:S(2)}) collective-permute-start(f32[24,1152]{1,0:T(8,128)S(1)} %add.94), channel_id=1, source_target_pairs={{0,2},{1,3},{2,0},{3,1},{4,6},{5,7},{6,4},{7,5},{8,10},{9,11},{10,... | collective-permute-start | bytes 331784 | tf_op jit(solution)/shard_map/ppermute | solution.py:1425
  172.1 3.4 %collective-permute-done.35 = f32[24,1152]{1,0:T(8,128)S(1)} collective-permute-done((f32[24,1152]{1,0:T(8,128)S(1)}, f32[24,1152]{1,0:T(8,128)S(1)}, u32[]{:S(2)}, u32[]{:S(2)}) %collective-permute-start.35) | collective-permute-done | bytes 110624 | tf_op jit(solution)/shard_map/ppermute | solution.py:1425
  175.5 1.0 collective-permute-start.36
  176.5 1.3 collective-permute-start.23
  177.8 5.1 %collective-permute-done.36 = f32[24,1152]{1,0:T(8,128)S(1)} collective-permute-done((f32[24,1152]{1,0:T(8,128)S(1)}, f32[24,1152]{1,0:T(8,128)S(1)}, u32[]{:S(2)}, u32[]{:S(2)}) %collective-permute-start.36) | collective-permute-done | bytes 110624 | tf_op jit(solution)/shard_map/ppermute | solution.py:1426
  183.8 1.2 collective-permute-start.37
  185.1 2.0 collective-permute-start.39
  187.0 3.4 %collective-permute-done.39 = f32[24,1152]{1,0:T(8,128)S(1)} collective-permute-done((f32[24,1152]{1,0:T(8,128)S(1)}, f32[24,1152]{1,0:T(8,128)S(1)}, u32[]{:S(2)}, u32[]{:S(2)}) %collective-permute-start.39) | collective-permute-done | bytes 110624 | tf_op jit(solution)/shard_map/ppermute | solution.py:1431
  190.5 3.2 %collective-permute-start.40 = (f32[24,1152]{1,0:T(8,128)S(1)}, f32[24,1152]{1,0:T(8,128)S(1)}, u32[]{:S(2)}, u32[]{:S(2)}) collective-permute-start(f32[24,1152]{1,0:T(8,128)S(1)} %add.97), channel_id=1, source_target_pairs={{0,16},{4,20},{8,24},{12,28},{16,0},{20,4},{24,8},{28,12},{1,17},{... | collective-permute-start | bytes 331784 | tf_op jit(solution)/shard_map/ppermute | solution.py:1431
  193.7 2.7 %collective-permute-done.40 = f32[24,1152]{1,0:T(8,128)S(1)} collective-permute-done((f32[24,1152]{1,0:T(8,128)S(1)}, f32[24,1152]{1,0:T(8,128)S(1)}, u32[]{:S(2)}, u32[]{:S(2)}) %collective-permute-start.40) | collective-permute-done | bytes 110624 | tf_op jit(solution)/shard_map/ppermute | solution.py:1431
  196.6 4.8 %collective-permute-done.37.shard1 = bf16[12,128,256]{2,1,0:T(8,128)(2,1)S(1)} collective-permute-done((bf16[12,128,256]{2,1,0:T(8,128)(2,1)S(1)}, bf16[12,128,256]{2,1,0:T(8,128)(2,1)S(1)}, u32[]{:S(2)}, u32[]{:S(2)}) %collective-permute-start.37) | collective-permute-done | bytes 786464 | tf_op jit(solution)/shard_map/ppermute | solution.py:1428
  202.7 1.1 collective-permute-done.42.small_other
  203.8 3.4 %shard_map.250 = (f32[3,128,1024]{2,1,0:T(8,128)}, f32[128,1024]{1,0:T(8,128)}, f32[128,4096]{1,0:T(8,128)}, f32[512,1024]{1,0:T(8,128)}, f32[1,1024]{1,0:T(1,12...) custom-call(bf16[12,128,256]{2,1,0:T(8,128)(2,1)S(1)} %add_convert_fus, ...), custom_call_target="tpu_custom_call" | custom-call | tf_op jit(solution)/shard_map/pallas_call | solution.py:1205
  (124 shorter events, 14.9 us)
Async XLA Ops:
  0.7 6.2 %collective-permute-start = (bf16[36,128]{1,0:T(8,128)(2,1)}, bf16[36,128]{1,0:T(8,128)(2,1)S(1)}, u32[]{:S(2)}, u32[]{:S(2)}) collective-permute-start(bf16[36,128]{1,0:T(8,128)(2,1)} %bitcast.49), channel_id=1, source_target_pairs={{0,4},{4,0},{8,12},{12,8},{16,20},{20,16},{24,28},{28,24},{1,5},{5... | collective-permute-start | bytes 27656 | tf_op jit(solution)/shard_map/ppermute | solution.py:1266
  6.9 4.7 %collective-permute-start.2 = (bf16[36,256]{1,0:T(8,128)(2,1)S(1)}, bf16[36,256]{1,0:T(8,128)(2,1)S(1)}, u32[]{:S(2)}, u32[]{:S(2)}) collective-permute-start(bf16[36,256]{1,0:T(8,128)(2,1)S(1)} %pad_maximum_fusion.up_own), channel_id=1, source_target_pairs={{0,16},{4,20},{8,24},{12,28},{16,0},{20,4},{24,8},{28,12},{1,17},{... | collective-permute-start | bytes 55304 | tf_op jit(solution)/shard_map/ppermute | solution.py:403
  9.6 4.0 %collective-permute-start.1 = (bf16[36,256]{1,0:T(8,128)(2,1)S(1)}, bf16[36,256]{1,0:T(8,128)(2,1)S(1)}, u32[]{:S(2)}, u32[]{:S(2)}) collective-permute-start(bf16[36,256]{1,0:T(8,128)(2,1)S(1)} %pad_maximum_fusion.up_own), channel_id=1, source_target_pairs={{8,0},{25,1},{10,2},{27,3},{12,4},{29,5},{14,6},{31,7},{16,8},{1,9... | collective-permute-start | bytes 55304 | tf_op jit(solution)/shard_map/ppermute | solution.py:403
  13.6 11.8 %collective-permute-start.12 = (bf16[12,128,256]{2,1,0:T(8,128)(2,1)}, bf16[12,128,256]{2,1,0:T(8,128)(2,1)S(1)}, u32[]{:S(2)}, u32[]{:S(2)}) collective-permute-start(bf16[12,128,256]{2,1,0:T(8,128)(2,1)} %shard_map.246.piece0), channel_id=1, source_target_pairs={{0,1},{1,0},{2,3},{3,2},{4,5},{5,4},{6,7},{7,6},{8,16},{9,17},{10,... | collective-permute-start | bytes 2359304 | tf_op jit(solution)/shard_map/ppermute | solution.py:403
  13.6 20.3 %collective-permute-start.11 = (bf16[12,128,256]{2,1,0:T(8,128)(2,1)}, bf16[12,128,256]{2,1,0:T(8,128)(2,1)}, u32[]{:S(2)}, u32[]{:S(2)}) collective-permute-start(bf16[12,128,256]{2,1,0:T(8,128)(2,1)} %shard_map.246.piece0), channel_id=1, source_target_pairs={{0,8},{4,12},{8,0},{12,4},{16,24},{20,28},{24,16},{28,20},{1,9},{5... | collective-permute-start | bytes 2359304 | tf_op jit(solution)/shard_map/ppermute | solution.py:403
  15.0 18.8 %collective-permute-start.10 = (bf16[12,128,256]{2,1,0:T(8,128)(2,1)}, bf16[12,128,256]{2,1,0:T(8,128)(2,1)}, u32[]{:S(2)}, u32[]{:S(2)}) collective-permute-start(bf16[12,128,256]{2,1,0:T(8,128)(2,1)} %shard_map.246.piece0), channel_id=1, source_target_pairs={{0,4},{4,0},{8,12},{12,8},{16,20},{20,16},{24,28},{28,24},{1,5},{5... | collective-permute-start | bytes 2359304 | tf_op jit(solution)/shard_map/ppermute | solution.py:403
  15.8 19.6 %collective-permute-start.7 = (bf16[128,1024]{1,0:T(8,128)(2,1)S(1)}, bf16[128,1024]{1,0:T(8,128)(2,1)}, u32[]{:S(2)}, u32[]{:S(2)}) collective-permute-start(bf16[128,1024]{1,0:T(8,128)(2,1)S(1)} %bitcast.43), channel_id=1, source_target_pairs={{0,2},{1,3},{2,0},{3,1},{4,6},{5,7},{6,4},{7,5},{8,10},{9,11},{10,... | collective-permute-start | bytes 786440 | tf_op jit(solution)/shard_map/ppermute | solution.py:1278
  17.2 1.2 collective-permute-start.3
  25.4 34.0 %copy-start.3 = (bf16[528,1024]{1,0:T(8,128)(2,1)}, bf16[528,1024]{1,0:T(8,128)(2,1)S(1)}, u32[]{:S(2)}) copy-start(bf16[528,1024]{1,0:T(8,128)(2,1)S(1)} %get-tuple-element.62.packet0) | copy-start | bytes 3244036
  35.4 4.7 %collective-permute-start.13 = (bf16[12,128,256]{2,1,0:T(8,128)(2,1)}, bf16[12,128,256]{2,1,0:T(8,128)(2,1)S(1)}, u32[]{:S(2)}, u32[]{:S(2)}) collective-permute-start(bf16[12,128,256]{2,1,0:T(8,128)(2,1)} %collective-permute-done.11.piece2), channel_id=1, source_target_pairs={{0,1},{1,0},{2,3},{3,2},{4,5},{5,4},{6,7},{7,6},{8,16},{9,17},{10,... | collective-permute-start | bytes 2359304 | tf_op jit(solution)/shard_map/ppermute | solution.py:403
  35.5 20.0 %collective-permute-start.14 = (bf16[12,128,256]{2,1,0:T(8,128)(2,1)S(1)}, bf16[12,128,256]{2,1,0:T(8,128)(2,1)S(1)}, u32[]{:S(2)}, u32[]{:S(2)}) collective-permute-start(bf16[12,128,256]{2,1,0:T(8,128)(2,1)S(1)} %get-tuple-element.65), channel_id=1, source_target_pairs={{0,8},{4,12},{8,0},{12,4},{16,24},{20,28},{24,16},{28,20},{1,9},{5... | collective-permute-start | bytes 2359304 | tf_op jit(solution)/shard_map/ppermute | solution.py:403
  37.9 24.6 %collective-permute-start.4 = (bf16[528,1024]{1,0:T(8,128)(2,1)S(1)}, bf16[528,1024]{1,0:T(8,128)(2,1)S(1)}, u32[]{:S(2)}, u32[]{:S(2)}) collective-permute-start(bf16[528,1024]{1,0:T(8,128)(2,1)S(1)} %get-tuple-element.62.packet0), channel_id=1, source_target_pairs={{0,2},{1,3},{2,0},{3,1},{4,6},{5,7},{6,4},{7,5},{8,10},{9,11},{10,... | collective-permute-start | bytes 3244040 | tf_op jit(solution)/shard_map/ppermute | solution.py:1311
  39.4 45.9 %copy-start.1 = (bf16[12,128,256]{2,1,0:T(8,128)(2,1)S(1)}, bf16[12,128,256]{2,1,0:T(8,128)(2,1)}, u32[]{:S(2)}) copy-start(bf16[12,128,256]{2,1,0:T(8,128)(2,1)} %shard_map.246.piece0) | copy-start | bytes 2359300
  39.4 45.9 %copy-start.11 = (f32[3,128,128]{2,1,0:T(8,128)S(1)}, f32[3,128,128]{2,1,0:T(8,128)}, u32[]{:S(2)}) copy-start(f32[3,128,128]{2,1,0:T(8,128)} %constant.39.clone.rope) | copy-start | bytes 589828
  39.4 18.0 %collective-permute-start.15 = (bf16[12,128,256]{2,1,0:T(8,128)(2,1)S(1)}, bf16[12,128,256]{2,1,0:T(8,128)(2,1)S(1)}, u32[]{:S(2)}, u32[]{:S(2)}) collective-permute-start(bf16[12,128,256]{2,1,0:T(8,128)(2,1)S(1)} %get-tuple-element.125), channel_id=1, source_target_pairs={{0,4},{4,0},{8,12},{12,8},{16,20},{20,16},{24,28},{28,24},{1,5},{5... | collective-permute-start | bytes 2359304 | tf_op jit(solution)/shard_map/ppermute | solution.py:403
  55.5 18.8 %collective-permute-start.17 = (bf16[12,128,256]{2,1,0:T(8,128)(2,1)S(1)}, bf16[12,128,256]{2,1,0:T(8,128)(2,1)S(1)}, u32[]{:S(2)}, u32[]{:S(2)}) collective-permute-start(bf16[12,128,256]{2,1,0:T(8,128)(2,1)S(1)} %broadcast_select_fusion), channel_id=1, source_target_pairs={{0,4},{4,0},{8,12},{12,8},{16,20},{20,16},{24,28},{28,24},{1,5},{5... | collective-permute-start | bytes 2359304 | tf_op jit(solution)/shard_map/ppermute | solution.py:403
  57.4 18.0 %collective-permute-start.16 = (bf16[12,128,256]{2,1,0:T(8,128)(2,1)S(1)}, bf16[12,128,256]{2,1,0:T(8,128)(2,1)S(1)}, u32[]{:S(2)}, u32[]{:S(2)}) collective-permute-start(bf16[12,128,256]{2,1,0:T(8,128)(2,1)S(1)} %collective-permute-done.13.piece4), channel_id=1, source_target_pairs={{0,8},{4,12},{8,0},{12,4},{16,24},{20,28},{24,16},{28,20},{1,9},{5... | collective-permute-start | bytes 2359304 | tf_op jit(solution)/shard_map/ppermute | solution.py:403
  59.3 18.6 %collective-permute-start.5 = (bf16[528,1024]{1,0:T(8,128)(2,1)S(1)}, bf16[528,1024]{1,0:T(8,128)(2,1)S(1)}, u32[]{:S(2)}, u32[]{:S(2)}) collective-permute-start(bf16[528,1024]{1,0:T(8,128)(2,1)S(1)} %get-tuple-element.62.packet0), channel_id=1, source_target_pairs={{0,1},{1,0},{2,3},{3,2},{4,5},{5,4},{6,7},{7,6},{8,9},{9,8},{10,11... | collective-permute-start | bytes 3244040 | tf_op jit(solution)/shard_map/ppermute | solution.py:1312
  62.5 22.8 %copy-start.21 = (bf16[528,1024]{1,0:T(8,128)(2,1)}, bf16[528,1024]{1,0:T(8,128)(2,1)S(1)}, u32[]{:S(2)}) copy-start(bf16[528,1024]{1,0:T(8,128)(2,1)S(1)} %collective-permute-done.4.packet1) | copy-start | bytes 3244036
  62.5 15.5 %collective-permute-start.6 = (bf16[528,1024]{1,0:T(8,128)(2,1)S(1)}, bf16[528,1024]{1,0:T(8,128)(2,1)S(1)}, u32[]{:S(2)}, u32[]{:S(2)}) collective-permute-start(bf16[528,1024]{1,0:T(8,128)(2,1)S(1)} %collective-permute-done.4.packet1), channel_id=1, source_target_pairs={{0,1},{1,0},{2,3},{3,2},{4,5},{5,4},{6,7},{7,6},{8,9},{9,8},{10,11... | collective-permute-start | bytes 3244040 | tf_op jit(solution)/shard_map/ppermute | solution.py:1313
  62.5 13.7 %collective-permute-start.8 = (bf16[128,1024]{1,0:T(8,128)(2,1)S(1)}, bf16[128,1024]{1,0:T(8,128)(2,1)S(1)}, u32[]{:S(2)}, u32[]{:S(2)}) collective-permute-start(bf16[128,1024]{1,0:T(8,128)(2,1)S(1)} %bitcast.44), channel_id=1, source_target_pairs={{0,1},{1,0},{2,3},{3,2},{4,5},{5,4},{6,7},{7,6},{8,9},{9,8},{10,11... | collective-permute-start | bytes 786440 | tf_op jit(solution)/shard_map/ppermute | solution.py:1282
  74.4 10.9 %collective-permute-start.18 = (bf16[7,128,256]{2,1,0:T(8,128)(2,1)S(1)}, bf16[7,128,256]{2,1,0:T(8,128)(2,1)S(1)}, u32[]{:S(2)}, u32[]{:S(2)}) collective-permute-start(bf16[7,128,256]{2,1,0:T(8,128)(2,1)S(1)} %slice.28), channel_id=1, source_target_pairs={{0,8},{4,12},{8,0},{12,4},{16,24},{20,28},{24,16},{28,20},{1,9},{5... | collective-permute-start | bytes 1376264 | tf_op jit(solution)/shard_map/ppermute | solution.py:403
  75.4 7.7 %collective-permute-start.19 = (bf16[5,128,256]{2,1,0:T(8,128)(2,1)S(1)}, bf16[5,128,256]{2,1,0:T(8,128)(2,1)S(1)}, u32[]{:S(2)}, u32[]{:S(2)}) collective-permute-start(bf16[5,128,256]{2,1,0:T(8,128)(2,1)S(1)} %slice.29), channel_id=1, source_target_pairs={{0,4},{4,0},{8,12},{12,8},{16,20},{20,16},{24,28},{28,24},{1,5},{5... | collective-permute-start | bytes 983048 | tf_op jit(solution)/shard_map/ppermute | solution.py:403
  76.2 1.7 collective-permute-start.9
  108.9 11.2 %collective-permute-start.20 = (bf16[2,4,128,1024]{3,2,1,0:T(8,128)(2,1)}, bf16[2,4,128,1024]{3,2,1,0:T(8,128)(2,1)S(1)}, u32[]{:S(2)}, u32[]{:S(2)}) collective-permute-start(bf16[2,4,128,1024]{3,2,1,0:T(8,128)(2,1)} %get-tuple-element.71), channel_id=1, source_target_pairs={{0,1},{1,0},{2,3},{3,2},{4,5},{5,4},{6,7},{7,6},{8,9},{9,8},{10,11... | collective-permute-start | bytes 6291464 | tf_op jit(solution)/shard_map/ppermute | solution.py:1355
  109.0 10.1 %collective-permute-start.24 = (bf16[5,128,256]{2,1,0:T(8,128)(2,1)S(1)}, bf16[5,128,256]{2,1,0:T(8,128)(2,1)S(1)}, u32[]{:S(2)}, u32[]{:S(2)}) collective-permute-start(bf16[5,128,256]{2,1,0:T(8,128)(2,1)S(1)} %get-tuple-element.83), channel_id=1, source_target_pairs={{0,8},{4,12},{8,0},{12,4},{16,24},{20,28},{24,16},{28,20},{1,9},{5... | collective-permute-start | bytes 983048 | tf_op jit(solution)/shard_map/ppermute | solution.py:403
  110.2 13.4 %collective-permute-start.28 = (bf16[7,128,256]{2,1,0:T(8,128)(2,1)S(1)}, bf16[7,128,256]{2,1,0:T(8,128)(2,1)S(1)}, u32[]{:S(2)}, u32[]{:S(2)}) collective-permute-start(bf16[7,128,256]{2,1,0:T(8,128)(2,1)S(1)} %get-tuple-element.82), channel_id=1, source_target_pairs={{0,4},{4,0},{8,12},{12,8},{16,20},{20,16},{24,28},{28,24},{1,5},{5... | collective-permute-start | bytes 1376264 | tf_op jit(solution)/shard_map/ppermute | solution.py:403
  119.3 21.0 %collective-permute-start.25 = (bf16[12,128,256]{2,1,0:T(8,128)(2,1)S(1)}, bf16[12,128,256]{2,1,0:T(8,128)(2,1)S(1)}, u32[]{:S(2)}, u32[]{:S(2)}) collective-permute-start(bf16[12,128,256]{2,1,0:T(8,128)(2,1)S(1)} %add_convert_fusion.2), channel_id=1, source_target_pairs={{0,4},{4,0},{8,12},{12,8},{16,20},{20,16},{24,28},{28,24},{1,5},{5... | collective-permute-start | bytes 2359304 | tf_op jit(solution)/shard_map/ppermute | solution.py:403
  123.7 18.1 %collective-permute-start.29 = (bf16[12,128,256]{2,1,0:T(8,128)(2,1)S(1)}, bf16[12,128,256]{2,1,0:T(8,128)(2,1)S(1)}, u32[]{:S(2)}, u32[]{:S(2)}) collective-permute-start(bf16[12,128,256]{2,1,0:T(8,128)(2,1)S(1)} %add_convert_fusion.1), channel_id=1, source_target_pairs={{0,8},{4,12},{8,0},{12,4},{16,24},{20,28},{24,16},{28,20},{1,9},{5... | collective-permute-start | bytes 2359304 | tf_op jit(solution)/shard_map/ppermute | solution.py:403
  124.7 23.7 %collective-permute-start.22 = (bf16[4,128,1024]{2,1,0:T(8,128)(2,1)}, bf16[4,128,1024]{2,1,0:T(8,128)(2,1)}, u32[]{:S(2)}, u32[]{:S(2)}) collective-permute-start(bf16[4,128,1024]{2,1,0:T(8,128)(2,1)} %fusion), channel_id=1, source_target_pairs={{0,2},{1,3},{2,0},{3,1},{4,6},{5,7},{6,4},{7,5},{8,10},{9,11},{10,... | collective-permute-start | bytes 3145736 | tf_op jit(solution)/shard_map/ppermute | solution.py:1357
  126.1 35.1 %collective-permute-start.31 = (bf16[12,128,256]{2,1,0:T(8,128)(2,1)}, bf16[12,128,256]{2,1,0:T(8,128)(2,1)S(1)}, u32[]{:S(2)}, u32[]{:S(2)}) collective-permute-start(bf16[12,128,256]{2,1,0:T(8,128)(2,1)} %get-tuple-element.90), channel_id=1, source_target_pairs={{0,4},{4,0},{8,12},{12,8},{16,20},{20,16},{24,28},{28,24},{1,5},{5... | collective-permute-start | bytes 2359304 | tf_op jit(solution)/shard_map/ppermute | solution.py:403
  143.5 17.7 %collective-permute-start.26 = (bf16[12,128,256]{2,1,0:T(8,128)(2,1)}, bf16[12,128,256]{2,1,0:T(8,128)(2,1)}, u32[]{:S(2)}, u32[]{:S(2)}) collective-permute-start(bf16[12,128,256]{2,1,0:T(8,128)(2,1)} %get-tuple-element.123), channel_id=1, source_target_pairs={{0,8},{4,12},{8,0},{12,4},{16,24},{20,28},{24,16},{28,20},{1,9},{5... | collective-permute-start | bytes 2359304 | tf_op jit(solution)/shard_map/ppermute | solution.py:403
  144.5 16.8 %collective-permute-start.30 = (bf16[12,128,256]{2,1,0:T(8,128)(2,1)}, bf16[12,128,256]{2,1,0:T(8,128)(2,1)}, u32[]{:S(2)}, u32[]{:S(2)}) collective-permute-start(bf16[12,128,256]{2,1,0:T(8,128)(2,1)} %get-tuple-element.124), channel_id=1, source_target_pairs={{0,1},{1,0},{2,3},{3,2},{4,5},{5,4},{6,7},{7,6},{8,16},{9,17},{10,... | collective-permute-start | bytes 2359304 | tf_op jit(solution)/shard_map/ppermute | solution.py:403
  163.7 19.3 %collective-permute-start.27 = (bf16[12,128,256]{2,1,0:T(8,128)(2,1)S(1)}, bf16[12,128,256]{2,1,0:T(8,128)(2,1)S(1)}, u32[]{:S(2)}, u32[]{:S(2)}) collective-permute-start(bf16[12,128,256]{2,1,0:T(8,128)(2,1)S(1)} %get-tuple-element.120), channel_id=1, source_target_pairs={{0,4},{4,0},{8,12},{12,8},{16,20},{20,16},{24,28},{28,24},{1,5},{5... | collective-permute-start | bytes 2359304 | tf_op jit(solution)/shard_map/ppermute | solution.py:403
  164.5 18.5 %collective-permute-start.32 = (bf16[12,128,256]{2,1,0:T(8,128)(2,1)S(1)}, bf16[12,128,256]{2,1,0:T(8,128)(2,1)S(1)}, u32[]{:S(2)}, u32[]{:S(2)}) collective-permute-start(bf16[12,128,256]{2,1,0:T(8,128)(2,1)S(1)} %get-tuple-element.92), channel_id=1, source_target_pairs={{0,8},{4,12},{8,0},{12,4},{16,24},{20,28},{24,16},{28,20},{1,9},{5... | collective-permute-start | bytes 2359304 | tf_op jit(solution)/shard_map/ppermute | solution.py:403
  166.7 16.2 %collective-permute-start.33 = (bf16[12,128,256]{2,1,0:T(8,128)(2,1)S(1)}, bf16[12,128,256]{2,1,0:T(8,128)(2,1)S(1)}, u32[]{:S(2)}, u32[]{:S(2)}) collective-permute-start(bf16[12,128,256]{2,1,0:T(8,128)(2,1)S(1)} %get-tuple-element.93), channel_id=1, source_target_pairs={{0,1},{1,0},{2,3},{3,2},{4,5},{5,4},{6,7},{7,6},{8,16},{9,17},{10,... | collective-permute-start | bytes 2359304 | tf_op jit(solution)/shard_map/ppermute | solution.py:403
  166.7 9.7 %collective-permute-start.21 = (bf16[2,128,1024]{2,1,0:T(8,128)(2,1)S(1)}, bf16[2,128,1024]{2,1,0:T(8,128)(2,1)S(1)}, u32[]{:S(2)}, u32[]{:S(2)}) collective-permute-start(bf16[2,128,1024]{2,1,0:T(8,128)(2,1)S(1)} %copy-done.19), channel_id=1, source_target_pairs={{0,1},{1,0},{2,3},{3,2},{4,5},{5,4},{6,7},{7,6},{8,9},{9,8},{10,11... | collective-permute-start | bytes 1572872 | tf_op jit(solution)/shard_map/ppermute | solution.py:1358
  167.2 2.7 %collective-permute-start.34 = (f32[24,1152]{1,0:T(8,128)S(1)}, f32[24,1152]{1,0:T(8,128)S(1)}, u32[]{:S(2)}, u32[]{:S(2)}) collective-permute-start(f32[24,1152]{1,0:T(8,128)S(1)} %copy-done.27), channel_id=1, source_target_pairs={{0,1},{1,0},{2,3},{3,2},{4,5},{5,4},{6,7},{7,6},{8,9},{9,8},{10,11... | collective-permute-start | bytes 331784 | tf_op jit(solution)/shard_map/ppermute | solution.py:1424
  169.9 5.5 %collective-permute-start.35 = (f32[24,1152]{1,0:T(8,128)S(1)}, f32[24,1152]{1,0:T(8,128)S(1)}, u32[]{:S(2)}, u32[]{:S(2)}) collective-permute-start(f32[24,1152]{1,0:T(8,128)S(1)} %add.94), channel_id=1, source_target_pairs={{0,2},{1,3},{2,0},{3,1},{4,6},{5,7},{6,4},{7,5},{8,10},{9,11},{10,... | collective-permute-start | bytes 331784 | tf_op jit(solution)/shard_map/ppermute | solution.py:1425
  175.5 7.4 %collective-permute-start.36 = (f32[24,1152]{1,0:T(8,128)S(1)}, f32[24,1152]{1,0:T(8,128)S(1)}, u32[]{:S(2)}, u32[]{:S(2)}) collective-permute-start(f32[24,1152]{1,0:T(8,128)S(1)} %add.95), channel_id=1, source_target_pairs={{0,4},{4,0},{8,12},{12,8},{16,20},{20,16},{24,28},{28,24},{1,5},{5... | collective-permute-start | bytes 331784 | tf_op jit(solution)/shard_map/ppermute | solution.py:1426
  176.5 7.3 %collective-permute-start.23 = (bf16[128,1024]{1,0:T(8,128)(2,1)S(1)}, bf16[128,1024]{1,0:T(8,128)(2,1)S(1)}, u32[]{:S(2)}, u32[]{:S(2)}) collective-permute-start(bf16[128,1024]{1,0:T(8,128)(2,1)S(1)} %fusion.12), channel_id=1, source_target_pairs={{0,2},{1,3},{2,0},{3,1},{4,6},{5,7},{6,4},{7,5},{8,10},{9,11},{10,... | collective-permute-start | bytes 786440 | tf_op jit(solution)/shard_map/ppermute | solution.py:1360
  182.9 18.9 %copy-start.8 = (f32[128,1024]{1,0:T(8,128)S(1)}, f32[128,1024]{1,0:T(8,128)}, u32[]{:S(2)}) copy-start(f32[128,1024]{1,0:T(8,128)} %copy-done.7) | copy-start | bytes 1572868
  183.8 17.6 %collective-permute-start.37 = (bf16[12,128,256]{2,1,0:T(8,128)(2,1)S(1)}, bf16[12,128,256]{2,1,0:T(8,128)(2,1)S(1)}, u32[]{:S(2)}, u32[]{:S(2)}) collective-permute-start(bf16[12,128,256]{2,1,0:T(8,128)(2,1)S(1)} %add_convert_fusion.shard0), channel_id=1, source_target_pairs={{0,2},{1,3},{2,0},{3,1},{4,6},{5,7},{6,4},{7,5},{8,10},{9,11},{10,... | collective-permute-start | bytes 2359304 | tf_op jit(solution)/shard_map/ppermute | solution.py:1428
  185.1 5.4 %collective-permute-start.39 = (f32[24,1152]{1,0:T(8,128)S(1)}, f32[24,1152]{1,0:T(8,128)S(1)}, u32[]{:S(2)}, u32[]{:S(2)}) collective-permute-start(f32[24,1152]{1,0:T(8,128)S(1)} %add.96), channel_id=1, source_target_pairs={{0,8},{4,12},{8,0},{12,4},{16,24},{20,28},{24,16},{28,20},{1,9},{5... | collective-permute-start | bytes 331784 | tf_op jit(solution)/shard_map/ppermute | solution.py:1431
  190.5 6.0 %collective-permute-start.40 = (f32[24,1152]{1,0:T(8,128)S(1)}, f32[24,1152]{1,0:T(8,128)S(1)}, u32[]{:S(2)}, u32[]{:S(2)}) collective-permute-start(f32[24,1152]{1,0:T(8,128)S(1)} %add.97), channel_id=1, source_target_pairs={{0,16},{4,20},{8,24},{12,28},{16,0},{20,4},{24,8},{28,12},{1,17},{... | collective-permute-start | bytes 331784 | tf_op jit(solution)/shard_map/ppermute | solution.py:1431
  196.5 7.3 %collective-permute-start.38 = (bf16[12,128,256]{2,1,0:T(8,128)(2,1)S(1)}, bf16[12,128,256]{2,1,0:T(8,128)(2,1)S(1)}, u32[]{:S(2)}, u32[]{:S(2)}) collective-permute-start(bf16[12,128,256]{2,1,0:T(8,128)(2,1)S(1)} %add_convert_fusion.shard0), channel_id=1, source_target_pairs={{0,1},{1,0},{2,3},{3,2},{4,5},{5,4},{6,7},{7,6},{8,9},{9,8},{10,11... | collective-permute-start | bytes 2359304 | tf_op jit(solution)/shard_map/ppermute | solution.py:1429
  201.4 2.5 %collective-permute-start.41 = (bf16[12,128,256]{2,1,0:T(8,128)(2,1)S(1)}, bf16[12,128,256]{2,1,0:T(8,128)(2,1)S(1)}, u32[]{:S(2)}, u32[]{:S(2)}) collective-permute-start(bf16[12,128,256]{2,1,0:T(8,128)(2,1)S(1)} %collective-permute-done.37.shard1), channel_id=1, source_target_pairs={{0,1},{1,0},{2,3},{3,2},{4,5},{5,4},{6,7},{7,6},{8,9},{9,8},{10,11... | collective-permute-start | bytes 2359304 | tf_op jit(solution)/shard_map/ppermute | solution.py:1433
  201.4 2.4 %collective-permute-start.42 = (f32[24,1152]{1,0:T(8,128)S(1)}, f32[24,1152]{1,0:T(8,128)S(1)}, u32[]{:S(2)}, u32[]{:S(2)}) collective-permute-start(f32[24,1152]{1,0:T(8,128)S(1)} %add.98.small_own), channel_id=1, source_target_pairs={{0,1},{1,0},{2,3},{3,2},{4,5},{5,4},{6,7},{7,6},{8,9},{9,8},{10,11... | collective-permute-start | bytes 331784 | tf_op jit(solution)/shard_map/ppermute | solution.py:1432
  (25 other events, 279.3 us)

commit v7 on v6

--- a/solution.py
+++ b/solution.py
@@ -399,6 +399,15 @@
 ]
 
 
+MIDDLE_OR_SIDE = [
+    (index, (index ^ 4) if index // 8 in (0, 3) else (24 - index // 8 * 8 + index % 8))
+    for index in range(32)
+]
+SIDE_OR_CORE = [
+    (index, (index ^ 1) if index // 8 in (0, 3) else (index ^ 4)) for index in range(32)
+]
+
+
 def fsdp_move(value, pairs):
     return lax.ppermute(value, "fsdp" if len(pairs) == 8 else ("fsdp", "replica"), pairs)
 
@@ -409,11 +418,11 @@
 def gather_fsdp(piece, z, front):
     inner = (z == 1) | (z == 2)
     near = fsdp_move(piece, Z_NEAR)
-    middle = fsdp_move(piece, Z_MIDDLE)
-    side = fsdp_move(piece, Y_SWAP)
+    middle = fsdp_move(piece, MIDDLE_OR_SIDE)
+    side = fsdp_move(piece, SIDE_OR_CORE)
     early, late = front()
     middle_near = fsdp_move(after(near, *early, side), Z_MIDDLE)
-    turned = fsdp_move(after(pick(inner, middle, side), *early), Z_NEAR)
+    turned = fsdp_move(after(middle, *early), Z_NEAR)
     side_two = fsdp_move(pick(inner, middle, near), Y_SWAP)
     third = pick(inner, middle_near, turned)
     near_twice = fsdp_move(after(middle_near, side_two, third), Z_NEAR)
@@ -701,7 +710,7 @@
     inner = (z == 1) | (z == 2)
     sources = (
         (piece, piece),
-        (side, side),
+        (side, middle),
         (near, near),
         (turned, side_two),
         (middle, turned),
@@ -871,7 +880,7 @@
             grad_lin[2, span, cols] = merge(grad_value, twin).astype(jnp.bfloat16)
         return carry
 
-    lax.fori_loop(0, 4, units, 0)
+    lax.fori_loop(0, 4, units, 0, unroll=2)
 
     for copy in third:
         copy.wait()
@@ -892,7 +901,7 @@
         grad_pre[:, cols] = (grad_gated * slope).astype(jnp.bfloat16)
         return carry
 
-    lax.fori_loop(0, 4, hidden, 0)
+    lax.fori_loop(0, 4, hidden, 0, unroll=4)
 
     def weights(pair, carry):
         cols = pl.ds(pl.multiple_of(pair * 256, 256), 256)
@@ -922,7 +931,7 @@
 
         return carry
 
-    lax.fori_loop(0, 4, weights, 0)
+    lax.fori_loop(0, 4, weights, 0, unroll=2)
     grad = outer_sum(lhs_all[:, WIDTH:], acts[4]).astype(jnp.bfloat16)
     for block in range(4):
         part = grad[:, block * 256 : block * 256 + 256]
@@ -977,7 +986,7 @@
         put(4, cols, matmul(lhs_all[...], jnp.concatenate(right)))
         return carry
 
-    lax.fori_loop(0, 4, feed, 0)
+    lax.fori_loop(0, 4, feed, 0, unroll=2)
     ship(3)
     ship(4)
     for copy in sent:
@@ -1306,7 +1315,7 @@
                 norm_bias,
             ),
             scratch=[pltpu.VMEM((4, ROWS, width), jnp.float32)],
-            vmem=36 << 20,
+            vmem=30 << 20,
         )
         across = lax.ppermute(packet, "replica", X_SWAP)
         beside = lax.ppermute(packet, "replica", CORE_SWAP)
@@ -1347,7 +1356,7 @@
             pltpu.SemaphoreType.DMA((9,)),
             pltpu.SemaphoreType.DMA((3, 5)),
         ],
-        vmem=38 << 20,
+        vmem=42 << 20,
     )
     chunks = results[:9]
     keep_own, keep_far, send_norm, keep_out, send_out = results[9:]

time: 207 us -> 206 us (level)
  waiting for transfers between devices: 103 us -> 99 us
  local copies, waits for them, and re-layouts: 1.56 us -> 5.36 us
    ppermute x22, waiting for transfers between devices: 70.9 us -> 66.2 us  [fsdp_move(): lax.ppermute(value, 'fsdp' if len(pairs) == 8 else ('fsdp', 'replica'), p...]
    unnamed x60 -> x72, local copies, waits for them, and re-layouts: 0.75 us -> 4.54 us
  transfers between devices with their start and end apart: 43 -> 43, of which waited for: 24 -> 25; matrix products, arithmetic and copies ran while one was open for 4% -> 4% of each run, Pallas kernels for 11% -> 11%
where the time goes in v7:
time: 206 us; the launch traced here: 205 us
  waiting for transfers between devices  99 us (48%)
  Pallas kernels  49.3 us (24%)
  starting transfers between devices  41.6 us (20%)
  other arithmetic  8.97 us (4%)
  local copies, waits for them, and re-layouts  5.36 us (3%)
    ppermute x22, waiting for transfers between devices, fsdp_move(): lax.ppermute(value, 'fsdp' if len(pairs) == 8 else ('fsdp', 'replica'), p...  66.2 us
    pallas_call x4, Pallas kernels, call(): pl.pallas_call(kernel, out_shape=outs, in_specs=specs, out_specs=out_spec...  36.2 us
    ppermute x22, starting transfers between devices, fsdp_move(): lax.ppermute(value, 'fsdp' if len(pairs) == 8 else ('fsdp', 'replica'), p...  23.2 us
    pallas_call x1, Pallas kernels, back(): pl.pallas_call(back_kernel, grid=(1,), out_shape=(shape_of((seqs, STREAMS...  13.1 us
    ppermute x2, waiting for transfers between devices, on_device_tensor(): small = small + lax.ppermute(small, 'fsdp', perm)  6.73 us
    ppermute x1, waiting for transfers between devices, on_device_tensor(): small = small + lax.ppermute(small, 'fsdp', Y_SWAP)  5.59 us
    convert_element_type x5, other arithmetic, low(): return value.astype(jnp.bfloat16)  4.89 us
    ppermute x1, waiting for transfers between devices, on_device_tensor(): shard_across = lax.ppermute(shard, 'replica', X_SWAP)  4.87 us
  transfers between devices with their start and end apart: 43, of which 25 were waited for; matrix products, arithmetic and copies ran while one was open for 4% of the time, Pallas kernels for 11%

profile of v7, /device:TPU:0, one launch (start us, length us, event | category | flops | bytes accessed | tf_op | source)
XLA Modules:
  0.0 205.4 jit_solution(1921306501899411486)
XLA Ops:
  0.7 3.0 %collective-permute-start = (bf16[36,128]{1,0:T(8,128)(2,1)}, bf16[36,128]{1,0:T(8,128)(2,1)S(1)}, u32[]{:S(2)}, u32[]{:S(2)}) collective-permute-start(bf16[36,128]{1,0:T(8,128)(2,1)} %bitcast.49), channel_id=1, source_target_pairs={{0,4},{4,0},{8,12},{12,8},{16,20},{20,16},{24,28},{28,24},{1,5},{5... | collective-permute-start | bytes 27656 | tf_op jit(solution)/shard_map/ppermute | solution.py:1275
  3.8 3.1 %shard_map.246.piece0 = bf16[12,128,256]{2,1,0:T(8,128)(2,1)} custom-call(bf16[3,128,1024]{2,1,0:T(8,128)(2,1)} %projection.1, bf16[128,1024]{1,0:T(8,128)(2,1)} %out_weight.1, bf16[128,4096]{1,0:T(8,128)(2,1)} %up_weight.1, bf16[512,1024]{1,0:T(8,128)(2,1)} %down_weight.1), custom_call_target="tpu_custom_call" | custom-call | tf_op jit(solution)/shard_map/pallas_call | solution.py:1214
  6.9 2.7 %collective-permute-start.2 = (bf16[36,256]{1,0:T(8,128)(2,1)S(1)}, bf16[36,256]{1,0:T(8,128)(2,1)S(1)}, u32[]{:S(2)}, u32[]{:S(2)}) collective-permute-start(bf16[36,256]{1,0:T(8,128)(2,1)S(1)} %pad_maximum_fusion.up_own), channel_id=1, source_target_pairs={{0,16},{4,20},{8,24},{12,28},{16,0},{20,4},{24,8},{28,12},{1,17},{... | collective-permute-start | bytes 55304 | tf_op jit(solution)/shard_map/ppermute | solution.py:412
  9.6 1.3 collective-permute-start.1
  11.7 1.9 collective-permute-done.1.up_one
  15.0 1.5 collective-permute-start.7
  17.8 6.3 %shard_map.247 = (bf16[528,1024]{1,0:T(8,128)(2,1)S(1)}, f32[4,128,1024]{2,1,0:T(8,128)S(1)}, f32[3,128,128]{2,1,0:T(8,128)S(1)}, f32[128,1024]{1,0:T(8,128)S(1)}, bf16[36,1024]{1,0:T(8,128)(2,1)S(1)}) custom-call(s32[4]{0:T(128)S(1)} %pad_add_fusion.bounds, bf16[2,9,64,1024]{3,2,1,0:T(8,128)(2,1)S(1)} %bitcast.41, f32[1,1024]{1,0:T(1,128)S(1)} %bitcast.47, ...), custom_call_target="tpu_custom_call" | custom-call | tf_op jit(solution)/shard_map/pallas_call | solution.py:1214
  24.1 1.3 copy-done.2
  28.4 4.6 %collective-permute-done.12.piece3 = bf16[12,128,256]{2,1,0:T(8,128)(2,1)S(1)} collective-permute-done((bf16[12,128,256]{2,1,0:T(8,128)(2,1)}, bf16[12,128,256]{2,1,0:T(8,128)(2,1)S(1)}, u32[]{:S(2)}, u32[]{:S(2)}) %collective-permute-start.12) | collective-permute-done | bytes 786464 | tf_op jit(solution)/shard_map/ppermute | solution.py:412
  33.6 1.7 collective-permute-start.14
  35.3 1.5 collective-permute-start.4
  36.8 1.2 broadcast_select_fusion.1
  38.1 1.4 collective-permute-start.15
  39.5 14.1 %collective-permute-done.14.piece5 = bf16[12,128,256]{2,1,0:T(8,128)(2,1)S(1)} collective-permute-done((bf16[12,128,256]{2,1,0:T(8,128)(2,1)S(1)}, bf16[12,128,256]{2,1,0:T(8,128)(2,1)S(1)}, u32[]{:S(2)}, u32[]{:S(2)}) %collective-permute-start.14) | collective-permute-done | bytes 786464 | tf_op jit(solution)/shard_map/ppermute | solution.py:412
  53.6 1.4 collective-permute-start.17
  56.1 1.6 collective-permute-start.16
  57.7 2.4 %collective-permute-done.4.packet1 = bf16[528,1024]{1,0:T(8,128)(2,1)S(1)} collective-permute-done((bf16[528,1024]{1,0:T(8,128)(2,1)}, bf16[528,1024]{1,0:T(8,128)(2,1)S(1)}, u32[]{:S(2)}, u32[]{:S(2)}) %collective-permute-start.4) | collective-permute-done | bytes 1081376 | tf_op jit(solution)/shard_map/ppermute | solution.py:1320
  60.6 12.3 %collective-permute-done.17.piece8 = bf16[12,128,256]{2,1,0:T(8,128)(2,1)S(1)} collective-permute-done((bf16[12,128,256]{2,1,0:T(8,128)(2,1)S(1)}, bf16[12,128,256]{2,1,0:T(8,128)(2,1)S(1)}, u32[]{:S(2)}, u32[]{:S(2)}) %collective-permute-start.17) | collective-permute-done | bytes 786464 | tf_op jit(solution)/shard_map/ppermute | solution.py:412
  75.1 1.7 collective-permute-done.9.cotangent3
  76.9 5.3 %collective-permute-done.19.piece10 = bf16[5,128,256]{2,1,0:T(8,128)(2,1)S(1)} collective-permute-done((bf16[5,128,256]{2,1,0:T(8,128)(2,1)S(1)}, bf16[5,128,256]{2,1,0:T(8,128)(2,1)S(1)}, u32[]{:S(2)}, u32[]{:S(2)}) %collective-permute-start.19) | collective-permute-done | bytes 327712 | tf_op jit(solution)/shard_map/ppermute | solution.py:412
  82.2 2.2 %collective-permute-done.18.piece9 = bf16[7,128,256]{2,1,0:T(8,128)(2,1)S(1)} collective-permute-done((bf16[7,128,256]{2,1,0:T(8,128)(2,1)S(1)}, bf16[7,128,256]{2,1,0:T(8,128)(2,1)S(1)}, u32[]{:S(2)}, u32[]{:S(2)}) %collective-permute-start.18) | collective-permute-done | bytes 458784 | tf_op jit(solution)/shard_map/ppermute | solution.py:412
  84.4 23.4 %shard_map.248 = (bf16[7,128,256]{2,1,0:T(8,128)(2,1)S(1)}, bf16[5,128,256]{2,1,0:T(8,128)(2,1)S(1)}, bf16[12,128,256]{2,1,0:T(8,128)(2,1)S(1)}, bf16[12,128,256...) custom-call(f32[3,128,128]{2,1,0:T(8,128)S(1)} %copy-done.12, ...), custom_call_target="tpu_custom_call" | custom-call | tf_op jit(solution)/shard_map/pallas_call | solution.py:1214
  109.0 1.3 collective-permute-start.28
  110.3 7.7 %collective-permute-done.24 = bf16[5,128,256]{2,1,0:T(8,128)(2,1)S(1)} collective-permute-done((bf16[5,128,256]{2,1,0:T(8,128)(2,1)S(1)}, bf16[5,128,256]{2,1,0:T(8,128)(2,1)S(1)}, u32[]{:S(2)}, u32[]{:S(2)}) %collective-permute-start.24) | collective-permute-done | bytes 327712 | tf_op jit(solution)/shard_map/ppermute | solution.py:412
  118.3 1.4 collective-permute-start.25
  119.6 1.7 fusion
  123.6 1.4 collective-permute-start.22
  125.0 1.3 collective-permute-start.31
  126.3 13.0 %collective-permute-done.25 = bf16[12,128,256]{2,1,0:T(8,128)(2,1)S(1)} collective-permute-done((bf16[12,128,256]{2,1,0:T(8,128)(2,1)S(1)}, bf16[12,128,256]{2,1,0:T(8,128)(2,1)S(1)}, u32[]{:S(2)}, u32[]{:S(2)}) %collective-permute-start.25) | collective-permute-done | bytes 786464 | tf_op jit(solution)/shard_map/ppermute | solution.py:412
  139.2 1.3 collective-permute-done.29
  140.6 1.9 fusion.2
  143.4 3.8 %collective-permute-done.22.across = bf16[4,128,1024]{2,1,0:T(8,128)(2,1)} collective-permute-done((bf16[4,128,1024]{2,1,0:T(8,128)(2,1)}, bf16[4,128,1024]{2,1,0:T(8,128)(2,1)}, u32[]{:S(2)}, u32[]{:S(2)}) %collective-permute-start.22) | collective-permute-done | bytes 1048608 | tf_op jit(solution)/shard_map/ppermute | solution.py:1366
  147.2 13.1 %shard_map.249 = (bf16[2,9,64,1024]{3,2,1,0:T(8,128)(2,1)}, f32[24,1152]{1,0:T(8,128)}, f32[24,1152]{1,0:T(8,128)}, f32[2,9,4,64]{3,2,1,0:T(4,128)}) custom-call(bf16[2,9,64,1024]{3,2,1,0:T(8,128)(2,1)} %bitcast.40, bf16[128,1024]{1,0:T(8,128)(2,1)} %bitcast.42, f32[4,128,1024]{2,1,0:T(8,128)} %copy-done.2, f32[3,128,128]{2,1,0:T(8,128)} %copy-done.13, ...), custom_call_target="tpu_custom_call" | custom-call | tf_op jit(solution)/shard_map/pallas_call | solution.py:1380
  160.5 2.3 %fusion.6 = (bf16[12,128,256]{2,1,0:T(8,128)(2,1)S(1)}, bf16[12,128,256]{2,1,0:T(8,128)(2,1)S(1)}, bf16[12,128,256]{2,1,0:T(8,128)(2,1)S(1)}) fusion(bf16[12,128,256]{2,1,0:T(8,128)(2,1)} %collective-permute-done.26, bf16[12,128,256]{2,1,0:T(8,128)(2,1)S(1)} %get-tuple-element.81, pred[]{:T(512)S(6)} %eq.15, ...), kind=kLoop, calls=%fused_computation.13 | loop fusion | flops 5898240 | bytes 7077890 | tf_op jit(solution)/shard_map/convert_element_type | solution.py:481
  162.8 1.4 collective-permute-start.27
  164.2 1.3 collective-permute-start.32
  166.0 2.6 %collective-permute-done.34 = f32[24,1152]{1,0:T(8,128)S(1)} collective-permute-done((f32[24,1152]{1,0:T(8,128)S(1)}, f32[24,1152]{1,0:T(8,128)S(1)}, u32[]{:S(2)}, u32[]{:S(2)}) %collective-permute-start.34) | collective-permute-done | bytes 110624 | tf_op jit(solution)/shard_map/ppermute | solution.py:1433
  168.7 1.2 collective-permute-start.35
  169.9 3.9 %collective-permute-done.35 = f32[24,1152]{1,0:T(8,128)S(1)} collective-permute-done((f32[24,1152]{1,0:T(8,128)S(1)}, f32[24,1152]{1,0:T(8,128)S(1)}, u32[]{:S(2)}, u32[]{:S(2)}) %collective-permute-start.35) | collective-permute-done | bytes 110624 | tf_op jit(solution)/shard_map/ppermute | solution.py:1434
  174.7 1.7 collective-permute-start.23
  176.4 5.6 %collective-permute-done.36 = f32[24,1152]{1,0:T(8,128)S(1)} collective-permute-done((f32[24,1152]{1,0:T(8,128)S(1)}, f32[24,1152]{1,0:T(8,128)S(1)}, u32[]{:S(2)}, u32[]{:S(2)}) %collective-permute-start.36) | collective-permute-done | bytes 110624 | tf_op jit(solution)/shard_map/ppermute | solution.py:1435
  182.6 1.4 collective-permute-start.37
  184.0 1.3 collective-permute-start.39
  185.4 3.5 %collective-permute-done.39 = f32[24,1152]{1,0:T(8,128)S(1)} collective-permute-done((f32[24,1152]{1,0:T(8,128)S(1)}, f32[24,1152]{1,0:T(8,128)S(1)}, u32[]{:S(2)}, u32[]{:S(2)}) %collective-permute-start.39) | collective-permute-done | bytes 110624 | tf_op jit(solution)/shard_map/ppermute | solution.py:1440
  188.9 2.5 %collective-permute-start.40 = (f32[24,1152]{1,0:T(8,128)S(1)}, f32[24,1152]{1,0:T(8,128)S(1)}, u32[]{:S(2)}, u32[]{:S(2)}) collective-permute-start(f32[24,1152]{1,0:T(8,128)S(1)} %add.97), channel_id=1, source_target_pairs={{0,16},{4,20},{8,24},{12,28},{16,0},{20,4},{24,8},{28,12},{1,17},{... | collective-permute-start | bytes 331784 | tf_op jit(solution)/shard_map/ppermute | solution.py:1440
  191.4 3.2 %collective-permute-done.40 = f32[24,1152]{1,0:T(8,128)S(1)} collective-permute-done((f32[24,1152]{1,0:T(8,128)S(1)}, f32[24,1152]{1,0:T(8,128)S(1)}, u32[]{:S(2)}, u32[]{:S(2)}) %collective-permute-start.40) | collective-permute-done | bytes 110624 | tf_op jit(solution)/shard_map/ppermute | solution.py:1440
  194.7 4.9 %collective-permute-done.37.shard1 = bf16[12,128,256]{2,1,0:T(8,128)(2,1)S(1)} collective-permute-done((bf16[12,128,256]{2,1,0:T(8,128)(2,1)S(1)}, bf16[12,128,256]{2,1,0:T(8,128)(2,1)S(1)}, u32[]{:S(2)}, u32[]{:S(2)}) %collective-permute-start.37) | collective-permute-done | bytes 786464 | tf_op jit(solution)/shard_map/ppermute | solution.py:1437
  202.0 3.4 %shard_map.250 = (f32[3,128,1024]{2,1,0:T(8,128)}, f32[128,1024]{1,0:T(8,128)}, f32[128,4096]{1,0:T(8,128)}, f32[512,1024]{1,0:T(8,128)}, f32[1,1024]{1,0:T(1,12...) custom-call(bf16[12,128,256]{2,1,0:T(8,128)(2,1)S(1)} %add_convert_fus, ...), custom_call_target="tpu_custom_call" | custom-call | tf_op jit(solution)/shard_map/pallas_call | solution.py:1214
  (136 shorter events, 20.1 us)
Async XLA Ops:
  0.7 6.2 %collective-permute-start = (bf16[36,128]{1,0:T(8,128)(2,1)}, bf16[36,128]{1,0:T(8,128)(2,1)S(1)}, u32[]{:S(2)}, u32[]{:S(2)}) collective-permute-start(bf16[36,128]{1,0:T(8,128)(2,1)} %bitcast.49), channel_id=1, source_target_pairs={{0,4},{4,0},{8,12},{12,8},{16,20},{20,16},{24,28},{28,24},{1,5},{5... | collective-permute-start | bytes 27656 | tf_op jit(solution)/shard_map/ppermute | solution.py:1275
  6.9 4.7 %collective-permute-start.2 = (bf16[36,256]{1,0:T(8,128)(2,1)S(1)}, bf16[36,256]{1,0:T(8,128)(2,1)S(1)}, u32[]{:S(2)}, u32[]{:S(2)}) collective-permute-start(bf16[36,256]{1,0:T(8,128)(2,1)S(1)} %pad_maximum_fusion.up_own), channel_id=1, source_target_pairs={{0,16},{4,20},{8,24},{12,28},{16,0},{20,4},{24,8},{28,12},{1,17},{... | collective-permute-start | bytes 55304 | tf_op jit(solution)/shard_map/ppermute | solution.py:412
  9.6 4.0 %collective-permute-start.1 = (bf16[36,256]{1,0:T(8,128)(2,1)S(1)}, bf16[36,256]{1,0:T(8,128)(2,1)S(1)}, u32[]{:S(2)}, u32[]{:S(2)}) collective-permute-start(bf16[36,256]{1,0:T(8,128)(2,1)S(1)} %pad_maximum_fusion.up_own), channel_id=1, source_target_pairs={{8,0},{25,1},{10,2},{27,3},{12,4},{29,5},{14,6},{31,7},{16,8},{1,9... | collective-permute-start | bytes 55304 | tf_op jit(solution)/shard_map/ppermute | solution.py:412
  13.6 19.5 %collective-permute-start.12 = (bf16[12,128,256]{2,1,0:T(8,128)(2,1)}, bf16[12,128,256]{2,1,0:T(8,128)(2,1)S(1)}, u32[]{:S(2)}, u32[]{:S(2)}) collective-permute-start(bf16[12,128,256]{2,1,0:T(8,128)(2,1)} %shard_map.246.piece0), channel_id=1, source_target_pairs={{0,4},{1,5},{2,6},{3,7},{4,0},{5,1},{6,2},{7,3},{8,16},{9,17},{10,... | collective-permute-start | bytes 2359304 | tf_op jit(solution)/shard_map/ppermute | solution.py:412
  14.3 19.3 %collective-permute-start.11 = (bf16[12,128,256]{2,1,0:T(8,128)(2,1)}, bf16[12,128,256]{2,1,0:T(8,128)(2,1)}, u32[]{:S(2)}, u32[]{:S(2)}) collective-permute-start(bf16[12,128,256]{2,1,0:T(8,128)(2,1)} %shard_map.246.piece0), channel_id=1, source_target_pairs={{0,8},{4,12},{8,0},{12,4},{16,24},{20,28},{24,16},{28,20},{1,9},{5... | collective-permute-start | bytes 2359304 | tf_op jit(solution)/shard_map/ppermute | solution.py:412
  15.0 18.6 %collective-permute-start.10 = (bf16[12,128,256]{2,1,0:T(8,128)(2,1)}, bf16[12,128,256]{2,1,0:T(8,128)(2,1)}, u32[]{:S(2)}, u32[]{:S(2)}) collective-permute-start(bf16[12,128,256]{2,1,0:T(8,128)(2,1)} %shard_map.246.piece0), channel_id=1, source_target_pairs={{0,1},{1,0},{2,3},{3,2},{4,5},{5,4},{6,7},{7,6},{8,12},{9,13},{10,... | collective-permute-start | bytes 2359304 | tf_op jit(solution)/shard_map/ppermute | solution.py:412
  15.0 13.4 %collective-permute-start.7 = (bf16[128,1024]{1,0:T(8,128)(2,1)S(1)}, bf16[128,1024]{1,0:T(8,128)(2,1)}, u32[]{:S(2)}, u32[]{:S(2)}) collective-permute-start(bf16[128,1024]{1,0:T(8,128)(2,1)S(1)} %bitcast.43), channel_id=1, source_target_pairs={{0,2},{1,3},{2,0},{3,1},{4,6},{5,7},{6,4},{7,5},{8,10},{9,11},{10,... | collective-permute-start | bytes 786440 | tf_op jit(solution)/shard_map/ppermute | solution.py:1287
  16.5 1.2 collective-permute-start.3
  33.6 5.9 %collective-permute-start.13 = (bf16[12,128,256]{2,1,0:T(8,128)(2,1)}, bf16[12,128,256]{2,1,0:T(8,128)(2,1)S(1)}, u32[]{:S(2)}, u32[]{:S(2)}) collective-permute-start(bf16[12,128,256]{2,1,0:T(8,128)(2,1)} %collective-permute-done.11.piece2), channel_id=1, source_target_pairs={{0,1},{1,0},{2,3},{3,2},{4,5},{5,4},{6,7},{7,6},{8,16},{9,17},{10,... | collective-permute-start | bytes 2359304 | tf_op jit(solution)/shard_map/ppermute | solution.py:412
  33.6 20.0 %collective-permute-start.14 = (bf16[12,128,256]{2,1,0:T(8,128)(2,1)S(1)}, bf16[12,128,256]{2,1,0:T(8,128)(2,1)S(1)}, u32[]{:S(2)}, u32[]{:S(2)}) collective-permute-start(bf16[12,128,256]{2,1,0:T(8,128)(2,1)S(1)} %collective-permute-done.12.piece3), channel_id=1, source_target_pairs={{0,8},{4,12},{8,0},{12,4},{16,24},{20,28},{24,16},{28,20},{1,9},{5... | collective-permute-start | bytes 2359304 | tf_op jit(solution)/shard_map/ppermute | solution.py:412
  35.3 24.7 %collective-permute-start.4 = (bf16[528,1024]{1,0:T(8,128)(2,1)}, bf16[528,1024]{1,0:T(8,128)(2,1)S(1)}, u32[]{:S(2)}, u32[]{:S(2)}) collective-permute-start(bf16[528,1024]{1,0:T(8,128)(2,1)} %copy-done.3), channel_id=1, source_target_pairs={{0,2},{1,3},{2,0},{3,1},{4,6},{5,7},{6,4},{7,5},{8,10},{9,11},{10,... | collective-permute-start | bytes 3244040 | tf_op jit(solution)/shard_map/ppermute | solution.py:1320
  38.1 46.4 %copy-start.1 = (bf16[12,128,256]{2,1,0:T(8,128)(2,1)S(1)}, bf16[12,128,256]{2,1,0:T(8,128)(2,1)}, u32[]{:S(2)}) copy-start(bf16[12,128,256]{2,1,0:T(8,128)(2,1)} %shard_map.246.piece0) | copy-start | bytes 2359300
  38.1 46.4 %copy-start.12 = (f32[3,128,128]{2,1,0:T(8,128)S(1)}, f32[3,128,128]{2,1,0:T(8,128)}, u32[]{:S(2)}) copy-start(f32[3,128,128]{2,1,0:T(8,128)} %constant.39.clone.rope) | copy-start | bytes 589828
  38.1 18.0 %collective-permute-start.15 = (bf16[12,128,256]{2,1,0:T(8,128)(2,1)S(1)}, bf16[12,128,256]{2,1,0:T(8,128)(2,1)S(1)}, u32[]{:S(2)}, u32[]{:S(2)}) collective-permute-start(bf16[12,128,256]{2,1,0:T(8,128)(2,1)S(1)} %broadcast_select_fusion.1), channel_id=1, source_target_pairs={{0,4},{4,0},{8,12},{12,8},{16,20},{20,16},{24,28},{28,24},{1,5},{5... | collective-permute-start | bytes 2359304 | tf_op jit(solution)/shard_map/ppermute | solution.py:412
  39.5 33.5 %copy-start.22 = (bf16[12,128,256]{2,1,0:T(8,128)(2,1)}, bf16[12,128,256]{2,1,0:T(8,128)(2,1)S(1)}, u32[]{:S(2)}) copy-start(bf16[12,128,256]{2,1,0:T(8,128)(2,1)S(1)} %collective-permute-done.13.piece4) | copy-start | bytes 2359300
  53.6 19.3 %collective-permute-start.17 = (bf16[12,128,256]{2,1,0:T(8,128)(2,1)S(1)}, bf16[12,128,256]{2,1,0:T(8,128)(2,1)S(1)}, u32[]{:S(2)}, u32[]{:S(2)}) collective-permute-start(bf16[12,128,256]{2,1,0:T(8,128)(2,1)S(1)} %broadcast_select_fusion), channel_id=1, source_target_pairs={{0,4},{4,0},{8,12},{12,8},{16,20},{20,16},{24,28},{28,24},{1,5},{5... | collective-permute-start | bytes 2359304 | tf_op jit(solution)/shard_map/ppermute | solution.py:412
  56.1 28.3 %copy-start.30 = (bf16[12,128,256]{2,1,0:T(8,128)(2,1)}, bf16[12,128,256]{2,1,0:T(8,128)(2,1)S(1)}, u32[]{:S(2)}) copy-start(bf16[12,128,256]{2,1,0:T(8,128)(2,1)S(1)} %collective-permute-done.15.piece7) | copy-start | bytes 2359300
  56.1 17.8 %collective-permute-start.16 = (bf16[12,128,256]{2,1,0:T(8,128)(2,1)S(1)}, bf16[12,128,256]{2,1,0:T(8,128)(2,1)S(1)}, u32[]{:S(2)}, u32[]{:S(2)}) collective-permute-start(bf16[12,128,256]{2,1,0:T(8,128)(2,1)S(1)} %collective-permute-done.13.piece4), channel_id=1, source_target_pairs={{0,8},{4,12},{8,0},{12,4},{16,24},{20,28},{24,16},{28,20},{1,9},{5... | collective-permute-start | bytes 2359304 | tf_op jit(solution)/shard_map/ppermute | solution.py:412
  57.7 19.1 %collective-permute-start.5 = (bf16[528,1024]{1,0:T(8,128)(2,1)S(1)}, bf16[528,1024]{1,0:T(8,128)(2,1)S(1)}, u32[]{:S(2)}, u32[]{:S(2)}) collective-permute-start(bf16[528,1024]{1,0:T(8,128)(2,1)S(1)} %copy-done.4), channel_id=1, source_target_pairs={{0,1},{1,0},{2,3},{3,2},{4,5},{5,4},{6,7},{7,6},{8,9},{9,8},{10,11... | collective-permute-start | bytes 3244040 | tf_op jit(solution)/shard_map/ppermute | solution.py:1321
  60.1 24.3 %copy-start.26 = (bf16[528,1024]{1,0:T(8,128)(2,1)}, bf16[528,1024]{1,0:T(8,128)(2,1)S(1)}, u32[]{:S(2)}) copy-start(bf16[528,1024]{1,0:T(8,128)(2,1)S(1)} %collective-permute-done.4.packet1) | copy-start | bytes 3244036
  60.1 16.8 %collective-permute-start.6 = (bf16[528,1024]{1,0:T(8,128)(2,1)S(1)}, bf16[528,1024]{1,0:T(8,128)(2,1)S(1)}, u32[]{:S(2)}, u32[]{:S(2)}) collective-permute-start(bf16[528,1024]{1,0:T(8,128)(2,1)S(1)} %collective-permute-done.4.packet1), channel_id=1, source_target_pairs={{0,1},{1,0},{2,3},{3,2},{4,5},{5,4},{6,7},{7,6},{8,9},{9,8},{10,11... | collective-permute-start | bytes 3244040 | tf_op jit(solution)/shard_map/ppermute | solution.py:1322
  60.1 15.0 %collective-permute-start.8 = (bf16[128,1024]{1,0:T(8,128)(2,1)S(1)}, bf16[128,1024]{1,0:T(8,128)(2,1)S(1)}, u32[]{:S(2)}, u32[]{:S(2)}) collective-permute-start(bf16[128,1024]{1,0:T(8,128)(2,1)S(1)} %bitcast.44), channel_id=1, source_target_pairs={{0,1},{1,0},{2,3},{3,2},{4,5},{5,4},{6,7},{7,6},{8,9},{9,8},{10,11... | collective-permute-start | bytes 786440 | tf_op jit(solution)/shard_map/ppermute | solution.py:1291
  73.0 11.4 %collective-permute-start.18 = (bf16[7,128,256]{2,1,0:T(8,128)(2,1)S(1)}, bf16[7,128,256]{2,1,0:T(8,128)(2,1)S(1)}, u32[]{:S(2)}, u32[]{:S(2)}) collective-permute-start(bf16[7,128,256]{2,1,0:T(8,128)(2,1)S(1)} %slice.28), channel_id=1, source_target_pairs={{0,8},{4,12},{8,0},{12,4},{16,24},{20,28},{24,16},{28,20},{1,9},{5... | collective-permute-start | bytes 1376264 | tf_op jit(solution)/shard_map/ppermute | solution.py:412
  73.9 8.3 %collective-permute-start.19 = (bf16[5,128,256]{2,1,0:T(8,128)(2,1)S(1)}, bf16[5,128,256]{2,1,0:T(8,128)(2,1)S(1)}, u32[]{:S(2)}, u32[]{:S(2)}) collective-permute-start(bf16[5,128,256]{2,1,0:T(8,128)(2,1)S(1)} %slice.29), channel_id=1, source_target_pairs={{0,4},{4,0},{8,12},{12,8},{16,20},{20,16},{24,28},{28,24},{1,5},{5... | collective-permute-start | bytes 983048 | tf_op jit(solution)/shard_map/ppermute | solution.py:412
  75.1 1.7 collective-permute-start.9
  107.9 11.8 %collective-permute-start.20 = (bf16[2,4,128,1024]{3,2,1,0:T(8,128)(2,1)}, bf16[2,4,128,1024]{3,2,1,0:T(8,128)(2,1)S(1)}, u32[]{:S(2)}, u32[]{:S(2)}) collective-permute-start(bf16[2,4,128,1024]{3,2,1,0:T(8,128)(2,1)} %get-tuple-element.71), channel_id=1, source_target_pairs={{0,1},{1,0},{2,3},{3,2},{4,5},{5,4},{6,7},{7,6},{8,9},{9,8},{10,11... | collective-permute-start | bytes 6291464 | tf_op jit(solution)/shard_map/ppermute | solution.py:1364
  107.9 10.1 %collective-permute-start.24 = (bf16[5,128,256]{2,1,0:T(8,128)(2,1)S(1)}, bf16[5,128,256]{2,1,0:T(8,128)(2,1)S(1)}, u32[]{:S(2)}, u32[]{:S(2)}) collective-permute-start(bf16[5,128,256]{2,1,0:T(8,128)(2,1)S(1)} %get-tuple-element.83), channel_id=1, source_target_pairs={{0,8},{4,12},{8,0},{12,4},{16,24},{20,28},{24,16},{28,20},{1,9},{5... | collective-permute-start | bytes 983048 | tf_op jit(solution)/shard_map/ppermute | solution.py:412
  109.0 13.4 %collective-permute-start.28 = (bf16[7,128,256]{2,1,0:T(8,128)(2,1)S(1)}, bf16[7,128,256]{2,1,0:T(8,128)(2,1)S(1)}, u32[]{:S(2)}, u32[]{:S(2)}) collective-permute-start(bf16[7,128,256]{2,1,0:T(8,128)(2,1)S(1)} %get-tuple-element.82), channel_id=1, source_target_pairs={{0,4},{4,0},{8,12},{12,8},{16,20},{20,16},{24,28},{28,24},{1,5},{5... | collective-permute-start | bytes 1376264 | tf_op jit(solution)/shard_map/ppermute | solution.py:412
  118.3 21.0 %collective-permute-start.25 = (bf16[12,128,256]{2,1,0:T(8,128)(2,1)S(1)}, bf16[12,128,256]{2,1,0:T(8,128)(2,1)S(1)}, u32[]{:S(2)}, u32[]{:S(2)}) collective-permute-start(bf16[12,128,256]{2,1,0:T(8,128)(2,1)S(1)} %add_convert_fusion.2), channel_id=1, source_target_pairs={{0,4},{4,0},{8,12},{12,8},{16,20},{20,16},{24,28},{28,24},{1,5},{5... | collective-permute-start | bytes 2359304 | tf_op jit(solution)/shard_map/ppermute | solution.py:412
  122.5 18.1 %collective-permute-start.29 = (bf16[12,128,256]{2,1,0:T(8,128)(2,1)S(1)}, bf16[12,128,256]{2,1,0:T(8,128)(2,1)S(1)}, u32[]{:S(2)}, u32[]{:S(2)}) collective-permute-start(bf16[12,128,256]{2,1,0:T(8,128)(2,1)S(1)} %add_convert_fusion.1), channel_id=1, source_target_pairs={{0,8},{4,12},{8,0},{12,4},{16,24},{20,28},{24,16},{28,20},{1,9},{5... | collective-permute-start | bytes 2359304 | tf_op jit(solution)/shard_map/ppermute | solution.py:412
  123.6 23.7 %collective-permute-start.22 = (bf16[4,128,1024]{2,1,0:T(8,128)(2,1)}, bf16[4,128,1024]{2,1,0:T(8,128)(2,1)}, u32[]{:S(2)}, u32[]{:S(2)}) collective-permute-start(bf16[4,128,1024]{2,1,0:T(8,128)(2,1)} %fusion), channel_id=1, source_target_pairs={{0,2},{1,3},{2,0},{3,1},{4,6},{5,7},{6,4},{7,5},{8,10},{9,11},{10,... | collective-permute-start | bytes 3145736 | tf_op jit(solution)/shard_map/ppermute | solution.py:1366
  125.0 35.4 %collective-permute-start.31 = (bf16[12,128,256]{2,1,0:T(8,128)(2,1)}, bf16[12,128,256]{2,1,0:T(8,128)(2,1)S(1)}, u32[]{:S(2)}, u32[]{:S(2)}) collective-permute-start(bf16[12,128,256]{2,1,0:T(8,128)(2,1)} %get-tuple-element.90), channel_id=1, source_target_pairs={{0,4},{4,0},{8,12},{12,8},{16,20},{20,16},{24,28},{28,24},{1,5},{5... | collective-permute-start | bytes 2359304 | tf_op jit(solution)/shard_map/ppermute | solution.py:412
  142.5 17.9 %collective-permute-start.26 = (bf16[12,128,256]{2,1,0:T(8,128)(2,1)}, bf16[12,128,256]{2,1,0:T(8,128)(2,1)}, u32[]{:S(2)}, u32[]{:S(2)}) collective-permute-start(bf16[12,128,256]{2,1,0:T(8,128)(2,1)} %get-tuple-element.123), channel_id=1, source_target_pairs={{0,8},{4,12},{8,0},{12,4},{16,24},{20,28},{24,16},{28,20},{1,9},{5... | collective-permute-start | bytes 2359304 | tf_op jit(solution)/shard_map/ppermute | solution.py:412
  143.4 16.9 %collective-permute-start.30 = (bf16[12,128,256]{2,1,0:T(8,128)(2,1)}, bf16[12,128,256]{2,1,0:T(8,128)(2,1)}, u32[]{:S(2)}, u32[]{:S(2)}) collective-permute-start(bf16[12,128,256]{2,1,0:T(8,128)(2,1)} %get-tuple-element.124), channel_id=1, source_target_pairs={{0,1},{1,0},{2,3},{3,2},{4,5},{5,4},{6,7},{7,6},{8,16},{9,17},{10,... | collective-permute-start | bytes 2359304 | tf_op jit(solution)/shard_map/ppermute | solution.py:412
  162.8 19.3 %collective-permute-start.27 = (bf16[12,128,256]{2,1,0:T(8,128)(2,1)S(1)}, bf16[12,128,256]{2,1,0:T(8,128)(2,1)S(1)}, u32[]{:S(2)}, u32[]{:S(2)}) collective-permute-start(bf16[12,128,256]{2,1,0:T(8,128)(2,1)S(1)} %get-tuple-element.120), channel_id=1, source_target_pairs={{0,4},{4,0},{8,12},{12,8},{16,20},{20,16},{24,28},{28,24},{1,5},{5... | collective-permute-start | bytes 2359304 | tf_op jit(solution)/shard_map/ppermute | solution.py:412
  164.2 17.9 %collective-permute-start.32 = (bf16[12,128,256]{2,1,0:T(8,128)(2,1)S(1)}, bf16[12,128,256]{2,1,0:T(8,128)(2,1)S(1)}, u32[]{:S(2)}, u32[]{:S(2)}) collective-permute-start(bf16[12,128,256]{2,1,0:T(8,128)(2,1)S(1)} %get-tuple-element.92), channel_id=1, source_target_pairs={{0,8},{4,12},{8,0},{12,4},{16,24},{20,28},{24,16},{28,20},{1,9},{5... | collective-permute-start | bytes 2359304 | tf_op jit(solution)/shard_map/ppermute | solution.py:412
  165.4 16.6 %collective-permute-start.33 = (bf16[12,128,256]{2,1,0:T(8,128)(2,1)S(1)}, bf16[12,128,256]{2,1,0:T(8,128)(2,1)S(1)}, u32[]{:S(2)}, u32[]{:S(2)}) collective-permute-start(bf16[12,128,256]{2,1,0:T(8,128)(2,1)S(1)} %get-tuple-element.93), channel_id=1, source_target_pairs={{0,1},{1,0},{2,3},{3,2},{4,5},{5,4},{6,7},{7,6},{8,16},{9,17},{10,... | collective-permute-start | bytes 2359304 | tf_op jit(solution)/shard_map/ppermute | solution.py:412
  165.4 9.2 %collective-permute-start.21 = (bf16[2,128,1024]{2,1,0:T(8,128)(2,1)S(1)}, bf16[2,128,1024]{2,1,0:T(8,128)(2,1)S(1)}, u32[]{:S(2)}, u32[]{:S(2)}) collective-permute-start(bf16[2,128,1024]{2,1,0:T(8,128)(2,1)S(1)} %copy-done.20), channel_id=1, source_target_pairs={{0,1},{1,0},{2,3},{3,2},{4,5},{5,4},{6,7},{7,6},{8,9},{9,8},{10,11... | collective-permute-start | bytes 1572872 | tf_op jit(solution)/shard_map/ppermute | solution.py:1367
  166.0 2.7 %collective-permute-start.34 = (f32[24,1152]{1,0:T(8,128)S(1)}, f32[24,1152]{1,0:T(8,128)S(1)}, u32[]{:S(2)}, u32[]{:S(2)}) collective-permute-start(f32[24,1152]{1,0:T(8,128)S(1)} %copy-done.33), channel_id=1, source_target_pairs={{0,1},{1,0},{2,3},{3,2},{4,5},{5,4},{6,7},{7,6},{8,9},{9,8},{10,11... | collective-permute-start | bytes 331784 | tf_op jit(solution)/shard_map/ppermute | solution.py:1433
  168.7 5.2 %collective-permute-start.35 = (f32[24,1152]{1,0:T(8,128)S(1)}, f32[24,1152]{1,0:T(8,128)S(1)}, u32[]{:S(2)}, u32[]{:S(2)}) collective-permute-start(f32[24,1152]{1,0:T(8,128)S(1)} %add.94), channel_id=1, source_target_pairs={{0,2},{1,3},{2,0},{3,1},{4,6},{5,7},{6,4},{7,5},{8,10},{9,11},{10,... | collective-permute-start | bytes 331784 | tf_op jit(solution)/shard_map/ppermute | solution.py:1434
  173.8 8.2 %collective-permute-start.36 = (f32[24,1152]{1,0:T(8,128)S(1)}, f32[24,1152]{1,0:T(8,128)S(1)}, u32[]{:S(2)}, u32[]{:S(2)}) collective-permute-start(f32[24,1152]{1,0:T(8,128)S(1)} %add.95), channel_id=1, source_target_pairs={{0,4},{4,0},{8,12},{12,8},{16,20},{20,16},{24,28},{28,24},{1,5},{5... | collective-permute-start | bytes 331784 | tf_op jit(solution)/shard_map/ppermute | solution.py:1435
  174.7 7.9 %collective-permute-start.23 = (bf16[128,1024]{1,0:T(8,128)(2,1)S(1)}, bf16[128,1024]{1,0:T(8,128)(2,1)S(1)}, u32[]{:S(2)}, u32[]{:S(2)}) collective-permute-start(bf16[128,1024]{1,0:T(8,128)(2,1)S(1)} %fusion.12), channel_id=1, source_target_pairs={{0,2},{1,3},{2,0},{3,1},{4,6},{5,7},{6,4},{7,5},{8,10},{9,11},{10,... | collective-permute-start | bytes 786440 | tf_op jit(solution)/shard_map/ppermute | solution.py:1369
  182.6 17.0 %collective-permute-start.37 = (bf16[12,128,256]{2,1,0:T(8,128)(2,1)S(1)}, bf16[12,128,256]{2,1,0:T(8,128)(2,1)S(1)}, u32[]{:S(2)}, u32[]{:S(2)}) collective-permute-start(bf16[12,128,256]{2,1,0:T(8,128)(2,1)S(1)} %add_convert_fusion.shard0), channel_id=1, source_target_pairs={{0,2},{1,3},{2,0},{3,1},{4,6},{5,7},{6,4},{7,5},{8,10},{9,11},{10,... | collective-permute-start | bytes 2359304 | tf_op jit(solution)/shard_map/ppermute | solution.py:1437
  184.0 4.8 %collective-permute-start.39 = (f32[24,1152]{1,0:T(8,128)S(1)}, f32[24,1152]{1,0:T(8,128)S(1)}, u32[]{:S(2)}, u32[]{:S(2)}) collective-permute-start(f32[24,1152]{1,0:T(8,128)S(1)} %add.96), channel_id=1, source_target_pairs={{0,8},{4,12},{8,0},{12,4},{16,24},{20,28},{24,16},{28,20},{1,9},{5... | collective-permute-start | bytes 331784 | tf_op jit(solution)/shard_map/ppermute | solution.py:1440
  188.9 5.7 %collective-permute-start.40 = (f32[24,1152]{1,0:T(8,128)S(1)}, f32[24,1152]{1,0:T(8,128)S(1)}, u32[]{:S(2)}, u32[]{:S(2)}) collective-permute-start(f32[24,1152]{1,0:T(8,128)S(1)} %add.97), channel_id=1, source_target_pairs={{0,16},{4,20},{8,24},{12,28},{16,0},{20,4},{24,8},{28,12},{1,17},{... | collective-permute-start | bytes 331784 | tf_op jit(solution)/shard_map/ppermute | solution.py:1440
  194.6 7.4 %collective-permute-start.38 = (bf16[12,128,256]{2,1,0:T(8,128)(2,1)S(1)}, bf16[12,128,256]{2,1,0:T(8,128)(2,1)S(1)}, u32[]{:S(2)}, u32[]{:S(2)}) collective-permute-start(bf16[12,128,256]{2,1,0:T(8,128)(2,1)S(1)} %add_convert_fusion.shard0), channel_id=1, source_target_pairs={{0,1},{1,0},{2,3},{3,2},{4,5},{5,4},{6,7},{7,6},{8,9},{9,8},{10,11... | collective-permute-start | bytes 2359304 | tf_op jit(solution)/shard_map/ppermute | solution.py:1438
  199.6 2.5 %collective-permute-start.41 = (bf16[12,128,256]{2,1,0:T(8,128)(2,1)S(1)}, bf16[12,128,256]{2,1,0:T(8,128)(2,1)S(1)}, u32[]{:S(2)}, u32[]{:S(2)}) collective-permute-start(bf16[12,128,256]{2,1,0:T(8,128)(2,1)S(1)} %collective-permute-done.37.shard1), channel_id=1, source_target_pairs={{0,1},{1,0},{2,3},{3,2},{4,5},{5,4},{6,7},{7,6},{8,9},{9,8},{10,11... | collective-permute-start | bytes 2359304 | tf_op jit(solution)/shard_map/ppermute | solution.py:1442
  199.6 2.4 %collective-permute-start.42 = (f32[24,1152]{1,0:T(8,128)S(1)}, f32[24,1152]{1,0:T(8,128)S(1)}, u32[]{:S(2)}, u32[]{:S(2)}) collective-permute-start(f32[24,1152]{1,0:T(8,128)S(1)} %add.98.small_own), channel_id=1, source_target_pairs={{0,1},{1,0},{2,3},{3,2},{4,5},{5,4},{6,7},{7,6},{8,9},{9,8},{10,11... | collective-permute-start | bytes 331784 | tf_op jit(solution)/shard_map/ppermute | solution.py:1441
  (31 other events, 326.1 us)

commit v8 on v7

--- a/solution.py
+++ b/solution.py
@@ -427,8 +427,8 @@
     third = pick(inner, middle_near, turned)
     near_twice = fsdp_move(after(middle_near, side_two, third), Z_NEAR)
     side_three = fsdp_move(third, Y_SWAP)
-    over_z = fsdp_move(side_three[:PART], Z_NEAR)
-    over_y = fsdp_move(after(near_twice[PART:], side_three, *late), Y_SWAP)
+    over_z = fsdp_move(side_three[:6], Z_NEAR)
+    over_y = fsdp_move(after(near_twice[6:], side_three, *late), Y_SWAP)
     return [
         piece,
         side,
@@ -517,51 +517,71 @@
     return lax.broadcasted_iota(jnp.int32, shape, 0)
 
 
-def prepare_kernel(projection, out_weight, up_weight, down_weight, piece):
+def prepare_kernel(
+    projection,
+    out_weight,
+    up_weight,
+    down_weight,
+    piece,
+    up_own,
+    up_lent,
+    heads,
+    down_own,
+    down_lent,
+    out_rows,
+    sems,
+):
     _, member_parity, x, core = position()
     quarter, other = 2 * x + core, 2 * x + 1 - core
+    copies = []
+
+    def fetch(source, goal):
+        copies.append(pltpu.make_async_copy(source, goal, sems.at[len(copies)]))
+        copies[-1].start()
+
+    def tile(place):
+        return pl.ds(pl.multiple_of(place * 128, 128), 128)
+
+    for index in range(8):
+        fetch(up_weight.at[:, tile(index * 4 + quarter)], up_own.at[index])
+    for pair in range(4):
+        fetch(up_weight.at[:, tile((2 * pair + 1 - core) * 4 + other)], up_lent.at[pair])
+    for low in range(4):
+        fetch(projection.at[:, :, tile(low * 2 + core)], heads.at[:, low])
+    fetch(down_weight.at[tile(quarter)], down_own)
+    fetch(down_weight.at[pl.ds(pl.multiple_of(other * 128 + 96, 32), 32)], down_lent)
+    fetch(out_weight.at[pl.ds(pl.multiple_of(x * 64, 64), 64)], out_rows)
+    for copy in copies:
+        copy.wait()
     lane = lanes_of((128, 128))
     for index in range(8):
         half = index % 2
-        own = up_weight[:, pl.ds(pl.multiple_of((index * 4 + quarter) * 128, 128), 128)]
-        extra = up_weight[:, pl.ds(pl.multiple_of(((index ^ 1) * 4 + other) * 128, 128), 128)]
         taken = (lane >= 96) & (core == half)
         piece[index // 2, :, half * 128 : half * 128 + 128] = jnp.where(
-            taken, wide(extra), wide(own)
+            taken, wide(up_lent[index // 2]), wide(up_own[index])
         ).astype(jnp.bfloat16)
     for stream in range(3):
         for twin in range(2):
-            tiles = [
-                wide(
-                    projection[
-                        stream,
-                        :,
-                        pl.ds(pl.multiple_of((2 * twin + low) * 256 + core * 128, 128), 128),
-                    ]
-                )
-                for low in range(2)
-            ]
+            tiles = [wide(heads[stream, 2 * twin + low]) for low in range(2)]
             first = jnp.where(x == 0, tiles[0], pltpu.roll(tiles[0], 64, 1))
             second = jnp.where(x == 0, pltpu.roll(tiles[1], 64, 1), tiles[1])
             piece[4 + stream, :, twin * 128 : twin * 128 + 128] = jnp.where(
                 lane < 64, first, second
             ).astype(jnp.bfloat16)
-    own_row = pl.multiple_of(quarter * 128, 128)
-    other_row = pl.multiple_of(other * 128, 128)
-    head_row = pl.multiple_of(x * 64, 64)
     for block in range(4):
         cols = slice(block * 256, block * 256 + 256)
-        piece[7 + block, 0:96] = down_weight[pl.ds(own_row, 96), cols]
+        band = slice(block * 32, block * 32 + 32)
+        piece[7 + block, 0:96] = down_own[0:96, cols]
 
         @pl.when(member_parity == core)
         def _():
-            piece[7 + block, 96:128] = out_weight[pl.ds(head_row, 32), cols]
-            piece[11, block * 32 : block * 32 + 32] = out_weight[pl.ds(head_row + 32, 32), cols]
+            piece[7 + block, 96:128] = out_rows[0:32, cols]
+            piece[11, band] = out_rows[32:64, cols]
 
         @pl.when(member_parity != core)
         def _():
-            piece[7 + block, 96:128] = down_weight[pl.ds(own_row + 96, 32), cols]
-            piece[11, block * 32 : block * 32 + 32] = down_weight[pl.ds(other_row + 96, 32), cols]
+            piece[7 + block, 96:128] = down_own[96:128, cols]
+            piece[11, band] = down_lent[:, cols]
 
 
 def front_kernel(
@@ -733,11 +753,19 @@
 
     def piece_copies(index, ref, tail_ref):
         rows = member_rows[index]
-        down = 7 if tail_ref is ref else 0
-        return [
+        down = 7 if tail_ref is ref else 1
+        lin_copies = [
             pltpu.make_async_copy(
-                ref.at[pl.ds(4, 3)], lin_all.at[:, rows], piece_sems.at[index, 0]
-            ),
+                source.at[pl.ds(at, count)],
+                lin_all.at[pl.ds(stream, count), rows],
+                piece_sems.at[index, place],
+            )
+            for place, source, at, stream, count in (
+                (0, ref, 4, 0, 2),
+                (3, tail_ref, down - 1, 2, 1),
+            )
+        ]
+        return lin_copies + [
             pltpu.make_async_copy(
                 tail_ref.at[pl.ds(down, 5)], down_all.at[origin[index]], piece_sems.at[index, 1]
             ),
@@ -766,9 +794,9 @@
         copy.start()
     for index, (for_inner, for_ends) in enumerate(sources):
         copies = piece_copies(index, for_inner, for_inner)
-        first.append(copies[0])
-        second.append(copies[1])
-        third.append(copies[2])
+        first += copies[:2]
+        second.append(copies[2])
+        third.append(copies[3])
         if for_inner is for_ends:
             for copy in copies:
                 copy.start()
@@ -1266,9 +1294,18 @@
     piece = call(
         prepare_kernel,
         shape_of((12, 128, 256)),
-        [VMEM_FULL] * 4,
+        [IN_PLACE] * 4,
         VMEM_FULL,
         (query_key_value, out_weight, up_weight, down_weight),
+        scratch=[
+            pltpu.VMEM((8, 128, 128), jnp.bfloat16),
+            pltpu.VMEM((4, 128, 128), jnp.bfloat16),
+            pltpu.VMEM((3, 4, 128, 128), jnp.bfloat16),
+            pltpu.VMEM((128, width), jnp.bfloat16),
+            pltpu.VMEM((32, width), jnp.bfloat16),
+            pltpu.VMEM((64, width), jnp.bfloat16),
+            pltpu.SemaphoreType.DMA((19,)),
+        ],
         vmem=60 << 20,
     )
     up_own = mix_up.T
@@ -1352,7 +1389,7 @@
             pltpu.VMEM((8, 12, 128, 256), jnp.bfloat16),
             pltpu.VMEM((2, 2, 5, ROWS, width), jnp.bfloat16),
             pltpu.SemaphoreType.DMA((4, 6)),
-            pltpu.SemaphoreType.DMA((8, 3)),
+            pltpu.SemaphoreType.DMA((8, 4)),
             pltpu.SemaphoreType.DMA((9,)),
             pltpu.SemaphoreType.DMA((3, 5)),
         ],

time: 206 us -> 205 us (level)
  waiting for transfers between devices: 99 us -> 105 us
  local copies, waits for them, and re-layouts: 5.36 us -> 0.99 us
  starting transfers between devices: 41.6 us -> 39 us
    ppermute x22, waiting for transfers between devices: 66.2 us -> 70.7 us  [fsdp_move(): lax.ppermute(value, 'fsdp' if len(pairs) == 8 else ('fsdp', 'replica'), p...]
    unnamed x72 -> x70, local copies, waits for them, and re-layouts: 4.54 us -> 0.17 us
    ppermute x2, waiting for transfers between devices: 6.73 us -> 10.6 us  [on_device_tensor(): small = small + lax.ppermute(small, 'fsdp', perm)]
    ppermute x2, starting transfers between devices: 3.82 us -> 1.49 us  [on_device_tensor(): small = small + lax.ppermute(small, 'fsdp', perm)]
where the time goes in v8:
time: 205 us
  waiting for transfers between devices  105 us (51%)
  Pallas kernels  49 us (24%)
  starting transfers between devices  39 us (19%)
  other arithmetic  8.98 us (4%)
    ppermute x22, waiting for transfers between devices, fsdp_move(): lax.ppermute(value, 'fsdp' if len(pairs) == 8 else ('fsdp', 'replica'), p...  70.7 us
    pallas_call x4, Pallas kernels, call(): pl.pallas_call(kernel, out_shape=outs, in_specs=specs, out_specs=out_spec...  35.8 us
    ppermute x22, starting transfers between devices, fsdp_move(): lax.ppermute(value, 'fsdp' if len(pairs) == 8 else ('fsdp', 'replica'), p...  22.7 us
    pallas_call x1, Pallas kernels, back(): pl.pallas_call(back_kernel, grid=(1,), out_shape=(shape_of((seqs, STREAMS...  13.1 us
    ppermute x2, waiting for transfers between devices, on_device_tensor(): small = small + lax.ppermute(small, 'fsdp', perm)  10.6 us
    ppermute x1, waiting for transfers between devices, on_device_tensor(): small = small + lax.ppermute(small, 'fsdp', Y_SWAP)  5.94 us
    convert_element_type x5, other arithmetic, low(): return value.astype(jnp.bfloat16)  4.89 us
  transfers between devices with their start and end apart: 43, of which 25 were waited for; matrix products, arithmetic and copies ran while one was open for 4% of the time, Pallas kernels for 11%

profile of v8, /device:TPU:0, one launch (start us, length us, event | category | flops | bytes accessed | tf_op | source)
XLA Modules:
  0.0 204.6 jit_solution(15034702979834744867)
XLA Ops:
  0.7 3.0 %collective-permute-start = (bf16[36,128]{1,0:T(8,128)(2,1)}, bf16[36,128]{1,0:T(8,128)(2,1)S(1)}, u32[]{:S(2)}, u32[]{:S(2)}) collective-permute-start(bf16[36,128]{1,0:T(8,128)(2,1)} %bitcast.49), channel_id=1, source_target_pairs={{0,4},{4,0},{8,12},{12,8},{16,20},{20,16},{24,28},{28,24},{1,5},{5... | collective-permute-start | bytes 27656 | tf_op jit(solution)/shard_map/ppermute | solution.py:1312
  3.8 2.7 %shard_map.246.piece0 = bf16[12,128,256]{2,1,0:T(8,128)(2,1)} custom-call(bf16[3,128,1024]{2,1,0:T(8,128)(2,1)} %projection.1, bf16[128,1024]{1,0:T(8,128)(2,1)} %out_weight.1, bf16[128,4096]{1,0:T(8,128)(2,1)} %up_weight.1, bf16[512,1024]{1,0:T(8,128)(2,1)} %down_weight.1), custom_call_target="tpu_custom_call" | custom-call | tf_op jit(solution)/shard_map/pallas_call | solution.py:1242
  6.5 2.7 %collective-permute-start.2 = (bf16[36,256]{1,0:T(8,128)(2,1)S(1)}, bf16[36,256]{1,0:T(8,128)(2,1)S(1)}, u32[]{:S(2)}, u32[]{:S(2)}) collective-permute-start(bf16[36,256]{1,0:T(8,128)(2,1)S(1)} %pad_maximum_fusion.up_own), channel_id=1, source_target_pairs={{0,16},{4,20},{8,24},{12,28},{16,0},{20,4},{24,8},{28,12},{1,17},{... | collective-permute-start | bytes 55304 | tf_op jit(solution)/shard_map/ppermute | solution.py:412
  9.2 1.3 collective-permute-start.1
  11.3 1.9 collective-permute-done.1.up_one
  14.6 1.5 collective-permute-start.7
  17.4 6.3 %shard_map.247 = (bf16[528,1024]{1,0:T(8,128)(2,1)S(1)}, f32[4,128,1024]{2,1,0:T(8,128)S(1)}, f32[3,128,128]{2,1,0:T(8,128)S(1)}, f32[128,1024]{1,0:T(8,128)S(1)}, bf16[36,1024]{1,0:T(8,128)(2,1)S(1)}) custom-call(s32[4]{0:T(128)S(1)} %pad_add_fusion.bounds, bf16[2,9,64,1024]{3,2,1,0:T(8,128)(2,1)S(1)} %bitcast.41, f32[1,1024]{1,0:T(1,128)S(1)} %bitcast.47, ...), custom_call_target="tpu_custom_call" | custom-call | tf_op jit(solution)/shard_map/pallas_call | solution.py:1242
  23.7 8.9 %collective-permute-done.12.piece3 = bf16[12,128,256]{2,1,0:T(8,128)(2,1)S(1)} collective-permute-done((bf16[12,128,256]{2,1,0:T(8,128)(2,1)}, bf16[12,128,256]{2,1,0:T(8,128)(2,1)S(1)}, u32[]{:S(2)}, u32[]{:S(2)}) %collective-permute-start.12) | collective-permute-done | bytes 786464 | tf_op jit(solution)/shard_map/ppermute | solution.py:412
  33.2 1.7 collective-permute-start.14
  34.9 1.5 collective-permute-start.4
  36.4 1.2 broadcast_select_fusion.1
  37.7 1.4 collective-permute-start.15
  39.1 14.1 %collective-permute-done.14.piece5 = bf16[12,128,256]{2,1,0:T(8,128)(2,1)S(1)} collective-permute-done((bf16[12,128,256]{2,1,0:T(8,128)(2,1)S(1)}, bf16[12,128,256]{2,1,0:T(8,128)(2,1)S(1)}, u32[]{:S(2)}, u32[]{:S(2)}) %collective-permute-start.14) | collective-permute-done | bytes 786464 | tf_op jit(solution)/shard_map/ppermute | solution.py:412
  53.3 1.4 collective-permute-start.17
  54.7 1.0 collective-permute-done.15.piece7
  55.7 1.6 collective-permute-start.16
  57.3 2.2 %collective-permute-done.4.packet1 = bf16[528,1024]{1,0:T(8,128)(2,1)S(1)} collective-permute-done((bf16[528,1024]{1,0:T(8,128)(2,1)S(1)}, bf16[528,1024]{1,0:T(8,128)(2,1)S(1)}, u32[]{:S(2)}, u32[]{:S(2)}) %collective-permute-start.4) | collective-permute-done | bytes 1081376 | tf_op jit(solution)/shard_map/ppermute | solution.py:1357
  60.0 12.5 %collective-permute-done.17.piece8 = bf16[12,128,256]{2,1,0:T(8,128)(2,1)S(1)} collective-permute-done((bf16[12,128,256]{2,1,0:T(8,128)(2,1)S(1)}, bf16[12,128,256]{2,1,0:T(8,128)(2,1)S(1)}, u32[]{:S(2)}, u32[]{:S(2)}) %collective-permute-start.17) | collective-permute-done | bytes 786464 | tf_op jit(solution)/shard_map/ppermute | solution.py:412
  73.6 1.1 collective-permute-start.19
  74.7 1.7 collective-permute-done.9.cotangent3
  76.4 6.0 %collective-permute-done.18.piece9 = bf16[6,128,256]{2,1,0:T(8,128)(2,1)S(1)} collective-permute-done((bf16[6,128,256]{2,1,0:T(8,128)(2,1)S(1)}, bf16[6,128,256]{2,1,0:T(8,128)(2,1)S(1)}, u32[]{:S(2)}, u32[]{:S(2)}) %collective-permute-start.18) | collective-permute-done | bytes 393248 | tf_op jit(solution)/shard_map/ppermute | solution.py:412
  83.2 23.5 %shard_map.248 = (bf16[7,128,256]{2,1,0:T(8,128)(2,1)S(1)}, bf16[5,128,256]{2,1,0:T(8,128)(2,1)S(1)}, bf16[12,128,256]{2,1,0:T(8,128)(2,1)S(1)}, bf16[12,128,256...) custom-call(f32[3,128,128]{2,1,0:T(8,128)S(1)} %copy-done.11, ...), custom_call_target="tpu_custom_call" | custom-call | tf_op jit(solution)/shard_map/pallas_call | solution.py:1242
  106.8 1.5 collective-permute-start.24
  108.3 1.3 collective-permute-start.28
  109.6 7.3 %collective-permute-done.24 = bf16[5,128,256]{2,1,0:T(8,128)(2,1)S(1)} collective-permute-done((bf16[5,128,256]{2,1,0:T(8,128)(2,1)S(1)}, bf16[5,128,256]{2,1,0:T(8,128)(2,1)S(1)}, u32[]{:S(2)}, u32[]{:S(2)}) %collective-permute-start.24) | collective-permute-done | bytes 327712 | tf_op jit(solution)/shard_map/ppermute | solution.py:412
  117.1 1.4 collective-permute-start.25
  118.6 1.7 fusion
  120.2 1.4 collective-permute-done.28
  122.3 1.5 collective-permute-start.22
  124.7 13.8 %collective-permute-done.25 = bf16[12,128,256]{2,1,0:T(8,128)(2,1)S(1)} collective-permute-done((bf16[12,128,256]{2,1,0:T(8,128)(2,1)S(1)}, bf16[12,128,256]{2,1,0:T(8,128)(2,1)S(1)}, u32[]{:S(2)}, u32[]{:S(2)}) %collective-permute-start.25) | collective-permute-done | bytes 786464 | tf_op jit(solution)/shard_map/ppermute | solution.py:412
  138.5 1.3 collective-permute-done.29
  139.8 1.9 fusion.2
  142.5 3.8 %collective-permute-done.22.across = bf16[4,128,1024]{2,1,0:T(8,128)(2,1)} collective-permute-done((bf16[4,128,1024]{2,1,0:T(8,128)(2,1)}, bf16[4,128,1024]{2,1,0:T(8,128)(2,1)}, u32[]{:S(2)}, u32[]{:S(2)}) %collective-permute-start.22) | collective-permute-done | bytes 1048608 | tf_op jit(solution)/shard_map/ppermute | solution.py:1403
  146.3 13.1 %shard_map.249 = (bf16[2,9,64,1024]{3,2,1,0:T(8,128)(2,1)}, f32[24,1152]{1,0:T(8,128)}, f32[24,1152]{1,0:T(8,128)}, f32[2,9,4,64]{3,2,1,0:T(4,128)}) custom-call(bf16[2,9,64,1024]{3,2,1,0:T(8,128)(2,1)} %bitcast.40, bf16[128,1024]{1,0:T(8,128)(2,1)} %bitcast.42, f32[4,128,1024]{2,1,0:T(8,128)} %copy-done.2, f32[3,128,128]{2,1,0:T(8,128)} %copy-done.12, ...), custom_call_target="tpu_custom_call" | custom-call | tf_op jit(solution)/shard_map/pallas_call | solution.py:1417
  159.5 2.3 %fusion.6 = (bf16[12,128,256]{2,1,0:T(8,128)(2,1)S(1)}, bf16[12,128,256]{2,1,0:T(8,128)(2,1)S(1)}, bf16[12,128,256]{2,1,0:T(8,128)(2,1)S(1)}) fusion(bf16[12,128,256]{2,1,0:T(8,128)(2,1)} %collective-permute-done.26, bf16[12,128,256]{2,1,0:T(8,128)(2,1)S(1)} %get-tuple-element.81, pred[]{:T(512)S(6)} %eq.15, ...), kind=kLoop, calls=%fused_computation.13 | loop fusion | flops 5898240 | bytes 7077890 | tf_op jit(solution)/shard_map/convert_element_type | solution.py:481
  161.8 1.2 collective-permute-start.27
  163.1 1.6 collective-permute-start.32
  165.3 2.6 %collective-permute-done.34 = f32[24,1152]{1,0:T(8,128)S(1)} collective-permute-done((f32[24,1152]{1,0:T(8,128)S(1)}, f32[24,1152]{1,0:T(8,128)S(1)}, u32[]{:S(2)}, u32[]{:S(2)}) %collective-permute-start.34) | collective-permute-done | bytes 110624 | tf_op jit(solution)/shard_map/ppermute | solution.py:1470
  167.9 1.5 collective-permute-start.35
  169.5 3.6 %collective-permute-done.35 = f32[24,1152]{1,0:T(8,128)S(1)} collective-permute-done((f32[24,1152]{1,0:T(8,128)S(1)}, f32[24,1152]{1,0:T(8,128)S(1)}, u32[]{:S(2)}, u32[]{:S(2)}) %collective-permute-start.35) | collective-permute-done | bytes 110624 | tf_op jit(solution)/shard_map/ppermute | solution.py:1471
  173.9 1.5 collective-permute-start.23
  175.5 5.9 %collective-permute-done.36 = f32[24,1152]{1,0:T(8,128)S(1)} collective-permute-done((f32[24,1152]{1,0:T(8,128)S(1)}, f32[24,1152]{1,0:T(8,128)S(1)}, u32[]{:S(2)}, u32[]{:S(2)}) %collective-permute-start.36) | collective-permute-done | bytes 110624 | tf_op jit(solution)/shard_map/ppermute | solution.py:1472
  182.0 1.5 collective-permute-start.37
  184.4 4.3 %collective-permute-done.39 = f32[24,1152]{1,0:T(8,128)S(1)} collective-permute-done((f32[24,1152]{1,0:T(8,128)S(1)}, f32[24,1152]{1,0:T(8,128)S(1)}, u32[]{:S(2)}, u32[]{:S(2)}) %collective-permute-start.39) | collective-permute-done | bytes 110624 | tf_op jit(solution)/shard_map/ppermute | solution.py:1477
  189.3 6.3 %collective-permute-done.40 = f32[24,1152]{1,0:T(8,128)S(1)} collective-permute-done((f32[24,1152]{1,0:T(8,128)S(1)}, f32[24,1152]{1,0:T(8,128)S(1)}, u32[]{:S(2)}, u32[]{:S(2)}) %collective-permute-start.40) | collective-permute-done | bytes 110624 | tf_op jit(solution)/shard_map/ppermute | solution.py:1477
  195.7 3.1 %collective-permute-done.37.shard1 = bf16[12,128,256]{2,1,0:T(8,128)(2,1)S(1)} collective-permute-done((bf16[12,128,256]{2,1,0:T(8,128)(2,1)S(1)}, bf16[12,128,256]{2,1,0:T(8,128)(2,1)S(1)}, u32[]{:S(2)}, u32[]{:S(2)}) %collective-permute-start.37) | collective-permute-done | bytes 786464 | tf_op jit(solution)/shard_map/ppermute | solution.py:1474
  200.2 1.1 collective-permute-done.42.small_other
  201.3 3.4 %shard_map.250 = (f32[3,128,1024]{2,1,0:T(8,128)}, f32[128,1024]{1,0:T(8,128)}, f32[128,4096]{1,0:T(8,128)}, f32[512,1024]{1,0:T(8,128)}, f32[1,1024]{1,0:T(1,12...) custom-call(bf16[12,128,256]{2,1,0:T(8,128)(2,1)S(1)} %add_convert_fus, ...), custom_call_target="tpu_custom_call" | custom-call | tf_op jit(solution)/shard_map/pallas_call | solution.py:1242
  (134 shorter events, 13.9 us)
Async XLA Ops:
  0.7 5.8 %collective-permute-start = (bf16[36,128]{1,0:T(8,128)(2,1)}, bf16[36,128]{1,0:T(8,128)(2,1)S(1)}, u32[]{:S(2)}, u32[]{:S(2)}) collective-permute-start(bf16[36,128]{1,0:T(8,128)(2,1)} %bitcast.49), channel_id=1, source_target_pairs={{0,4},{4,0},{8,12},{12,8},{16,20},{20,16},{24,28},{28,24},{1,5},{5... | collective-permute-start | bytes 27656 | tf_op jit(solution)/shard_map/ppermute | solution.py:1312
  6.5 4.7 %collective-permute-start.2 = (bf16[36,256]{1,0:T(8,128)(2,1)S(1)}, bf16[36,256]{1,0:T(8,128)(2,1)S(1)}, u32[]{:S(2)}, u32[]{:S(2)}) collective-permute-start(bf16[36,256]{1,0:T(8,128)(2,1)S(1)} %pad_maximum_fusion.up_own), channel_id=1, source_target_pairs={{0,16},{4,20},{8,24},{12,28},{16,0},{20,4},{24,8},{28,12},{1,17},{... | collective-permute-start | bytes 55304 | tf_op jit(solution)/shard_map/ppermute | solution.py:412
  9.2 4.0 %collective-permute-start.1 = (bf16[36,256]{1,0:T(8,128)(2,1)S(1)}, bf16[36,256]{1,0:T(8,128)(2,1)S(1)}, u32[]{:S(2)}, u32[]{:S(2)}) collective-permute-start(bf16[36,256]{1,0:T(8,128)(2,1)S(1)} %pad_maximum_fusion.up_own), channel_id=1, source_target_pairs={{8,0},{25,1},{10,2},{27,3},{12,4},{29,5},{14,6},{31,7},{16,8},{1,9... | collective-permute-start | bytes 55304 | tf_op jit(solution)/shard_map/ppermute | solution.py:412
  13.2 19.5 %collective-permute-start.12 = (bf16[12,128,256]{2,1,0:T(8,128)(2,1)}, bf16[12,128,256]{2,1,0:T(8,128)(2,1)S(1)}, u32[]{:S(2)}, u32[]{:S(2)}) collective-permute-start(bf16[12,128,256]{2,1,0:T(8,128)(2,1)} %shard_map.246.piece0), channel_id=1, source_target_pairs={{0,4},{1,5},{2,6},{3,7},{4,0},{5,1},{6,2},{7,3},{8,16},{9,17},{10,... | collective-permute-start | bytes 2359304 | tf_op jit(solution)/shard_map/ppermute | solution.py:412
  14.1 19.1 %collective-permute-start.11 = (bf16[12,128,256]{2,1,0:T(8,128)(2,1)}, bf16[12,128,256]{2,1,0:T(8,128)(2,1)}, u32[]{:S(2)}, u32[]{:S(2)}) collective-permute-start(bf16[12,128,256]{2,1,0:T(8,128)(2,1)} %shard_map.246.piece0), channel_id=1, source_target_pairs={{0,8},{4,12},{8,0},{12,4},{16,24},{20,28},{24,16},{28,20},{1,9},{5... | collective-permute-start | bytes 2359304 | tf_op jit(solution)/shard_map/ppermute | solution.py:412
  14.6 18.5 %collective-permute-start.10 = (bf16[12,128,256]{2,1,0:T(8,128)(2,1)}, bf16[12,128,256]{2,1,0:T(8,128)(2,1)}, u32[]{:S(2)}, u32[]{:S(2)}) collective-permute-start(bf16[12,128,256]{2,1,0:T(8,128)(2,1)} %shard_map.246.piece0), channel_id=1, source_target_pairs={{0,1},{1,0},{2,3},{3,2},{4,5},{5,4},{6,7},{7,6},{8,12},{9,13},{10,... | collective-permute-start | bytes 2359304 | tf_op jit(solution)/shard_map/ppermute | solution.py:412
  14.6 9.1 %collective-permute-start.7 = (bf16[128,1024]{1,0:T(8,128)(2,1)S(1)}, bf16[128,1024]{1,0:T(8,128)(2,1)}, u32[]{:S(2)}, u32[]{:S(2)}) collective-permute-start(bf16[128,1024]{1,0:T(8,128)(2,1)S(1)} %bitcast.43), channel_id=1, source_target_pairs={{0,2},{1,3},{2,0},{3,1},{4,6},{5,7},{6,4},{7,5},{8,10},{9,11},{10,... | collective-permute-start | bytes 786440 | tf_op jit(solution)/shard_map/ppermute | solution.py:1324
  16.1 1.2 collective-permute-start.3
  23.7 33.6 %copy-start.3 = (bf16[528,1024]{1,0:T(8,128)(2,1)}, bf16[528,1024]{1,0:T(8,128)(2,1)S(1)}, u32[]{:S(2)}) copy-start(bf16[528,1024]{1,0:T(8,128)(2,1)S(1)} %get-tuple-element.62.packet0) | copy-start | bytes 3244036
  33.2 5.9 %collective-permute-start.13 = (bf16[12,128,256]{2,1,0:T(8,128)(2,1)}, bf16[12,128,256]{2,1,0:T(8,128)(2,1)S(1)}, u32[]{:S(2)}, u32[]{:S(2)}) collective-permute-start(bf16[12,128,256]{2,1,0:T(8,128)(2,1)} %collective-permute-done.11.piece2), channel_id=1, source_target_pairs={{0,1},{1,0},{2,3},{3,2},{4,5},{5,4},{6,7},{7,6},{8,16},{9,17},{10,... | collective-permute-start | bytes 2359304 | tf_op jit(solution)/shard_map/ppermute | solution.py:412
  33.2 20.0 %collective-permute-start.14 = (bf16[12,128,256]{2,1,0:T(8,128)(2,1)S(1)}, bf16[12,128,256]{2,1,0:T(8,128)(2,1)S(1)}, u32[]{:S(2)}, u32[]{:S(2)}) collective-permute-start(bf16[12,128,256]{2,1,0:T(8,128)(2,1)S(1)} %collective-permute-done.12.piece3), channel_id=1, source_target_pairs={{0,8},{4,12},{8,0},{12,4},{16,24},{20,28},{24,16},{28,20},{1,9},{5... | collective-permute-start | bytes 2359304 | tf_op jit(solution)/shard_map/ppermute | solution.py:412
  34.9 24.5 %collective-permute-start.4 = (bf16[528,1024]{1,0:T(8,128)(2,1)S(1)}, bf16[528,1024]{1,0:T(8,128)(2,1)S(1)}, u32[]{:S(2)}, u32[]{:S(2)}) collective-permute-start(bf16[528,1024]{1,0:T(8,128)(2,1)S(1)} %get-tuple-element.62.packet0), channel_id=1, source_target_pairs={{0,2},{1,3},{2,0},{3,1},{4,6},{5,7},{6,4},{7,5},{8,10},{9,11},{10,... | collective-permute-start | bytes 3244040 | tf_op jit(solution)/shard_map/ppermute | solution.py:1357
  37.6 45.6 %copy-start.1 = (bf16[12,128,256]{2,1,0:T(8,128)(2,1)S(1)}, bf16[12,128,256]{2,1,0:T(8,128)(2,1)}, u32[]{:S(2)}) copy-start(bf16[12,128,256]{2,1,0:T(8,128)(2,1)} %shard_map.246.piece0) | copy-start | bytes 2359300
  37.6 45.6 %copy-start.11 = (f32[3,128,128]{2,1,0:T(8,128)S(1)}, f32[3,128,128]{2,1,0:T(8,128)}, u32[]{:S(2)}) copy-start(f32[3,128,128]{2,1,0:T(8,128)} %constant.39.clone.rope) | copy-start | bytes 589828
  37.7 18.0 %collective-permute-start.15 = (bf16[12,128,256]{2,1,0:T(8,128)(2,1)S(1)}, bf16[12,128,256]{2,1,0:T(8,128)(2,1)S(1)}, u32[]{:S(2)}, u32[]{:S(2)}) collective-permute-start(bf16[12,128,256]{2,1,0:T(8,128)(2,1)S(1)} %broadcast_select_fusion.1), channel_id=1, source_target_pairs={{0,4},{4,0},{8,12},{12,8},{16,20},{20,16},{24,28},{28,24},{1,5},{5... | collective-permute-start | bytes 2359304 | tf_op jit(solution)/shard_map/ppermute | solution.py:412
  39.1 33.5 %copy-start.21 = (bf16[12,128,256]{2,1,0:T(8,128)(2,1)}, bf16[12,128,256]{2,1,0:T(8,128)(2,1)S(1)}, u32[]{:S(2)}) copy-start(bf16[12,128,256]{2,1,0:T(8,128)(2,1)S(1)} %collective-permute-done.13.piece4) | copy-start | bytes 2359300
  53.1 30.0 %copy-start.22 = (bf16[12,128,256]{2,1,0:T(8,128)(2,1)}, bf16[12,128,256]{2,1,0:T(8,128)(2,1)S(1)}, u32[]{:S(2)}) copy-start(bf16[12,128,256]{2,1,0:T(8,128)(2,1)S(1)} %collective-permute-done.14.piece5) | copy-start | bytes 2359300
  53.3 19.2 %collective-permute-start.17 = (bf16[12,128,256]{2,1,0:T(8,128)(2,1)S(1)}, bf16[12,128,256]{2,1,0:T(8,128)(2,1)S(1)}, u32[]{:S(2)}, u32[]{:S(2)}) collective-permute-start(bf16[12,128,256]{2,1,0:T(8,128)(2,1)S(1)} %broadcast_select_fusion), channel_id=1, source_target_pairs={{0,4},{4,0},{8,12},{12,8},{16,20},{20,16},{24,28},{28,24},{1,5},{5... | collective-permute-start | bytes 2359304 | tf_op jit(solution)/shard_map/ppermute | solution.py:412
  55.7 17.9 %collective-permute-start.16 = (bf16[12,128,256]{2,1,0:T(8,128)(2,1)S(1)}, bf16[12,128,256]{2,1,0:T(8,128)(2,1)S(1)}, u32[]{:S(2)}, u32[]{:S(2)}) collective-permute-start(bf16[12,128,256]{2,1,0:T(8,128)(2,1)S(1)} %collective-permute-done.13.piece4), channel_id=1, source_target_pairs={{0,8},{4,12},{8,0},{12,4},{16,24},{20,28},{24,16},{28,20},{1,9},{5... | collective-permute-start | bytes 2359304 | tf_op jit(solution)/shard_map/ppermute | solution.py:412
  57.3 19.1 %collective-permute-start.5 = (bf16[528,1024]{1,0:T(8,128)(2,1)S(1)}, bf16[528,1024]{1,0:T(8,128)(2,1)S(1)}, u32[]{:S(2)}, u32[]{:S(2)}) collective-permute-start(bf16[528,1024]{1,0:T(8,128)(2,1)S(1)} %get-tuple-element.62.packet0), channel_id=1, source_target_pairs={{0,1},{1,0},{2,3},{3,2},{4,5},{5,4},{6,7},{7,6},{8,9},{9,8},{10,11... | collective-permute-start | bytes 3244040 | tf_op jit(solution)/shard_map/ppermute | solution.py:1358
  59.5 17.0 %collective-permute-start.6 = (bf16[528,1024]{1,0:T(8,128)(2,1)S(1)}, bf16[528,1024]{1,0:T(8,128)(2,1)S(1)}, u32[]{:S(2)}, u32[]{:S(2)}) collective-permute-start(bf16[528,1024]{1,0:T(8,128)(2,1)S(1)} %collective-permute-done.4.packet1), channel_id=1, source_target_pairs={{0,1},{1,0},{2,3},{3,2},{4,5},{5,4},{6,7},{7,6},{8,9},{9,8},{10,11... | collective-permute-start | bytes 3244040 | tf_op jit(solution)/shard_map/ppermute | solution.py:1359
  59.5 15.2 %collective-permute-start.8 = (bf16[128,1024]{1,0:T(8,128)(2,1)S(1)}, bf16[128,1024]{1,0:T(8,128)(2,1)S(1)}, u32[]{:S(2)}, u32[]{:S(2)}) collective-permute-start(bf16[128,1024]{1,0:T(8,128)(2,1)S(1)} %bitcast.44), channel_id=1, source_target_pairs={{0,1},{1,0},{2,3},{3,2},{4,5},{5,4},{6,7},{7,6},{8,9},{9,8},{10,11... | collective-permute-start | bytes 786440 | tf_op jit(solution)/shard_map/ppermute | solution.py:1328
  72.6 9.9 %collective-permute-start.18 = (bf16[6,128,256]{2,1,0:T(8,128)(2,1)S(1)}, bf16[6,128,256]{2,1,0:T(8,128)(2,1)S(1)}, u32[]{:S(2)}, u32[]{:S(2)}) collective-permute-start(bf16[6,128,256]{2,1,0:T(8,128)(2,1)S(1)} %slice.28), channel_id=1, source_target_pairs={{0,8},{4,12},{8,0},{12,4},{16,24},{20,28},{24,16},{28,20},{1,9},{5... | collective-permute-start | bytes 1179656 | tf_op jit(solution)/shard_map/ppermute | solution.py:412
  73.6 9.6 %collective-permute-start.19 = (bf16[6,128,256]{2,1,0:T(8,128)(2,1)S(1)}, bf16[6,128,256]{2,1,0:T(8,128)(2,1)S(1)}, u32[]{:S(2)}, u32[]{:S(2)}) collective-permute-start(bf16[6,128,256]{2,1,0:T(8,128)(2,1)S(1)} %slice.29), channel_id=1, source_target_pairs={{0,4},{4,0},{8,12},{12,8},{16,20},{20,16},{24,28},{28,24},{1,5},{5... | collective-permute-start | bytes 1179656 | tf_op jit(solution)/shard_map/ppermute | solution.py:412
  74.7 1.7 collective-permute-start.9
  106.7 11.8 %collective-permute-start.20 = (bf16[2,4,128,1024]{3,2,1,0:T(8,128)(2,1)}, bf16[2,4,128,1024]{3,2,1,0:T(8,128)(2,1)S(1)}, u32[]{:S(2)}, u32[]{:S(2)}) collective-permute-start(bf16[2,4,128,1024]{3,2,1,0:T(8,128)(2,1)} %get-tuple-element.71), channel_id=1, source_target_pairs={{0,1},{1,0},{2,3},{3,2},{4,5},{5,4},{6,7},{7,6},{8,9},{9,8},{10,11... | collective-permute-start | bytes 6291464 | tf_op jit(solution)/shard_map/ppermute | solution.py:1401
  106.8 10.1 %collective-permute-start.24 = (bf16[5,128,256]{2,1,0:T(8,128)(2,1)S(1)}, bf16[5,128,256]{2,1,0:T(8,128)(2,1)S(1)}, u32[]{:S(2)}, u32[]{:S(2)}) collective-permute-start(bf16[5,128,256]{2,1,0:T(8,128)(2,1)S(1)} %get-tuple-element.83), channel_id=1, source_target_pairs={{0,8},{4,12},{8,0},{12,4},{16,24},{20,28},{24,16},{28,20},{1,9},{5... | collective-permute-start | bytes 983048 | tf_op jit(solution)/shard_map/ppermute | solution.py:412
  108.3 13.4 %collective-permute-start.28 = (bf16[7,128,256]{2,1,0:T(8,128)(2,1)S(1)}, bf16[7,128,256]{2,1,0:T(8,128)(2,1)S(1)}, u32[]{:S(2)}, u32[]{:S(2)}) collective-permute-start(bf16[7,128,256]{2,1,0:T(8,128)(2,1)S(1)} %get-tuple-element.82), channel_id=1, source_target_pairs={{0,4},{4,0},{8,12},{12,8},{16,20},{20,16},{24,28},{28,24},{1,5},{5... | collective-permute-start | bytes 1376264 | tf_op jit(solution)/shard_map/ppermute | solution.py:412
  117.1 21.3 %collective-permute-start.25 = (bf16[12,128,256]{2,1,0:T(8,128)(2,1)S(1)}, bf16[12,128,256]{2,1,0:T(8,128)(2,1)S(1)}, u32[]{:S(2)}, u32[]{:S(2)}) collective-permute-start(bf16[12,128,256]{2,1,0:T(8,128)(2,1)S(1)} %add_convert_fusion.2), channel_id=1, source_target_pairs={{0,4},{4,0},{8,12},{12,8},{16,20},{20,16},{24,28},{28,24},{1,5},{5... | collective-permute-start | bytes 2359304 | tf_op jit(solution)/shard_map/ppermute | solution.py:412
  121.8 18.1 %collective-permute-start.29 = (bf16[12,128,256]{2,1,0:T(8,128)(2,1)S(1)}, bf16[12,128,256]{2,1,0:T(8,128)(2,1)S(1)}, u32[]{:S(2)}, u32[]{:S(2)}) collective-permute-start(bf16[12,128,256]{2,1,0:T(8,128)(2,1)S(1)} %add_convert_fusion.1), channel_id=1, source_target_pairs={{0,8},{4,12},{8,0},{12,4},{16,24},{20,28},{24,16},{28,20},{1,9},{5... | collective-permute-start | bytes 2359304 | tf_op jit(solution)/shard_map/ppermute | solution.py:412
  122.3 24.0 %collective-permute-start.22 = (bf16[4,128,1024]{2,1,0:T(8,128)(2,1)}, bf16[4,128,1024]{2,1,0:T(8,128)(2,1)}, u32[]{:S(2)}, u32[]{:S(2)}) collective-permute-start(bf16[4,128,1024]{2,1,0:T(8,128)(2,1)} %fusion), channel_id=1, source_target_pairs={{0,2},{1,3},{2,0},{3,1},{4,6},{5,7},{6,4},{7,5},{8,10},{9,11},{10,... | collective-permute-start | bytes 3145736 | tf_op jit(solution)/shard_map/ppermute | solution.py:1403
  123.8 35.7 %collective-permute-start.31 = (bf16[12,128,256]{2,1,0:T(8,128)(2,1)}, bf16[12,128,256]{2,1,0:T(8,128)(2,1)S(1)}, u32[]{:S(2)}, u32[]{:S(2)}) collective-permute-start(bf16[12,128,256]{2,1,0:T(8,128)(2,1)} %get-tuple-element.90), channel_id=1, source_target_pairs={{0,4},{4,0},{8,12},{12,8},{16,20},{20,16},{24,28},{28,24},{1,5},{5... | collective-permute-start | bytes 2359304 | tf_op jit(solution)/shard_map/ppermute | solution.py:412
  141.7 17.7 %collective-permute-start.26 = (bf16[12,128,256]{2,1,0:T(8,128)(2,1)}, bf16[12,128,256]{2,1,0:T(8,128)(2,1)}, u32[]{:S(2)}, u32[]{:S(2)}) collective-permute-start(bf16[12,128,256]{2,1,0:T(8,128)(2,1)} %get-tuple-element.123), channel_id=1, source_target_pairs={{0,8},{4,12},{8,0},{12,4},{16,24},{20,28},{24,16},{28,20},{1,9},{5... | collective-permute-start | bytes 2359304 | tf_op jit(solution)/shard_map/ppermute | solution.py:412
  142.5 16.9 %collective-permute-start.30 = (bf16[12,128,256]{2,1,0:T(8,128)(2,1)}, bf16[12,128,256]{2,1,0:T(8,128)(2,1)}, u32[]{:S(2)}, u32[]{:S(2)}) collective-permute-start(bf16[12,128,256]{2,1,0:T(8,128)(2,1)} %get-tuple-element.124), channel_id=1, source_target_pairs={{0,1},{1,0},{2,3},{3,2},{4,5},{5,4},{6,7},{7,6},{8,16},{9,17},{10,... | collective-permute-start | bytes 2359304 | tf_op jit(solution)/shard_map/ppermute | solution.py:412
  161.8 19.6 %collective-permute-start.27 = (bf16[12,128,256]{2,1,0:T(8,128)(2,1)S(1)}, bf16[12,128,256]{2,1,0:T(8,128)(2,1)S(1)}, u32[]{:S(2)}, u32[]{:S(2)}) collective-permute-start(bf16[12,128,256]{2,1,0:T(8,128)(2,1)S(1)} %get-tuple-element.120), channel_id=1, source_target_pairs={{0,4},{4,0},{8,12},{12,8},{16,20},{20,16},{24,28},{28,24},{1,5},{5... | collective-permute-start | bytes 2359304 | tf_op jit(solution)/shard_map/ppermute | solution.py:412
  163.1 18.4 %collective-permute-start.32 = (bf16[12,128,256]{2,1,0:T(8,128)(2,1)S(1)}, bf16[12,128,256]{2,1,0:T(8,128)(2,1)S(1)}, u32[]{:S(2)}, u32[]{:S(2)}) collective-permute-start(bf16[12,128,256]{2,1,0:T(8,128)(2,1)S(1)} %get-tuple-element.92), channel_id=1, source_target_pairs={{0,8},{4,12},{8,0},{12,4},{16,24},{20,28},{24,16},{28,20},{1,9},{5... | collective-permute-start | bytes 2359304 | tf_op jit(solution)/shard_map/ppermute | solution.py:412
  164.7 16.7 %collective-permute-start.33 = (bf16[12,128,256]{2,1,0:T(8,128)(2,1)S(1)}, bf16[12,128,256]{2,1,0:T(8,128)(2,1)S(1)}, u32[]{:S(2)}, u32[]{:S(2)}) collective-permute-start(bf16[12,128,256]{2,1,0:T(8,128)(2,1)S(1)} %get-tuple-element.93), channel_id=1, source_target_pairs={{0,1},{1,0},{2,3},{3,2},{4,5},{5,4},{6,7},{7,6},{8,16},{9,17},{10,... | collective-permute-start | bytes 2359304 | tf_op jit(solution)/shard_map/ppermute | solution.py:412
  164.7 9.2 %collective-permute-start.21 = (bf16[2,128,1024]{2,1,0:T(8,128)(2,1)S(1)}, bf16[2,128,1024]{2,1,0:T(8,128)(2,1)S(1)}, u32[]{:S(2)}, u32[]{:S(2)}) collective-permute-start(bf16[2,128,1024]{2,1,0:T(8,128)(2,1)S(1)} %copy-done.19), channel_id=1, source_target_pairs={{0,1},{1,0},{2,3},{3,2},{4,5},{5,4},{6,7},{7,6},{8,9},{9,8},{10,11... | collective-permute-start | bytes 1572872 | tf_op jit(solution)/shard_map/ppermute | solution.py:1404
  165.2 2.7 %collective-permute-start.34 = (f32[24,1152]{1,0:T(8,128)S(1)}, f32[24,1152]{1,0:T(8,128)S(1)}, u32[]{:S(2)}, u32[]{:S(2)}) collective-permute-start(f32[24,1152]{1,0:T(8,128)S(1)} %copy-done.32), channel_id=1, source_target_pairs={{0,1},{1,0},{2,3},{3,2},{4,5},{5,4},{6,7},{7,6},{8,9},{9,8},{10,11... | collective-permute-start | bytes 331784 | tf_op jit(solution)/shard_map/ppermute | solution.py:1470
  167.9 5.2 %collective-permute-start.35 = (f32[24,1152]{1,0:T(8,128)S(1)}, f32[24,1152]{1,0:T(8,128)S(1)}, u32[]{:S(2)}, u32[]{:S(2)}) collective-permute-start(f32[24,1152]{1,0:T(8,128)S(1)} %add.94), channel_id=1, source_target_pairs={{0,2},{1,3},{2,0},{3,1},{4,6},{5,7},{6,4},{7,5},{8,10},{9,11},{10,... | collective-permute-start | bytes 331784 | tf_op jit(solution)/shard_map/ppermute | solution.py:1471
  173.1 8.3 %collective-permute-start.36 = (f32[24,1152]{1,0:T(8,128)S(1)}, f32[24,1152]{1,0:T(8,128)S(1)}, u32[]{:S(2)}, u32[]{:S(2)}) collective-permute-start(f32[24,1152]{1,0:T(8,128)S(1)} %add.95), channel_id=1, source_target_pairs={{0,4},{4,0},{8,12},{12,8},{16,20},{20,16},{24,28},{28,24},{1,5},{5... | collective-permute-start | bytes 331784 | tf_op jit(solution)/shard_map/ppermute | solution.py:1472
  173.9 8.0 %collective-permute-start.23 = (bf16[128,1024]{1,0:T(8,128)(2,1)S(1)}, bf16[128,1024]{1,0:T(8,128)(2,1)S(1)}, u32[]{:S(2)}, u32[]{:S(2)}) collective-permute-start(bf16[128,1024]{1,0:T(8,128)(2,1)S(1)} %fusion.12), channel_id=1, source_target_pairs={{0,2},{1,3},{2,0},{3,1},{4,6},{5,7},{6,4},{7,5},{8,10},{9,11},{10,... | collective-permute-start | bytes 786440 | tf_op jit(solution)/shard_map/ppermute | solution.py:1406
  182.0 16.8 %collective-permute-start.37 = (bf16[12,128,256]{2,1,0:T(8,128)(2,1)S(1)}, bf16[12,128,256]{2,1,0:T(8,128)(2,1)S(1)}, u32[]{:S(2)}, u32[]{:S(2)}) collective-permute-start(bf16[12,128,256]{2,1,0:T(8,128)(2,1)S(1)} %add_convert_fusion.shard0), channel_id=1, source_target_pairs={{0,2},{1,3},{2,0},{3,1},{4,6},{5,7},{6,4},{7,5},{8,10},{9,11},{10,... | collective-permute-start | bytes 2359304 | tf_op jit(solution)/shard_map/ppermute | solution.py:1474
  183.5 5.2 %collective-permute-start.39 = (f32[24,1152]{1,0:T(8,128)S(1)}, f32[24,1152]{1,0:T(8,128)S(1)}, u32[]{:S(2)}, u32[]{:S(2)}) collective-permute-start(f32[24,1152]{1,0:T(8,128)S(1)} %add.96), channel_id=1, source_target_pairs={{0,8},{4,12},{8,0},{12,4},{16,24},{20,28},{24,16},{28,20},{1,9},{5... | collective-permute-start | bytes 331784 | tf_op jit(solution)/shard_map/ppermute | solution.py:1477
  188.7 6.9 %collective-permute-start.40 = (f32[24,1152]{1,0:T(8,128)S(1)}, f32[24,1152]{1,0:T(8,128)S(1)}, u32[]{:S(2)}, u32[]{:S(2)}) collective-permute-start(f32[24,1152]{1,0:T(8,128)S(1)} %add.97), channel_id=1, source_target_pairs={{0,16},{4,20},{8,24},{12,28},{16,0},{20,4},{24,8},{28,12},{1,17},{... | collective-permute-start | bytes 331784 | tf_op jit(solution)/shard_map/ppermute | solution.py:1477
  195.6 5.6 %collective-permute-start.38 = (bf16[12,128,256]{2,1,0:T(8,128)(2,1)S(1)}, bf16[12,128,256]{2,1,0:T(8,128)(2,1)S(1)}, u32[]{:S(2)}, u32[]{:S(2)}) collective-permute-start(bf16[12,128,256]{2,1,0:T(8,128)(2,1)S(1)} %add_convert_fusion.shard0), channel_id=1, source_target_pairs={{0,1},{1,0},{2,3},{3,2},{4,5},{5,4},{6,7},{7,6},{8,9},{9,8},{10,11... | collective-permute-start | bytes 2359304 | tf_op jit(solution)/shard_map/ppermute | solution.py:1475
  198.8 2.5 %collective-permute-start.41 = (bf16[12,128,256]{2,1,0:T(8,128)(2,1)S(1)}, bf16[12,128,256]{2,1,0:T(8,128)(2,1)S(1)}, u32[]{:S(2)}, u32[]{:S(2)}) collective-permute-start(bf16[12,128,256]{2,1,0:T(8,128)(2,1)S(1)} %collective-permute-done.37.shard1), channel_id=1, source_target_pairs={{0,1},{1,0},{2,3},{3,2},{4,5},{5,4},{6,7},{7,6},{8,9},{9,8},{10,11... | collective-permute-start | bytes 2359304 | tf_op jit(solution)/shard_map/ppermute | solution.py:1479
  198.8 2.4 %collective-permute-start.42 = (f32[24,1152]{1,0:T(8,128)S(1)}, f32[24,1152]{1,0:T(8,128)S(1)}, u32[]{:S(2)}, u32[]{:S(2)}) collective-permute-start(f32[24,1152]{1,0:T(8,128)S(1)} %add.98.small_own), channel_id=1, source_target_pairs={{0,1},{1,0},{2,3},{3,2},{4,5},{5,4},{6,7},{7,6},{8,9},{9,8},{10,11... | collective-permute-start | bytes 331784 | tf_op jit(solution)/shard_map/ppermute | solution.py:1478
  (30 other events, 445.8 us)

commit v9 on v8

--- a/solution.py
+++ b/solution.py
@@ -908,7 +908,7 @@
             grad_lin[2, span, cols] = merge(grad_value, twin).astype(jnp.bfloat16)
         return carry
 
-    lax.fori_loop(0, 4, units, 0, unroll=2)
+    lax.fori_loop(0, 4, units, 0, unroll=4)
 
     for copy in third:
         copy.wait()
@@ -959,7 +959,7 @@
 
         return carry
 
-    lax.fori_loop(0, 4, weights, 0, unroll=2)
+    lax.fori_loop(0, 4, weights, 0, unroll=4)
     grad = outer_sum(lhs_all[:, WIDTH:], acts[4]).astype(jnp.bfloat16)
     for block in range(4):
         part = grad[:, block * 256 : block * 256 + 256]
@@ -1014,7 +1014,7 @@
         put(4, cols, matmul(lhs_all[...], jnp.concatenate(right)))
         return carry
 
-    lax.fori_loop(0, 4, feed, 0, unroll=2)
+    lax.fori_loop(0, 4, feed, 0, unroll=4)
     ship(3)
     ship(4)
     for copy in sent:

time: 205 us -> 204 us (level)
  no operation moved by 1% of the time
where the time goes in v9:
time: 204 us
  waiting for transfers between devices  105 us (51%)
  Pallas kernels  47.8 us (23%)
  starting transfers between devices  39.7 us (19%)
  other arithmetic  8.98 us (4%)
    ppermute x22, waiting for transfers between devices, fsdp_move(): lax.ppermute(value, 'fsdp' if len(pairs) == 8 else ('fsdp', 'replica'), p...  70.7 us
    pallas_call x4, Pallas kernels, call(): pl.pallas_call(kernel, out_shape=outs, in_specs=specs, out_specs=out_spec...  34.9 us
    ppermute x22, starting transfers between devices, fsdp_move(): lax.ppermute(value, 'fsdp' if len(pairs) == 8 else ('fsdp', 'replica'), p...  22.9 us
    pallas_call x1, Pallas kernels, back(): pl.pallas_call(back_kernel, grid=(1,), out_shape=(shape_of((seqs, STREAMS...  12.9 us
    ppermute x2, waiting for transfers between devices, on_device_tensor(): small = small + lax.ppermute(small, 'fsdp', perm)  9.97 us
    ppermute x1, waiting for transfers between devices, on_device_tensor(): small = small + lax.ppermute(small, 'fsdp', Y_SWAP)  5.72 us
    convert_element_type x5, other arithmetic, low(): return value.astype(jnp.bfloat16)  4.89 us
  transfers between devices with their start and end apart: 43, of which 25 were waited for; matrix products, arithmetic and copies ran while one was open for 4% of the time, Pallas kernels for 11%

profile of v9, /device:TPU:0, one launch (start us, length us, event | category | flops | bytes accessed | tf_op | source)
XLA Modules:
  0.0 203.7 jit_solution(11948506482859446518)
XLA Ops:
  0.7 3.0 %collective-permute-start = (bf16[36,128]{1,0:T(8,128)(2,1)}, bf16[36,128]{1,0:T(8,128)(2,1)S(1)}, u32[]{:S(2)}, u32[]{:S(2)}) collective-permute-start(bf16[36,128]{1,0:T(8,128)(2,1)} %bitcast.49), channel_id=1, source_target_pairs={{0,4},{4,0},{8,12},{12,8},{16,20},{20,16},{24,28},{28,24},{1,5},{5... | collective-permute-start | bytes 27656 | tf_op jit(solution)/shard_map/ppermute | solution.py:1312
  3.8 2.7 %shard_map.246.piece0 = bf16[12,128,256]{2,1,0:T(8,128)(2,1)} custom-call(bf16[3,128,1024]{2,1,0:T(8,128)(2,1)} %projection.1, bf16[128,1024]{1,0:T(8,128)(2,1)} %out_weight.1, bf16[128,4096]{1,0:T(8,128)(2,1)} %up_weight.1, bf16[512,1024]{1,0:T(8,128)(2,1)} %down_weight.1), custom_call_target="tpu_custom_call" | custom-call | tf_op jit(solution)/shard_map/pallas_call | solution.py:1242
  6.5 2.7 %collective-permute-start.2 = (bf16[36,256]{1,0:T(8,128)(2,1)S(1)}, bf16[36,256]{1,0:T(8,128)(2,1)S(1)}, u32[]{:S(2)}, u32[]{:S(2)}) collective-permute-start(bf16[36,256]{1,0:T(8,128)(2,1)S(1)} %pad_maximum_fusion.up_own), channel_id=1, source_target_pairs={{0,16},{4,20},{8,24},{12,28},{16,0},{20,4},{24,8},{28,12},{1,17},{... | collective-permute-start | bytes 55304 | tf_op jit(solution)/shard_map/ppermute | solution.py:412
  9.2 1.3 collective-permute-start.1
  11.3 1.9 collective-permute-done.1.up_one
  14.6 1.5 collective-permute-start.7
  17.4 6.3 %shard_map.247 = (bf16[528,1024]{1,0:T(8,128)(2,1)S(1)}, f32[4,128,1024]{2,1,0:T(8,128)S(1)}, f32[3,128,128]{2,1,0:T(8,128)S(1)}, f32[128,1024]{1,0:T(8,128)S(1)}, bf16[36,1024]{1,0:T(8,128)(2,1)S(1)}) custom-call(s32[4]{0:T(128)S(1)} %pad_add_fusion.bounds, bf16[2,9,64,1024]{3,2,1,0:T(8,128)(2,1)S(1)} %bitcast.41, f32[1,1024]{1,0:T(1,128)S(1)} %bitcast.47, ...), custom_call_target="tpu_custom_call" | custom-call | tf_op jit(solution)/shard_map/pallas_call | solution.py:1242
  23.7 8.9 %collective-permute-done.12.piece3 = bf16[12,128,256]{2,1,0:T(8,128)(2,1)S(1)} collective-permute-done((bf16[12,128,256]{2,1,0:T(8,128)(2,1)}, bf16[12,128,256]{2,1,0:T(8,128)(2,1)S(1)}, u32[]{:S(2)}, u32[]{:S(2)}) %collective-permute-start.12) | collective-permute-done | bytes 786464 | tf_op jit(solution)/shard_map/ppermute | solution.py:412
  33.2 1.7 collective-permute-start.14
  34.9 1.5 collective-permute-start.4
  36.4 1.2 broadcast_select_fusion.1
  37.7 1.4 collective-permute-start.15
  39.1 14.1 %collective-permute-done.14.piece5 = bf16[12,128,256]{2,1,0:T(8,128)(2,1)S(1)} collective-permute-done((bf16[12,128,256]{2,1,0:T(8,128)(2,1)S(1)}, bf16[12,128,256]{2,1,0:T(8,128)(2,1)S(1)}, u32[]{:S(2)}, u32[]{:S(2)}) %collective-permute-start.14) | collective-permute-done | bytes 786464 | tf_op jit(solution)/shard_map/ppermute | solution.py:412
  53.3 1.4 collective-permute-start.17
  55.7 1.6 collective-permute-start.16
  57.3 2.2 %collective-permute-done.4.packet1 = bf16[528,1024]{1,0:T(8,128)(2,1)S(1)} collective-permute-done((bf16[528,1024]{1,0:T(8,128)(2,1)S(1)}, bf16[528,1024]{1,0:T(8,128)(2,1)S(1)}, u32[]{:S(2)}, u32[]{:S(2)}) %collective-permute-start.4) | collective-permute-done | bytes 1081376 | tf_op jit(solution)/shard_map/ppermute | solution.py:1357
  60.0 12.5 %collective-permute-done.17.piece8 = bf16[12,128,256]{2,1,0:T(8,128)(2,1)S(1)} collective-permute-done((bf16[12,128,256]{2,1,0:T(8,128)(2,1)S(1)}, bf16[12,128,256]{2,1,0:T(8,128)(2,1)S(1)}, u32[]{:S(2)}, u32[]{:S(2)}) %collective-permute-start.17) | collective-permute-done | bytes 786464 | tf_op jit(solution)/shard_map/ppermute | solution.py:412
  73.6 1.1 collective-permute-start.19
  74.7 1.7 collective-permute-done.9.cotangent3
  76.4 6.0 %collective-permute-done.18.piece9 = bf16[6,128,256]{2,1,0:T(8,128)(2,1)S(1)} collective-permute-done((bf16[6,128,256]{2,1,0:T(8,128)(2,1)S(1)}, bf16[6,128,256]{2,1,0:T(8,128)(2,1)S(1)}, u32[]{:S(2)}, u32[]{:S(2)}) %collective-permute-start.18) | collective-permute-done | bytes 393248 | tf_op jit(solution)/shard_map/ppermute | solution.py:412
  83.2 22.5 %shard_map.248 = (bf16[7,128,256]{2,1,0:T(8,128)(2,1)S(1)}, bf16[5,128,256]{2,1,0:T(8,128)(2,1)S(1)}, bf16[12,128,256]{2,1,0:T(8,128)(2,1)S(1)}, bf16[12,128,256...) custom-call(f32[3,128,128]{2,1,0:T(8,128)S(1)} %copy-done.11, ...), custom_call_target="tpu_custom_call" | custom-call | tf_op jit(solution)/shard_map/pallas_call | solution.py:1242
  105.9 1.5 collective-permute-start.24
  107.3 1.3 collective-permute-start.28
  108.7 7.3 %collective-permute-done.24 = bf16[5,128,256]{2,1,0:T(8,128)(2,1)S(1)} collective-permute-done((bf16[5,128,256]{2,1,0:T(8,128)(2,1)S(1)}, bf16[5,128,256]{2,1,0:T(8,128)(2,1)S(1)}, u32[]{:S(2)}, u32[]{:S(2)}) %collective-permute-start.24) | collective-permute-done | bytes 327712 | tf_op jit(solution)/shard_map/ppermute | solution.py:412
  116.2 1.4 collective-permute-start.25
  117.6 1.7 fusion
  119.3 1.4 collective-permute-done.28
  121.3 1.5 collective-permute-start.22
  123.8 13.8 %collective-permute-done.25 = bf16[12,128,256]{2,1,0:T(8,128)(2,1)S(1)} collective-permute-done((bf16[12,128,256]{2,1,0:T(8,128)(2,1)S(1)}, bf16[12,128,256]{2,1,0:T(8,128)(2,1)S(1)}, u32[]{:S(2)}, u32[]{:S(2)}) %collective-permute-start.25) | collective-permute-done | bytes 786464 | tf_op jit(solution)/shard_map/ppermute | solution.py:412
  137.5 1.3 collective-permute-done.29
  138.9 1.9 fusion.2
  141.5 3.8 %collective-permute-done.22.across = bf16[4,128,1024]{2,1,0:T(8,128)(2,1)} collective-permute-done((bf16[4,128,1024]{2,1,0:T(8,128)(2,1)}, bf16[4,128,1024]{2,1,0:T(8,128)(2,1)}, u32[]{:S(2)}, u32[]{:S(2)}) %collective-permute-start.22) | collective-permute-done | bytes 1048608 | tf_op jit(solution)/shard_map/ppermute | solution.py:1403
  145.3 12.9 %shard_map.249 = (bf16[2,9,64,1024]{3,2,1,0:T(8,128)(2,1)}, f32[24,1152]{1,0:T(8,128)}, f32[24,1152]{1,0:T(8,128)}, f32[2,9,4,64]{3,2,1,0:T(4,128)}) custom-call(bf16[2,9,64,1024]{3,2,1,0:T(8,128)(2,1)} %bitcast.40, bf16[128,1024]{1,0:T(8,128)(2,1)} %bitcast.42, f32[4,128,1024]{2,1,0:T(8,128)} %copy-done.2, f32[3,128,128]{2,1,0:T(8,128)} %copy-done.12, ...), custom_call_target="tpu_custom_call" | custom-call | tf_op jit(solution)/shard_map/pallas_call | solution.py:1417
  158.3 2.3 %fusion.6 = (bf16[12,128,256]{2,1,0:T(8,128)(2,1)S(1)}, bf16[12,128,256]{2,1,0:T(8,128)(2,1)S(1)}, bf16[12,128,256]{2,1,0:T(8,128)(2,1)S(1)}) fusion(bf16[12,128,256]{2,1,0:T(8,128)(2,1)} %collective-permute-done.26, bf16[12,128,256]{2,1,0:T(8,128)(2,1)S(1)} %get-tuple-element.81, pred[]{:T(512)S(6)} %eq.15, ...), kind=kLoop, calls=%fused_computation.13 | loop fusion | flops 5898240 | bytes 7077890 | tf_op jit(solution)/shard_map/convert_element_type | solution.py:481
  160.7 1.4 collective-permute-start.27
  162.0 1.7 collective-permute-start.32
  164.3 2.6 %collective-permute-done.34 = f32[24,1152]{1,0:T(8,128)S(1)} collective-permute-done((f32[24,1152]{1,0:T(8,128)S(1)}, f32[24,1152]{1,0:T(8,128)S(1)}, u32[]{:S(2)}, u32[]{:S(2)}) %collective-permute-start.34) | collective-permute-done | bytes 110624 | tf_op jit(solution)/shard_map/ppermute | solution.py:1470
  167.0 1.5 collective-permute-start.35
  168.5 3.6 %collective-permute-done.35 = f32[24,1152]{1,0:T(8,128)S(1)} collective-permute-done((f32[24,1152]{1,0:T(8,128)S(1)}, f32[24,1152]{1,0:T(8,128)S(1)}, u32[]{:S(2)}, u32[]{:S(2)}) %collective-permute-start.35) | collective-permute-done | bytes 110624 | tf_op jit(solution)/shard_map/ppermute | solution.py:1471
  173.0 1.5 collective-permute-start.23
  174.5 5.7 %collective-permute-done.36 = f32[24,1152]{1,0:T(8,128)S(1)} collective-permute-done((f32[24,1152]{1,0:T(8,128)S(1)}, f32[24,1152]{1,0:T(8,128)S(1)}, u32[]{:S(2)}, u32[]{:S(2)}) %collective-permute-start.36) | collective-permute-done | bytes 110624 | tf_op jit(solution)/shard_map/ppermute | solution.py:1472
  180.8 1.5 collective-permute-start.37
  183.2 4.1 %collective-permute-done.39 = f32[24,1152]{1,0:T(8,128)S(1)} collective-permute-done((f32[24,1152]{1,0:T(8,128)S(1)}, f32[24,1152]{1,0:T(8,128)S(1)}, u32[]{:S(2)}, u32[]{:S(2)}) %collective-permute-start.39) | collective-permute-done | bytes 110624 | tf_op jit(solution)/shard_map/ppermute | solution.py:1477
  187.3 1.0 collective-permute-start.40
  188.3 5.9 %collective-permute-done.40 = f32[24,1152]{1,0:T(8,128)S(1)} collective-permute-done((f32[24,1152]{1,0:T(8,128)S(1)}, f32[24,1152]{1,0:T(8,128)S(1)}, u32[]{:S(2)}, u32[]{:S(2)}) %collective-permute-start.40) | collective-permute-done | bytes 110624 | tf_op jit(solution)/shard_map/ppermute | solution.py:1477
  194.3 3.5 %collective-permute-done.37.shard1 = bf16[12,128,256]{2,1,0:T(8,128)(2,1)S(1)} collective-permute-done((bf16[12,128,256]{2,1,0:T(8,128)(2,1)S(1)}, bf16[12,128,256]{2,1,0:T(8,128)(2,1)S(1)}, u32[]{:S(2)}, u32[]{:S(2)}) %collective-permute-start.37) | collective-permute-done | bytes 786464 | tf_op jit(solution)/shard_map/ppermute | solution.py:1474
  199.2 1.1 collective-permute-done.42.small_other
  200.3 3.4 %shard_map.250 = (f32[3,128,1024]{2,1,0:T(8,128)}, f32[128,1024]{1,0:T(8,128)}, f32[128,4096]{1,0:T(8,128)}, f32[512,1024]{1,0:T(8,128)}, f32[1,1024]{1,0:T(1,12...) custom-call(bf16[12,128,256]{2,1,0:T(8,128)(2,1)S(1)} %add_convert_fus, ...), custom_call_target="tpu_custom_call" | custom-call | tf_op jit(solution)/shard_map/pallas_call | solution.py:1242
  (134 shorter events, 14.3 us)
Async XLA Ops:
  0.7 5.8 %collective-permute-start = (bf16[36,128]{1,0:T(8,128)(2,1)}, bf16[36,128]{1,0:T(8,128)(2,1)S(1)}, u32[]{:S(2)}, u32[]{:S(2)}) collective-permute-start(bf16[36,128]{1,0:T(8,128)(2,1)} %bitcast.49), channel_id=1, source_target_pairs={{0,4},{4,0},{8,12},{12,8},{16,20},{20,16},{24,28},{28,24},{1,5},{5... | collective-permute-start | bytes 27656 | tf_op jit(solution)/shard_map/ppermute | solution.py:1312
  6.5 4.7 %collective-permute-start.2 = (bf16[36,256]{1,0:T(8,128)(2,1)S(1)}, bf16[36,256]{1,0:T(8,128)(2,1)S(1)}, u32[]{:S(2)}, u32[]{:S(2)}) collective-permute-start(bf16[36,256]{1,0:T(8,128)(2,1)S(1)} %pad_maximum_fusion.up_own), channel_id=1, source_target_pairs={{0,16},{4,20},{8,24},{12,28},{16,0},{20,4},{24,8},{28,12},{1,17},{... | collective-permute-start | bytes 55304 | tf_op jit(solution)/shard_map/ppermute | solution.py:412
  9.2 4.0 %collective-permute-start.1 = (bf16[36,256]{1,0:T(8,128)(2,1)S(1)}, bf16[36,256]{1,0:T(8,128)(2,1)S(1)}, u32[]{:S(2)}, u32[]{:S(2)}) collective-permute-start(bf16[36,256]{1,0:T(8,128)(2,1)S(1)} %pad_maximum_fusion.up_own), channel_id=1, source_target_pairs={{8,0},{25,1},{10,2},{27,3},{12,4},{29,5},{14,6},{31,7},{16,8},{1,9... | collective-permute-start | bytes 55304 | tf_op jit(solution)/shard_map/ppermute | solution.py:412
  13.2 19.5 %collective-permute-start.12 = (bf16[12,128,256]{2,1,0:T(8,128)(2,1)}, bf16[12,128,256]{2,1,0:T(8,128)(2,1)S(1)}, u32[]{:S(2)}, u32[]{:S(2)}) collective-permute-start(bf16[12,128,256]{2,1,0:T(8,128)(2,1)} %shard_map.246.piece0), channel_id=1, source_target_pairs={{0,4},{1,5},{2,6},{3,7},{4,0},{5,1},{6,2},{7,3},{8,16},{9,17},{10,... | collective-permute-start | bytes 2359304 | tf_op jit(solution)/shard_map/ppermute | solution.py:412
  14.1 19.1 %collective-permute-start.11 = (bf16[12,128,256]{2,1,0:T(8,128)(2,1)}, bf16[12,128,256]{2,1,0:T(8,128)(2,1)}, u32[]{:S(2)}, u32[]{:S(2)}) collective-permute-start(bf16[12,128,256]{2,1,0:T(8,128)(2,1)} %shard_map.246.piece0), channel_id=1, source_target_pairs={{0,8},{4,12},{8,0},{12,4},{16,24},{20,28},{24,16},{28,20},{1,9},{5... | collective-permute-start | bytes 2359304 | tf_op jit(solution)/shard_map/ppermute | solution.py:412
  14.6 18.5 %collective-permute-start.10 = (bf16[12,128,256]{2,1,0:T(8,128)(2,1)}, bf16[12,128,256]{2,1,0:T(8,128)(2,1)}, u32[]{:S(2)}, u32[]{:S(2)}) collective-permute-start(bf16[12,128,256]{2,1,0:T(8,128)(2,1)} %shard_map.246.piece0), channel_id=1, source_target_pairs={{0,1},{1,0},{2,3},{3,2},{4,5},{5,4},{6,7},{7,6},{8,12},{9,13},{10,... | collective-permute-start | bytes 2359304 | tf_op jit(solution)/shard_map/ppermute | solution.py:412
  14.6 9.1 %collective-permute-start.7 = (bf16[128,1024]{1,0:T(8,128)(2,1)S(1)}, bf16[128,1024]{1,0:T(8,128)(2,1)}, u32[]{:S(2)}, u32[]{:S(2)}) collective-permute-start(bf16[128,1024]{1,0:T(8,128)(2,1)S(1)} %bitcast.43), channel_id=1, source_target_pairs={{0,2},{1,3},{2,0},{3,1},{4,6},{5,7},{6,4},{7,5},{8,10},{9,11},{10,... | collective-permute-start | bytes 786440 | tf_op jit(solution)/shard_map/ppermute | solution.py:1324
  16.1 1.2 collective-permute-start.3
  23.7 33.6 %copy-start.3 = (bf16[528,1024]{1,0:T(8,128)(2,1)}, bf16[528,1024]{1,0:T(8,128)(2,1)S(1)}, u32[]{:S(2)}) copy-start(bf16[528,1024]{1,0:T(8,128)(2,1)S(1)} %get-tuple-element.62.packet0) | copy-start | bytes 3244036
  33.2 5.9 %collective-permute-start.13 = (bf16[12,128,256]{2,1,0:T(8,128)(2,1)}, bf16[12,128,256]{2,1,0:T(8,128)(2,1)S(1)}, u32[]{:S(2)}, u32[]{:S(2)}) collective-permute-start(bf16[12,128,256]{2,1,0:T(8,128)(2,1)} %collective-permute-done.11.piece2), channel_id=1, source_target_pairs={{0,1},{1,0},{2,3},{3,2},{4,5},{5,4},{6,7},{7,6},{8,16},{9,17},{10,... | collective-permute-start | bytes 2359304 | tf_op jit(solution)/shard_map/ppermute | solution.py:412
  33.2 20.0 %collective-permute-start.14 = (bf16[12,128,256]{2,1,0:T(8,128)(2,1)S(1)}, bf16[12,128,256]{2,1,0:T(8,128)(2,1)S(1)}, u32[]{:S(2)}, u32[]{:S(2)}) collective-permute-start(bf16[12,128,256]{2,1,0:T(8,128)(2,1)S(1)} %collective-permute-done.12.piece3), channel_id=1, source_target_pairs={{0,8},{4,12},{8,0},{12,4},{16,24},{20,28},{24,16},{28,20},{1,9},{5... | collective-permute-start | bytes 2359304 | tf_op jit(solution)/shard_map/ppermute | solution.py:412
  34.9 24.5 %collective-permute-start.4 = (bf16[528,1024]{1,0:T(8,128)(2,1)S(1)}, bf16[528,1024]{1,0:T(8,128)(2,1)S(1)}, u32[]{:S(2)}, u32[]{:S(2)}) collective-permute-start(bf16[528,1024]{1,0:T(8,128)(2,1)S(1)} %get-tuple-element.62.packet0), channel_id=1, source_target_pairs={{0,2},{1,3},{2,0},{3,1},{4,6},{5,7},{6,4},{7,5},{8,10},{9,11},{10,... | collective-permute-start | bytes 3244040 | tf_op jit(solution)/shard_map/ppermute | solution.py:1357
  37.6 45.6 %copy-start.1 = (bf16[12,128,256]{2,1,0:T(8,128)(2,1)S(1)}, bf16[12,128,256]{2,1,0:T(8,128)(2,1)}, u32[]{:S(2)}) copy-start(bf16[12,128,256]{2,1,0:T(8,128)(2,1)} %shard_map.246.piece0) | copy-start | bytes 2359300
  37.6 45.6 %copy-start.11 = (f32[3,128,128]{2,1,0:T(8,128)S(1)}, f32[3,128,128]{2,1,0:T(8,128)}, u32[]{:S(2)}) copy-start(f32[3,128,128]{2,1,0:T(8,128)} %constant.39.clone.rope) | copy-start | bytes 589828
  37.7 18.0 %collective-permute-start.15 = (bf16[12,128,256]{2,1,0:T(8,128)(2,1)S(1)}, bf16[12,128,256]{2,1,0:T(8,128)(2,1)S(1)}, u32[]{:S(2)}, u32[]{:S(2)}) collective-permute-start(bf16[12,128,256]{2,1,0:T(8,128)(2,1)S(1)} %broadcast_select_fusion.1), channel_id=1, source_target_pairs={{0,4},{4,0},{8,12},{12,8},{16,20},{20,16},{24,28},{28,24},{1,5},{5... | collective-permute-start | bytes 2359304 | tf_op jit(solution)/shard_map/ppermute | solution.py:412
  39.1 33.5 %copy-start.21 = (bf16[12,128,256]{2,1,0:T(8,128)(2,1)}, bf16[12,128,256]{2,1,0:T(8,128)(2,1)S(1)}, u32[]{:S(2)}) copy-start(bf16[12,128,256]{2,1,0:T(8,128)(2,1)S(1)} %collective-permute-done.13.piece4) | copy-start | bytes 2359300
  53.1 30.0 %copy-start.22 = (bf16[12,128,256]{2,1,0:T(8,128)(2,1)}, bf16[12,128,256]{2,1,0:T(8,128)(2,1)S(1)}, u32[]{:S(2)}) copy-start(bf16[12,128,256]{2,1,0:T(8,128)(2,1)S(1)} %collective-permute-done.14.piece5) | copy-start | bytes 2359300
  53.3 19.2 %collective-permute-start.17 = (bf16[12,128,256]{2,1,0:T(8,128)(2,1)S(1)}, bf16[12,128,256]{2,1,0:T(8,128)(2,1)S(1)}, u32[]{:S(2)}, u32[]{:S(2)}) collective-permute-start(bf16[12,128,256]{2,1,0:T(8,128)(2,1)S(1)} %broadcast_select_fusion), channel_id=1, source_target_pairs={{0,4},{4,0},{8,12},{12,8},{16,20},{20,16},{24,28},{28,24},{1,5},{5... | collective-permute-start | bytes 2359304 | tf_op jit(solution)/shard_map/ppermute | solution.py:412
  55.7 17.9 %collective-permute-start.16 = (bf16[12,128,256]{2,1,0:T(8,128)(2,1)S(1)}, bf16[12,128,256]{2,1,0:T(8,128)(2,1)S(1)}, u32[]{:S(2)}, u32[]{:S(2)}) collective-permute-start(bf16[12,128,256]{2,1,0:T(8,128)(2,1)S(1)} %collective-permute-done.13.piece4), channel_id=1, source_target_pairs={{0,8},{4,12},{8,0},{12,4},{16,24},{20,28},{24,16},{28,20},{1,9},{5... | collective-permute-start | bytes 2359304 | tf_op jit(solution)/shard_map/ppermute | solution.py:412
  57.3 19.1 %collective-permute-start.5 = (bf16[528,1024]{1,0:T(8,128)(2,1)S(1)}, bf16[528,1024]{1,0:T(8,128)(2,1)S(1)}, u32[]{:S(2)}, u32[]{:S(2)}) collective-permute-start(bf16[528,1024]{1,0:T(8,128)(2,1)S(1)} %get-tuple-element.62.packet0), channel_id=1, source_target_pairs={{0,1},{1,0},{2,3},{3,2},{4,5},{5,4},{6,7},{7,6},{8,9},{9,8},{10,11... | collective-permute-start | bytes 3244040 | tf_op jit(solution)/shard_map/ppermute | solution.py:1358
  59.5 17.0 %collective-permute-start.6 = (bf16[528,1024]{1,0:T(8,128)(2,1)S(1)}, bf16[528,1024]{1,0:T(8,128)(2,1)S(1)}, u32[]{:S(2)}, u32[]{:S(2)}) collective-permute-start(bf16[528,1024]{1,0:T(8,128)(2,1)S(1)} %collective-permute-done.4.packet1), channel_id=1, source_target_pairs={{0,1},{1,0},{2,3},{3,2},{4,5},{5,4},{6,7},{7,6},{8,9},{9,8},{10,11... | collective-permute-start | bytes 3244040 | tf_op jit(solution)/shard_map/ppermute | solution.py:1359
  59.5 15.2 %collective-permute-start.8 = (bf16[128,1024]{1,0:T(8,128)(2,1)S(1)}, bf16[128,1024]{1,0:T(8,128)(2,1)S(1)}, u32[]{:S(2)}, u32[]{:S(2)}) collective-permute-start(bf16[128,1024]{1,0:T(8,128)(2,1)S(1)} %bitcast.44), channel_id=1, source_target_pairs={{0,1},{1,0},{2,3},{3,2},{4,5},{5,4},{6,7},{7,6},{8,9},{9,8},{10,11... | collective-permute-start | bytes 786440 | tf_op jit(solution)/shard_map/ppermute | solution.py:1328
  72.6 9.9 %collective-permute-start.18 = (bf16[6,128,256]{2,1,0:T(8,128)(2,1)S(1)}, bf16[6,128,256]{2,1,0:T(8,128)(2,1)S(1)}, u32[]{:S(2)}, u32[]{:S(2)}) collective-permute-start(bf16[6,128,256]{2,1,0:T(8,128)(2,1)S(1)} %slice.28), channel_id=1, source_target_pairs={{0,8},{4,12},{8,0},{12,4},{16,24},{20,28},{24,16},{28,20},{1,9},{5... | collective-permute-start | bytes 1179656 | tf_op jit(solution)/shard_map/ppermute | solution.py:412
  73.6 9.6 %collective-permute-start.19 = (bf16[6,128,256]{2,1,0:T(8,128)(2,1)S(1)}, bf16[6,128,256]{2,1,0:T(8,128)(2,1)S(1)}, u32[]{:S(2)}, u32[]{:S(2)}) collective-permute-start(bf16[6,128,256]{2,1,0:T(8,128)(2,1)S(1)} %slice.29), channel_id=1, source_target_pairs={{0,4},{4,0},{8,12},{12,8},{16,20},{20,16},{24,28},{28,24},{1,5},{5... | collective-permute-start | bytes 1179656 | tf_op jit(solution)/shard_map/ppermute | solution.py:412
  74.7 1.7 collective-permute-start.9
  105.8 11.8 %collective-permute-start.20 = (bf16[2,4,128,1024]{3,2,1,0:T(8,128)(2,1)}, bf16[2,4,128,1024]{3,2,1,0:T(8,128)(2,1)S(1)}, u32[]{:S(2)}, u32[]{:S(2)}) collective-permute-start(bf16[2,4,128,1024]{3,2,1,0:T(8,128)(2,1)} %get-tuple-element.71), channel_id=1, source_target_pairs={{0,1},{1,0},{2,3},{3,2},{4,5},{5,4},{6,7},{7,6},{8,9},{9,8},{10,11... | collective-permute-start | bytes 6291464 | tf_op jit(solution)/shard_map/ppermute | solution.py:1401
  105.9 10.1 %collective-permute-start.24 = (bf16[5,128,256]{2,1,0:T(8,128)(2,1)S(1)}, bf16[5,128,256]{2,1,0:T(8,128)(2,1)S(1)}, u32[]{:S(2)}, u32[]{:S(2)}) collective-permute-start(bf16[5,128,256]{2,1,0:T(8,128)(2,1)S(1)} %get-tuple-element.83), channel_id=1, source_target_pairs={{0,8},{4,12},{8,0},{12,4},{16,24},{20,28},{24,16},{28,20},{1,9},{5... | collective-permute-start | bytes 983048 | tf_op jit(solution)/shard_map/ppermute | solution.py:412
  107.3 13.4 %collective-permute-start.28 = (bf16[7,128,256]{2,1,0:T(8,128)(2,1)S(1)}, bf16[7,128,256]{2,1,0:T(8,128)(2,1)S(1)}, u32[]{:S(2)}, u32[]{:S(2)}) collective-permute-start(bf16[7,128,256]{2,1,0:T(8,128)(2,1)S(1)} %get-tuple-element.82), channel_id=1, source_target_pairs={{0,4},{4,0},{8,12},{12,8},{16,20},{20,16},{24,28},{28,24},{1,5},{5... | collective-permute-start | bytes 1376264 | tf_op jit(solution)/shard_map/ppermute | solution.py:412
  116.2 21.3 %collective-permute-start.25 = (bf16[12,128,256]{2,1,0:T(8,128)(2,1)S(1)}, bf16[12,128,256]{2,1,0:T(8,128)(2,1)S(1)}, u32[]{:S(2)}, u32[]{:S(2)}) collective-permute-start(bf16[12,128,256]{2,1,0:T(8,128)(2,1)S(1)} %add_convert_fusion.2), channel_id=1, source_target_pairs={{0,4},{4,0},{8,12},{12,8},{16,20},{20,16},{24,28},{28,24},{1,5},{5... | collective-permute-start | bytes 2359304 | tf_op jit(solution)/shard_map/ppermute | solution.py:412
  120.8 18.1 %collective-permute-start.29 = (bf16[12,128,256]{2,1,0:T(8,128)(2,1)S(1)}, bf16[12,128,256]{2,1,0:T(8,128)(2,1)S(1)}, u32[]{:S(2)}, u32[]{:S(2)}) collective-permute-start(bf16[12,128,256]{2,1,0:T(8,128)(2,1)S(1)} %add_convert_fusion.1), channel_id=1, source_target_pairs={{0,8},{4,12},{8,0},{12,4},{16,24},{20,28},{24,16},{28,20},{1,9},{5... | collective-permute-start | bytes 2359304 | tf_op jit(solution)/shard_map/ppermute | solution.py:412
  121.3 24.0 %collective-permute-start.22 = (bf16[4,128,1024]{2,1,0:T(8,128)(2,1)}, bf16[4,128,1024]{2,1,0:T(8,128)(2,1)}, u32[]{:S(2)}, u32[]{:S(2)}) collective-permute-start(bf16[4,128,1024]{2,1,0:T(8,128)(2,1)} %fusion), channel_id=1, source_target_pairs={{0,2},{1,3},{2,0},{3,1},{4,6},{5,7},{6,4},{7,5},{8,10},{9,11},{10,... | collective-permute-start | bytes 3145736 | tf_op jit(solution)/shard_map/ppermute | solution.py:1403
  122.8 35.4 %collective-permute-start.31 = (bf16[12,128,256]{2,1,0:T(8,128)(2,1)}, bf16[12,128,256]{2,1,0:T(8,128)(2,1)S(1)}, u32[]{:S(2)}, u32[]{:S(2)}) collective-permute-start(bf16[12,128,256]{2,1,0:T(8,128)(2,1)} %get-tuple-element.90), channel_id=1, source_target_pairs={{0,4},{4,0},{8,12},{12,8},{16,20},{20,16},{24,28},{28,24},{1,5},{5... | collective-permute-start | bytes 2359304 | tf_op jit(solution)/shard_map/ppermute | solution.py:412
  140.7 17.5 %collective-permute-start.26 = (bf16[12,128,256]{2,1,0:T(8,128)(2,1)}, bf16[12,128,256]{2,1,0:T(8,128)(2,1)}, u32[]{:S(2)}, u32[]{:S(2)}) collective-permute-start(bf16[12,128,256]{2,1,0:T(8,128)(2,1)} %get-tuple-element.123), channel_id=1, source_target_pairs={{0,8},{4,12},{8,0},{12,4},{16,24},{20,28},{24,16},{28,20},{1,9},{5... | collective-permute-start | bytes 2359304 | tf_op jit(solution)/shard_map/ppermute | solution.py:412
  141.5 16.7 %collective-permute-start.30 = (bf16[12,128,256]{2,1,0:T(8,128)(2,1)}, bf16[12,128,256]{2,1,0:T(8,128)(2,1)}, u32[]{:S(2)}, u32[]{:S(2)}) collective-permute-start(bf16[12,128,256]{2,1,0:T(8,128)(2,1)} %get-tuple-element.124), channel_id=1, source_target_pairs={{0,1},{1,0},{2,3},{3,2},{4,5},{5,4},{6,7},{7,6},{8,16},{9,17},{10,... | collective-permute-start | bytes 2359304 | tf_op jit(solution)/shard_map/ppermute | solution.py:412
  160.7 19.6 %collective-permute-start.27 = (bf16[12,128,256]{2,1,0:T(8,128)(2,1)S(1)}, bf16[12,128,256]{2,1,0:T(8,128)(2,1)S(1)}, u32[]{:S(2)}, u32[]{:S(2)}) collective-permute-start(bf16[12,128,256]{2,1,0:T(8,128)(2,1)S(1)} %get-tuple-element.120), channel_id=1, source_target_pairs={{0,4},{4,0},{8,12},{12,8},{16,20},{20,16},{24,28},{28,24},{1,5},{5... | collective-permute-start | bytes 2359304 | tf_op jit(solution)/shard_map/ppermute | solution.py:412
  162.0 18.3 %collective-permute-start.32 = (bf16[12,128,256]{2,1,0:T(8,128)(2,1)S(1)}, bf16[12,128,256]{2,1,0:T(8,128)(2,1)S(1)}, u32[]{:S(2)}, u32[]{:S(2)}) collective-permute-start(bf16[12,128,256]{2,1,0:T(8,128)(2,1)S(1)} %get-tuple-element.92), channel_id=1, source_target_pairs={{0,8},{4,12},{8,0},{12,4},{16,24},{20,28},{24,16},{28,20},{1,9},{5... | collective-permute-start | bytes 2359304 | tf_op jit(solution)/shard_map/ppermute | solution.py:412
  163.8 16.5 %collective-permute-start.33 = (bf16[12,128,256]{2,1,0:T(8,128)(2,1)S(1)}, bf16[12,128,256]{2,1,0:T(8,128)(2,1)S(1)}, u32[]{:S(2)}, u32[]{:S(2)}) collective-permute-start(bf16[12,128,256]{2,1,0:T(8,128)(2,1)S(1)} %get-tuple-element.93), channel_id=1, source_target_pairs={{0,1},{1,0},{2,3},{3,2},{4,5},{5,4},{6,7},{7,6},{8,16},{9,17},{10,... | collective-permute-start | bytes 2359304 | tf_op jit(solution)/shard_map/ppermute | solution.py:412
  163.8 9.2 %collective-permute-start.21 = (bf16[2,128,1024]{2,1,0:T(8,128)(2,1)S(1)}, bf16[2,128,1024]{2,1,0:T(8,128)(2,1)S(1)}, u32[]{:S(2)}, u32[]{:S(2)}) collective-permute-start(bf16[2,128,1024]{2,1,0:T(8,128)(2,1)S(1)} %copy-done.19), channel_id=1, source_target_pairs={{0,1},{1,0},{2,3},{3,2},{4,5},{5,4},{6,7},{7,6},{8,9},{9,8},{10,11... | collective-permute-start | bytes 1572872 | tf_op jit(solution)/shard_map/ppermute | solution.py:1404
  164.3 2.7 %collective-permute-start.34 = (f32[24,1152]{1,0:T(8,128)S(1)}, f32[24,1152]{1,0:T(8,128)S(1)}, u32[]{:S(2)}, u32[]{:S(2)}) collective-permute-start(f32[24,1152]{1,0:T(8,128)S(1)} %copy-done.32), channel_id=1, source_target_pairs={{0,1},{1,0},{2,3},{3,2},{4,5},{5,4},{6,7},{7,6},{8,9},{9,8},{10,11... | collective-permute-start | bytes 331784 | tf_op jit(solution)/shard_map/ppermute | solution.py:1470
  167.0 5.2 %collective-permute-start.35 = (f32[24,1152]{1,0:T(8,128)S(1)}, f32[24,1152]{1,0:T(8,128)S(1)}, u32[]{:S(2)}, u32[]{:S(2)}) collective-permute-start(f32[24,1152]{1,0:T(8,128)S(1)} %add.94), channel_id=1, source_target_pairs={{0,2},{1,3},{2,0},{3,1},{4,6},{5,7},{6,4},{7,5},{8,10},{9,11},{10,... | collective-permute-start | bytes 331784 | tf_op jit(solution)/shard_map/ppermute | solution.py:1471
  172.2 8.1 %collective-permute-start.36 = (f32[24,1152]{1,0:T(8,128)S(1)}, f32[24,1152]{1,0:T(8,128)S(1)}, u32[]{:S(2)}, u32[]{:S(2)}) collective-permute-start(f32[24,1152]{1,0:T(8,128)S(1)} %add.95), channel_id=1, source_target_pairs={{0,4},{4,0},{8,12},{12,8},{16,20},{20,16},{24,28},{28,24},{1,5},{5... | collective-permute-start | bytes 331784 | tf_op jit(solution)/shard_map/ppermute | solution.py:1472
  173.0 7.8 %collective-permute-start.23 = (bf16[128,1024]{1,0:T(8,128)(2,1)S(1)}, bf16[128,1024]{1,0:T(8,128)(2,1)S(1)}, u32[]{:S(2)}, u32[]{:S(2)}) collective-permute-start(bf16[128,1024]{1,0:T(8,128)(2,1)S(1)} %fusion.12), channel_id=1, source_target_pairs={{0,2},{1,3},{2,0},{3,1},{4,6},{5,7},{6,4},{7,5},{8,10},{9,11},{10,... | collective-permute-start | bytes 786440 | tf_op jit(solution)/shard_map/ppermute | solution.py:1406
  180.8 17.0 %collective-permute-start.37 = (bf16[12,128,256]{2,1,0:T(8,128)(2,1)S(1)}, bf16[12,128,256]{2,1,0:T(8,128)(2,1)S(1)}, u32[]{:S(2)}, u32[]{:S(2)}) collective-permute-start(bf16[12,128,256]{2,1,0:T(8,128)(2,1)S(1)} %add_convert_fusion.shard0), channel_id=1, source_target_pairs={{0,2},{1,3},{2,0},{3,1},{4,6},{5,7},{6,4},{7,5},{8,10},{9,11},{10,... | collective-permute-start | bytes 2359304 | tf_op jit(solution)/shard_map/ppermute | solution.py:1474
  182.3 5.0 %collective-permute-start.39 = (f32[24,1152]{1,0:T(8,128)S(1)}, f32[24,1152]{1,0:T(8,128)S(1)}, u32[]{:S(2)}, u32[]{:S(2)}) collective-permute-start(f32[24,1152]{1,0:T(8,128)S(1)} %add.96), channel_id=1, source_target_pairs={{0,8},{4,12},{8,0},{12,4},{16,24},{20,28},{24,16},{28,20},{1,9},{5... | collective-permute-start | bytes 331784 | tf_op jit(solution)/shard_map/ppermute | solution.py:1477
  187.3 6.9 %collective-permute-start.40 = (f32[24,1152]{1,0:T(8,128)S(1)}, f32[24,1152]{1,0:T(8,128)S(1)}, u32[]{:S(2)}, u32[]{:S(2)}) collective-permute-start(f32[24,1152]{1,0:T(8,128)S(1)} %add.97), channel_id=1, source_target_pairs={{0,16},{4,20},{8,24},{12,28},{16,0},{20,4},{24,8},{28,12},{1,17},{... | collective-permute-start | bytes 331784 | tf_op jit(solution)/shard_map/ppermute | solution.py:1477
  194.2 6.1 %collective-permute-start.38 = (bf16[12,128,256]{2,1,0:T(8,128)(2,1)S(1)}, bf16[12,128,256]{2,1,0:T(8,128)(2,1)S(1)}, u32[]{:S(2)}, u32[]{:S(2)}) collective-permute-start(bf16[12,128,256]{2,1,0:T(8,128)(2,1)S(1)} %add_convert_fusion.shard0), channel_id=1, source_target_pairs={{0,1},{1,0},{2,3},{3,2},{4,5},{5,4},{6,7},{7,6},{8,9},{9,8},{10,11... | collective-permute-start | bytes 2359304 | tf_op jit(solution)/shard_map/ppermute | solution.py:1475
  197.9 2.5 %collective-permute-start.41 = (bf16[12,128,256]{2,1,0:T(8,128)(2,1)S(1)}, bf16[12,128,256]{2,1,0:T(8,128)(2,1)S(1)}, u32[]{:S(2)}, u32[]{:S(2)}) collective-permute-start(bf16[12,128,256]{2,1,0:T(8,128)(2,1)S(1)} %collective-permute-done.37.shard1), channel_id=1, source_target_pairs={{0,1},{1,0},{2,3},{3,2},{4,5},{5,4},{6,7},{7,6},{8,9},{9,8},{10,11... | collective-permute-start | bytes 2359304 | tf_op jit(solution)/shard_map/ppermute | solution.py:1479
  197.9 2.4 %collective-permute-start.42 = (f32[24,1152]{1,0:T(8,128)S(1)}, f32[24,1152]{1,0:T(8,128)S(1)}, u32[]{:S(2)}, u32[]{:S(2)}) collective-permute-start(f32[24,1152]{1,0:T(8,128)S(1)} %add.98.small_own), channel_id=1, source_target_pairs={{0,1},{1,0},{2,3},{3,2},{4,5},{5,4},{6,7},{7,6},{8,9},{9,8},{10,11... | collective-permute-start | bytes 331784 | tf_op jit(solution)/shard_map/ppermute | solution.py:1478
  (30 other events, 446.6 us)
